TPU v7x, 512 devices: a whole 4x4x16 slice. The times are simulated.
512 devices in a mesh: dp: 128 (over z_lo, y, x, core), tensor: 4 (over z_hi).
Axes of the slice: x: 4, y: 4, z: 16 (z_hi: 4, z_lo: 4; z = z_hi * 4 + z_lo), core: 2. Of those that a mesh axis runs over, the one named last changes fastest.
Arguments:
- hidden_in: bfloat16 [16384, 2048], P('dp', 'tensor'), may hold values from -6 to 6
- lengths: int32 [128, 4], P('dp'), may hold values from 1 to 80, 128 in all within a row
- routes: int32 [16384, 6], P('dp'), may hold values from 0 to 63, all different within a row; in each aligned block of 128 rows (0 to 127, 128 to 255, ...) at most 14 rows name the same one
- gate_weights: bfloat16 [16384, 6], P('dp'), may hold values from 0.099609375 to 0.59765625
- norm_gain: float32 [2048], replicated, may hold values from 0.1 to 1.9
- latent_gain: float32 [512], replicated, may hold values from 0.1 to 1.9
- moe_gain: float32 [2048], replicated, may hold values from 0.1 to 1.9
- query_train: float32 [2048, 1536], P(('dp', 'tensor')), may hold values from -1 to 1
- latent_train: float32 [2048, 576], P(('dp', 'tensor')), may hold values from -1 to 1
- expand_train: float32 [512, 2048], P(('dp', 'tensor')), may hold values from -1 to 1
- output_train: float32 [2048, 1024], P(('dp', 'tensor')), may hold values from -0.1875 to 0.1875
- expert_gate: bfloat16 [128, 2048, 704], P('dp', None, 'tensor'), may hold values from -0.125 to 0.125
- expert_up: bfloat16 [128, 2048, 704], P('dp', None, 'tensor'), may hold values from -0.125 to 0.125
- expert_down: bfloat16 [128, 704, 2048], P('dp', None, 'tensor'), may hold values from -0.21875 to 0.21875
Outputs:
- hidden_out: bfloat16 [16384, 2048], P('dp', 'tensor')
- expand_server: bfloat16 [512, 2048], P(None, 'tensor')
- output_server: bfloat16 [2048, 1024], P(None, 'tensor')
- latent_cache: bfloat16 [16384, 576], P('dp', 'tensor')
Inputs may be any that keep to these rules, and one draw needn't show every extreme that they name: `lengths`: the prompts of each data group fill its 128 tokens; in every draw some prompt has exactly 80 tokens. `routes`: A token names 6 different experts; within the 128 rows of one data group no expert is named by more than 14 tokens, and in every draw some expert is named by exactly 14.
All inputs are finite; a program needn't handle non-finite values.
Results may differ from a plain program's by a relative error of at most 0.02.
Values may be sent and summed in bfloat16 or wider, within the bound.
No kernel may reach another device: no remote copies, remote signals or barrier semaphores. Data moves between devices by JAX's collectives and lax.ppermute only.
A program may use at most 64 MiB of HBM per device.

v0:
```python
import math

import jax
import jax.numpy as jnp
from jax import lax
from jax.sharding import PartitionSpec as P

D = 2048
NOPE = 128
ROPE = 64
VDIM = 128
LATENT = 512
EXPERTS = 64
CAP = 14


rope_base = 50000.0


def rms_norm(values, gain_vector):
    mean_square = jnp.mean(values * values, axis=-1, keepdims=True)
    return values * lax.rsqrt(mean_square + 1e-06) * gain_vector


def rotate(values, positions):
    half_width = values.shape[-1] // 2
    frequency = jnp.exp(
        jnp.arange(half_width, dtype=jnp.float32) * (-2.0 * math.log(rope_base) / values.shape[-1])
    )
    angles = positions.astype(jnp.float32)[:, None] * frequency[None, :]
    if values.ndim == 3:
        angles = angles[:, None, :]
    cosine = jnp.cos(angles)
    sine = jnp.sin(angles)
    first_half = values[..., :half_width]
    second_half = values[..., half_width:]
    return jnp.concatenate(
        [first_half * cosine - second_half * sine, second_half * cosine + first_half * sine],
        axis=-1,
    )


def positions_of(lengths, row_count):
    prompt_ends = jnp.cumsum(lengths, axis=1)
    starts = prompt_ends - lengths
    token_index = jnp.arange(row_count, dtype=jnp.int32)
    segment = jnp.sum(
        (token_index[None, :, None] >= prompt_ends[:, None, :]).astype(jnp.int32), axis=2
    )
    member = segment[:, :, None] == jnp.arange(lengths.shape[1], dtype=jnp.int32)[None, None, :]
    offset = jnp.sum(jnp.where(member, starts[:, None, :], 0), axis=2)
    return (segment, token_index[None, :] - offset)


def expert_ranks(route_groups):
    onehot = (route_groups[..., None] == jnp.arange(EXPERTS, dtype=jnp.int32)).astype(jnp.int32)
    per_token = jnp.sum(onehot, axis=2)
    before = jnp.cumsum(per_token, axis=1) - per_token
    return jnp.sum(onehot * before[:, :, None, :], axis=3)


def body(
    hidden_in,
    lengths,
    routes,
    gate_weights,
    norm_gain,
    latent_gain,
    moe_gain,
    query_train,
    latent_train,
    expand_train,
    output_train,
    expert_gate,
    expert_up,
    expert_down,
):
    shards = (
        query_train.astype(jnp.bfloat16),
        latent_train.astype(jnp.bfloat16),
        expand_train.astype(jnp.bfloat16),
        output_train.astype(jnp.bfloat16),
    )
    regrouped = (
        lax.all_to_all(shards[0], "tensor", split_axis=1, concat_axis=0, tiled=True),
        lax.all_to_all(shards[1], "tensor", split_axis=1, concat_axis=0, tiled=True),
        lax.all_to_all(shards[2], "tensor", split_axis=1, concat_axis=0, tiled=True),
        lax.all_to_all(shards[3], "tensor", split_axis=1, concat_axis=0, tiled=True),
    )
    query_block, latent_block, expand_block, output_block = (
        lax.all_gather(regrouped[0], "dp", axis=0, tiled=True),
        lax.all_gather(regrouped[1], "dp", axis=0, tiled=True),
        lax.all_gather(regrouped[2], "dp", axis=0, tiled=True),
        lax.all_gather(regrouped[3], "dp", axis=0, tiled=True),
    )
    token_count = hidden_in.shape[0]
    tensor_rank = lax.axis_index("tensor")
    full_input = lax.all_gather(hidden_in, "tensor", axis=1, tiled=True)
    normed = rms_norm(full_input.astype(jnp.float32), norm_gain).astype(jnp.bfloat16)
    query = jnp.dot(normed, query_block, preferred_element_type=jnp.float32).reshape(
        token_count, -1, NOPE + ROPE
    )
    latent_part = jnp.dot(normed, latent_block, preferred_element_type=jnp.float32).astype(
        jnp.bfloat16
    )
    compressed = lax.all_gather(latent_part, "tensor", axis=1, tiled=True)
    segment, position = positions_of(lengths, token_count)
    segment = segment[0]
    position = position[0]
    latent_normed = rms_norm(compressed[:, :LATENT].astype(jnp.float32), latent_gain).astype(
        jnp.bfloat16
    )
    key_rope = rotate(compressed[:, LATENT:].astype(jnp.float32), position).astype(jnp.bfloat16)
    cache_full = jnp.concatenate([latent_normed, key_rope], axis=1)
    cache_width = latent_part.shape[1]
    cache_cols = lax.dynamic_slice_in_dim(cache_full, tensor_rank * cache_width, cache_width, 1)
    expanded = jnp.dot(latent_normed, expand_block, preferred_element_type=jnp.float32).astype(
        jnp.bfloat16
    )
    expanded = expanded.reshape(token_count, -1, NOPE + VDIM)
    query_nope = query[..., :NOPE].astype(jnp.bfloat16)
    query_rope = rotate(query[..., NOPE:], position).astype(jnp.bfloat16)
    scores = jnp.einsum(
        "qhd,khd->hqk", query_nope, expanded[..., :NOPE], preferred_element_type=jnp.float32
    )
    scores = scores + jnp.einsum(
        "qhd,kd->hqk", query_rope, key_rope, preferred_element_type=jnp.float32
    )
    scores = scores * (1.0 / math.sqrt(NOPE + ROPE))
    token_index = jnp.arange(token_count, dtype=jnp.int32)
    allowed = (segment[:, None] == segment[None, :]) & (
        token_index[None, :] <= token_index[:, None]
    )
    scores = jnp.where(allowed[None], scores, -1e30)
    largest = jnp.max(scores, axis=-1, keepdims=True)
    powers = jnp.exp(scores - largest)
    probs = (powers / jnp.sum(powers, axis=-1, keepdims=True)).astype(jnp.bfloat16)
    attended = jnp.einsum(
        "hqk,khd->qhd", probs, expanded[..., NOPE:], preferred_element_type=jnp.float32
    )
    attended = attended.astype(jnp.bfloat16).reshape(token_count, -1)
    head_terms = lax.dot_general(
        attended, output_block, (((1,), (1,)), ((), ())), preferred_element_type=jnp.float32
    )
    head_total = lax.psum_scatter(
        head_terms.astype(jnp.bfloat16), "tensor", scatter_dimension=1, tiled=True
    ).astype(jnp.float32)
    mixed_cols = (hidden_in.astype(jnp.float32) + head_total).astype(jnp.bfloat16)
    mixed_full = lax.all_gather(mixed_cols, "tensor", axis=1, tiled=True)
    moe_in = rms_norm(mixed_full.astype(jnp.float32), moe_gain).astype(jnp.bfloat16)
    slot_rank = expert_ranks(routes[None])[0]
    slot_index = routes * CAP + slot_rank
    slot_ids = jnp.arange(EXPERTS * CAP, dtype=jnp.int32)
    matches = slot_index[None, :, :] == slot_ids[:, None, None]
    dispatch_matrix = jnp.sum(matches.astype(jnp.float32), axis=2).astype(jnp.bfloat16)
    combine_matrix = jnp.sum(
        jnp.where(matches, gate_weights.astype(jnp.float32)[None], 0.0), axis=2
    ).T.astype(jnp.bfloat16)
    out_width = mixed_cols.shape[1]
    outgoing = jnp.dot(dispatch_matrix, moe_in, preferred_element_type=jnp.float32).astype(
        jnp.bfloat16
    )
    doubled = jnp.broadcast_to(outgoing.reshape(EXPERTS, 1, CAP, D), (EXPERTS, 2, CAP, D)).reshape(
        2 * EXPERTS, CAP, D
    )
    received = lax.all_to_all(doubled, "dp", split_axis=0, concat_axis=1, tiled=True)
    gate_part = jnp.einsum(
        "srd,sdf->srf", received, expert_gate, preferred_element_type=jnp.float32
    )
    up_part = jnp.einsum("srd,sdf->srf", received, expert_up, preferred_element_type=jnp.float32)
    hidden_part = (jax.nn.silu(gate_part) * up_part).astype(jnp.bfloat16)
    hidden_full = lax.all_gather(hidden_part, "tensor", axis=2, tiled=True)
    half_out = jnp.einsum(
        "srf,sfd->srd", hidden_full, expert_down, preferred_element_type=jnp.float32
    ).astype(jnp.bfloat16)
    returned = lax.all_to_all(half_out, "dp", split_axis=1, concat_axis=0, tiled=True)
    returned = returned.reshape(EXPERTS, 2, CAP, out_width)
    first_half = returned[:, 0].reshape(EXPERTS * CAP, out_width)
    second_half = returned[:, 1].reshape(EXPERTS * CAP, out_width)
    expert_sum = jnp.dot(combine_matrix, first_half, preferred_element_type=jnp.float32)
    expert_sum = expert_sum + jnp.dot(
        combine_matrix, second_half, preferred_element_type=jnp.float32
    )
    hidden_out = (mixed_cols.astype(jnp.float32) + expert_sum).astype(jnp.bfloat16)
    return (hidden_out, expand_block, output_block, cache_cols)


def solution(mesh):
    in_specs = (
        P("dp", "tensor"),
        P("dp", None),
        P("dp", None),
        P("dp", None),
        P(),
        P(),
        P(),
        P(("dp", "tensor"), None),
        P(("dp", "tensor"), None),
        P(("dp", "tensor"), None),
        P(("dp", "tensor"), None),
        P("dp", None, "tensor"),
        P("dp", None, "tensor"),
        P("dp", None, "tensor"),
    )
    out_specs = (P("dp", "tensor"), P(None, "tensor"), P(None, "tensor"), P("dp", "tensor"))
    return jax.shard_map(body, mesh=mesh, in_specs=in_specs, out_specs=out_specs, check_vma=False)
```

profile of v0, /device:TPU:1, one launch (start us, length us, event | category | flops | bytes accessed | tf_op | source)
XLA Modules:
  0.0 1221.2 jit_solution(1057019033618953464)
XLA Ops:
  7.2 0.8 convert_element_type.137
  8.0 26.9 %all_to_all.91 = bf16[4,4,384]{2,0,1:T(4,128)(2,1)S(1)} all-to-all(bf16[4,4,384]{2,0,1:T(4,128)(2,1)S(1)} %bitcast.64), channel_id=1, replica_groups=mesh['dp'=128,'tensor'=4] {'tensor'}, dimensions={1} | all-to-all | bytes 24576 | tf_op jit(solution)/shard_map/all_to_all | solution.py:85
  34.9 0.6 all_to_all.78
  35.6 0.7 convert_element_type.134
  37.4 0.6 reshape.376
  38.0 3.4 all-to-all-start.1
  41.4 0.8 reduce_window_sum.22
  42.3 0.7 subtract_bitcast_fusion
  43.1 25.9 %all_gather.24 = bf16[128,2048]{1,0:T(8,128)(2,1)S(1)} all-gather(bf16[128,512]{1,0:T(8,128)(2,1)} %param.14), channel_id=1, replica_groups=mesh['dp'=128,'tensor'=4] {'tensor'}, dimensions={1}, use_global_device_ids=true | all-gather | bytes 655360 | tf_op jit(solution)/shard_map/all_gather | solution.py:98
  69.3 0.7 convert_element_type.130
  70.1 0.6 copy.75
  70.7 1.3 convert_element_type.143
  72.0 6.9 all-to-all-start
  78.9 196.1 %all-gather = bf16[1,512,512]{2,0,1:T(2,128)(2,1)S(1)} all-gather(bf16[1,4,512]{2,0,1:T(2,128)(2,1)S(1)} %bitcast.65), channel_id=2, replica_groups=mesh['dp'=128,'tensor'=4] {'dp'}, dimensions={1}, use_global_device_ids=true | all-gather | bytes 528384 | tf_op jit(solution)/shard_map/all_gather | solution.py:93
  275.1 11.7 all-to-all-start.3
  286.8 182.8 %all_gather.25 = bf16[2048,144]{1,0:T(8,128)(2,1)S(1)} all-gather(bf16[16,144]{1,0:T(8,128)(2,1)S(1)} %all_to_all.71), channel_id=1, replica_groups=mesh['dp'=128,'tensor'=4] {'dp'}, dimensions={0}, use_global_device_ids=true | all-gather | bytes 594432 | tf_op jit(solution)/shard_map/all_gather | solution.py:92
  470.1 20.2 %all_gather.26 = bf16[128,576]{0,1:T(8,128)(2,1)S(1)} all-gather(bf16[128,144]{0,1:T(8,128)(2,1)S(1)} %convolution_convert_fusion.5), channel_id=1, replica_groups=mesh['dp'=128,'tensor'=4] {'tensor'}, dimensions={1}, use_global_device_ids=true | all-gather | bytes 184320 | tf_op jit(solution)/shard_map/all_gather | solution.py:106
  490.5 0.6 all_to_all.82
  491.8 2.2 fusion.26
  494.7 189.3 %all-gather.8.cloned.1.call-done = bf16[2048,256]{1,0:T(8,128)(2,1)} async-done(((bf16[16,256]{1,0:T(8,128)(2,1)}), bf16[2048,256]{1,0:T(8,128)(2,1)}) %all-gather.8.cloned.1.call-update) | async-done | bytes 1048592 | tf_op jit(solution)/shard_map/all_gather | solution.py:94
  684.0 2.5 convolution_convert_fusion.2
  687.6 42.3 %reduce-scatter.2.cloned.1.call-done = bf16[128,512]{1,0:T(8,128)(2,1)} async-done(((bf16[128,2048]{1,0:T(8,128)(2,1)}), bf16[128,512]{1,0:T(8,128)(2,1)}) %reduce-scatter.2.cloned.1.call-update) | async-done | bytes 131088 | tf_op jit(solution)/shard_map/reduce_scatter | solution.py:145
  729.9 0.9 add_convert_fusion
  730.9 24.6 %all_gather.30 = bf16[128,2048]{1,0:T(8,128)(2,1)S(1)} all-gather(bf16[128,512]{1,0:T(8,128)(2,1)S(1)} %add_convert_fusion), channel_id=1, replica_groups=mesh['dp'=128,'tensor'=4] {'tensor'}, dimensions={1}, use_global_device_ids=true | all-gather | bytes 655360 | tf_op jit(solution)/shard_map/all_gather | solution.py:149
  755.7 3.0 convolution_convert_fusion
  758.7 5.9 broadcast_in_dim.45
  764.5 6.8 broadcast_in_dim.46
  771.3 200.5 %all_to_all.92 = bf16[128,14,2048]{2,1,0:T(8,128)(2,1)} all-to-all(bf16[128,14,2048]{2,1,0:T(8,128)(2,1)} %bitcast.56), channel_id=1, replica_groups=mesh['dp'=128,'tensor'=4] {'dp'}, dimensions={0} | all-to-all | bytes 14680064 | tf_op jit(solution)/shard_map/all_to_all | solution.py:166
  971.8 10.9 reshape.365
  982.8 5.8 fusion.17
  988.6 3.5 fusion.2
  992.1 102.5 %all-gather.10.cloned.1.call-done = bf16[1792,704]{0,1:T(8,128)(2,1)} async-done(((bf16[1792,176]{0,1:T(8,128)(2,1)}), bf16[1792,704]{0,1:T(8,128)(2,1)}) %all-gather.10.cloned.1.call-update) | async-done | bytes 2523152 | tf_op jit(solution)/shard_map/all_gather | solution.py:172
  1094.7 3.3 fusion.1
  1098.0 16.3 %copy.101 = bf16[1,1792,512]{2,0,1:T(2,128)(2,1)} copy(bf16[1,1792,512]{2,1,0:T(8,128)(2,1)S(1)} %fusion.1) | data formatting | bytes 3670016 | tf_op jit(solution)/shard_map/convert_element_type | solution.py:175
  1114.3 12.4 %reduce.7 = bf16[1792,512]{1,0:T(8,128)(2,1)S(1)} reduce(bf16[1792,1,512]{2,1,0:T(2,128)(2,1)} %bitcast.57, bf16[]{:T(256)} %broadcast.237), dimensions={1}, to_apply=%bitcast.55.reduce_sub_computation | reduce | bytes 3670018
  1126.8 1.9 reshape.378
  1128.6 10.3 all-to-all-start.5
  1139.0 0.8 fusion.37
  1139.8 45.6 %all-to-all-done.5 = bf16[128,2,3584]{2,1,0:T(2,128)(2,1)S(1)} async-done(((bf16[128,2,3584]{2,1,0:T(2,128)(2,1)}), bf16[128,2,3584]{2,1,0:T(2,128)(2,1)S(1)}, u32[]{:S(2)}, u32[]{:S(2)}) %all-to-all-start.5) | async-done | bytes 1835040 | tf_op jit(solution)/shard_map/all_to_all | solution.py:176
  1185.4 4.0 reshape.379
  1189.3 13.2 %bitcast_reduce_fusion = bf16[1792,512]{1,0:T(8,128)(2,1)} fusion(bf16[1792,1,512]{2,1,0:T(2,128)(2,1)} %reshape.379), kind=kLoop, calls=%fused_computation.94 | loop fusion | bytes 3670016 | tf_op jit(solution)/shard_map/all_to_all | solution.py:176
  1202.5 2.5 reshape.370
  1205.0 1.5 fusion.45
  1206.6 2.3 reshape_squeeze.7
  1208.8 1.2 reshape_squeeze.6
  1210.0 1.5 fusion.48
  1211.5 2.2 fusion.5
  1213.7 1.0 copy.103
  (76 shorter events, 5.2 us)
Async XLA Ops:
  7.2 1087.5 %copy-start = (bf16[1,704,512]{2,1,0:T(8,128)(2,1)S(1)}, bf16[1,704,512]{2,1,0:T(8,128)(2,1)}, u32[]{:S(2)}) copy-start(bf16[1,704,512]{2,1,0:T(8,128)(2,1)} %param.27) | copy-start | bytes 2162692
  7.2 484.6 %all-gather.6.cloned.1.call-start = ((), (), s32[]{:S(2)}) async-start(), calls=%async_computation.7 | async-start | bytes 1585152 | tf_op jit(solution)/shard_map/all_gather | solution.py:91
  38.0 431.6 %copy-start.7 = (f32[2048]{0:T(1024)S(1)}, f32[2048]{0:T(1024)}, u32[]{:S(2)}) copy-start(f32[2048]{0:T(1024)} %param.18) | copy-start | bytes 24580
  38.0 34.0 %all-to-all-start.1 = ((bf16[4,2,256]{2,1,0:T(2,128)(2,1)}), bf16[4,2,256]{2,1,0:T(2,128)(2,1)S(1)}, u32[]{:S(2)}, u32[]{:S(2)}) async-start(bf16[4,2,256]{2,1,0:T(2,128)(2,1)} %reshape.376), calls=%async_computation.1 | async-start | bytes 8192 | tf_op jit(solution)/shard_map/all_to_all | solution.py:87
  72.0 203.1 %all-to-all-start = ((bf16[4,4,144]{2,0,1:T(4,128)(2,1)}), bf16[4,4,144]{2,0,1:T(4,128)(2,1)S(1)}, u32[]{:S(2)}, u32[]{:S(2)}) async-start(bf16[4,4,144]{2,0,1:T(4,128)(2,1)} %copy.75), calls=%async_computation | async-start | bytes 16384 | tf_op jit(solution)/shard_map/all_to_all | solution.py:86
  275.0 215.4 %copy-start.9 = (f32[512]{0:T(512)S(1)}, f32[512]{0:T(512)}, u32[]{:S(2)}) copy-start(f32[512]{0:T(512)} %param.19) | copy-start | bytes 6148
  275.1 218.9 %copy-start.4 = (bf16[1,512,512]{2,1,0:T(8,128)(2,1)}, bf16[1,512,512]{2,1,0:T(8,128)(2,1)S(1)}, u32[]{:S(2)}) copy-start(bf16[1,512,512]{2,1,0:T(8,128)(2,1)S(1)} %copy.100) | copy-start | bytes 1572868
  275.1 215.4 %all-to-all-start.3 = ((bf16[4,4,256]{2,0,1:T(4,128)(2,1)}), bf16[4,4,256]{2,0,1:T(4,128)(2,1)S(1)}, u32[]{:S(2)}, u32[]{:S(2)}) async-start(bf16[4,4,256]{2,0,1:T(4,128)(2,1)} %bitcast.11), calls=%async_computation.3 | async-start | bytes 16384 | tf_op jit(solution)/shard_map/all_to_all | solution.py:88
  286.8 397.2 %all-gather.8.cloned.1.call-start = ((), (), s32[]{:S(2)}) async-start(), calls=%async_computation.8 | async-start | bytes 1056768 | tf_op jit(solution)/shard_map/all_gather | solution.py:94
  491.2 238.8 %reduce-scatter.2.cloned.1.call-start = ((), (), s32[]{:S(2)}) async-start(), calls=%async_computation.9 | async-start | bytes 655360 | tf_op jit(solution)/shard_map/reduce_scatter | solution.py:145
  491.8 194.8 %copy-start.10 = (bf16[128,6]{0,1:T(8,128)(2,1)S(1)}, bf16[128,6]{0,1:T(8,128)(2,1)}, u32[]{:S(2)}) copy-start(bf16[128,6]{0,1:T(8,128)(2,1)} %param.17) | copy-start | bytes 4612
  491.8 194.8 %copy-start.6 = (s32[128,6]{0,1:T(8,128)S(1)}, s32[128,6]{0,1:T(8,128)}, u32[]{:S(2)}) copy-start(s32[128,6]{0,1:T(8,128)} %param.16) | copy-start | bytes 9220
  494.0 235.9 %copy-start.5 = (bf16[128,512]{1,0:T(8,128)(2,1)S(1)}, bf16[128,512]{1,0:T(8,128)(2,1)}, u32[]{:S(2)}) copy-start(bf16[128,512]{1,0:T(8,128)(2,1)} %param.14) | copy-start | bytes 393220
  494.7 261.0 %copy-start.8 = (f32[2048]{0:T(1024)S(1)}, f32[2048]{0:T(1024)}, u32[]{:S(2)}) copy-start(f32[2048]{0:T(1024)} %param.20) | copy-start | bytes 24580
  686.5 408.2 %all-gather.10.cloned.1.call-start = ((), (), s32[]{:S(2)}) async-start(), calls=%async_computation.10 | async-start | bytes 3153920 | tf_op jit(solution)/shard_map/all_gather | solution.py:172
  971.8 10.9 copy-start.11
  982.8 5.8 copy-start.1
  982.8 5.8 copy-start.12
  1128.6 56.7 %all-to-all-start.5 = ((bf16[128,2,3584]{2,1,0:T(2,128)(2,1)}), bf16[128,2,3584]{2,1,0:T(2,128)(2,1)S(1)}, u32[]{:S(2)}, u32[]{:S(2)}) async-start(bf16[128,2,3584]{2,1,0:T(2,128)(2,1)} %reshape.378), calls=%async_computation.6 | async-start | bytes 3670016 | tf_op jit(solution)/shard_map/all_to_all | solution.py:176
  1206.6 2.3 copy-start.3
  1208.8 4.9 copy-start.2
Sparse Core Ops, SparseCore 0:
  35.7 195.8 all-gather.5
  491.3 192.6 all-gather.7
  687.4 42.5 reduce-scatter.1
  992.3 102.3 all-gather.9
where the time goes:
time: 1220 us
  blocking collectives  677 us (55%)
  waiting for transfers between devices  380 us (31%)
  local copies, waits for them, and re-layouts  70.9 us (6%)
  starting transfers between devices  32.4 us (3%)
  matrix products  25.3 us (2%)
  other arithmetic  21.8 us (2%)
  between operations  14.1 us (1%)
    all_to_all x1, blocking collectives, body(): lax.all_to_all(doubled, 'dp', split_axis=0, concat_axis=1, tiled=True)  201 us
    all_gather x1, blocking collectives, body(): lax.all_gather(regrouped[2], 'dp', axis=0, tiled=True)  196 us
    all_gather x1, waiting for transfers between devices, body(): lax.all_gather(regrouped[3], 'dp', axis=0, tiled=True)  189 us
    all_gather x1, blocking collectives, body(): lax.all_gather(regrouped[1], 'dp', axis=0, tiled=True)  183 us
    all_gather x1, waiting for transfers between devices, body(): hidden_full = lax.all_gather(hidden_part, 'tensor', axis=2, tiled=True)  103 us
    all_to_all x1, waiting for transfers between devices, body(): lax.all_to_all(half_out, 'dp', split_axis=1, concat_axis=0, tiled=True)  45.6 us
    reduce_scatter x1, waiting for transfers between devices, body(): lax.psum_scatter(head_terms.astype(jnp.bfloat16), 'tensor', scatter_dimen...  42.3 us
    all_to_all x1, blocking collectives, body(): lax.all_to_all(shards[0], 'tensor', split_axis=1, concat_axis=0, tiled=True)  26.9 us
  transfers between devices with their start and end apart: 8, of which 4 were waited for; matrix products, arithmetic and copies ran while one was open for 1% of the time, Pallas kernels for 0%

commit v1 on v0

v1 whole, which is shorter than its diff:
```python
import math

import jax
import jax.numpy as jnp
from jax import lax
from jax.experimental import pallas as pl
from jax.experimental.pallas import tpu as pltpu
from jax.sharding import Mesh
from jax.sharding import PartitionSpec as P

D = 2048
NOPE = 128
ROPE = 64
VDIM = 128
LATENT = 512
EXPERTS = 64
CAP = 14
TOK = 128
CHUNKS = 2
SLOTS = CAP // CHUNKS
ROWS = 8

DP = ("zl", "y", "x", "c")
T = "t"
BF = jnp.bfloat16
F32 = jnp.float32

QW = 384
EW = 128
LW = 576
OW = 1024
SET1 = QW + EW + LW

rope_base = 50000.0


def rms_norm(values, gain_vector):
    mean_square = jnp.mean(values * values, axis=-1, keepdims=True)
    return values * lax.rsqrt(mean_square + 1e-06) * gain_vector


def rotate(values, positions):
    half_width = values.shape[-1] // 2
    frequency = jnp.exp(
        jnp.arange(half_width, dtype=F32) * (-2.0 * math.log(rope_base) / values.shape[-1])
    )
    angles = positions.astype(F32)[:, None] * frequency[None, :]
    if values.ndim == 3:
        angles = angles[:, None, :]
    cosine = jnp.cos(angles)
    sine = jnp.sin(angles)
    first_half = values[..., :half_width]
    second_half = values[..., half_width:]
    return jnp.concatenate(
        [first_half * cosine - second_half * sine, second_half * cosine + first_half * sine],
        axis=-1,
    )


def positions_of(lengths, row_count):
    prompt_ends = jnp.cumsum(lengths, axis=1)
    starts = prompt_ends - lengths
    token_index = jnp.arange(row_count, dtype=jnp.int32)
    segment = jnp.sum(
        (token_index[None, :, None] >= prompt_ends[:, None, :]).astype(jnp.int32), axis=2
    )
    member = segment[:, :, None] == jnp.arange(lengths.shape[1], dtype=jnp.int32)[None, None, :]
    offset = jnp.sum(jnp.where(member, starts[:, None, :], 0), axis=2)
    return (segment, token_index[None, :] - offset)


def expert_ranks(routes):
    onehot = (routes[..., None] == jnp.arange(EXPERTS, dtype=jnp.int32)).astype(BF)
    per_token = jnp.sum(onehot, axis=1)
    index = jnp.arange(TOK, dtype=jnp.int32)
    earlier = (index[None, :] < index[:, None]).astype(BF)
    before = jnp.dot(earlier, per_token, preferred_element_type=F32)
    return jnp.sum(onehot.astype(F32) * before[:, None, :], axis=2).astype(jnp.int32)


def shifted(block, axis):
    return [block] + [
        lax.ppermute(block, axis, [(j, (j + s) % 4) for j in range(4)]) for s in range(1, 4)
    ]


def other_core(block):
    return lax.ppermute(block, "c", [(0, 1), (1, 0)])


def ordered(place, mine, theirs, widths):
    total = sum(widths)

    def kernel(place_ref, mine_ref, theirs_ref, *out_refs):
        zl, y, x, c = place_ref[0], place_ref[1], place_ref[2], place_ref[3]

        def step(i, carry):
            row_zl, row_y, row_x = i // 16, (i // 4) % 4, i % 4
            source = ((x - row_x + 4) % 4 * 4 + (y - row_y + 4) % 4) * 4 + (zl - row_zl + 4) % 4
            for ref, core in ((mine_ref, c), (theirs_ref, 1 - c)):
                at = 0
                for out_ref, width in zip(out_refs, widths):
                    out_ref[i * 2 + core] = ref[source, :, at : at + width]
                    at += width
            return carry

        lax.fori_loop(0, 64, step, 0)

    vmem = pl.BlockSpec(memory_space=pltpu.VMEM)
    outs = pl.pallas_call(
        kernel,
        out_shape=[jax.ShapeDtypeStruct((128, 16, w), BF) for w in widths],
        in_specs=[pl.BlockSpec(memory_space=pltpu.SMEM), vmem, vmem],
        out_specs=[vmem for _ in widths],
        name="ordered",
    )(place, mine.reshape(64, 16, total), theirs.reshape(64, 16, total))
    return [o.reshape(2048, w) for o, w in zip(outs, widths)]


def body(
    hidden_in,
    lengths,
    routes,
    gate_weights,
    norm_gain,
    latent_gain,
    moe_gain,
    query_train,
    latent_train,
    expand_train,
    output_train,
    expert_gate,
    expert_up,
    expert_down,
):
    rank = lax.axis_index(T)
    core = lax.axis_index("c")
    place = jnp.stack([lax.axis_index(a) for a in DP]).astype(jnp.int32)

    packed = jnp.concatenate(
        [
            query_train.reshape(4, 4, QW).transpose(1, 0, 2),
            expand_train.reshape(4, 4, EW),
            jnp.broadcast_to(latent_train[None], (4, 4, LW)),
            jnp.broadcast_to(output_train[None], (4, 4, OW)),
        ],
        axis=2,
    ).astype(BF)
    packed = lax.all_to_all(packed, T, split_axis=0, concat_axis=0, tiled=True)
    packed = packed.reshape(16, SET1 + OW)
    gathered = jnp.stack(shifted(packed, "zl"))
    gathered = jnp.stack(shifted(gathered, "y"))
    first_set = gathered[..., :SET1]
    second_set = gathered[..., SET1:]
    first_parts = shifted(first_set, "x")
    hidden_gated, _ = lax.optimization_barrier((hidden_in, first_set))
    full_input = lax.all_gather(hidden_gated, T, axis=1, tiled=True)
    first_mine = jnp.stack(first_parts)
    query_block, expand_rows, latent_full = ordered(
        place, first_mine, other_core(first_mine), (QW, EW, LW)
    )
    second_gated, _ = lax.optimization_barrier((second_set, first_mine))
    second_mine = jnp.stack(shifted(second_gated, "x"))
    (output_full,) = ordered(place, second_mine, other_core(second_mine), (OW,))
    expand_block = expand_rows.reshape(LATENT, LATENT)
    output_block = lax.dynamic_slice_in_dim(output_full, rank * 256, 256, 1)

    token_count = TOK
    normed = rms_norm(full_input.astype(F32), norm_gain).astype(BF)
    query = jnp.dot(normed, query_block, preferred_element_type=F32).reshape(
        token_count, -1, NOPE + ROPE
    )
    compressed = jnp.dot(normed, latent_full, preferred_element_type=F32).astype(BF)
    segment, position = positions_of(lengths, token_count)
    segment = segment[0]
    position = position[0]
    latent_normed = rms_norm(compressed[:, :LATENT].astype(F32), latent_gain).astype(BF)
    key_rope = rotate(compressed[:, LATENT:].astype(F32), position).astype(BF)
    cache_full = jnp.concatenate([latent_normed, key_rope], axis=1)
    cache_cols = lax.dynamic_slice_in_dim(cache_full, rank * 144, 144, 1)
    expanded = jnp.dot(latent_normed, expand_block, preferred_element_type=F32).astype(BF)
    expanded = expanded.reshape(token_count, -1, NOPE + VDIM)
    query_nope = query[..., :NOPE].astype(BF)
    query_rope = rotate(query[..., NOPE:], position).astype(BF)
    scores = jnp.einsum("qhd,khd->hqk", query_nope, expanded[..., :NOPE], preferred_element_type=F32)
    scores = scores + jnp.einsum("qhd,kd->hqk", query_rope, key_rope, preferred_element_type=F32)
    scores = scores * (1.0 / math.sqrt(NOPE + ROPE))
    token_index = jnp.arange(token_count, dtype=jnp.int32)
    allowed = (segment[:, None] == segment[None, :]) & (token_index[None, :] <= token_index[:, None])
    scores = jnp.where(allowed[None], scores, -1e30)
    largest = jnp.max(scores, axis=-1, keepdims=True)
    powers = jnp.exp(scores - largest)
    probs = (powers / jnp.sum(powers, axis=-1, keepdims=True)).astype(BF)
    attended = jnp.einsum("hqk,khd->qhd", probs, expanded[..., NOPE:], preferred_element_type=F32)
    attended = attended.astype(BF).reshape(token_count, -1)
    attended_full = lax.all_gather(attended, T, axis=1, tiled=True)
    head_total = lax.dot_general(
        attended_full, output_full, (((1,), (1,)), ((), ())), preferred_element_type=F32
    )
    mixed_full = (full_input.astype(F32) + head_total).astype(BF)
    mixed_cols = lax.dynamic_slice_in_dim(mixed_full, rank * 512, 512, 1)
    moe_in = rms_norm(mixed_full.astype(F32), moe_gain).astype(BF)

    slot_rank = expert_ranks(routes)
    row_ids = jnp.arange(EXPERTS * 2 * ROWS, dtype=jnp.int32)
    row_core = (row_ids // ROWS) % 2
    moe_halves = jnp.concatenate([moe_in[:, : D // 2], moe_in[:, D // 2 :]], axis=0)
    gates = gate_weights.astype(F32)
    compact = jnp.arange(TOK * SLOTS, dtype=jnp.int32)
    spread = (compact // SLOTS) * ROWS + compact % SLOTS
    squeeze = (jnp.arange(TOK * ROWS, dtype=jnp.int32)[:, None] == spread[None, :]).astype(BF)
    gate_mat = expert_gate[0]
    up_mat = expert_up[0]
    mine_at = core * (D // 2)
    other_at = (1 - core) * (D // 2)

    def halves(matrix):
        return (
            lax.dynamic_slice_in_dim(matrix, mine_at, D // 2, 0),
            lax.dynamic_slice_in_dim(matrix, other_at, D // 2, 0),
        )

    gate_mine, gate_other = halves(gate_mat)
    up_mine, up_other = halves(up_mat)

    def rows_by(weight, rows):
        return lax.dot_general(weight, rows, (((0,), (1,)), ((), ())), preferred_element_type=F32)

    hidden_chunks = []
    combine = []
    gate_on = None
    for k in range(CHUNKS):
        in_chunk = (slot_rank >= k * SLOTS) & (slot_rank < (k + 1) * SLOTS)
        target = jnp.where(in_chunk, routes * (2 * ROWS) + (slot_rank - k * SLOTS), -1)
        matches = (row_ids - row_core * ROWS)[:, None, None] == target[None, :, :]
        picked = jnp.sum(matches.astype(F32), axis=2)
        dispatch = jnp.concatenate(
            [
                jnp.where(row_core[:, None] == 0, picked, 0.0),
                jnp.where(row_core[:, None] == 1, picked, 0.0),
            ],
            axis=1,
        ).astype(BF)
        weighted = jnp.sum(jnp.where(matches, gates[None], 0.0), axis=2)
        combine.append(
            [jnp.where(row_core[:, None] == h, weighted, 0.0).astype(BF) for h in range(2)]
        )
        outgoing = jnp.dot(dispatch, moe_halves, preferred_element_type=F32).astype(BF)
        if gate_on is not None:
            outgoing, _ = lax.optimization_barrier((outgoing, gate_on))
        mine = lax.all_to_all(outgoing, DP, split_axis=0, concat_axis=0, tiled=True)
        theirs = other_core(mine)
        gate_part = rows_by(gate_mine, mine) + rows_by(gate_other, theirs)
        up_part = rows_by(up_mine, mine) + rows_by(up_other, theirs)
        hidden = (jax.nn.silu(gate_part) * up_part).astype(BF)
        hidden = jnp.dot(hidden, squeeze, preferred_element_type=F32).astype(BF)
        gate_on = hidden
        hidden_chunks.append(lax.all_gather(hidden, T, axis=0, tiled=True))

    result = mixed_cols.astype(F32)
    sums = [0.0, 0.0]
    for k in range(CHUNKS):
        half_out = lax.dot_general(
            hidden_chunks[k], expert_down[0], (((0,), (0,)), ((), ())), preferred_element_type=F32
        ).astype(BF)
        half_out = jnp.dot(squeeze, half_out, preferred_element_type=F32).astype(BF)
        keep = lax.dynamic_slice_in_dim(half_out, core * 256, 256, 1)
        give = lax.dynamic_slice_in_dim(half_out, (1 - core) * 256, 256, 1)
        both = (keep.astype(F32) + other_core(give).astype(F32)).astype(BF)
        returned = lax.all_to_all(both, DP, split_axis=0, concat_axis=0, tiled=True)
        for h in range(2):
            sums[h] = sums[h] + lax.dot_general(
                combine[k][h], returned, (((0,), (0,)), ((), ())), preferred_element_type=F32
            )
    hidden_out = (result + jnp.concatenate(sums, axis=1)).astype(BF)
    return (hidden_out, expand_block, output_block, cache_cols)


def solution(mesh):
    fine = Mesh(mesh.devices.reshape(4, 4, 4, 2, 4), DP + (T,))
    rows_both = P(DP + (T,), None)
    in_specs = (
        P(DP, T),
        P(DP, None),
        P(DP, None),
        P(DP, None),
        P(),
        P(),
        P(),
        rows_both,
        rows_both,
        rows_both,
        rows_both,
        P(DP, None, T),
        P(DP, None, T),
        P(DP, None, T),
    )
    out_specs = (P(DP, T), P(None, T), P(None, T), P(DP, T))
    return jax.shard_map(body, mesh=fine, in_specs=in_specs, out_specs=out_specs, check_vma=False)
```

time: 1220 us -> 530 us (0.43)
  blocking collectives: 677 us -> 162 us
  waiting for transfers between devices: 380 us -> 160 us
  starting transfers between devices: 32.4 us -> 102 us
  local copies, waits for them, and re-layouts: 70.9 us -> 13.6 us
  matrix products: 25.3 us -> 46 us
  Pallas kernels: 0 us -> 12.8 us
    all_gather x5 -> x2, blocking collectives: 450 us -> 36.4 us  [the longest x1 18.9 us: body(): full_input = lax.all_gather(hidden_gated, T, axis=1, tiled=True)]
    all_gather x3 -> x2, waiting for transfers between devices: 292 us -> 88 us  [body(): hidden_chunks.append(lax.all_gather(hidden, T, axis=0, tiled=True))]
    all_to_all x2, blocking collectives: 227 us -> 126 us  [body(): mine = lax.all_to_all(outgoing, DP, split_axis=0, concat_axis=0, tiled=True)]
    ppermute x0 -> x18, starting transfers between devices: none -> 52.3 us  [the longest x12 33.7 us: shifted(): lax.ppermute(block, axis, [(j, (j + s) % 4) for j in range(4)])]
    ppermute x0 -> x18, waiting for transfers between devices: none -> 44.5 us  [the longest x12 41.4 us: shifted(): lax.ppermute(block, axis, [(j, (j + s) % 4) for j in range(4)])]
    reduce_scatter x1 -> x0, waiting for transfers between devices: 42.3 us -> none  [body(): lax.psum_scatter(head_terms.astype(jnp.bfloat16), 'tensor', scatter_dimen...]
    dot_general x11 -> x22, matrix products: 24.9 us -> 44.8 us  [the longest x6 13.1 us: rows_by(): lax.dot_general(weight, rows, (((0,), (1,)), ((), ())), preferred_element...]
    all_to_all x4 -> x3, waiting for transfers between devices: 45.6 us -> 27.4 us  [the longest x2 16.5 us: body(): returned = lax.all_to_all(both, DP, split_axis=0, concat_axis=0, tiled=True)]
  transfers between devices with their start and end apart: 8 -> 23, of which waited for: 4 -> 15; matrix products, arithmetic and copies ran while one was open for 1% -> 10% of each run, Pallas kernels for 0% -> 1%
where the time goes in v1:
time: 530 us; the launch traced here: 528 us
  blocking collectives  162 us (31%)
  waiting for transfers between devices  160 us (30%)
  starting transfers between devices  102 us (19%)
  matrix products  46 us (9%)
  other arithmetic  17 us (3%)
  between operations  14.7 us (3%)
  local copies, waits for them, and re-layouts  13.6 us (3%)
  Pallas kernels  12.8 us (2%)
    all_to_all x2, blocking collectives, body(): mine = lax.all_to_all(outgoing, DP, split_axis=0, concat_axis=0, tiled=True)  126 us
    all_gather x2, waiting for transfers between devices, body(): hidden_chunks.append(lax.all_gather(hidden, T, axis=0, tiled=True))  88 us
    ppermute x12, waiting for transfers between devices, shifted(): lax.ppermute(block, axis, [(j, (j + s) % 4) for j in range(4)])  41.4 us
    ppermute x12, starting transfers between devices, shifted(): lax.ppermute(block, axis, [(j, (j + s) % 4) for j in range(4)])  33.7 us
    all_to_all x2, starting transfers between devices, body(): returned = lax.all_to_all(both, DP, split_axis=0, concat_axis=0, tiled=True)  33.6 us
    all_gather x1, blocking collectives, body(): full_input = lax.all_gather(hidden_gated, T, axis=1, tiled=True)  18.9 us
    ppermute x6, starting transfers between devices, other_core(): return lax.ppermute(block, 'c', [(0, 1), (1, 0)])  18.6 us
    all_gather x1, blocking collectives, body(): attended_full = lax.all_gather(attended, T, axis=1, tiled=True)  17.5 us
  transfers between devices with their start and end apart: 23, of which 15 were waited for; matrix products, arithmetic and copies ran while one was open for 10% of the time, Pallas kernels for 1%

profile of v1, /device:TPU:1, one launch (start us, length us, event | category | flops | bytes accessed | tf_op | source)
XLA Modules:
  0.0 528.4 jit_solution(9984102765561092839)
XLA Ops:
  11.0 15.6 %all-to-all-start = ((bf16[4,4,2112]{2,1,0:T(4,128)(2,1)}), bf16[4,4,2112]{2,1,0:T(4,128)(2,1)S(1)}, u32[]{:S(2)}, u32[]{:S(2)}) async-start(bf16[4,4,2112]{2,1,0:T(4,128)(2,1)} %concatenate.30), calls=%async_computation | async-start | bytes 139264 | tf_op jit(solution)/shard_map/all_to_all | solution.py:149
  28.1 11.0 %all-to-all-done = bf16[4,4,2112]{2,1,0:T(4,128)(2,1)S(1)} async-done(((bf16[4,4,2112]{2,1,0:T(4,128)(2,1)}), bf16[4,4,2112]{2,1,0:T(4,128)(2,1)S(1)}, u32[]{:S(2)}, u32[]{:S(2)}) %all-to-all-start) | async-done | bytes 67616 | tf_op jit(solution)/shard_map/all_to_all | solution.py:149
  39.1 3.6 collective-permute-start.2
  46.8 2.3 collective-permute-done.1
  49.1 2.4 collective-permute-done
  51.6 4.6 collective-permute-start.5
  56.2 2.3 collective-permute-start.4
  58.5 2.6 collective-permute-start.3
  62.0 3.1 collective-permute-done.4
  65.1 4.1 collective-permute-done.3
  69.5 4.4 collective-permute-start.8
  73.9 2.4 collective-permute-start.7
  76.4 2.5 collective-permute-start.6
  79.2 3.2 collective-permute-done.8
  82.4 4.2 collective-permute-done.7
  86.6 17.6 %collective-permute-done.6 = bf16[4,4,16,1088]{3,2,1,0:T(8,128)(2,1)S(1)} collective-permute-done((bf16[4,4,16,1088]{3,2,1,0:T(8,128)(2,1)S(1)}, bf16[4,4,16,1088]{3,2,1,0:T(8,128)(2,1)S(1)}, u32[]{:S(2)}, u32[]{:S(2)}) %collective-permute-start.6) | collective-permute-done | bytes 557088 | tf_op jit(solution)/shard_map/ppermute | solution.py:83
  104.6 3.4 collective-permute-start.9
  114.8 2.4 collective-permute-start.11
  117.2 2.5 collective-permute-start.10
  119.8 18.9 %all_gather.12 = bf16[128,2048]{1,0:T(8,128)(2,1)S(1)} all-gather(bf16[128,512]{1,0:T(8,128)(2,1)S(1)} %copy-done.19), channel_id=1, replica_groups=mesh['zl'=4,'y'=4,'x'=4,'c'=2,'t'=4] {'t'}, dimensions={1}, use_global_device_ids=true | all-gather | bytes 655360 | tf_op jit(solution)/shard_map/all_gather | solution.py:157
  138.9 4.4 collective-permute-done.10
  143.6 3.7 collective-permute-start.13
  148.7 6.8 %ordered.2 = (bf16[128,16,384]{2,1,0:T(8,128)(2,1)}, bf16[128,16,128]{2,1,0:T(8,128)(2,1)}, bf16[128,16,576]{2,1,0:T(8,128)(2,1)}) custom-call(s32[4]{0:T(128)} %pad_add_fusion.place_ref, bf16[64,16,1088]{2,1,0:T(8,128)(2,1)} %bitcast.122, bf16[64,16,1088]{2,1,0:T(8,128)(2,1)} %bitcast.126), custom_call_target="tpu_custom_call" | custom-call | tf_op jit(solution)/shard_map/ordered/pallas_call | solution.py:110
  155.5 2.9 convolution_convert_fusion.3
  165.0 2.6 copy.31
  172.6 17.5 %all_gather.13 = bf16[128,1024]{0,1:T(8,128)(2,1)} all-gather(bf16[128,256]{0,1:T(8,128)(2,1)S(1)} %bitcast.145), channel_id=1, replica_groups=mesh['zl'=4,'y'=4,'x'=4,'c'=2,'t'=4] {'t'}, dimensions={1}, use_global_device_ids=true | all-gather | bytes 327680 | tf_op jit(solution)/shard_map/all_gather | solution.py:196
  190.1 6.0 %ordered.3 = bf16[128,16,1024]{2,1,0:T(8,128)(2,1)} custom-call(s32[4]{0:T(128)} %pad_add_fusion.place_ref, bf16[64,16,1024]{2,1,0:T(8,128)(2,1)} %bitcast.124, bf16[64,16,1024]{2,1,0:T(8,128)(2,1)} %bitcast.34.theirs_ref), custom_call_target="tpu_custom_call" | custom-call | tf_op jit(solution)/shard_map/ordered/pallas_call | solution.py:110
  196.2 3.8 fusion.26
  201.9 68.5 %all_to_all.53 = bf16[128,8,1024]{2,1,0:T(8,128)(2,1)S(1)} all-to-all(bf16[128,8,1024]{2,1,0:T(8,128)(2,1)S(1)} %convert_bitcast_fusion), channel_id=1, replica_groups=mesh['zl'=4,'y'=4,'x'=4,'c'=2,'t'=4] {'zl','y','x','c'}, dimensions={0} | all-to-all | bytes 4194304 | tf_op jit(solution)/shard_map/all_to_all | solution.py:251
  270.5 3.0 collective-permute-start.14
  274.1 3.1 convolution_convert_fusion
  279.8 3.5 convolution_add_fusion.4
  283.3 4.1 fusion.20
  287.5 57.6 %all_to_all.54 = bf16[128,8,1024]{2,1,0:T(8,128)(2,1)S(1)} all-to-all(bf16[128,8,1024]{2,1,0:T(8,128)(2,1)} %bitcast.123), channel_id=1, replica_groups=mesh['zl'=4,'y'=4,'x'=4,'c'=2,'t'=4] {'zl','y','x','c'}, dimensions={0} | all-to-all | bytes 4194304 | tf_op jit(solution)/shard_map/all_to_all | solution.py:251
  345.1 3.0 collective-permute-start.16
  348.4 2.7 fusion.66
  352.0 3.5 convolution_add_fusion.2
  355.5 4.3 fusion.21
  359.8 49.5 %all-gather.3.cloned.1.call-done = bf16[704,896]{1,0:T(8,128)(2,1)} async-done(((bf16[176,896]{1,0:T(8,128)(2,1)}), bf16[704,896]{1,0:T(8,128)(2,1)}) %all-gather.3.cloned.1.call-update) | async-done | bytes 1261584 | tf_op jit(solution)/shard_map/all_gather | solution.py:258
  409.3 3.3 fusion.14
  412.7 2.8 collective-permute-start.15
  417.9 8.3 %all-to-all-start.2 = ((bf16[128,8,256]{2,1,0:T(8,128)(2,1)}), bf16[128,8,256]{2,1,0:T(8,128)(2,1)S(1)}, u32[]{:S(2)}, u32[]{:S(2)}) async-start(bf16[128,8,256]{2,1,0:T(8,128)(2,1)} %fusion.46), calls=%async_computation.2 | async-start | bytes 1048576 | tf_op jit(solution)/shard_map/all_to_all | solution.py:270
  426.2 38.5 %all-gather.5.cloned.1.call-done = bf16[704,896]{1,0:T(8,128)(2,1)} async-done(((bf16[176,896]{1,0:T(8,128)(2,1)}), bf16[704,896]{1,0:T(8,128)(2,1)}) %all-gather.5.cloned.1.call-update) | async-done | bytes 1261584 | tf_op jit(solution)/shard_map/all_gather | solution.py:258
  464.7 3.3 fusion.15
  468.1 2.6 collective-permute-start.17
  475.4 25.3 %all-to-all-start.4 = ((bf16[128,8,256]{2,1,0:T(8,128)(2,1)}), bf16[128,8,256]{2,1,0:T(8,128)(2,1)S(1)}, u32[]{:S(2)}, u32[]{:S(2)}) async-start(bf16[128,8,256]{2,1,0:T(8,128)(2,1)} %fusion.47), calls=%async_computation.4 | async-start | bytes 1048576 | tf_op jit(solution)/shard_map/all_to_all | solution.py:270
  501.5 2.3 constant_dynamic-slice_fusion
  504.7 14.3 %all-to-all-done.4 = bf16[128,8,256]{2,1,0:T(8,128)(2,1)S(1)} async-done(((bf16[128,8,256]{2,1,0:T(8,128)(2,1)}), bf16[128,8,256]{2,1,0:T(8,128)(2,1)S(1)}, u32[]{:S(2)}, u32[]{:S(2)}) %all-to-all-start.4) | async-done | bytes 524320 | tf_op jit(solution)/shard_map/all_to_all | solution.py:270
  (147 shorter events, 49.2 us)
Async XLA Ops:
  7.2 402.2 %copy-start = (bf16[1,704,512]{2,1,0:T(8,128)(2,1)S(1)}, bf16[1,704,512]{2,1,0:T(8,128)(2,1)}, u32[]{:S(2)}) copy-start(bf16[1,704,512]{2,1,0:T(8,128)(2,1)} %param.27) | copy-start | bytes 2162692
  11.0 28.1 %all-to-all-start = ((bf16[4,4,2112]{2,1,0:T(4,128)(2,1)}), bf16[4,4,2112]{2,1,0:T(4,128)(2,1)S(1)}, u32[]{:S(2)}, u32[]{:S(2)}) async-start(bf16[4,4,2112]{2,1,0:T(4,128)(2,1)} %concatenate.30), calls=%async_computation | async-start | bytes 139264 | tf_op jit(solution)/shard_map/all_to_all | solution.py:149
  26.6 382.7 %all-gather.3.cloned.1.call-start = ((), (), s32[]{:S(2)}) async-start(), calls=%async_computation.5 | async-start | bytes 1576960 | tf_op jit(solution)/shard_map/all_gather | solution.py:258
  39.1 7.7 %collective-permute-start.2 = (bf16[16,2112]{1,0:T(8,128)(2,1)S(1)}, bf16[16,2112]{1,0:T(8,128)(2,1)S(1)}, u32[]{:S(2)}, u32[]{:S(2)}) collective-permute-start(bf16[16,2112]{1,0:T(8,128)(2,1)S(1)} %reshape.390), channel_id=1, source_target_pairs={{0,384},{128,0},{256,128},{384,256},{1,385},{129,1},{257,129},{385... | collective-permute-start | bytes 202760 | tf_op jit(solution)/shard_map/ppermute | solution.py:83
  42.7 6.4 %collective-permute-start.1 = (bf16[16,2112]{1,0:T(8,128)(2,1)S(1)}, bf16[16,2112]{1,0:T(8,128)(2,1)S(1)}, u32[]{:S(2)}, u32[]{:S(2)}) collective-permute-start(bf16[16,2112]{1,0:T(8,128)(2,1)S(1)} %reshape.390), channel_id=1, source_target_pairs={{0,256},{128,384},{256,0},{384,128},{1,257},{129,385},{257,1},{385... | collective-permute-start | bytes 202760 | tf_op jit(solution)/shard_map/ppermute | solution.py:83
  44.6 6.9 %collective-permute-start = (bf16[16,2112]{1,0:T(8,128)(2,1)S(1)}, bf16[16,2112]{1,0:T(8,128)(2,1)S(1)}, u32[]{:S(2)}, u32[]{:S(2)}) collective-permute-start(bf16[16,2112]{1,0:T(8,128)(2,1)S(1)} %reshape.390), channel_id=1, source_target_pairs={{0,128},{128,256},{256,384},{384,0},{1,129},{129,257},{257,385},{3... | collective-permute-start | bytes 202760 | tf_op jit(solution)/shard_map/ppermute | solution.py:83
  51.6 27.3 %copy-start.20 = (s32[128,6]{0,1:T(8,128)S(1)}, s32[128,6]{0,1:T(8,128)}, u32[]{:S(2)}) copy-start(s32[128,6]{0,1:T(8,128)} %param.16) | copy-start | bytes 9220
  51.6 10.4 %collective-permute-start.5 = (bf16[4,16,2112]{2,1,0:T(8,128)(2,1)S(1)}, bf16[4,16,2112]{2,1,0:T(8,128)(2,1)S(1)}, u32[]{:S(2)}, u32[]{:S(2)}) collective-permute-start(bf16[4,16,2112]{2,1,0:T(8,128)(2,1)S(1)} %get-tuple-element.25), channel_id=1, source_target_pairs={{0,96},{32,0},{64,32},{96,64},{1,97},{33,1},{65,33},{97,65},{2,98}... | collective-permute-start | bytes 811016 | tf_op jit(solution)/shard_map/ppermute | solution.py:83
  56.2 8.9 %collective-permute-start.4 = (bf16[4,16,2112]{2,1,0:T(8,128)(2,1)S(1)}, bf16[4,16,2112]{2,1,0:T(8,128)(2,1)S(1)}, u32[]{:S(2)}, u32[]{:S(2)}) collective-permute-start(bf16[4,16,2112]{2,1,0:T(8,128)(2,1)S(1)} %get-tuple-element.25), channel_id=1, source_target_pairs={{0,64},{32,96},{64,0},{96,32},{1,65},{33,97},{65,1},{97,33},{2,66}... | collective-permute-start | bytes 811016 | tf_op jit(solution)/shard_map/ppermute | solution.py:83
  58.5 10.8 %collective-permute-start.3 = (bf16[4,16,2112]{2,1,0:T(8,128)(2,1)S(1)}, bf16[4,16,2112]{2,1,0:T(8,128)(2,1)S(1)}, u32[]{:S(2)}, u32[]{:S(2)}) collective-permute-start(bf16[4,16,2112]{2,1,0:T(8,128)(2,1)S(1)} %get-tuple-element.25), channel_id=1, source_target_pairs={{0,32},{32,64},{64,96},{96,0},{1,33},{33,65},{65,97},{97,1},{2,34}... | collective-permute-start | bytes 811016 | tf_op jit(solution)/shard_map/ppermute | solution.py:83
  61.1 49.5 %copy-start.21 = (pred[1024]{0:T(1024)(128)(4,1)}, pred[1024]{0:T(1024)(128)(4,1)S(1)}, u32[]{:S(2)}) copy-start(pred[1024]{0:T(1024)(128)(4,1)S(1)} %get-tuple-element.44) | copy-start | bytes 3076
  61.1 49.5 %copy-start.23 = (pred[1024]{0:T(1024)(128)(4,1)}, pred[1024]{0:T(1024)(128)(4,1)S(1)}, u32[]{:S(2)}) copy-start(pred[1024]{0:T(1024)(128)(4,1)S(1)} %get-tuple-element.45) | copy-start | bytes 3076
  69.5 12.8 %collective-permute-start.8 = (bf16[4,4,16,1088]{3,2,1,0:T(8,128)(2,1)S(1)}, bf16[4,4,16,1088]{3,2,1,0:T(8,128)(2,1)S(1)}, u32[]{:S(2)}, u32[]{:S(2)}) collective-permute-start(bf16[4,4,16,1088]{3,2,1,0:T(8,128)(2,1)S(1)} %get-tuple-element.21), channel_id=1, source_target_pairs={{0,24},{8,0},{16,8},{24,16},{1,25},{9,1},{17,9},{25,17},{2,26},{10... | collective-permute-start | bytes 1671176 | tf_op jit(solution)/shard_map/ppermute | solution.py:83
  73.9 12.6 %collective-permute-start.7 = (bf16[4,4,16,1088]{3,2,1,0:T(8,128)(2,1)S(1)}, bf16[4,4,16,1088]{3,2,1,0:T(8,128)(2,1)S(1)}, u32[]{:S(2)}, u32[]{:S(2)}) collective-permute-start(bf16[4,4,16,1088]{3,2,1,0:T(8,128)(2,1)S(1)} %get-tuple-element.21), channel_id=1, source_target_pairs={{0,16},{8,24},{16,0},{24,8},{1,17},{9,25},{17,1},{25,9},{2,18},{10... | collective-permute-start | bytes 1671176 | tf_op jit(solution)/shard_map/ppermute | solution.py:83
  76.4 27.8 %collective-permute-start.6 = (bf16[4,4,16,1088]{3,2,1,0:T(8,128)(2,1)S(1)}, bf16[4,4,16,1088]{3,2,1,0:T(8,128)(2,1)S(1)}, u32[]{:S(2)}, u32[]{:S(2)}) collective-permute-start(bf16[4,4,16,1088]{3,2,1,0:T(8,128)(2,1)S(1)} %get-tuple-element.21), channel_id=1, source_target_pairs={{0,8},{8,16},{16,24},{24,0},{1,9},{9,17},{17,25},{25,1},{2,10},{10... | collective-permute-start | bytes 1671176 | tf_op jit(solution)/shard_map/ppermute | solution.py:83
  104.6 7.9 %copy-start.1 = (bf16[4,4,4,16,1088]{4,3,2,1,0:T(8,128)(2,1)}, bf16[4,4,4,16,1088]{4,3,2,1,0:T(8,128)(2,1)S(1)}, u32[]{:S(2)}) copy-start(bf16[4,4,4,16,1088]{4,3,2,1,0:T(8,128)(2,1)S(1)} %pad_maximum_fusion) | copy-start | bytes 6684676
  104.6 42.6 %collective-permute-start.9 = (bf16[4,4,4,16,1088]{4,3,2,1,0:T(8,128)(2,1)S(1)}, bf16[4,4,4,16,1088]{4,3,2,1,0:T(8,128)(2,1)S(1)}, u32[]{:S(2)}, u32[]{:S(2)}) collective-permute-start(bf16[4,4,4,16,1088]{4,3,2,1,0:T(8,128)(2,1)S(1)} %pad_maximum_fusion), channel_id=1, source_target_pairs={{0,4},{4,0},{1,5},{5,1},{2,6},{6,2},{3,7},{7,3},{8,12},{12,8},{9,1... | collective-permute-start | bytes 6684680 | tf_op jit(solution)/shard_map/ppermute | solution.py:88
  108.8 11.0 %copy-start.19 = (bf16[128,512]{1,0:T(8,128)(2,1)S(1)}, bf16[128,512]{1,0:T(8,128)(2,1)}, u32[]{:S(2)}) copy-start(bf16[128,512]{1,0:T(8,128)(2,1)} %param.14) | copy-start | bytes 393220
  112.5 26.3 %collective-permute-start.12 = (bf16[4,4,16,1024]{3,2,1,0:T(8,128)(2,1)S(1)}, bf16[4,4,16,1024]{3,2,1,0:T(8,128)(2,1)S(1)}, u32[]{:S(2)}, u32[]{:S(2)}) collective-permute-start(bf16[4,4,16,1024]{3,2,1,0:T(8,128)(2,1)S(1)} %pad_maximum_fusion.3), channel_id=1, source_target_pairs={{0,24},{8,0},{16,8},{24,16},{1,25},{9,1},{17,9},{25,17},{2,26},{10... | collective-permute-start | bytes 1572872 | tf_op jit(solution)/shard_map/ppermute | solution.py:83
  114.8 24.1 %collective-permute-start.11 = (bf16[4,4,16,1024]{3,2,1,0:T(8,128)(2,1)S(1)}, bf16[4,4,16,1024]{3,2,1,0:T(8,128)(2,1)S(1)}, u32[]{:S(2)}, u32[]{:S(2)}) collective-permute-start(bf16[4,4,16,1024]{3,2,1,0:T(8,128)(2,1)S(1)} %pad_maximum_fusion.3), channel_id=1, source_target_pairs={{0,16},{8,24},{16,0},{24,8},{1,17},{9,25},{17,1},{25,9},{2,18},{10... | collective-permute-start | bytes 1572872 | tf_op jit(solution)/shard_map/ppermute | solution.py:83
  117.2 26.1 %collective-permute-start.10 = (bf16[4,4,16,1024]{3,2,1,0:T(8,128)(2,1)S(1)}, bf16[4,4,16,1024]{3,2,1,0:T(8,128)(2,1)S(1)}, u32[]{:S(2)}, u32[]{:S(2)}) collective-permute-start(bf16[4,4,16,1024]{3,2,1,0:T(8,128)(2,1)S(1)} %pad_maximum_fusion.3), channel_id=1, source_target_pairs={{0,8},{8,16},{16,24},{24,0},{1,9},{9,17},{17,25},{25,1},{2,10},{10... | collective-permute-start | bytes 1572872 | tf_op jit(solution)/shard_map/ppermute | solution.py:83
  143.6 11.9 %copy-start.2 = (bf16[4,4,4,16,1024]{4,3,2,1,0:T(8,128)(2,1)}, bf16[4,4,4,16,1024]{4,3,2,1,0:T(8,128)(2,1)S(1)}, u32[]{:S(2)}) copy-start(bf16[4,4,4,16,1024]{4,3,2,1,0:T(8,128)(2,1)S(1)} %pad_maximum_fusion.1) | copy-start | bytes 6291460
  143.6 46.6 %collective-permute-start.13 = (bf16[4,4,4,16,1024]{4,3,2,1,0:T(8,128)(2,1)S(1)}, bf16[4,4,4,16,1024]{4,3,2,1,0:T(8,128)(2,1)}, u32[]{:S(2)}, u32[]{:S(2)}) collective-permute-start(bf16[4,4,4,16,1024]{4,3,2,1,0:T(8,128)(2,1)S(1)} %pad_maximum_fusion.1), channel_id=1, source_target_pairs={{0,4},{4,0},{1,5},{5,1},{2,6},{6,2},{3,7},{7,3},{8,12},{12,8},{9,1... | collective-permute-start | bytes 6291464 | tf_op jit(solution)/shard_map/ppermute | solution.py:88
  148.7 6.8 %copy-start.25 = (f32[2048]{0:T(1024)S(1)}, f32[2048]{0:T(1024)}, u32[]{:S(2)}) copy-start(f32[2048]{0:T(1024)} %param.18) | copy-start | bytes 24580
  155.5 5.2 copy-start.29
  167.6 2.4 copy-start.18
  190.1 6.0 %copy-start.10 = (bf16[128,1024]{0,1:T(8,128)(2,1)S(1)}, bf16[128,1024]{0,1:T(8,128)(2,1)}, u32[]{:S(2)}) copy-start(bf16[128,1024]{0,1:T(8,128)(2,1)} %all_gather.13) | copy-start | bytes 786436
  196.2 3.9 copy-start.26
  200.0 2.0 copy-start.4
  270.5 9.3 %collective-permute-start.14 = (bf16[1024,1024]{1,0:T(8,128)(2,1)S(1)}, bf16[1024,1024]{1,0:T(8,128)(2,1)}, u32[]{:S(2)}, u32[]{:S(2)}) collective-permute-start(bf16[1024,1024]{1,0:T(8,128)(2,1)S(1)} %bitcast.120), channel_id=1, source_target_pairs={{0,4},{4,0},{1,5},{5,1},{2,6},{6,2},{3,7},{7,3},{8,12},{12,8},{9,1... | collective-permute-start | bytes 6291464 | tf_op jit(solution)/shard_map/ppermute | solution.py:88
  273.5 3.7 copy-start.13
  279.8 3.5 copy-start.14
  279.8 3.5 copy-start.17
  279.8 3.5 copy-start.27
  345.1 7.0 %collective-permute-start.16 = (bf16[1024,1024]{1,0:T(8,128)(2,1)S(1)}, bf16[1024,1024]{1,0:T(8,128)(2,1)}, u32[]{:S(2)}, u32[]{:S(2)}) collective-permute-start(bf16[1024,1024]{1,0:T(8,128)(2,1)S(1)} %bitcast.121), channel_id=1, source_target_pairs={{0,4},{4,0},{1,5},{5,1},{2,6},{6,2},{3,7},{7,3},{8,12},{12,8},{9,1... | collective-permute-start | bytes 6291464 | tf_op jit(solution)/shard_map/ppermute | solution.py:88
  348.1 116.6 %all-gather.5.cloned.1.call-start = ((), (), s32[]{:S(2)}) async-start(), calls=%async_computation.6 | async-start | bytes 1576960 | tf_op jit(solution)/shard_map/all_gather | solution.py:258
  352.0 3.5 copy-start.15
  352.0 3.5 copy-start.16
  352.0 3.5 copy-start.28
  412.7 4.3 collective-permute-start.15
  417.9 57.5 %all-to-all-start.2 = ((bf16[128,8,256]{2,1,0:T(8,128)(2,1)}), bf16[128,8,256]{2,1,0:T(8,128)(2,1)S(1)}, u32[]{:S(2)}, u32[]{:S(2)}) async-start(bf16[128,8,256]{2,1,0:T(8,128)(2,1)} %fusion.46), calls=%async_computation.2 | async-start | bytes 1048576 | tf_op jit(solution)/shard_map/all_to_all | solution.py:270
  468.0 32.7 %copy-start.9 = (bf16[128,512]{0,1:T(8,128)(2,1)S(1)}, bf16[128,512]{0,1:T(8,128)(2,1)}, u32[]{:S(2)}) copy-start(bf16[128,512]{0,1:T(8,128)(2,1)} %copy-done.8) | copy-start | bytes 393220
  468.1 35.7 %copy-start.7 = (bf16[1024,128]{1,0:T(8,128)(2,1)S(1)}, bf16[1024,128]{1,0:T(8,128)(2,1)}, u32[]{:S(2)}) copy-start(bf16[1024,128]{1,0:T(8,128)(2,1)} %get-tuple-element.17) | copy-start | bytes 786436
  468.1 35.7 %copy-start.24 = (pred[1024]{0:T(1024)(128)(4,1)S(1)}, pred[1024]{0:T(1024)(128)(4,1)}, u32[]{:S(2)}) copy-start(pred[1024]{0:T(1024)(128)(4,1)} %copy-done.23) | copy-start | bytes 3076
  468.1 4.2 collective-permute-start.17
  473.2 31.1 %copy-start.22 = (pred[1024]{0:T(1024)(128)(4,1)S(1)}, pred[1024]{0:T(1024)(128)(4,1)}, u32[]{:S(2)}) copy-start(pred[1024]{0:T(1024)(128)(4,1)} %copy-done.21) | copy-start | bytes 3076
  475.4 43.6 %all-to-all-start.4 = ((bf16[128,8,256]{2,1,0:T(8,128)(2,1)}), bf16[128,8,256]{2,1,0:T(8,128)(2,1)S(1)}, u32[]{:S(2)}, u32[]{:S(2)}) async-start(bf16[128,8,256]{2,1,0:T(8,128)(2,1)} %fusion.47), calls=%async_computation.4 | async-start | bytes 1048576 | tf_op jit(solution)/shard_map/all_to_all | solution.py:270
  500.7 18.3 %copy-start.5 = (bf16[1024,128]{1,0:T(8,128)(2,1)S(1)}, bf16[1024,128]{1,0:T(8,128)(2,1)}, u32[]{:S(2)}) copy-start(bf16[1024,128]{1,0:T(8,128)(2,1)} %get-tuple-element.16) | copy-start | bytes 786436
  (5 other events, 6.1 us)
Sparse Core Ops, SparseCore 0:
  348.3 61.0 all-gather.2
  411.4 53.2 all-gather.4

commit v2 on v1

--- a/solution.py
+++ b/solution.py
@@ -16,9 +16,7 @@
 EXPERTS = 64
 CAP = 14
 TOK = 128
-CHUNKS = 2
-SLOTS = CAP // CHUNKS
-ROWS = 8
+PADDED = 16
 
 DP = ("zl", "y", "x", "c")
 T = "t"
@@ -202,76 +200,81 @@
     moe_in = rms_norm(mixed_full.astype(F32), moe_gain).astype(BF)
 
     slot_rank = expert_ranks(routes)
-    row_ids = jnp.arange(EXPERTS * 2 * ROWS, dtype=jnp.int32)
-    row_core = (row_ids // ROWS) % 2
+    gates = gate_weights.astype(F32)
+    pad_ids = jnp.arange(EXPERTS * 2 * PADDED, dtype=jnp.int32)
+    pad_core = (pad_ids // PADDED) % 2
+    slot_at = routes * (2 * PADDED) + slot_rank
+    matches = (pad_ids - pad_core * PADDED)[:, None, None] == slot_at[None, :, :]
+
+    def placed_by(values):
+        return jnp.sum(jnp.where(matches, values, 0.0), axis=2)
+
+    placed = placed_by(1.0)
+    dispatch = jnp.concatenate(
+        [
+            jnp.where(pad_core[:, None] == 0, placed, 0.0),
+            jnp.where(pad_core[:, None] == 1, placed, 0.0),
+        ],
+        axis=1,
+    ).astype(BF)
     moe_halves = jnp.concatenate([moe_in[:, : D // 2], moe_in[:, D // 2 :]], axis=0)
-    gates = gate_weights.astype(F32)
-    compact = jnp.arange(TOK * SLOTS, dtype=jnp.int32)
-    spread = (compact // SLOTS) * ROWS + compact % SLOTS
-    squeeze = (jnp.arange(TOK * ROWS, dtype=jnp.int32)[:, None] == spread[None, :]).astype(BF)
-    gate_mat = expert_gate[0]
-    up_mat = expert_up[0]
-    mine_at = core * (D // 2)
-    other_at = (1 - core) * (D // 2)
+
+    weighted = placed_by(gates[None])
+    combine = [jnp.where(pad_core[:, None] == h, weighted, 0.0).astype(BF) for h in range(2)]
+
+    compact = jnp.arange(TOK * CAP, dtype=jnp.int32)
+    taken = (compact // CAP) * PADDED + compact % CAP
+    squeeze = (jnp.arange(TOK * PADDED, dtype=jnp.int32)[:, None] == taken[None, :]).astype(BF)
 
     def halves(matrix):
         return (
-            lax.dynamic_slice_in_dim(matrix, mine_at, D // 2, 0),
-            lax.dynamic_slice_in_dim(matrix, other_at, D // 2, 0),
+            lax.dynamic_slice_in_dim(matrix, core * (D // 2), D // 2, 0),
+            lax.dynamic_slice_in_dim(matrix, (1 - core) * (D // 2), D // 2, 0),
         )
 
-    gate_mine, gate_other = halves(gate_mat)
-    up_mine, up_other = halves(up_mat)
+    gate_mine, gate_other = halves(expert_gate[0])
+    up_mine, up_other = halves(expert_up[0])
+    around = [(rank + 4 - back) % 4 for back in (0, 1, 3, 2)]
+    down_around = jnp.concatenate(
+        [lax.dynamic_slice_in_dim(expert_down[0], at * 176, 176, 0) for at in around], axis=0
+    )
 
     def rows_by(weight, rows):
         return lax.dot_general(weight, rows, (((0,), (1,)), ((), ())), preferred_element_type=F32)
 
-    hidden_chunks = []
-    combine = []
-    gate_on = None
-    for k in range(CHUNKS):
-        in_chunk = (slot_rank >= k * SLOTS) & (slot_rank < (k + 1) * SLOTS)
-        target = jnp.where(in_chunk, routes * (2 * ROWS) + (slot_rank - k * SLOTS), -1)
-        matches = (row_ids - row_core * ROWS)[:, None, None] == target[None, :, :]
-        picked = jnp.sum(matches.astype(F32), axis=2)
-        dispatch = jnp.concatenate(
-            [
-                jnp.where(row_core[:, None] == 0, picked, 0.0),
-                jnp.where(row_core[:, None] == 1, picked, 0.0),
-            ],
-            axis=1,
-        ).astype(BF)
-        weighted = jnp.sum(jnp.where(matches, gates[None], 0.0), axis=2)
-        combine.append(
-            [jnp.where(row_core[:, None] == h, weighted, 0.0).astype(BF) for h in range(2)]
+    outgoing = jnp.dot(dispatch, moe_halves, preferred_element_type=F32).astype(BF)
+    mine = lax.all_to_all(outgoing, DP, split_axis=0, concat_axis=0, tiled=True)
+    theirs = other_core(mine)
+    gate_part = rows_by(gate_mine, mine) + rows_by(gate_other, theirs)
+    up_part = rows_by(up_mine, mine) + rows_by(up_other, theirs)
+    hidden = (jax.nn.silu(gate_part) * up_part).astype(BF)
+
+    up_ring = [(j, (j + 1) % 4) for j in range(4)]
+    down_ring = [(j, (j + 3) % 4) for j in range(4)]
+    own = jnp.dot(hidden, squeeze, preferred_element_type=F32).astype(BF)
+    below = lax.ppermute(own, T, up_ring)
+    above = lax.ppermute(own, T, down_ring)
+    far_first = lax.ppermute(below[:88], T, up_ring)
+    far_second = lax.ppermute(above[88:], T, down_ring)
+
+    def out_of(pieces, at):
+        rows = jnp.concatenate(pieces, axis=0)
+        return lax.dot_general(
+            rows, down_around[at : at + rows.shape[0]], (((0,), (0,)), ((), ())),
+            preferred_element_type=F32,
         )
-        outgoing = jnp.dot(dispatch, moe_halves, preferred_element_type=F32).astype(BF)
-        if gate_on is not None:
-            outgoing, _ = lax.optimization_barrier((outgoing, gate_on))
-        mine = lax.all_to_all(outgoing, DP, split_axis=0, concat_axis=0, tiled=True)
-        theirs = other_core(mine)
-        gate_part = rows_by(gate_mine, mine) + rows_by(gate_other, theirs)
-        up_part = rows_by(up_mine, mine) + rows_by(up_other, theirs)
-        hidden = (jax.nn.silu(gate_part) * up_part).astype(BF)
-        hidden = jnp.dot(hidden, squeeze, preferred_element_type=F32).astype(BF)
-        gate_on = hidden
-        hidden_chunks.append(lax.all_gather(hidden, T, axis=0, tiled=True))
-
+
+    half_out = (out_of([own, below, above], 0) + out_of([far_first, far_second], 528)).astype(BF)
+    half_out = jnp.dot(squeeze, half_out, preferred_element_type=F32).astype(BF)
+    keep = lax.dynamic_slice_in_dim(half_out, core * 256, 256, 1)
+    give = lax.dynamic_slice_in_dim(half_out, (1 - core) * 256, 256, 1)
+    both = (keep.astype(F32) + other_core(give).astype(F32)).astype(BF)
+    returned = lax.all_to_all(both, DP, split_axis=0, concat_axis=0, tiled=True)
+    sums = [
+        lax.dot_general(part, returned, (((0,), (0,)), ((), ())), preferred_element_type=F32)
+        for part in combine
+    ]
     result = mixed_cols.astype(F32)
-    sums = [0.0, 0.0]
-    for k in range(CHUNKS):
-        half_out = lax.dot_general(
-            hidden_chunks[k], expert_down[0], (((0,), (0,)), ((), ())), preferred_element_type=F32
-        ).astype(BF)
-        half_out = jnp.dot(squeeze, half_out, preferred_element_type=F32).astype(BF)
-        keep = lax.dynamic_slice_in_dim(half_out, core * 256, 256, 1)
-        give = lax.dynamic_slice_in_dim(half_out, (1 - core) * 256, 256, 1)
-        both = (keep.astype(F32) + other_core(give).astype(F32)).astype(BF)
-        returned = lax.all_to_all(both, DP, split_axis=0, concat_axis=0, tiled=True)
-        for h in range(2):
-            sums[h] = sums[h] + lax.dot_general(
-                combine[k][h], returned, (((0,), (0,)), ((), ())), preferred_element_type=F32
-            )
     hidden_out = (result + jnp.concatenate(sums, axis=1)).astype(BF)
     return (hidden_out, expand_block, output_block, cache_cols)
 

time: 530 us -> 485 us (0.915)
  waiting for transfers between devices: 160 us -> 137 us
  between operations: 14.7 us -> 1.39 us
  blocking collectives: 162 us -> 150 us
  starting transfers between devices: 102 us -> 110 us
    all_gather x2 -> x0, waiting for transfers between devices: 88 us -> none  [body(): hidden_chunks.append(lax.all_gather(hidden, T, axis=0, tiled=True))]
    ppermute x0 -> x4, waiting for transfers between devices: none -> 66.4 us  [the longest x1 26.7 us: body(): below = lax.ppermute(own, T, up_ring)]
    ppermute x0 -> x4, starting transfers between devices: none -> 18.6 us  [the longest x1 7.27 us: body(): far_second = lax.ppermute(above[88:], T, down_ring)]
    all_to_all x2 -> x1, starting transfers between devices: 33.6 us -> 15.6 us  [body(): returned = lax.all_to_all(both, DP, split_axis=0, concat_axis=0, tiled=True)]
    all_to_all x2 -> x1, blocking collectives: 126 us -> 111 us  [body(): mine = lax.all_to_all(outgoing, DP, split_axis=0, concat_axis=0, tiled=True)]
    ppermute x12, waiting for transfers between devices: 41.4 us -> 30.5 us  [shifted(): lax.ppermute(block, axis, [(j, (j + s) % 4) for j in range(4)])]
    all_to_all x2 -> x1, waiting for transfers between devices: 16.5 us -> 26.4 us  [body(): returned = lax.all_to_all(both, DP, split_axis=0, concat_axis=0, tiled=True)]
    ppermute x12, starting transfers between devices: 33.7 us -> 40.8 us  [shifted(): lax.ppermute(block, axis, [(j, (j + s) % 4) for j in range(4)])]
  transfers between devices with their start and end apart: 23 -> 22, of which waited for: 15 -> 13; matrix products, arithmetic and copies ran while one was open for 10% -> 6% of each run, Pallas kernels for 1% -> 1%
where the time goes in v2:
time: 485 us; the launch traced here: 484 us
  blocking collectives  150 us (31%)
  waiting for transfers between devices  137 us (28%)
  starting transfers between devices  110 us (23%)
  matrix products  42.6 us (9%)
  other arithmetic  18.2 us (4%)
  local copies, waits for them, and re-layouts  13.1 us (3%)
  Pallas kernels  12.8 us (3%)
    all_to_all x1, blocking collectives, body(): mine = lax.all_to_all(outgoing, DP, split_axis=0, concat_axis=0, tiled=True)  111 us
    ppermute x12, starting transfers between devices, shifted(): lax.ppermute(block, axis, [(j, (j + s) % 4) for j in range(4)])  40.8 us
    ppermute x12, waiting for transfers between devices, shifted(): lax.ppermute(block, axis, [(j, (j + s) % 4) for j in range(4)])  30.5 us
    ppermute x1, waiting for transfers between devices, body(): below = lax.ppermute(own, T, up_ring)  26.7 us
    all_to_all x1, waiting for transfers between devices, body(): returned = lax.all_to_all(both, DP, split_axis=0, concat_axis=0, tiled=True)  26.4 us
    ppermute x1, waiting for transfers between devices, body(): above = lax.ppermute(own, T, down_ring)  25.9 us
    all_gather x1, blocking collectives, body(): full_input = lax.all_gather(hidden_gated, T, axis=1, tiled=True)  21.4 us
    ppermute x4, starting transfers between devices, other_core(): return lax.ppermute(block, 'c', [(0, 1), (1, 0)])  19 us
  transfers between devices with their start and end apart: 22, of which 13 were waited for; matrix products, arithmetic and copies ran while one was open for 6% of the time, Pallas kernels for 1%

profile of v2, /device:TPU:1, one launch (start us, length us, event | category | flops | bytes accessed | tf_op | source)
XLA Modules:
  0.0 484.1 jit_solution(13797458076774989862)
XLA Ops:
  4.4 15.6 %all-to-all-start = ((bf16[4,4,2112]{2,1,0:T(4,128)(2,1)}), bf16[4,4,2112]{2,1,0:T(4,128)(2,1)S(1)}, u32[]{:S(2)}, u32[]{:S(2)}) async-start(bf16[4,4,2112]{2,1,0:T(4,128)(2,1)} %concatenate.35), calls=%async_computation | async-start | bytes 139264 | tf_op jit(solution)/shard_map/all_to_all | solution.py:147
  21.7 10.9 %all-to-all-done = bf16[4,4,2112]{2,1,0:T(4,128)(2,1)S(1)} async-done(((bf16[4,4,2112]{2,1,0:T(4,128)(2,1)}), bf16[4,4,2112]{2,1,0:T(4,128)(2,1)S(1)}, u32[]{:S(2)}, u32[]{:S(2)}) %all-to-all-start) | async-done | bytes 67616 | tf_op jit(solution)/shard_map/all_to_all | solution.py:147
  34.5 3.8 collective-permute-start.1
  38.3 3.3 collective-permute-start.2
  41.7 2.2 collective-permute-done.2
  43.9 3.2 collective-permute-start.3
  47.1 4.5 collective-permute-start.4
  51.7 3.0 collective-permute-start.5
  55.5 3.2 collective-permute-done.4
  58.7 3.4 collective-permute-done.5
  62.4 3.1 collective-permute-start.6
  65.5 4.4 collective-permute-start.7
  69.8 3.1 collective-permute-start.8
  73.1 3.6 collective-permute-done.6
  76.7 13.6 %collective-permute-done.7 = bf16[4,4,16,1088]{3,2,1,0:T(8,128)(2,1)S(1)} collective-permute-done((bf16[4,4,16,1088]{3,2,1,0:T(8,128)(2,1)S(1)}, bf16[4,4,16,1088]{3,2,1,0:T(8,128)(2,1)S(1)}, u32[]{:S(2)}, u32[]{:S(2)}) %collective-permute-start.7) | collective-permute-done | bytes 557088 | tf_op jit(solution)/shard_map/ppermute | solution.py:81
  90.4 4.5 collective-permute-done.8
  95.2 3.5 collective-permute-start.9
  101.7 2.3 select_convert_fusion.2
  104.3 4.0 collective-permute-start.10
  108.3 3.3 collective-permute-start.11
  111.7 3.2 collective-permute-start.12
  114.9 21.4 %all_gather.6 = bf16[128,2048]{1,0:T(8,128)(2,1)S(1)} all-gather(bf16[128,512]{1,0:T(8,128)(2,1)S(1)} %copy-done.18), channel_id=1, replica_groups=mesh['zl'=4,'y'=4,'x'=4,'c'=2,'t'=4] {'t'}, dimensions={1}, use_global_device_ids=true | all-gather | bytes 655360 | tf_op jit(solution)/shard_map/all_gather | solution.py:155
  139.0 7.2 %collective-permute-start.13 = (bf16[4,4,4,16,1024]{4,3,2,1,0:T(8,128)(2,1)}, bf16[4,4,4,16,1024]{4,3,2,1,0:T(8,128)(2,1)}, u32[]{:S(2)}, u32[]{:S(2)}) collective-permute-start(bf16[4,4,4,16,1024]{4,3,2,1,0:T(8,128)(2,1)} %pad_maximum_fusion.1), channel_id=1, source_target_pairs={{0,4},{4,0},{1,5},{5,1},{2,6},{6,2},{3,7},{7,3},{8,12},{12,8},{9,1... | collective-permute-start | bytes 6291464 | tf_op jit(solution)/shard_map/ppermute | solution.py:86
  147.7 6.8 %ordered.2 = (bf16[128,16,384]{2,1,0:T(8,128)(2,1)}, bf16[128,16,128]{2,1,0:T(8,128)(2,1)}, bf16[128,16,576]{2,1,0:T(8,128)(2,1)}) custom-call(s32[4]{0:T(128)} %pad_add_fusion.place_ref, bf16[64,16,1088]{2,1,0:T(8,128)(2,1)} %bitcast.90, bf16[64,16,1088]{2,1,0:T(8,128)(2,1)} %bitcast.95), custom_call_target="tpu_custom_call" | custom-call | tf_op jit(solution)/shard_map/ordered/pallas_call | solution.py:108
  154.6 2.9 convolution_convert_fusion.1
  163.9 17.0 %all_gather.7 = bf16[128,1024]{0,1:T(8,128)(2,1)S(1)} all-gather(bf16[128,256]{0,1:T(8,128)(2,1)S(1)} %bitcast.114), channel_id=1, replica_groups=mesh['zl'=4,'y'=4,'x'=4,'c'=2,'t'=4] {'t'}, dimensions={1}, use_global_device_ids=true | all-gather | bytes 327680 | tf_op jit(solution)/shard_map/all_gather | solution.py:194
  180.9 6.0 %ordered.3 = bf16[128,16,1024]{2,1,0:T(8,128)(2,1)} custom-call(s32[4]{0:T(128)} %pad_add_fusion.place_ref, bf16[64,16,1024]{2,1,0:T(8,128)(2,1)} %bitcast.33.mine_ref, bf16[64,16,1024]{2,1,0:T(8,128)(2,1)} %bitcast.34.theirs_ref), custom_call_target="tpu_custom_call" | custom-call | tf_op jit(solution)/shard_map/ordered/pallas_call | solution.py:108
  186.9 3.8 fusion.19
  193.2 111.3 %all_to_all.29 = bf16[128,16,1024]{2,1,0:T(8,128)(2,1)} all-to-all(bf16[128,16,1024]{2,1,0:T(8,128)(2,1)S(1)} %bitcast.93), channel_id=1, replica_groups=mesh['zl'=4,'y'=4,'x'=4,'c'=2,'t'=4] {'zl','y','x','c'}, dimensions={0} | all-to-all | bytes 8388608 | tf_op jit(solution)/shard_map/all_to_all | solution.py:246
  304.5 3.1 collective-permute-start.14
  307.6 3.8 fusion.53
  311.4 3.7 fusion.57
  315.2 4.9 %convolution_add_fusion = f32[176,2048]{1,0:T(8,128)} fusion(f32[176,2048]{1,0:T(8,128)S(1)} %fusion.53, bf16[2048,1024]{1,0:T(8,128)(2,1)} %collective-permute-done.14, bf16[1,2048,176]{1,2,0:T(8,128)(2,1)S(1)} %copy-done, s32[]{:T(128)S(6)} %select_n.176), kind=kOutput, calls=%fused_computation.13 | convolution fusion | flops 738557952 | bytes 7438340 | tf_op jit(solution)/shard_map/dot_general | solution.py:243
  320.1 7.9 %fusion.8 = bf16[176,1792]{1,0:T(8,128)(2,1)} fusion(s32[1792]{0:T(1024)S(1)} %fusion.93, f32[176,2048]{1,0:T(8,128)} %convolution_add_fusion, f32[176,2048]{1,0:T(8,128)S(1)} %fusion.57, bf16[2048,1024]{1,0:T(8,128)(2,1)} %collective-permute-done.14, bf16[1,2048,176]{1,2,0:T(8,128)(2,1)S(1)} %copy-done.15, s32[]{:T(128)S(6)} %select_n.176), kind=kOutput, calls=%fused_computation.15 | convolution fusion | flops 2036551680 | bytes 8077316 | tf_op jit(solution)/shard_map/dot_general | solution.py:254
  329.8 7.3 %collective-permute-start.16 = (bf16[176,1792]{1,0:T(8,128)(2,1)}, bf16[176,1792]{1,0:T(8,128)(2,1)S(1)}, u32[]{:S(2)}, u32[]{:S(2)}) collective-permute-start(bf16[176,1792]{1,0:T(8,128)(2,1)} %fusion.8), channel_id=1, source_target_pairs={{0,3},{1,0},{2,1},{3,2},{4,7},{5,4},{6,5},{7,6},{8,11},{9,8},{10,9... | collective-permute-start | bytes 1892360 | tf_op jit(solution)/shard_map/ppermute | solution.py:256
  337.1 26.7 %collective-permute-done.15 = bf16[176,1792]{1,0:T(8,128)(2,1)S(1)} collective-permute-done((bf16[176,1792]{1,0:T(8,128)(2,1)}, bf16[176,1792]{1,0:T(8,128)(2,1)S(1)}, u32[]{:S(2)}, u32[]{:S(2)}) %collective-permute-start.15) | collective-permute-done | bytes 630816 | tf_op jit(solution)/shard_map/ppermute | solution.py:255
  366.0 25.9 %collective-permute-done.16 = bf16[176,1792]{1,0:T(8,128)(2,1)S(1)} collective-permute-done((bf16[176,1792]{1,0:T(8,128)(2,1)}, bf16[176,1792]{1,0:T(8,128)(2,1)S(1)}, u32[]{:S(2)}, u32[]{:S(2)}) %collective-permute-start.16) | collective-permute-done | bytes 630816 | tf_op jit(solution)/shard_map/ppermute | solution.py:256
  392.8 7.3 %collective-permute-start.18 = (bf16[88,1792]{1,0:T(8,128)(2,1)S(1)}, bf16[88,1792]{1,0:T(8,128)(2,1)S(1)}, u32[]{:S(2)}, u32[]{:S(2)}) collective-permute-start(bf16[88,1792]{1,0:T(8,128)(2,1)S(1)} %slice.77), channel_id=1, source_target_pairs={{0,3},{1,0},{2,1},{3,2},{4,7},{5,4},{6,5},{7,6},{8,11},{9,8},{10,9... | collective-permute-start | bytes 946184 | tf_op jit(solution)/shard_map/ppermute | solution.py:258
  401.0 6.1 %collective-permute-done.17 = bf16[88,1792]{1,0:T(8,128)(2,1)S(1)} collective-permute-done((bf16[88,1792]{1,0:T(8,128)(2,1)S(1)}, bf16[88,1792]{1,0:T(8,128)(2,1)S(1)}, u32[]{:S(2)}, u32[]{:S(2)}) %collective-permute-start.17) | collective-permute-done | bytes 315424 | tf_op jit(solution)/shard_map/ppermute | solution.py:257
  407.1 7.6 %collective-permute-done.18 = bf16[88,1792]{1,0:T(8,128)(2,1)S(1)} collective-permute-done((bf16[88,1792]{1,0:T(8,128)(2,1)S(1)}, bf16[88,1792]{1,0:T(8,128)(2,1)S(1)}, u32[]{:S(2)}, u32[]{:S(2)}) %collective-permute-start.18) | collective-permute-done | bytes 315424 | tf_op jit(solution)/shard_map/ppermute | solution.py:258
  414.7 2.5 fusion.28
  417.2 8.2 %fusion.7 = bf16[2048,512]{1,0:T(8,128)(2,1)S(1)} fusion(s32[1792]{0:T(1024)S(1)} %fusion.93, f32[1792,512]{1,0:T(8,128)} %fusion.28, bf16[176,1792]{1,0:T(8,128)(2,1)} %copy-done.17, bf16[176,1792]{1,0:T(8,128)(2,1)} %copy-done.16, bf16[176,1792]{1,0:T(8,128)(2,1)} %fusion.8, bf16[176,512]{1,0:T(8,128)(2,1)} %get-tuple-element.20, ...), kind=kOutput, calls=%fused_computation.12 | convolution fusion | flops 4740833280 | bytes 8207360 | tf_op jit(solution)/shard_map/dot_general | solution.py:268
  426.5 5.2 %collective-permute-start.19 = (bf16[2048,256]{1,0:T(8,128)(2,1)}, bf16[2048,256]{1,0:T(8,128)(2,1)}, u32[]{:S(2)}, u32[]{:S(2)}) collective-permute-start(bf16[2048,256]{1,0:T(8,128)(2,1)} %constant_dynamic-slice_fusion.1), channel_id=1, source_target_pairs={{0,4},{4,0},{1,5},{5,1},{2,6},{6,2},{3,7},{7,3},{8,12},{12,8},{9,1... | collective-permute-start | bytes 3145736 | tf_op jit(solution)/shard_map/ppermute | solution.py:86
  431.7 2.6 collective-permute-done.19
  434.3 2.5 add_convert_fusion.1
  436.8 15.6 %all-to-all-start.2 = ((bf16[128,16,256]{2,1,0:T(8,128)(2,1)}), bf16[128,16,256]{2,1,0:T(8,128)(2,1)S(1)}, u32[]{:S(2)}, u32[]{:S(2)}) async-start(bf16[128,16,256]{2,1,0:T(8,128)(2,1)} %bitcast.46), calls=%async_computation.2 | async-start | bytes 2097152 | tf_op jit(solution)/shard_map/all_to_all | solution.py:272
  453.3 2.3 constant_dynamic-slice_fusion
  455.6 26.4 %all-to-all-done.2 = bf16[128,16,256]{2,1,0:T(8,128)(2,1)S(1)} async-done(((bf16[128,16,256]{2,1,0:T(8,128)(2,1)}), bf16[128,16,256]{2,1,0:T(8,128)(2,1)S(1)}, u32[]{:S(2)}, u32[]{:S(2)}) %all-to-all-start.2) | async-done | bytes 1048608 | tf_op jit(solution)/shard_map/all_to_all | solution.py:272
  (128 shorter events, 34.9 us)
Async XLA Ops:
  0.6 307.0 %copy-start = (bf16[1,2048,176]{1,2,0:T(8,128)(2,1)S(1)}, bf16[1,2048,176]{1,2,0:T(8,128)(2,1)}, u32[]{:S(2)}) copy-start(bf16[1,2048,176]{1,2,0:T(8,128)(2,1)} %param.26) | copy-start | bytes 2162692
  4.4 28.1 %all-to-all-start = ((bf16[4,4,2112]{2,1,0:T(4,128)(2,1)}), bf16[4,4,2112]{2,1,0:T(4,128)(2,1)S(1)}, u32[]{:S(2)}, u32[]{:S(2)}) async-start(bf16[4,4,2112]{2,1,0:T(4,128)(2,1)} %concatenate.35), calls=%async_computation | async-start | bytes 139264 | tf_op jit(solution)/shard_map/all_to_all | solution.py:147
  32.6 9.1 %collective-permute-start = (bf16[16,2112]{1,0:T(8,128)(2,1)S(1)}, bf16[16,2112]{1,0:T(8,128)(2,1)S(1)}, u32[]{:S(2)}, u32[]{:S(2)}) collective-permute-start(bf16[16,2112]{1,0:T(8,128)(2,1)S(1)} %reshape.389), channel_id=1, source_target_pairs={{0,128},{128,256},{256,384},{384,0},{1,129},{129,257},{257,385},{3... | collective-permute-start | bytes 202760 | tf_op jit(solution)/shard_map/ppermute | solution.py:81
  34.5 7.2 %collective-permute-start.1 = (bf16[16,2112]{1,0:T(8,128)(2,1)S(1)}, bf16[16,2112]{1,0:T(8,128)(2,1)S(1)}, u32[]{:S(2)}, u32[]{:S(2)}) collective-permute-start(bf16[16,2112]{1,0:T(8,128)(2,1)S(1)} %reshape.389), channel_id=1, source_target_pairs={{0,256},{128,384},{256,0},{384,128},{1,257},{129,385},{257,1},{385... | collective-permute-start | bytes 202760 | tf_op jit(solution)/shard_map/ppermute | solution.py:81
  38.3 5.5 %collective-permute-start.2 = (bf16[16,2112]{1,0:T(8,128)(2,1)S(1)}, bf16[16,2112]{1,0:T(8,128)(2,1)S(1)}, u32[]{:S(2)}, u32[]{:S(2)}) collective-permute-start(bf16[16,2112]{1,0:T(8,128)(2,1)S(1)} %reshape.389), channel_id=1, source_target_pairs={{0,384},{128,0},{256,128},{384,256},{1,385},{129,1},{257,129},{385... | collective-permute-start | bytes 202760 | tf_op jit(solution)/shard_map/ppermute | solution.py:81
  43.9 29.1 %copy-start.19 = (s32[128,6]{0,1:T(8,128)S(1)}, s32[128,6]{0,1:T(8,128)}, u32[]{:S(2)}) copy-start(s32[128,6]{0,1:T(8,128)} %param.16) | copy-start | bytes 9220
  43.9 11.6 %collective-permute-start.3 = (bf16[4,16,2112]{2,1,0:T(8,128)(2,1)S(1)}, bf16[4,16,2112]{2,1,0:T(8,128)(2,1)S(1)}, u32[]{:S(2)}, u32[]{:S(2)}) collective-permute-start(bf16[4,16,2112]{2,1,0:T(8,128)(2,1)S(1)} %get-tuple-element.26), channel_id=1, source_target_pairs={{0,32},{32,64},{64,96},{96,0},{1,33},{33,65},{65,97},{97,1},{2,34}... | collective-permute-start | bytes 811016 | tf_op jit(solution)/shard_map/ppermute | solution.py:81
  47.1 11.5 %collective-permute-start.4 = (bf16[4,16,2112]{2,1,0:T(8,128)(2,1)S(1)}, bf16[4,16,2112]{2,1,0:T(8,128)(2,1)S(1)}, u32[]{:S(2)}, u32[]{:S(2)}) collective-permute-start(bf16[4,16,2112]{2,1,0:T(8,128)(2,1)S(1)} %get-tuple-element.26), channel_id=1, source_target_pairs={{0,64},{32,96},{64,0},{96,32},{1,65},{33,97},{65,1},{97,33},{2,66}... | collective-permute-start | bytes 811016 | tf_op jit(solution)/shard_map/ppermute | solution.py:81
  51.7 10.4 %collective-permute-start.5 = (bf16[4,16,2112]{2,1,0:T(8,128)(2,1)S(1)}, bf16[4,16,2112]{2,1,0:T(8,128)(2,1)S(1)}, u32[]{:S(2)}, u32[]{:S(2)}) collective-permute-start(bf16[4,16,2112]{2,1,0:T(8,128)(2,1)S(1)} %get-tuple-element.26), channel_id=1, source_target_pairs={{0,96},{32,0},{64,32},{96,64},{1,97},{33,1},{65,33},{97,65},{2,98}... | collective-permute-start | bytes 811016 | tf_op jit(solution)/shard_map/ppermute | solution.py:81
  62.4 14.4 %collective-permute-start.6 = (bf16[4,4,16,1088]{3,2,1,0:T(8,128)(2,1)S(1)}, bf16[4,4,16,1088]{3,2,1,0:T(8,128)(2,1)S(1)}, u32[]{:S(2)}, u32[]{:S(2)}) collective-permute-start(bf16[4,4,16,1088]{3,2,1,0:T(8,128)(2,1)S(1)} %get-tuple-element.17), channel_id=1, source_target_pairs={{0,8},{8,16},{16,24},{24,0},{1,9},{9,17},{17,25},{25,1},{2,10},{10... | collective-permute-start | bytes 1671176 | tf_op jit(solution)/shard_map/ppermute | solution.py:81
  65.5 24.9 %collective-permute-start.7 = (bf16[4,4,16,1088]{3,2,1,0:T(8,128)(2,1)S(1)}, bf16[4,4,16,1088]{3,2,1,0:T(8,128)(2,1)S(1)}, u32[]{:S(2)}, u32[]{:S(2)}) collective-permute-start(bf16[4,4,16,1088]{3,2,1,0:T(8,128)(2,1)S(1)} %get-tuple-element.17), channel_id=1, source_target_pairs={{0,16},{8,24},{16,0},{24,8},{1,17},{9,25},{17,1},{25,9},{2,18},{10... | collective-permute-start | bytes 1671176 | tf_op jit(solution)/shard_map/ppermute | solution.py:81
  69.8 25.0 %collective-permute-start.8 = (bf16[4,4,16,1088]{3,2,1,0:T(8,128)(2,1)S(1)}, bf16[4,4,16,1088]{3,2,1,0:T(8,128)(2,1)S(1)}, u32[]{:S(2)}, u32[]{:S(2)}) collective-permute-start(bf16[4,4,16,1088]{3,2,1,0:T(8,128)(2,1)S(1)} %get-tuple-element.17), channel_id=1, source_target_pairs={{0,24},{8,0},{16,8},{24,16},{1,25},{9,1},{17,9},{25,17},{2,26},{10... | collective-permute-start | bytes 1671176 | tf_op jit(solution)/shard_map/ppermute | solution.py:81
  94.8 4.6 copy-start.23
  95.2 9.1 %copy-start.2 = (bf16[4,4,4,16,1088]{4,3,2,1,0:T(8,128)(2,1)}, bf16[4,4,4,16,1088]{4,3,2,1,0:T(8,128)(2,1)S(1)}, u32[]{:S(2)}) copy-start(bf16[4,4,4,16,1088]{4,3,2,1,0:T(8,128)(2,1)S(1)} %pad_maximum_fusion) | copy-start | bytes 6684676
  95.2 51.0 %collective-permute-start.9 = (bf16[4,4,4,16,1088]{4,3,2,1,0:T(8,128)(2,1)S(1)}, bf16[4,4,4,16,1088]{4,3,2,1,0:T(8,128)(2,1)S(1)}, u32[]{:S(2)}, u32[]{:S(2)}) collective-permute-start(bf16[4,4,4,16,1088]{4,3,2,1,0:T(8,128)(2,1)S(1)} %pad_maximum_fusion), channel_id=1, source_target_pairs={{0,4},{4,0},{1,5},{5,1},{2,6},{6,2},{3,7},{7,3},{8,12},{12,8},{9,1... | collective-permute-start | bytes 6684680 | tf_op jit(solution)/shard_map/ppermute | solution.py:86
  99.5 15.4 %copy-start.18 = (bf16[128,512]{1,0:T(8,128)(2,1)S(1)}, bf16[128,512]{1,0:T(8,128)(2,1)}, u32[]{:S(2)}) copy-start(bf16[128,512]{1,0:T(8,128)(2,1)} %param.14) | copy-start | bytes 393220
  104.3 33.0 %collective-permute-start.10 = (bf16[4,4,16,1024]{3,2,1,0:T(8,128)(2,1)S(1)}, bf16[4,4,16,1024]{3,2,1,0:T(8,128)(2,1)S(1)}, u32[]{:S(2)}, u32[]{:S(2)}) collective-permute-start(bf16[4,4,16,1024]{3,2,1,0:T(8,128)(2,1)S(1)} %pad_maximum_fusion.3), channel_id=1, source_target_pairs={{0,8},{8,16},{16,24},{24,0},{1,9},{9,17},{17,25},{25,1},{2,10},{10... | collective-permute-start | bytes 1572872 | tf_op jit(solution)/shard_map/ppermute | solution.py:81
  108.3 29.0 %collective-permute-start.11 = (bf16[4,4,16,1024]{3,2,1,0:T(8,128)(2,1)S(1)}, bf16[4,4,16,1024]{3,2,1,0:T(8,128)(2,1)S(1)}, u32[]{:S(2)}, u32[]{:S(2)}) collective-permute-start(bf16[4,4,16,1024]{3,2,1,0:T(8,128)(2,1)S(1)} %pad_maximum_fusion.3), channel_id=1, source_target_pairs={{0,16},{8,24},{16,0},{24,8},{1,17},{9,25},{17,1},{25,9},{2,18},{10... | collective-permute-start | bytes 1572872 | tf_op jit(solution)/shard_map/ppermute | solution.py:81
  111.7 25.7 %collective-permute-start.12 = (bf16[4,4,16,1024]{3,2,1,0:T(8,128)(2,1)S(1)}, bf16[4,4,16,1024]{3,2,1,0:T(8,128)(2,1)S(1)}, u32[]{:S(2)}, u32[]{:S(2)}) collective-permute-start(bf16[4,4,16,1024]{3,2,1,0:T(8,128)(2,1)S(1)} %pad_maximum_fusion.3), channel_id=1, source_target_pairs={{0,24},{8,0},{16,8},{24,16},{1,25},{9,1},{17,9},{25,17},{2,26},{10... | collective-permute-start | bytes 1572872 | tf_op jit(solution)/shard_map/ppermute | solution.py:81
  136.3 0.8 copy-start.3
  137.3 17.2 %copy-start.24 = (f32[128]{0:T(128)}, f32[128]{0:T(128)S(1)}, u32[]{:S(2)}) copy-start(f32[128]{0:T(128)S(1)} %add_rsqrt_fusion.2) | copy-start | bytes 1540
  139.0 41.9 %collective-permute-start.13 = (bf16[4,4,4,16,1024]{4,3,2,1,0:T(8,128)(2,1)}, bf16[4,4,4,16,1024]{4,3,2,1,0:T(8,128)(2,1)}, u32[]{:S(2)}, u32[]{:S(2)}) collective-permute-start(bf16[4,4,4,16,1024]{4,3,2,1,0:T(8,128)(2,1)} %pad_maximum_fusion.1), channel_id=1, source_target_pairs={{0,4},{4,0},{1,5},{5,1},{2,6},{6,2},{3,7},{7,3},{8,12},{12,8},{9,1... | collective-permute-start | bytes 6291464 | tf_op jit(solution)/shard_map/ppermute | solution.py:86
  146.3 1.4 copy-start.6
  147.7 6.8 %copy-start.4 = (bf16[128,2048]{1,0:T(8,128)(2,1)S(1)}, bf16[128,2048]{1,0:T(8,128)(2,1)}, u32[]{:S(2)}) copy-start(bf16[128,2048]{1,0:T(8,128)(2,1)} %copy-done.3) | copy-start | bytes 1572868
  147.7 6.8 %copy-start.20 = (f32[2048]{0:T(1024)S(1)}, f32[2048]{0:T(1024)}, u32[]{:S(2)}) copy-start(f32[2048]{0:T(1024)} %param.18) | copy-start | bytes 24580
  154.5 3.1 copy-start.13
  154.6 3.4 copy-start.22
  158.0 2.8 copy-start.7
  158.1 0.9 copy-start.8
  158.1 4.4 copy-start.25
  162.4 1.0 copy-start.14
  186.9 3.8 copy-start.21
  190.7 1.1 copy-start.11
  190.7 1.2 copy-start.12
  304.5 10.7 %collective-permute-start.14 = (bf16[2048,1024]{1,0:T(8,128)(2,1)}, bf16[2048,1024]{1,0:T(8,128)(2,1)}, u32[]{:S(2)}, u32[]{:S(2)}) collective-permute-start(bf16[2048,1024]{1,0:T(8,128)(2,1)} %bitcast.38), channel_id=1, source_target_pairs={{0,4},{4,0},{1,5},{5,1},{2,6},{6,2},{3,7},{7,3},{8,12},{12,8},{9,1... | collective-permute-start | bytes 12582920 | tf_op jit(solution)/shard_map/ppermute | solution.py:86
  307.6 3.8 copy-start.15
  320.1 80.1 %copy-start.10 = (bf16[1,704,512]{2,1,0:T(8,128)(2,1)S(1)}, bf16[1,704,512]{2,1,0:T(8,128)(2,1)}, u32[]{:S(2)}) copy-start(bf16[1,704,512]{2,1,0:T(8,128)(2,1)} %param.27) | copy-start | bytes 2162692
  327.9 35.9 %collective-permute-start.15 = (bf16[176,1792]{1,0:T(8,128)(2,1)}, bf16[176,1792]{1,0:T(8,128)(2,1)S(1)}, u32[]{:S(2)}, u32[]{:S(2)}) collective-permute-start(bf16[176,1792]{1,0:T(8,128)(2,1)} %fusion.8), channel_id=1, source_target_pairs={{0,1},{1,2},{2,3},{3,0},{4,5},{5,6},{6,7},{7,4},{8,9},{9,10},{10,1... | collective-permute-start | bytes 1892360 | tf_op jit(solution)/shard_map/ppermute | solution.py:255
  329.8 62.1 %collective-permute-start.16 = (bf16[176,1792]{1,0:T(8,128)(2,1)}, bf16[176,1792]{1,0:T(8,128)(2,1)S(1)}, u32[]{:S(2)}, u32[]{:S(2)}) collective-permute-start(bf16[176,1792]{1,0:T(8,128)(2,1)} %fusion.8), channel_id=1, source_target_pairs={{0,3},{1,0},{2,1},{3,2},{4,7},{5,4},{6,5},{7,6},{8,11},{9,8},{10,9... | collective-permute-start | bytes 1892360 | tf_op jit(solution)/shard_map/ppermute | solution.py:256
  363.8 28.1 %copy-start.16 = (bf16[176,1792]{1,0:T(8,128)(2,1)}, bf16[176,1792]{1,0:T(8,128)(2,1)S(1)}, u32[]{:S(2)}) copy-start(bf16[176,1792]{1,0:T(8,128)(2,1)S(1)} %collective-permute-done.15) | copy-start | bytes 1892356
  363.9 43.2 %collective-permute-start.17 = (bf16[88,1792]{1,0:T(8,128)(2,1)S(1)}, bf16[88,1792]{1,0:T(8,128)(2,1)S(1)}, u32[]{:S(2)}, u32[]{:S(2)}) collective-permute-start(bf16[88,1792]{1,0:T(8,128)(2,1)S(1)} %slice.76), channel_id=1, source_target_pairs={{0,1},{1,2},{2,3},{3,0},{4,5},{5,6},{6,7},{7,4},{8,9},{9,10},{10,1... | collective-permute-start | bytes 946184 | tf_op jit(solution)/shard_map/ppermute | solution.py:257
  391.9 0.9 copy-start.17
  392.8 21.9 %collective-permute-start.18 = (bf16[88,1792]{1,0:T(8,128)(2,1)S(1)}, bf16[88,1792]{1,0:T(8,128)(2,1)S(1)}, u32[]{:S(2)}, u32[]{:S(2)}) collective-permute-start(bf16[88,1792]{1,0:T(8,128)(2,1)S(1)} %slice.77), channel_id=1, source_target_pairs={{0,3},{1,0},{2,1},{3,2},{4,7},{5,4},{6,5},{7,6},{8,11},{9,8},{10,9... | collective-permute-start | bytes 946184 | tf_op jit(solution)/shard_map/ppermute | solution.py:258
  426.5 7.8 %collective-permute-start.19 = (bf16[2048,256]{1,0:T(8,128)(2,1)}, bf16[2048,256]{1,0:T(8,128)(2,1)}, u32[]{:S(2)}, u32[]{:S(2)}) collective-permute-start(bf16[2048,256]{1,0:T(8,128)(2,1)} %constant_dynamic-slice_fusion.1), channel_id=1, source_target_pairs={{0,4},{4,0},{1,5},{5,1},{2,6},{6,2},{3,7},{7,3},{8,12},{12,8},{9,1... | collective-permute-start | bytes 3145736 | tf_op jit(solution)/shard_map/ppermute | solution.py:86
  431.7 20.8 %copy-start.9 = (bf16[128,512]{0,1:T(8,128)(2,1)S(1)}, bf16[128,512]{0,1:T(8,128)(2,1)}, u32[]{:S(2)}) copy-start(bf16[128,512]{0,1:T(8,128)(2,1)} %copy-done.8) | copy-start | bytes 393220
  436.8 45.2 %copy-start.5 = (bf16[2048,128]{1,0:T(8,128)(2,1)S(1)}, bf16[2048,128]{1,0:T(8,128)(2,1)}, u32[]{:S(2)}) copy-start(bf16[2048,128]{1,0:T(8,128)(2,1)} %get-tuple-element.14) | copy-start | bytes 1572868
  436.8 45.2 %all-to-all-start.2 = ((bf16[128,16,256]{2,1,0:T(8,128)(2,1)}), bf16[128,16,256]{2,1,0:T(8,128)(2,1)S(1)}, u32[]{:S(2)}, u32[]{:S(2)}) async-start(bf16[128,16,256]{2,1,0:T(8,128)(2,1)} %bitcast.46), calls=%async_computation.2 | async-start | bytes 2097152 | tf_op jit(solution)/shard_map/all_to_all | solution.py:272
  453.3 30.8 %copy-start.1 = (bf16[1,2048,176]{1,2,0:T(8,128)(2,1)S(1)}, bf16[1,2048,176]{1,2,0:T(8,128)(2,1)}, u32[]{:S(2)}) copy-start(bf16[1,2048,176]{1,2,0:T(8,128)(2,1)} %param.26) | copy-start | bytes 2162692

commit v3 on v2

v3 whole, which is shorter than its diff:
```python
import math

import jax
import jax.numpy as jnp
from jax import lax
from jax.experimental import pallas as pl
from jax.experimental.pallas import tpu as pltpu
from jax.sharding import Mesh
from jax.sharding import PartitionSpec as P

D = 2048
NOPE = 128
ROPE = 64
VDIM = 128
LATENT = 512
EXPERTS = 64
CAP = 14
TOK = 128
PADDED = 16

DP = ("zl", "y", "x", "c")
T = "t"
BF = jnp.bfloat16
F32 = jnp.float32

rope_base = 50000.0


def rms_norm(values, gain_vector):
    mean_square = jnp.mean(values * values, axis=-1, keepdims=True)
    return values * lax.rsqrt(mean_square + 1e-06) * gain_vector


def positions_of(lengths, row_count):
    prompt_ends = jnp.cumsum(lengths, axis=1)
    starts = prompt_ends - lengths
    token_index = jnp.arange(row_count, dtype=jnp.int32)
    segment = jnp.sum(
        (token_index[None, :, None] >= prompt_ends[:, None, :]).astype(jnp.int32), axis=2
    )
    member = segment[:, :, None] == jnp.arange(lengths.shape[1], dtype=jnp.int32)[None, None, :]
    offset = jnp.sum(jnp.where(member, starts[:, None, :], 0), axis=2)
    return (segment, token_index[None, :] - offset)


def expert_ranks(routes):
    onehot = (routes[..., None] == jnp.arange(EXPERTS, dtype=jnp.int32)).astype(BF)
    per_token = jnp.sum(onehot, axis=1)
    index = jnp.arange(TOK, dtype=jnp.int32)
    earlier = (index[None, :] < index[:, None]).astype(BF)
    before = jnp.dot(earlier, per_token, preferred_element_type=F32)
    return jnp.sum(onehot.astype(F32) * before[:, None, :], axis=2).astype(jnp.int32)


def shifted(block, axis):
    return [block] + [
        lax.ppermute(block, axis, [(j, (j + s) % 4) for j in range(4)]) for s in range(1, 4)
    ]


def ring(block, axis):
    half = block.shape[0] // 2
    up, down = [(j, (j + 1) % 4) for j in range(4)], [(j, (j + 3) % 4) for j in range(4)]
    below, above = lax.ppermute(block, axis, up), lax.ppermute(block, axis, down)
    far = [lax.ppermute(below[:half], axis, up), lax.ppermute(above[half:], axis, down)]
    return [block, below, jnp.concatenate(far), above]


def other_core(block):
    return lax.ppermute(block, "c", [(0, 1), (1, 0)])


VMEM = pl.BlockSpec(memory_space=pltpu.VMEM)
SMEM = pl.BlockSpec(memory_space=pltpu.SMEM)
NT = (((1,), (1,)), ((), ()))


def pack_rows(hidden_in, query, latent, expand, output):
    def kernel(hidden_ref, q_ref, l_ref, e_ref, o_ref, out_ref, rows):
        out_ref[0:128, :] = hidden_ref[...]
        tail_a, tail_b = l_ref[:, 512:544], l_ref[:, 544:576]
        tail = [tail_a, tail_a, tail_b, tail_b]
        for t in range(4):
            q = q_ref[:, t * 384 : (t + 1) * 384]
            parts = [
                q[:, 0:128], q[:, 192:320],
                q[:, 128:160], q[:, 320:352], q[:, 160:192], q[:, 352:384],
            ]
            rows[t * 4 : t * 4 + 4, :] = jnp.concatenate(parts + tail, axis=1)
            rows[20 + t : 21 + t, :] = e_ref[:, t * 512 : (t + 1) * 512]
        rows[16:20, :] = l_ref[:, 0:512]
        rows[24:28, :] = o_ref[:, 0:512]
        rows[28:32, :] = o_ref[:, 512:1024]
        out_ref[128:160, :] = rows[...].astype(BF)

    return pl.pallas_call(
        kernel,
        out_shape=jax.ShapeDtypeStruct((160, 512), BF),
        in_specs=[VMEM] * 5,
        out_specs=VMEM,
        scratch_shapes=[pltpu.VMEM((32, 512), F32)],
        name="pack_rows",
    )(hidden_in, query, latent, expand, output)


def pick_rows(place, everything):
    def kernel(place_ref, in_ref, out_ref, wide, rows):
        t = place_ref[4]
        wide[...] = in_ref[...].astype(F32)
        for s in range(4):
            lanes = slice(s * 512, (s + 1) * 512)
            q = wide[0:4, lanes]
            e = wide[20:21, lanes]
            for k in range(1, 4):
                q = jnp.where(t == k, wide[k * 4 : k * 4 + 4, lanes], q)
                e = jnp.where(t == k, wide[20 + k : 21 + k, lanes], e)
            rows[s * 4 : s * 4 + 4, :] = q
            rows[16 + s * 4 : 20 + s * 4, :] = wide[16:20, lanes]
            rows[32 + s : 33 + s, :] = e
            rows[36 + s : 37 + s, :] = e
            rows[40 + s * 4 : 44 + s * 4, :] = wide[24:28, lanes]
            rows[56 + s * 4 : 60 + s * 4, :] = wide[28:32, lanes]
        out_ref[...] = rows[...].astype(BF)

    return pl.pallas_call(
        kernel,
        grid=(1,),
        out_shape=jax.ShapeDtypeStruct((72, 512), BF),
        in_specs=[SMEM, pl.BlockSpec((32, 2048), lambda i: (4, 0))],
        out_specs=pl.BlockSpec((72, 512), lambda i: (0, 0)),
        scratch_shapes=[pltpu.VMEM((32, 2048), F32), pltpu.VMEM((72, 512), F32)],
        name="pick_rows",
    )(place, everything)


def in_order(place_ref, visit):
    zl, y, x = place_ref[0], place_ref[1], place_ref[2]

    def source_of(i):
        row_zl, row_y, row_x = i // 16, (i // 4) % 4, i % 4
        return ((x - row_x + 4) % 4 * 4 + (y - row_y + 4) % 4) * 4 + (zl - row_zl + 4) % 4

    def step(j, carry):
        visit(j, (source_of(2 * j), source_of(2 * j + 1)))
        return carry

    lax.fori_loop(0, 32, step, 0)


def attention(place, everything, mine, theirs, norm_gain, latent_gain, cosines, sines, allowed):
    def kernel(
        place_ref, in_ref, mine_ref, theirs_ref, norm_ref, gain_ref, cos_ref, sin_ref, allowed_ref,
        attended_ref, latent_ref, rope_ref, expand_ref, q_rows, l_rows,
    ):
        c = place_ref[3]
        low = lax.broadcasted_iota(jnp.int32, (8, 512), 0) < 4

        def visit(j, sources):
            pair = []
            for n, source in enumerate(sources):
                for ref, at in ((mine_ref, c), (theirs_ref, 1 - c)):
                    row = pl.multiple_of(((2 * j + n) * 2 + at) * 16, 16)
                    q_rows[pl.ds(row, 16), :] = ref[source, 0:16, :]
                    l_rows[pl.ds(row, 16), :] = ref[source, 16:32, :]
                own = mine_ref[source, 32:40, :].astype(F32)
                other = theirs_ref[source, 32:40, :].astype(F32)
                first = jnp.where(c == 0, own, other)
                second = jnp.where(c == 0, other, own)
                pair.append(jnp.where(low, first, second))
            row = pl.multiple_of(j * 16, 16)
            expand_ref[pl.ds(row, 16), :] = jnp.concatenate(pair, axis=0).astype(BF)

        in_order(place_ref, visit)
        normed = rms_norm(in_ref[...].astype(F32), norm_ref[...]).astype(BF)
        query = jnp.dot(normed, q_rows[...], preferred_element_type=F32)
        latent = jnp.dot(normed, l_rows[...], preferred_element_type=F32).astype(BF)
        latent = rms_norm(latent.astype(F32), gain_ref[...]).astype(BF)
        latent_ref[...] = latent
        cosine, sine = cos_ref[...], sin_ref[...]

        def rotated(v):
            return (v * cosine + pltpu.roll(v, 64, 1) * sine).astype(BF)

        key_rope = rotated(query[:, 384:512].astype(BF).astype(F32))
        rope_ref[...] = key_rope
        query_rope = rotated(query[:, 256:384])
        expanded = jnp.dot(latent, expand_ref[...], preferred_element_type=F32).astype(BF)
        head_of = (lax.broadcasted_iota(jnp.int32, (128, 128), 1) // 32) % 2
        for h in range(2):
            own_rope = jnp.where(head_of == h, query_rope.astype(F32), 0.0).astype(BF)
            scores = lax.dot_general(
                query[:, h * 128 : (h + 1) * 128].astype(BF),
                expanded[:, h * 256 : h * 256 + 128],
                NT,
                preferred_element_type=F32,
            )
            scores = scores + lax.dot_general(own_rope, key_rope, NT, preferred_element_type=F32)
            scores = scores * (1.0 / math.sqrt(NOPE + ROPE))
            scores = jnp.where(allowed_ref[...] > 0.0, scores, -1e30)
            powers = jnp.exp(scores - jnp.max(scores, axis=-1, keepdims=True))
            probs = (powers / jnp.sum(powers, axis=-1, keepdims=True)).astype(BF)
            out = jnp.dot(
                probs, expanded[:, h * 256 + 128 : h * 256 + 256], preferred_element_type=F32
            )
            attended_ref[:, h * 128 : (h + 1) * 128] = out.astype(BF)

    def whole(*shape):
        return pl.BlockSpec(shape, lambda i: (0,) * len(shape))

    return pl.pallas_call(
        kernel,
        grid=(1,),
        out_shape=[
            jax.ShapeDtypeStruct((128, 256), BF),
            jax.ShapeDtypeStruct((128, 512), BF),
            jax.ShapeDtypeStruct((128, 128), BF),
            jax.ShapeDtypeStruct((512, 512), BF),
        ],
        in_specs=[
            SMEM, whole(128, 2048), VMEM, VMEM,
            whole(1, 2048), whole(1, 512), whole(128, 128), whole(128, 128), whole(128, 128),
        ],
        out_specs=[whole(128, 256), whole(128, 512), whole(128, 128), whole(512, 512)],
        scratch_shapes=[pltpu.VMEM((2048, 512), BF), pltpu.VMEM((2048, 512), BF)],
        name="attention",
    )(
        place, everything, mine, theirs, norm_gain.reshape(1, 2048), latent_gain.reshape(1, 512),
        cosines, sines, allowed,
    )


def mix(place, everything, attended, mine, theirs, moe_gain):
    def kernel(
        place_ref, in_ref, attended_ref, mine_ref, theirs_ref, gain_ref,
        moe_ref, cols_ref, server_ref, w_first, w_second,
    ):
        c, t = place_ref[3], place_ref[4]

        def visit(j, sources):
            for n, source in enumerate(sources):
                for ref, at in ((mine_ref, c), (theirs_ref, 1 - c)):
                    row = pl.multiple_of(((2 * j + n) * 2 + at) * 16, 16)
                    first, second = ref[source, 0:16, :], ref[source, 16:32, :]
                    w_first[pl.ds(row, 16), :] = first
                    w_second[pl.ds(row, 16), :] = second
                    half = jnp.where(t < 2, first.astype(F32), second.astype(F32))
                    quarter = jnp.where(t % 2 == 0, half[:, 0:256], half[:, 256:512])
                    server_ref[pl.ds(row, 16), :] = quarter.astype(BF)

        in_order(place_ref, visit)
        total = lax.dot_general(
            attended_ref[:, 0:512], w_first[...], NT, preferred_element_type=F32
        ) + lax.dot_general(
            attended_ref[:, 512:1024], w_second[...], NT, preferred_element_type=F32
        )
        mixed = (in_ref[...].astype(F32) + total).astype(BF).astype(F32)
        cols = mixed[:, 0:512]
        for k in range(1, 4):
            cols = jnp.where(t == k, mixed[:, k * 512 : (k + 1) * 512], cols)
        cols_ref[...] = cols.astype(BF)
        moe = rms_norm(mixed, gain_ref[...]).astype(BF)
        moe_ref[0:128, :] = moe[:, 0:1024]
        moe_ref[128:256, :] = moe[:, 1024:2048]

    def whole(*shape):
        return pl.BlockSpec(shape, lambda i: (0,) * len(shape))

    return pl.pallas_call(
        kernel,
        grid=(1,),
        out_shape=[
            jax.ShapeDtypeStruct((256, 1024), BF),
            jax.ShapeDtypeStruct((128, 512), BF),
            jax.ShapeDtypeStruct((2048, 256), BF),
        ],
        in_specs=[SMEM, whole(128, 2048), whole(128, 1024), VMEM, VMEM, whole(1, 2048)],
        out_specs=[whole(256, 1024), whole(128, 512), whole(2048, 256)],
        scratch_shapes=[pltpu.VMEM((2048, 512), BF), pltpu.VMEM((2048, 512), BF)],
        name="mix",
    )(place, everything, attended, mine, theirs, moe_gain.reshape(1, 2048))


def body(
    hidden_in,
    lengths,
    routes,
    gate_weights,
    norm_gain,
    latent_gain,
    moe_gain,
    query_train,
    latent_train,
    expand_train,
    output_train,
    expert_gate,
    expert_up,
    expert_down,
):
    rank = lax.axis_index(T)
    core = lax.axis_index("c")
    place = jnp.stack([lax.axis_index(a) for a in DP + (T,)]).astype(jnp.int32)

    packed = pack_rows(hidden_in, query_train, latent_train, expand_train, output_train)
    everything = lax.all_gather(packed, T, axis=1, tiled=True)
    rows = pick_rows(place, everything)
    gathered = jnp.stack(shifted(rows, "zl"))
    gathered = jnp.stack(shifted(gathered, "y")).reshape(16, 72, 512)
    first_set = gathered[:, :40]
    second_set = gathered[:, 40:]
    first_mine = jnp.stack(ring(first_set, "x")).reshape(64, 40, 512)
    first_theirs = other_core(first_mine)
    second_gated, _ = lax.optimization_barrier((second_set, first_mine))
    second_mine = jnp.stack(ring(second_gated, "x")).reshape(64, 32, 512)
    second_theirs = other_core(second_mine)

    segment, position = positions_of(lengths, TOK)
    segment = segment[0]
    frequency = jnp.exp(jnp.arange(32, dtype=F32) * (-2.0 * math.log(rope_base) / 64))
    angles = position[0].astype(F32)[:, None] * frequency[None, :]
    cosine, sine = jnp.cos(angles), jnp.sin(angles)
    token_index = jnp.arange(TOK, dtype=jnp.int32)
    allowed = (segment[:, None] == segment[None, :]) & (token_index[None, :] <= token_index[:, None])
    attended, latent_normed, key_rope, expand_block = attention(
        place,
        everything,
        first_mine,
        first_theirs,
        norm_gain,
        latent_gain,
        jnp.concatenate([cosine] * 4, axis=1),
        jnp.concatenate([-sine, -sine, sine, sine], axis=1),
        allowed.astype(F32),
    )
    cache_full = jnp.concatenate([latent_normed, key_rope[:, 0:32], key_rope[:, 64:96]], axis=1)
    cache_cols = lax.dynamic_slice_in_dim(cache_full, rank * 144, 144, 1)
    attended_full = lax.all_gather(attended, T, axis=1, tiled=True)
    moe_halves, mixed_cols, output_block = mix(
        place, everything, attended_full, second_mine, second_theirs, moe_gain
    )

    slot_rank = expert_ranks(routes)
    gates = gate_weights.astype(F32)
    pad_ids = jnp.arange(EXPERTS * 2 * PADDED, dtype=jnp.int32)
    pad_core = (pad_ids // PADDED) % 2
    slot_at = routes * (2 * PADDED) + slot_rank
    matches = (pad_ids - pad_core * PADDED)[:, None, None] == slot_at[None, :, :]

    def placed_by(values):
        return jnp.sum(jnp.where(matches, values, 0.0), axis=2)

    placed = placed_by(1.0)
    dispatch = jnp.concatenate(
        [
            jnp.where(pad_core[:, None] == 0, placed, 0.0),
            jnp.where(pad_core[:, None] == 1, placed, 0.0),
        ],
        axis=1,
    ).astype(BF)

    weighted = placed_by(gates[None])
    combine = [jnp.where(pad_core[:, None] == h, weighted, 0.0).astype(BF) for h in range(2)]

    compact = jnp.arange(TOK * CAP, dtype=jnp.int32)
    taken = (compact // CAP) * PADDED + compact % CAP
    squeeze = (jnp.arange(TOK * PADDED, dtype=jnp.int32)[:, None] == taken[None, :]).astype(BF)

    def halves(matrix):
        return (
            lax.dynamic_slice_in_dim(matrix, core * (D // 2), D // 2, 0),
            lax.dynamic_slice_in_dim(matrix, (1 - core) * (D // 2), D // 2, 0),
        )

    gate_mine, gate_other = halves(expert_gate[0])
    up_mine, up_other = halves(expert_up[0])
    around = [(rank + 4 - back) % 4 for back in (0, 1, 3, 2)]
    down_around = jnp.concatenate(
        [lax.dynamic_slice_in_dim(expert_down[0], at * 176, 176, 0) for at in around], axis=0
    )

    def rows_by(weight, rows):
        return lax.dot_general(weight, rows, (((0,), (1,)), ((), ())), preferred_element_type=F32)

    outgoing = jnp.dot(dispatch, moe_halves, preferred_element_type=F32).astype(BF)
    mine = lax.all_to_all(outgoing, DP, split_axis=0, concat_axis=0, tiled=True)
    theirs = other_core(mine)
    gate_part = rows_by(gate_mine, mine) + rows_by(gate_other, theirs)
    up_part = rows_by(up_mine, mine) + rows_by(up_other, theirs)
    hidden = (jax.nn.silu(gate_part) * up_part).astype(BF)

    up_ring = [(j, (j + 1) % 4) for j in range(4)]
    down_ring = [(j, (j + 3) % 4) for j in range(4)]
    own = jnp.dot(hidden, squeeze, preferred_element_type=F32).astype(BF)
    below = lax.ppermute(own, T, up_ring)
    above = lax.ppermute(own, T, down_ring)
    far_first = lax.ppermute(below[:88], T, up_ring)
    far_second = lax.ppermute(above[88:], T, down_ring)

    def out_of(pieces, at):
        rows = jnp.concatenate(pieces, axis=0)
        return lax.dot_general(
            rows, down_around[at : at + rows.shape[0]], (((0,), (0,)), ((), ())),
            preferred_element_type=F32,
        )

    half_out = (out_of([own, below, above], 0) + out_of([far_first, far_second], 528)).astype(BF)
    half_out = jnp.dot(squeeze, half_out, preferred_element_type=F32).astype(BF)
    keep = lax.dynamic_slice_in_dim(half_out, core * 256, 256, 1)
    give = lax.dynamic_slice_in_dim(half_out, (1 - core) * 256, 256, 1)
    both = (keep.astype(F32) + other_core(give).astype(F32)).astype(BF)
    returned = lax.all_to_all(both, DP, split_axis=0, concat_axis=0, tiled=True)
    sums = [
        lax.dot_general(part, returned, (((0,), (0,)), ((), ())), preferred_element_type=F32)
        for part in combine
    ]
    result = mixed_cols.astype(F32)
    hidden_out = (result + jnp.concatenate(sums, axis=1)).astype(BF)
    return (hidden_out, expand_block, output_block, cache_cols)


def solution(mesh):
    fine = Mesh(mesh.devices.reshape(4, 4, 4, 2, 4), DP + (T,))
    rows_both = P(DP + (T,), None)
    in_specs = (
        P(DP, T),
        P(DP, None),
        P(DP, None),
        P(DP, None),
        P(),
        P(),
        P(),
        rows_both,
        rows_both,
        rows_both,
        rows_both,
        P(DP, None, T),
        P(DP, None, T),
        P(DP, None, T),
    )
    out_specs = (P(DP, T), P(None, T), P(None, T), P(DP, T))
    return jax.shard_map(body, mesh=fine, in_specs=in_specs, out_specs=out_specs, check_vma=False)
```

time: 485 us -> 471 us (0.971)
  blocking collectives: 150 us -> 165 us
  waiting for transfers between devices: 137 us -> 128 us
  matrix products: 42.6 us -> 34 us
  starting transfers between devices: 110 us -> 102 us
  Pallas kernels: 12.8 us -> 17.9 us
  local copies, waits for them, and re-layouts: 13.1 us -> 8.21 us
    ppermute x0 -> x8, starting transfers between devices: none -> 26.4 us  [the longest x2 9.13 us: ring(): lax.ppermute(above[half:], axis, down)]
    ppermute x12 -> x6, starting transfers between devices: 40.8 us -> 19.7 us  [shifted(): lax.ppermute(block, axis, [(j, (j + s) % 4) for j in range(4)])]
    ppermute x12 -> x6, waiting for transfers between devices: 30.5 us -> 9.56 us  [shifted(): lax.ppermute(block, axis, [(j, (j + s) % 4) for j in range(4)])]
    all_to_all x1 -> x0, starting transfers between devices: 15.6 us -> none  [body(): packed = lax.all_to_all(packed, T, split_axis=0, concat_axis=0, tiled=True)]
    ppermute x0 -> x8, waiting for transfers between devices: none -> 15.3 us  [the longest x2 8.03 us: ring(): lax.ppermute(block, axis, up)]
    all_gather x1, blocking collectives: 21.4 us -> 35.8 us  [body(): everything = lax.all_gather(packed, T, axis=1, tiled=True)]
    all_to_all x1 -> x0, waiting for transfers between devices: 10.9 us -> none  [body(): packed = lax.all_to_all(packed, T, split_axis=0, concat_axis=0, tiled=True)]
    dot_general x7 -> x0, matrix products: 8.87 us -> none  [the longest x1 3.81 us: body(): lax.dot_general(attended_full, output_full, (((1,), (1,)), ((), ())), pre...]
  transfers between devices with their start and end apart: 22 -> 23, of which waited for: 13 -> 14; matrix products, arithmetic and copies ran while one was open for 6% -> 4% of each run, Pallas kernels for 1% -> 2%
where the time goes in v3:
time: 471 us; the launch traced here: 470 us
  blocking collectives  165 us (35%)
  waiting for transfers between devices  128 us (27%)
  starting transfers between devices  102 us (22%)
  matrix products  34 us (7%)
  Pallas kernels  17.9 us (4%)
  other arithmetic  14.3 us (3%)
  local copies, waits for them, and re-layouts  8.21 us (2%)
    all_to_all x1, blocking collectives, body(): mine = lax.all_to_all(outgoing, DP, split_axis=0, concat_axis=0, tiled=True)  109 us
    all_gather x1, blocking collectives, body(): everything = lax.all_gather(packed, T, axis=1, tiled=True)  35.8 us
    ppermute x1, waiting for transfers between devices, body(): above = lax.ppermute(own, T, down_ring)  30.1 us
    all_to_all x1, waiting for transfers between devices, body(): returned = lax.all_to_all(both, DP, split_axis=0, concat_axis=0, tiled=True)  28.6 us
    ppermute x1, waiting for transfers between devices, body(): below = lax.ppermute(own, T, up_ring)  28.1 us
    ppermute x4, starting transfers between devices, other_core(): return lax.ppermute(block, 'c', [(0, 1), (1, 0)])  22.1 us
    ppermute x6, starting transfers between devices, shifted(): lax.ppermute(block, axis, [(j, (j + s) % 4) for j in range(4)])  19.7 us
    all_gather x1, blocking collectives, body(): attended_full = lax.all_gather(attended, T, axis=1, tiled=True)  19.6 us
  transfers between devices with their start and end apart: 23, of which 14 were waited for; matrix products, arithmetic and copies ran while one was open for 4% of the time, Pallas kernels for 2%

profile of v3, /device:TPU:1, one launch (start us, length us, event | category | flops | bytes accessed | tf_op | source)
XLA Modules:
  0.0 470.1 jit_solution(2193737542228337467)
XLA Ops:
  2.4 35.8 %all_gather.6.in_ref = bf16[160,2048]{1,0:T(8,128)(2,1)} all-gather(bf16[160,512]{1,0:T(8,128)(2,1)} %pack_rows.1), channel_id=1, replica_groups=mesh['zl'=4,'y'=4,'x'=4,'c'=2,'t'=4] {'t'}, dimensions={1}, use_global_device_ids=true | all-gather | bytes 819200 | tf_op jit(solution)/shard_map/all_gather | solution.py:304
  40.4 1.9 collective-permute-start
  42.3 4.1 collective-permute-start.1
  46.4 3.0 collective-permute-start.2
  49.4 2.9 collective-permute-done.2
  53.2 3.2 collective-permute-start.3
  56.5 4.5 collective-permute-start.4
  61.0 3.0 collective-permute-start.5
  64.0 3.6 collective-permute-done.4
  67.6 3.1 collective-permute-done.5
  70.9 3.1 collective-permute-start.6
  74.1 3.4 collective-permute-start.8
  77.5 8.0 %collective-permute-done.6 = bf16[16,40,512]{2,1,0:T(8,128)(2,1)S(1)} collective-permute-done((bf16[16,40,512]{2,1,0:T(8,128)(2,1)S(1)}, bf16[16,40,512]{2,1,0:T(8,128)(2,1)S(1)}, u32[]{:S(2)}, u32[]{:S(2)}) %collective-permute-start.6) | collective-permute-done | bytes 655392 | tf_op jit(solution)/shard_map/ppermute | solution.py:64
  89.7 4.6 collective-permute-start.9
  95.4 3.2 collective-permute-done.9
  100.0 2.5 collective-permute-start.11
  102.6 4.4 collective-permute-start.13
  107.1 9.3 %collective-permute-start.10 = (bf16[64,40,512]{2,1,0:T(8,128)(2,1)S(1)}, bf16[64,40,512]{2,1,0:T(8,128)(2,1)S(1)}, u32[]{:S(2)}, u32[]{:S(2)}) collective-permute-start(bf16[64,40,512]{2,1,0:T(8,128)(2,1)S(1)} %bitcast.69), channel_id=1, source_target_pairs={{0,4},{4,0},{1,5},{5,1},{2,6},{6,2},{3,7},{7,3},{8,12},{12,8},{9,1... | collective-permute-start | bytes 7864328 | tf_op jit(solution)/shard_map/ppermute | solution.py:70
  116.5 1.9 collective-permute-start.12
  118.5 4.6 collective-permute-start.14
  128.0 6.2 %collective-permute-start.15 = (bf16[64,32,512]{2,1,0:T(8,128)(2,1)}, bf16[64,32,512]{2,1,0:T(8,128)(2,1)}, u32[]{:S(2)}, u32[]{:S(2)}) collective-permute-start(bf16[64,32,512]{2,1,0:T(8,128)(2,1)} %bitcast.27.mine_ref), channel_id=1, source_target_pairs={{0,4},{4,0},{1,5},{5,1},{2,6},{6,2},{3,7},{7,3},{8,12},{12,8},{9,1... | collective-permute-start | bytes 6291464 | tf_op jit(solution)/shard_map/ppermute | solution.py:70
  136.2 2.2 fusion.4
  138.4 2.4 select_convert_fusion.2
  142.3 7.2 %attention.1 = (bf16[128,256]{1,0:T(8,128)(2,1)}, bf16[128,512]{1,0:T(8,128)(2,1)}, bf16[128,128]{1,0:T(8,128)(2,1)}, bf16[512,512]{1,0:T(8,128)(2,1)}) custom-call(s32[5]{0:T(128)} %stack.83.place_ref, bf16[160,2048]{1,0:T(8,128)(2,1)} %all_gather.6.in_ref, bf16[64,40,512]{2,1,0:T(8,128)(2,1)} %bitcast.70, bf16[64,40,512]{2,1,0:T(8,128)(2,1)} %copy-done.3, ...), custom_call_target="tpu_custom_call" | custom-call | tf_op jit(solution)/shard_map/attention/pallas_call | solution.py:210
  149.5 19.6 %all_gather.7.attended_ref = bf16[128,1024]{1,0:T(8,128)(2,1)} all-gather(bf16[128,256]{1,0:T(8,128)(2,1)} %get-tuple-element.12), channel_id=1, replica_groups=mesh['zl'=4,'y'=4,'x'=4,'c'=2,'t'=4] {'t'}, dimensions={1}, use_global_device_ids=true | all-gather | bytes 327680 | tf_op jit(solution)/shard_map/all_gather | solution.py:336
  169.1 7.3 %mix.1 = (bf16[256,1024]{1,0:T(8,128)(2,1)}, bf16[128,512]{1,0:T(8,128)(2,1)}, bf16[2048,256]{1,0:T(8,128)(2,1)}) custom-call(s32[5]{0:T(128)} %stack.83.place_ref, bf16[160,2048]{1,0:T(8,128)(2,1)} %all_gather.6.in_ref, bf16[128,1024]{1,0:T(8,128)(2,1)} %all_gather.7.attended_ref, bf16[64,32,512]{2,1,0:T(8,128)(2,1)} %bitcast.27.mine_ref, ...), custom_call_target="tpu_custom_call" | custom-call | tf_op jit(solution)/shard_map/mix/pallas_call | solution.py:268
  176.4 2.3 convolution_convert_fusion
  178.7 109.4 %all_to_all.24 = bf16[128,16,1024]{2,1,0:T(8,128)(2,1)} all-to-all(bf16[128,16,1024]{2,1,0:T(8,128)(2,1)S(1)} %bitcast.68), channel_id=1, replica_groups=mesh['zl'=4,'y'=4,'x'=4,'c'=2,'t'=4] {'zl','y','x','c'}, dimensions={0} | all-to-all | bytes 8388608 | tf_op jit(solution)/shard_map/all_to_all | solution.py:384
  288.1 3.2 collective-permute-start.16
  291.4 3.8 fusion.36
  295.2 3.7 fusion.40
  298.9 4.9 %convolution_add_fusion = f32[176,2048]{1,0:T(8,128)} fusion(f32[176,2048]{1,0:T(8,128)S(1)} %fusion.36, bf16[2048,1024]{1,0:T(8,128)(2,1)} %collective-permute-done.16, bf16[1,2048,176]{1,2,0:T(8,128)(2,1)S(1)} %copy-done, s32[]{:T(128)S(6)} %select_n.164), kind=kOutput, calls=%fused_computation.13 | convolution fusion | flops 738557952 | bytes 7438340 | tf_op jit(solution)/shard_map/dot_general | solution.py:381
  303.8 7.1 %fusion.7 = bf16[176,1792]{1,0:T(8,128)(2,1)S(1)} fusion(s32[1792]{0:T(1024)S(1)} %fusion.65, f32[176,2048]{1,0:T(8,128)} %convolution_add_fusion, f32[176,2048]{1,0:T(8,128)S(1)} %fusion.40, bf16[2048,1024]{1,0:T(8,128)(2,1)} %collective-permute-done.16, bf16[1,2048,176]{1,2,0:T(8,128)(2,1)} %param.25, s32[]{:T(128)S(6)} %select_n.164), kind=kOutput, calls=%fused_computation.15 | convolution fusion | flops 2036551680 | bytes 8076292 | tf_op jit(solution)/shard_map/dot_general | solution.py:392
  310.9 7.3 %collective-permute-start.17 = (bf16[176,1792]{1,0:T(8,128)(2,1)S(1)}, bf16[176,1792]{1,0:T(8,128)(2,1)S(1)}, u32[]{:S(2)}, u32[]{:S(2)}) collective-permute-start(bf16[176,1792]{1,0:T(8,128)(2,1)S(1)} %fusion.7), channel_id=1, source_target_pairs={{0,1},{1,2},{2,3},{3,0},{4,5},{5,6},{6,7},{7,4},{8,9},{9,10},{10,1... | collective-permute-start | bytes 1892360 | tf_op jit(solution)/shard_map/ppermute | solution.py:393
  318.2 1.9 collective-permute-start.18
  320.2 28.1 %collective-permute-done.17 = bf16[176,1792]{1,0:T(8,128)(2,1)S(1)} collective-permute-done((bf16[176,1792]{1,0:T(8,128)(2,1)S(1)}, bf16[176,1792]{1,0:T(8,128)(2,1)S(1)}, u32[]{:S(2)}, u32[]{:S(2)}) %collective-permute-start.17) | collective-permute-done | bytes 630816 | tf_op jit(solution)/shard_map/ppermute | solution.py:393
  348.3 7.3 %collective-permute-start.19 = (bf16[88,1792]{1,0:T(8,128)(2,1)S(1)}, bf16[88,1792]{1,0:T(8,128)(2,1)S(1)}, u32[]{:S(2)}, u32[]{:S(2)}) collective-permute-start(bf16[88,1792]{1,0:T(8,128)(2,1)S(1)} %slice.46), channel_id=1, source_target_pairs={{0,1},{1,2},{2,3},{3,0},{4,5},{5,6},{6,7},{7,4},{8,9},{9,10},{10,1... | collective-permute-start | bytes 946184 | tf_op jit(solution)/shard_map/ppermute | solution.py:395
  355.6 30.1 %collective-permute-done.18 = bf16[176,1792]{1,0:T(8,128)(2,1)S(1)} collective-permute-done((bf16[176,1792]{1,0:T(8,128)(2,1)S(1)}, bf16[176,1792]{1,0:T(8,128)(2,1)S(1)}, u32[]{:S(2)}, u32[]{:S(2)}) %collective-permute-start.18) | collective-permute-done | bytes 630816 | tf_op jit(solution)/shard_map/ppermute | solution.py:394
  386.5 2.6 collective-permute-start.20
  390.0 2.8 collective-permute-done.19
  392.8 10.7 %collective-permute-done.20 = bf16[88,1792]{1,0:T(8,128)(2,1)S(1)} collective-permute-done((bf16[88,1792]{1,0:T(8,128)(2,1)S(1)}, bf16[88,1792]{1,0:T(8,128)(2,1)S(1)}, u32[]{:S(2)}, u32[]{:S(2)}) %collective-permute-start.20) | collective-permute-done | bytes 315424 | tf_op jit(solution)/shard_map/ppermute | solution.py:396
  403.5 2.5 fusion.16
  405.9 8.2 %fusion.6 = bf16[2048,512]{1,0:T(8,128)(2,1)S(1)} fusion(s32[1792]{0:T(1024)S(1)} %fusion.65, f32[1792,512]{1,0:T(8,128)} %fusion.16, bf16[176,1792]{1,0:T(8,128)(2,1)} %copy-done.11, bf16[176,1792]{1,0:T(8,128)(2,1)} %copy-done.10, bf16[176,1792]{1,0:T(8,128)(2,1)} %copy-done.17, bf16[176,512]{1,0:T(8,128)(2,1)} %get-tuple-element.38, ...), kind=kOutput, calls=%fused_computation.11 | convolution fusion | flops 4740833280 | bytes 8207360 | tf_op jit(solution)/shard_map/dot_general | solution.py:406
  415.2 3.3 collective-permute-start.21
  418.6 2.6 collective-permute-done.21
  421.1 2.5 add_convert_fusion.1
  423.7 14.8 %all-to-all-start.1 = ((bf16[128,16,256]{2,1,0:T(8,128)(2,1)}), bf16[128,16,256]{2,1,0:T(8,128)(2,1)S(1)}, u32[]{:S(2)}, u32[]{:S(2)}) async-start(bf16[128,16,256]{2,1,0:T(8,128)(2,1)} %bitcast.39), calls=%async_computation.1 | async-start | bytes 2097152 | tf_op jit(solution)/shard_map/all_to_all | solution.py:410
  439.4 28.6 %all-to-all-done.1 = bf16[128,16,256]{2,1,0:T(8,128)(2,1)S(1)} async-done(((bf16[128,16,256]{2,1,0:T(8,128)(2,1)}), bf16[128,16,256]{2,1,0:T(8,128)(2,1)S(1)}, u32[]{:S(2)}, u32[]{:S(2)}) %all-to-all-start.1) | async-done | bytes 1048608 | tf_op jit(solution)/shard_map/all_to_all | solution.py:410
  (93 shorter events, 26.3 us)
Async XLA Ops:
  0.6 290.7 %copy-start = (bf16[1,2048,176]{1,2,0:T(8,128)(2,1)S(1)}, bf16[1,2048,176]{1,2,0:T(8,128)(2,1)}, u32[]{:S(2)}) copy-start(bf16[1,2048,176]{1,2,0:T(8,128)(2,1)} %param.26) | copy-start | bytes 2162692
  40.4 9.0 %collective-permute-start = (bf16[72,512]{1,0:T(8,128)(2,1)}, bf16[72,512]{1,0:T(8,128)(2,1)S(1)}, u32[]{:S(2)}, u32[]{:S(2)}) collective-permute-start(bf16[72,512]{1,0:T(8,128)(2,1)} %pick_rows.1), channel_id=1, source_target_pairs={{0,128},{128,256},{256,384},{384,0},{1,129},{129,257},{257,385},{3... | collective-permute-start | bytes 221192 | tf_op jit(solution)/shard_map/ppermute | solution.py:57
  42.3 7.1 %collective-permute-start.1 = (bf16[72,512]{1,0:T(8,128)(2,1)}, bf16[72,512]{1,0:T(8,128)(2,1)S(1)}, u32[]{:S(2)}, u32[]{:S(2)}) collective-permute-start(bf16[72,512]{1,0:T(8,128)(2,1)} %pick_rows.1), channel_id=1, source_target_pairs={{0,256},{128,384},{256,0},{384,128},{1,257},{129,385},{257,1},{385... | collective-permute-start | bytes 221192 | tf_op jit(solution)/shard_map/ppermute | solution.py:57
  46.4 5.9 %collective-permute-start.2 = (bf16[72,512]{1,0:T(8,128)(2,1)}, bf16[72,512]{1,0:T(8,128)(2,1)S(1)}, u32[]{:S(2)}, u32[]{:S(2)}) collective-permute-start(bf16[72,512]{1,0:T(8,128)(2,1)} %pick_rows.1), channel_id=1, source_target_pairs={{0,384},{128,0},{256,128},{384,256},{1,385},{129,1},{257,129},{385... | collective-permute-start | bytes 221192 | tf_op jit(solution)/shard_map/ppermute | solution.py:57
  53.2 10.7 %collective-permute-start.3 = (bf16[4,72,512]{2,1,0:T(8,128)(2,1)S(1)}, bf16[4,72,512]{2,1,0:T(8,128)(2,1)S(1)}, u32[]{:S(2)}, u32[]{:S(2)}) collective-permute-start(bf16[4,72,512]{2,1,0:T(8,128)(2,1)S(1)} %get-tuple-element.42), channel_id=1, source_target_pairs={{0,32},{32,64},{64,96},{96,0},{1,33},{33,65},{65,97},{97,1},{2,34}... | collective-permute-start | bytes 884744 | tf_op jit(solution)/shard_map/ppermute | solution.py:57
  56.5 11.1 %collective-permute-start.4 = (bf16[4,72,512]{2,1,0:T(8,128)(2,1)S(1)}, bf16[4,72,512]{2,1,0:T(8,128)(2,1)S(1)}, u32[]{:S(2)}, u32[]{:S(2)}) collective-permute-start(bf16[4,72,512]{2,1,0:T(8,128)(2,1)S(1)} %get-tuple-element.42), channel_id=1, source_target_pairs={{0,64},{32,96},{64,0},{96,32},{1,65},{33,97},{65,1},{97,33},{2,66}... | collective-permute-start | bytes 884744 | tf_op jit(solution)/shard_map/ppermute | solution.py:57
  61.0 9.7 %collective-permute-start.5 = (bf16[4,72,512]{2,1,0:T(8,128)(2,1)S(1)}, bf16[4,72,512]{2,1,0:T(8,128)(2,1)S(1)}, u32[]{:S(2)}, u32[]{:S(2)}) collective-permute-start(bf16[4,72,512]{2,1,0:T(8,128)(2,1)S(1)} %get-tuple-element.42), channel_id=1, source_target_pairs={{0,96},{32,0},{64,32},{96,64},{1,97},{33,1},{65,33},{97,65},{2,98}... | collective-permute-start | bytes 884744 | tf_op jit(solution)/shard_map/ppermute | solution.py:57
  70.8 23.5 %copy-start.18 = (s32[1,4]{1,0:T(1,128)S(1)}, s32[1,4]{1,0:T(1,128)}, u32[]{:S(2)}) copy-start(s32[1,4]{1,0:T(1,128)} %param.15) | copy-start | bytes 52
  70.9 14.5 %collective-permute-start.6 = (bf16[16,40,512]{2,1,0:T(8,128)(2,1)S(1)}, bf16[16,40,512]{2,1,0:T(8,128)(2,1)S(1)}, u32[]{:S(2)}, u32[]{:S(2)}) collective-permute-start(bf16[16,40,512]{2,1,0:T(8,128)(2,1)S(1)} %get-tuple-element.35), channel_id=1, source_target_pairs={{0,8},{8,16},{16,24},{24,0},{1,9},{9,17},{17,25},{25,1},{2,10},{10... | collective-permute-start | bytes 1966088 | tf_op jit(solution)/shard_map/ppermute | solution.py:64
  74.1 14.1 %collective-permute-start.8 = (bf16[16,40,512]{2,1,0:T(8,128)(2,1)S(1)}, bf16[16,40,512]{2,1,0:T(8,128)(2,1)S(1)}, u32[]{:S(2)}, u32[]{:S(2)}) collective-permute-start(bf16[16,40,512]{2,1,0:T(8,128)(2,1)S(1)} %get-tuple-element.35), channel_id=1, source_target_pairs={{0,24},{8,0},{16,8},{24,16},{1,25},{9,1},{17,9},{25,17},{2,26},{10... | collective-permute-start | bytes 1966088 | tf_op jit(solution)/shard_map/ppermute | solution.py:64
  86.2 9.2 %collective-permute-start.7 = (bf16[8,40,512]{2,1,0:T(8,128)(2,1)}, bf16[8,40,512]{2,1,0:T(8,128)(2,1)S(1)}, u32[]{:S(2)}, u32[]{:S(2)}) collective-permute-start(bf16[8,40,512]{2,1,0:T(8,128)(2,1)} %slice.41), channel_id=1, source_target_pairs={{0,8},{8,16},{16,24},{24,0},{1,9},{9,17},{17,25},{25,1},{2,10},{10... | collective-permute-start | bytes 983048 | tf_op jit(solution)/shard_map/ppermute | solution.py:65
  88.1 0.8 copy-start.6
  89.7 8.9 %collective-permute-start.9 = (bf16[8,40,512]{2,1,0:T(8,128)(2,1)}, bf16[8,40,512]{2,1,0:T(8,128)(2,1)}, u32[]{:S(2)}, u32[]{:S(2)}) collective-permute-start(bf16[8,40,512]{2,1,0:T(8,128)(2,1)} %slice.42), channel_id=1, source_target_pairs={{0,24},{8,0},{16,8},{24,16},{1,25},{9,1},{17,9},{25,17},{2,26},{10... | collective-permute-start | bytes 983048 | tf_op jit(solution)/shard_map/ppermute | solution.py:65
  94.5 5.2 %copy-start.7 = (bf16[16,40,512]{2,1,0:T(8,128)(2,1)S(1)}, bf16[16,40,512]{2,1,0:T(8,128)(2,1)}, u32[]{:S(2)}) copy-start(bf16[16,40,512]{2,1,0:T(8,128)(2,1)} %copy-done.6) | copy-start | bytes 1966084
  99.7 7.4 %copy-start.15 = (s32[128,6]{0,1:T(8,128)S(1)}, s32[128,6]{0,1:T(8,128)}, u32[]{:S(2)}) copy-start(s32[128,6]{0,1:T(8,128)} %param.16) | copy-start | bytes 9220
  99.7 23.4 %copy-start.16 = (bf16[128,6]{0,1:T(8,128)(2,1)S(1)}, bf16[128,6]{0,1:T(8,128)(2,1)}, u32[]{:S(2)}) copy-start(bf16[128,6]{0,1:T(8,128)(2,1)} %param.17) | copy-start | bytes 4612
  100.0 28.0 %copy-start.1 = (bf16[4,16,40,512]{3,2,1,0:T(8,128)(2,1)}, bf16[4,16,40,512]{3,2,1,0:T(8,128)(2,1)S(1)}, u32[]{:S(2)}) copy-start(bf16[4,16,40,512]{3,2,1,0:T(8,128)(2,1)S(1)} %pad_maximum_fusion) | copy-start | bytes 7864324
  100.0 16.4 %collective-permute-start.11 = (bf16[16,32,512]{2,1,0:T(8,128)(2,1)S(1)}, bf16[16,32,512]{2,1,0:T(8,128)(2,1)S(1)}, u32[]{:S(2)}, u32[]{:S(2)}) collective-permute-start(bf16[16,32,512]{2,1,0:T(8,128)(2,1)S(1)} %slice.43), channel_id=1, source_target_pairs={{0,8},{8,16},{16,24},{24,0},{1,9},{9,17},{17,25},{25,1},{2,10},{10... | collective-permute-start | bytes 1572872 | tf_op jit(solution)/shard_map/ppermute | solution.py:64
  102.6 15.9 %collective-permute-start.13 = (bf16[16,32,512]{2,1,0:T(8,128)(2,1)S(1)}, bf16[16,32,512]{2,1,0:T(8,128)(2,1)S(1)}, u32[]{:S(2)}, u32[]{:S(2)}) collective-permute-start(bf16[16,32,512]{2,1,0:T(8,128)(2,1)S(1)} %slice.43), channel_id=1, source_target_pairs={{0,24},{8,0},{16,8},{24,16},{1,25},{9,1},{17,9},{25,17},{2,26},{10... | collective-permute-start | bytes 1572872 | tf_op jit(solution)/shard_map/ppermute | solution.py:64
  107.1 33.6 %collective-permute-start.10 = (bf16[64,40,512]{2,1,0:T(8,128)(2,1)S(1)}, bf16[64,40,512]{2,1,0:T(8,128)(2,1)S(1)}, u32[]{:S(2)}, u32[]{:S(2)}) collective-permute-start(bf16[64,40,512]{2,1,0:T(8,128)(2,1)S(1)} %bitcast.69), channel_id=1, source_target_pairs={{0,4},{4,0},{1,5},{5,1},{2,6},{6,2},{3,7},{7,3},{8,12},{12,8},{9,1... | collective-permute-start | bytes 7864328 | tf_op jit(solution)/shard_map/ppermute | solution.py:70
  116.5 8.3 %collective-permute-start.12 = (bf16[8,32,512]{2,1,0:T(8,128)(2,1)S(1)}, bf16[8,32,512]{2,1,0:T(8,128)(2,1)S(1)}, u32[]{:S(2)}, u32[]{:S(2)}) collective-permute-start(bf16[8,32,512]{2,1,0:T(8,128)(2,1)S(1)} %slice.44), channel_id=1, source_target_pairs={{0,8},{8,16},{16,24},{24,0},{1,9},{9,17},{17,25},{25,1},{2,10},{10... | collective-permute-start | bytes 786440 | tf_op jit(solution)/shard_map/ppermute | solution.py:65
  118.5 7.9 %collective-permute-start.14 = (bf16[8,32,512]{2,1,0:T(8,128)(2,1)S(1)}, bf16[8,32,512]{2,1,0:T(8,128)(2,1)S(1)}, u32[]{:S(2)}, u32[]{:S(2)}) collective-permute-start(bf16[8,32,512]{2,1,0:T(8,128)(2,1)S(1)} %slice.45), channel_id=1, source_target_pairs={{0,24},{8,0},{16,8},{24,16},{1,25},{9,1},{17,9},{25,17},{2,26},{10... | collective-permute-start | bytes 786440 | tf_op jit(solution)/shard_map/ppermute | solution.py:65
  128.0 41.1 %collective-permute-start.15 = (bf16[64,32,512]{2,1,0:T(8,128)(2,1)}, bf16[64,32,512]{2,1,0:T(8,128)(2,1)}, u32[]{:S(2)}, u32[]{:S(2)}) collective-permute-start(bf16[64,32,512]{2,1,0:T(8,128)(2,1)} %bitcast.27.mine_ref), channel_id=1, source_target_pairs={{0,4},{4,0},{1,5},{5,1},{2,6},{6,2},{3,7},{7,3},{8,12},{12,8},{9,1... | collective-permute-start | bytes 6291464 | tf_op jit(solution)/shard_map/ppermute | solution.py:70
  140.8 1.5 copy-start.3
  169.1 7.3 %copy-start.4 = (bf16[2048,128]{1,0:T(8,128)(2,1)S(1)}, bf16[2048,128]{1,0:T(8,128)(2,1)}, u32[]{:S(2)}) copy-start(bf16[2048,128]{1,0:T(8,128)(2,1)} %get-tuple-element.39) | copy-start | bytes 1572868
  169.1 7.3 %copy-start.5 = (bf16[2048,128]{1,0:T(8,128)(2,1)S(1)}, bf16[2048,128]{1,0:T(8,128)(2,1)}, u32[]{:S(2)}) copy-start(bf16[2048,128]{1,0:T(8,128)(2,1)} %get-tuple-element.40) | copy-start | bytes 1572868
  288.1 10.9 %collective-permute-start.16 = (bf16[2048,1024]{1,0:T(8,128)(2,1)}, bf16[2048,1024]{1,0:T(8,128)(2,1)}, u32[]{:S(2)}, u32[]{:S(2)}) collective-permute-start(bf16[2048,1024]{1,0:T(8,128)(2,1)} %bitcast.31), channel_id=1, source_target_pairs={{0,4},{4,0},{1,5},{5,1},{2,6},{6,2},{3,7},{7,3},{8,12},{12,8},{9,1... | collective-permute-start | bytes 12582920 | tf_op jit(solution)/shard_map/ppermute | solution.py:70
  291.4 3.8 copy-start.9
  303.8 85.4 %copy-start.8 = (bf16[1,704,512]{2,1,0:T(8,128)(2,1)S(1)}, bf16[1,704,512]{2,1,0:T(8,128)(2,1)}, u32[]{:S(2)}) copy-start(bf16[1,704,512]{2,1,0:T(8,128)(2,1)} %param.27) | copy-start | bytes 2162692
  310.9 78.2 %copy-start.17 = (bf16[176,1792]{1,0:T(8,128)(2,1)}, bf16[176,1792]{1,0:T(8,128)(2,1)S(1)}, u32[]{:S(2)}) copy-start(bf16[176,1792]{1,0:T(8,128)(2,1)S(1)} %fusion.7) | copy-start | bytes 1892356
  310.9 37.3 %collective-permute-start.17 = (bf16[176,1792]{1,0:T(8,128)(2,1)S(1)}, bf16[176,1792]{1,0:T(8,128)(2,1)S(1)}, u32[]{:S(2)}, u32[]{:S(2)}) collective-permute-start(bf16[176,1792]{1,0:T(8,128)(2,1)S(1)} %fusion.7), channel_id=1, source_target_pairs={{0,1},{1,2},{2,3},{3,0},{4,5},{5,6},{6,7},{7,4},{8,9},{9,10},{10,1... | collective-permute-start | bytes 1892360 | tf_op jit(solution)/shard_map/ppermute | solution.py:393
  318.2 67.4 %collective-permute-start.18 = (bf16[176,1792]{1,0:T(8,128)(2,1)S(1)}, bf16[176,1792]{1,0:T(8,128)(2,1)S(1)}, u32[]{:S(2)}, u32[]{:S(2)}) collective-permute-start(bf16[176,1792]{1,0:T(8,128)(2,1)S(1)} %fusion.7), channel_id=1, source_target_pairs={{0,3},{1,0},{2,1},{3,2},{4,7},{5,4},{6,5},{7,6},{8,11},{9,8},{10,9... | collective-permute-start | bytes 1892360 | tf_op jit(solution)/shard_map/ppermute | solution.py:394
  348.2 37.4 %copy-start.10 = (bf16[176,1792]{1,0:T(8,128)(2,1)}, bf16[176,1792]{1,0:T(8,128)(2,1)S(1)}, u32[]{:S(2)}) copy-start(bf16[176,1792]{1,0:T(8,128)(2,1)S(1)} %collective-permute-done.17) | copy-start | bytes 1892356
  348.3 44.5 %collective-permute-start.19 = (bf16[88,1792]{1,0:T(8,128)(2,1)S(1)}, bf16[88,1792]{1,0:T(8,128)(2,1)S(1)}, u32[]{:S(2)}, u32[]{:S(2)}) collective-permute-start(bf16[88,1792]{1,0:T(8,128)(2,1)S(1)} %slice.46), channel_id=1, source_target_pairs={{0,1},{1,2},{2,3},{3,0},{4,5},{5,6},{6,7},{7,4},{8,9},{9,10},{10,1... | collective-permute-start | bytes 946184 | tf_op jit(solution)/shard_map/ppermute | solution.py:395
  385.6 0.8 copy-start.11
  386.5 17.0 %collective-permute-start.20 = (bf16[88,1792]{1,0:T(8,128)(2,1)S(1)}, bf16[88,1792]{1,0:T(8,128)(2,1)S(1)}, u32[]{:S(2)}, u32[]{:S(2)}) collective-permute-start(bf16[88,1792]{1,0:T(8,128)(2,1)S(1)} %slice.47), channel_id=1, source_target_pairs={{0,3},{1,0},{2,1},{3,2},{4,7},{5,4},{6,5},{7,6},{8,11},{9,8},{10,9... | collective-permute-start | bytes 946184 | tf_op jit(solution)/shard_map/ppermute | solution.py:396
  415.2 5.9 %collective-permute-start.21 = (bf16[2048,256]{1,0:T(8,128)(2,1)}, bf16[2048,256]{1,0:T(8,128)(2,1)}, u32[]{:S(2)}, u32[]{:S(2)}) collective-permute-start(bf16[2048,256]{1,0:T(8,128)(2,1)} %constant_dynamic-slice_fusion), channel_id=1, source_target_pairs={{0,4},{4,0},{1,5},{5,1},{2,6},{6,2},{3,7},{7,3},{8,12},{12,8},{9,1... | collective-permute-start | bytes 3145736 | tf_op jit(solution)/shard_map/ppermute | solution.py:70
  418.5 19.9 %copy-start.13 = (bf16[128,128]{1,0:T(8,128)(2,1)S(1)}, bf16[128,128]{1,0:T(8,128)(2,1)}, u32[]{:S(2)}) copy-start(bf16[128,128]{1,0:T(8,128)(2,1)} %get-tuple-element.19) | copy-start | bytes 98308
  418.6 20.0 %copy-start.12 = (bf16[128,512]{1,0:T(8,128)(2,1)S(1)}, bf16[128,512]{1,0:T(8,128)(2,1)}, u32[]{:S(2)}) copy-start(bf16[128,512]{1,0:T(8,128)(2,1)} %get-tuple-element.18) | copy-start | bytes 393220
  418.6 49.5 %copy-start.2 = (bf16[2048,128]{1,0:T(8,128)(2,1)S(1)}, bf16[2048,128]{1,0:T(8,128)(2,1)}, u32[]{:S(2)}) copy-start(bf16[2048,128]{1,0:T(8,128)(2,1)} %get-tuple-element.32) | copy-start | bytes 1572868
  423.7 44.4 %all-to-all-start.1 = ((bf16[128,16,256]{2,1,0:T(8,128)(2,1)}), bf16[128,16,256]{2,1,0:T(8,128)(2,1)S(1)}, u32[]{:S(2)}, u32[]{:S(2)}) async-start(bf16[128,16,256]{2,1,0:T(8,128)(2,1)} %bitcast.39), calls=%async_computation.1 | async-start | bytes 2097152 | tf_op jit(solution)/shard_map/all_to_all | solution.py:410
  438.5 30.9 %copy-start.14 = (bf16[128,512]{1,0:T(8,128)(2,1)S(1)}, bf16[128,512]{1,0:T(8,128)(2,1)}, u32[]{:S(2)}) copy-start(bf16[128,512]{1,0:T(8,128)(2,1)} %get-tuple-element.14) | copy-start | bytes 393220

commit v4 on v3

--- a/solution.py
+++ b/solution.py
@@ -16,10 +16,13 @@
 EXPERTS = 64
 CAP = 14
 TOK = 128
-PADDED = 16
+LAYER_ROWS = 16 * 4 * CAP
 
 DP = ("zl", "y", "x", "c")
 T = "t"
+LAYER = ("c", "y", "x")
+UP = [(j, (j + 1) % 4) for j in range(4)]
+DOWN = [(j, (j + 3) % 4) for j in range(4)]
 BF = jnp.bfloat16
 F32 = jnp.float32
 
@@ -44,12 +47,16 @@
 
 
 def expert_ranks(routes):
-    onehot = (routes[..., None] == jnp.arange(EXPERTS, dtype=jnp.int32)).astype(BF)
-    per_token = jnp.sum(onehot, axis=1)
+    experts = jnp.arange(EXPERTS, dtype=jnp.int32)[None, :, None]
+    named = [(routes[:, k : k + 1] == experts) for k in range(6)]
+    per_token = sum(n.astype(F32) for n in named).astype(BF)
     index = jnp.arange(TOK, dtype=jnp.int32)
-    earlier = (index[None, :] < index[:, None]).astype(BF)
-    before = jnp.dot(earlier, per_token, preferred_element_type=F32)
-    return jnp.sum(onehot.astype(F32) * before[:, None, :], axis=2).astype(jnp.int32)
+    earlier = (index[:, None] < index[None, :]).astype(BF)
+    before = lax.dot_general(
+        per_token, earlier, (((2,), (0,)), ((), ())), preferred_element_type=F32
+    )
+    ranks = [jnp.sum(jnp.where(n, before, 0.0), axis=1) for n in named]
+    return jnp.stack(ranks, axis=1).astype(jnp.int32)
 
 
 def shifted(block, axis):
@@ -60,9 +67,8 @@
 
 def ring(block, axis):
     half = block.shape[0] // 2
-    up, down = [(j, (j + 1) % 4) for j in range(4)], [(j, (j + 3) % 4) for j in range(4)]
-    below, above = lax.ppermute(block, axis, up), lax.ppermute(block, axis, down)
-    far = [lax.ppermute(below[:half], axis, up), lax.ppermute(above[half:], axis, down)]
+    below, above = lax.ppermute(block, axis, UP), lax.ppermute(block, axis, DOWN)
+    far = [lax.ppermute(below[:half], axis, UP), lax.ppermute(above[half:], axis, DOWN)]
     return [block, below, jnp.concatenate(far), above]
 
 
@@ -103,8 +109,8 @@
     )(hidden_in, query, latent, expand, output)
 
 
-def pick_rows(place, everything):
-    def kernel(place_ref, in_ref, out_ref, wide, rows):
+def pick_rows(place, everything, routes, gates):
+    def kernel(place_ref, in_ref, routes_ref, gates_ref, out_ref, wide, rows):
         t = place_ref[4]
         wide[...] = in_ref[...].astype(F32)
         for s in range(4):
@@ -120,17 +126,23 @@
             rows[36 + s : 37 + s, :] = e
             rows[40 + s * 4 : 44 + s * 4, :] = wide[24:28, lanes]
             rows[56 + s * 4 : 60 + s * 4, :] = wide[28:32, lanes]
+        rows[72:88, :] = jnp.zeros((16, 512), F32)
+        rows[72:78, 0:128] = routes_ref[...].astype(F32)
+        rows[80:86, 0:128] = gates_ref[...].astype(F32)
         out_ref[...] = rows[...].astype(BF)
+
+    def small(rows):
+        return pl.BlockSpec((rows, 128), lambda i: (0, 0))
 
     return pl.pallas_call(
         kernel,
         grid=(1,),
-        out_shape=jax.ShapeDtypeStruct((72, 512), BF),
-        in_specs=[SMEM, pl.BlockSpec((32, 2048), lambda i: (4, 0))],
-        out_specs=pl.BlockSpec((72, 512), lambda i: (0, 0)),
-        scratch_shapes=[pltpu.VMEM((32, 2048), F32), pltpu.VMEM((72, 512), F32)],
+        out_shape=jax.ShapeDtypeStruct((88, 512), BF),
+        in_specs=[SMEM, pl.BlockSpec((32, 2048), lambda i: (4, 0)), small(6), small(6)],
+        out_specs=pl.BlockSpec((88, 512), lambda i: (0, 0)),
+        scratch_shapes=[pltpu.VMEM((32, 2048), F32), pltpu.VMEM((88, 512), F32)],
         name="pick_rows",
-    )(place, everything)
+    )(place, everything, routes.T, gates.T)
 
 
 def in_order(place_ref, visit):
@@ -302,16 +314,17 @@
 
     packed = pack_rows(hidden_in, query_train, latent_train, expand_train, output_train)
     everything = lax.all_gather(packed, T, axis=1, tiled=True)
-    rows = pick_rows(place, everything)
+    rows = pick_rows(place, everything, routes, gate_weights)
     gathered = jnp.stack(shifted(rows, "zl"))
-    gathered = jnp.stack(shifted(gathered, "y")).reshape(16, 72, 512)
+    column_routes = gathered[:, 72:78, 0:128].astype(jnp.int32)
+    column_gates = gathered[:, 80:86, 0:128].astype(F32)
+    gathered = jnp.stack(shifted(gathered[:, :72], "y")).reshape(16, 72, 512)
     first_set = gathered[:, :40]
-    second_set = gathered[:, 40:]
     first_mine = jnp.stack(ring(first_set, "x")).reshape(64, 40, 512)
     first_theirs = other_core(first_mine)
-    second_gated, _ = lax.optimization_barrier((second_set, first_mine))
-    second_mine = jnp.stack(ring(second_gated, "x")).reshape(64, 32, 512)
-    second_theirs = other_core(second_mine)
+    second_set, _ = lax.optimization_barrier((gathered[:, 40:], first_mine))
+    second_below = lax.ppermute(second_set, "x", UP)
+    second_above = lax.ppermute(second_set, "x", DOWN)
 
     segment, position = positions_of(lengths, TOK)
     segment = segment[0]
@@ -333,36 +346,34 @@
     )
     cache_full = jnp.concatenate([latent_normed, key_rope[:, 0:32], key_rope[:, 64:96]], axis=1)
     cache_cols = lax.dynamic_slice_in_dim(cache_full, rank * 144, 144, 1)
+    below_part, above_part, attended = lax.optimization_barrier(
+        (second_below[:8], second_above[8:], attended)
+    )
+    second_far = jnp.concatenate(
+        [lax.ppermute(below_part, "x", UP), lax.ppermute(above_part, "x", DOWN)]
+    )
     attended_full = lax.all_gather(attended, T, axis=1, tiled=True)
+    second_mine = jnp.stack([second_set, second_below, second_far, second_above]).reshape(64, 32, 512)
+    second_theirs = other_core(second_mine)
     moe_halves, mixed_cols, output_block = mix(
         place, everything, attended_full, second_mine, second_theirs, moe_gain
     )
 
-    slot_rank = expert_ranks(routes)
-    gates = gate_weights.astype(F32)
-    pad_ids = jnp.arange(EXPERTS * 2 * PADDED, dtype=jnp.int32)
-    pad_core = (pad_ids // PADDED) % 2
-    slot_at = routes * (2 * PADDED) + slot_rank
-    matches = (pad_ids - pad_core * PADDED)[:, None, None] == slot_at[None, :, :]
-
-    def placed_by(values):
-        return jnp.sum(jnp.where(matches, values, 0.0), axis=2)
-
-    placed = placed_by(1.0)
-    dispatch = jnp.concatenate(
-        [
-            jnp.where(pad_core[:, None] == 0, placed, 0.0),
-            jnp.where(pad_core[:, None] == 1, placed, 0.0),
-        ],
-        axis=1,
-    ).astype(BF)
-
-    weighted = placed_by(gates[None])
-    combine = [jnp.where(pad_core[:, None] == h, weighted, 0.0).astype(BF) for h in range(2)]
-
-    compact = jnp.arange(TOK * CAP, dtype=jnp.int32)
-    taken = (compact // CAP) * PADDED + compact % CAP
-    squeeze = (jnp.arange(TOK * PADDED, dtype=jnp.int32)[:, None] == taken[None, :]).astype(BF)
+    slot_rank = expert_ranks(column_routes)
+    local = column_routes - lax.axis_index("zl") * 16
+    group = jnp.arange(4, dtype=jnp.int32)[:, None, None]
+    target = jnp.where(
+        (local >= 0) & (local < 16), local * (4 * CAP) + group * CAP + slot_rank, -1
+    )
+    row_ids = jnp.arange(LAYER_ROWS, dtype=jnp.int32)[:, None]
+    dispatch = jnp.zeros((LAYER_ROWS, 4 * TOK), F32)
+    combine = jnp.zeros((LAYER_ROWS, 4 * TOK), F32)
+    for k in range(6):
+        hit = row_ids == target[:, k].reshape(1, 4 * TOK)
+        dispatch = dispatch + hit.astype(F32)
+        combine = combine + jnp.where(hit, column_gates[:, k].reshape(1, 4 * TOK), 0.0)
+    dispatch = jnp.broadcast_to(dispatch.astype(BF)[None], (2, LAYER_ROWS, 4 * TOK))
+    combine = jnp.broadcast_to(combine.astype(BF)[None], (2, LAYER_ROWS, 4 * TOK))
 
     def halves(matrix):
         return (
@@ -380,20 +391,34 @@
     def rows_by(weight, rows):
         return lax.dot_general(weight, rows, (((0,), (1,)), ((), ())), preferred_element_type=F32)
 
-    outgoing = jnp.dot(dispatch, moe_halves, preferred_element_type=F32).astype(BF)
-    mine = lax.all_to_all(outgoing, DP, split_axis=0, concat_axis=0, tiled=True)
+    at_z = [(z % 4) * 4 + z // 4 for z in range(16)]
+    z_up = [(at_z[z], at_z[(z + 1) % 16]) for z in range(16)]
+    z_down = [(at_z[z], at_z[(z + 15) % 16]) for z in range(16)]
+    back_one = lax.ppermute(moe_halves, ("zl", T), z_up)
+    on_one = lax.ppermute(moe_halves, ("zl", T), z_down)
+    far_left = lax.ppermute(back_one[:TOK], ("zl", T), z_up)
+    far_right = lax.ppermute(on_one[TOK:], ("zl", T), z_down)
+    tokens = jnp.stack(
+        [
+            jnp.concatenate([moe_halves[:TOK], back_one[:TOK], far_left, on_one[:TOK]]),
+            jnp.concatenate([moe_halves[TOK:], back_one[TOK:], far_right, on_one[TOK:]]),
+        ]
+    )
+    outgoing = lax.dot_general(
+        dispatch, tokens, (((2,), (1,)), ((0,), (0,))), preferred_element_type=F32
+    ).astype(BF)
+    mine = lax.all_to_all(
+        outgoing.reshape(2 * LAYER_ROWS, D // 2), LAYER, split_axis=0, concat_axis=0, tiled=True
+    )
     theirs = other_core(mine)
     gate_part = rows_by(gate_mine, mine) + rows_by(gate_other, theirs)
     up_part = rows_by(up_mine, mine) + rows_by(up_other, theirs)
-    hidden = (jax.nn.silu(gate_part) * up_part).astype(BF)
-
-    up_ring = [(j, (j + 1) % 4) for j in range(4)]
-    down_ring = [(j, (j + 3) % 4) for j in range(4)]
-    own = jnp.dot(hidden, squeeze, preferred_element_type=F32).astype(BF)
-    below = lax.ppermute(own, T, up_ring)
-    above = lax.ppermute(own, T, down_ring)
-    far_first = lax.ppermute(below[:88], T, up_ring)
-    far_second = lax.ppermute(above[88:], T, down_ring)
+    own = (jax.nn.silu(gate_part) * up_part).astype(BF)
+
+    below = lax.ppermute(own, T, UP)
+    above = lax.ppermute(own, T, DOWN)
+    far_first = lax.ppermute(below[:88], T, UP)
+    far_second = lax.ppermute(above[88:], T, DOWN)
 
     def out_of(pieces, at):
         rows = jnp.concatenate(pieces, axis=0)
@@ -403,17 +428,22 @@
         )
 
     half_out = (out_of([own, below, above], 0) + out_of([far_first, far_second], 528)).astype(BF)
-    half_out = jnp.dot(squeeze, half_out, preferred_element_type=F32).astype(BF)
     keep = lax.dynamic_slice_in_dim(half_out, core * 256, 256, 1)
     give = lax.dynamic_slice_in_dim(half_out, (1 - core) * 256, 256, 1)
     both = (keep.astype(F32) + other_core(give).astype(F32)).astype(BF)
-    returned = lax.all_to_all(both, DP, split_axis=0, concat_axis=0, tiled=True)
-    sums = [
-        lax.dot_general(part, returned, (((0,), (0,)), ((), ())), preferred_element_type=F32)
-        for part in combine
-    ]
+    returned = lax.all_to_all(both, LAYER, split_axis=0, concat_axis=0, tiled=True)
+    partial = lax.dot_general(
+        combine,
+        returned.reshape(2, LAYER_ROWS, 256),
+        (((1,), (1,)), ((0,), (0,))),
+        preferred_element_type=F32,
+    ).reshape(2, 4, TOK, 256)
+    sums = partial[:, 0]
+    for s in range(1, 4):
+        sent = partial[:, s].astype(BF)
+        sums = sums + lax.ppermute(sent, "zl", [(j, (j - s) % 4) for j in range(4)]).astype(F32)
     result = mixed_cols.astype(F32)
-    hidden_out = (result + jnp.concatenate(sums, axis=1)).astype(BF)
+    hidden_out = (result + jnp.concatenate([sums[0], sums[1]], axis=1)).astype(BF)
     return (hidden_out, expand_block, output_block, cache_cols)
 
 

time: 471 us -> 435 us (0.924)
  blocking collectives: 165 us -> 106 us
  waiting for transfers between devices: 128 us -> 151 us
  matrix products: 34 us -> 20.1 us
  starting transfers between devices: 102 us -> 113 us
    all_to_all x1, blocking collectives: 109 us -> 51.2 us  [body(): lax.all_to_all(outgoing.reshape(2 * LAYER_ROWS, D // 2), LAYER, split_axi...]
    ppermute x12 -> x19, waiting for transfers between devices: 86.9 us -> 120 us  [the longest x1 51.1 us: body(): above = lax.ppermute(own, T, DOWN)]
    ppermute x12 -> x19, starting transfers between devices: 45.5 us -> 70.8 us  [the longest x3 9.54 us: body(): lax.ppermute(sent, 'zl', [(j, (j - s) % 4) for j in range(4)]).astype(F32)]
    dot_general x6 -> x3, matrix products: 19.1 us -> 3.08 us  [the longest x1 2.08 us: body(): lax.dot_general(dispatch, tokens, (((2,), (1,)), ((0,), (0,))), preferred...]
    all_to_all x1, waiting for transfers between devices: 28.6 us -> 15.2 us  [body(): lax.all_to_all(both, LAYER, split_axis=0, concat_axis=0, tiled=True)]
    all_to_all x1, starting transfers between devices: 14.8 us -> 4.01 us  [body(): lax.all_to_all(both, LAYER, split_axis=0, concat_axis=0, tiled=True)]
    slice x3 -> x10, local copies, waits for them, and re-layouts: 0.09 us -> 4.87 us  [the longest x1 1.08 us: body(): second_set, _ = lax.optimization_barrier((gathered[:, 40:], first_mine))]
    dot_general x3 -> x4, matrix products: 12.4 us -> 13.8 us  [rows_by(): lax.dot_general(weight, rows, (((0,), (1,)), ((), ())), preferred_element...]
  transfers between devices with their start and end apart: 23 -> 30, of which waited for: 14 -> 21; matrix products, arithmetic and copies ran while one was open for 4% -> 4% of each run, Pallas kernels for 2% -> 0%
where the time goes in v4:
time: 435 us; the launch traced here: 432 us
  waiting for transfers between devices  151 us (35%)
  starting transfers between devices  113 us (26%)
  blocking collectives  106 us (24%)
  matrix products  20.1 us (5%)
  Pallas kernels  17.8 us (4%)
  other arithmetic  12.3 us (3%)
  local copies, waits for them, and re-layouts  10.9 us (3%)
    all_to_all x1, blocking collectives, body(): lax.all_to_all(outgoing.reshape(2 * LAYER_ROWS, D // 2), LAYER, split_axi...  51.2 us
    ppermute x1, waiting for transfers between devices, body(): above = lax.ppermute(own, T, DOWN)  51.1 us
    all_gather x1, blocking collectives, body(): everything = lax.all_gather(packed, T, axis=1, tiled=True)  35.8 us
    ppermute x4, starting transfers between devices, other_core(): return lax.ppermute(block, 'c', [(0, 1), (1, 0)])  21 us
    all_gather x1, blocking collectives, body(): attended_full = lax.all_gather(attended, T, axis=1, tiled=True)  18.6 us
    ppermute x6, starting transfers between devices, shifted(): lax.ppermute(block, axis, [(j, (j + s) % 4) for j in range(4)])  17.4 us
    all_to_all x1, waiting for transfers between devices, body(): lax.all_to_all(both, LAYER, split_axis=0, concat_axis=0, tiled=True)  15.2 us
    dot_general x4, matrix products, rows_by(): lax.dot_general(weight, rows, (((0,), (1,)), ((), ())), preferred_element...  13.8 us
  transfers between devices with their start and end apart: 30, of which 21 were waited for; matrix products, arithmetic and copies ran while one was open for 4% of the time, Pallas kernels for 0%

profile of v4, /device:TPU:1, one launch (start us, length us, event | category | flops | bytes accessed | tf_op | source)
XLA Modules:
  0.0 432.4 jit_solution(17337718340879124931)
XLA Ops:
  2.4 35.8 %all_gather.6.in_ref = bf16[160,2048]{1,0:T(8,128)(2,1)} all-gather(bf16[160,512]{1,0:T(8,128)(2,1)} %pack_rows.1), channel_id=1, replica_groups=mesh['zl'=4,'y'=4,'x'=4,'c'=2,'t'=4] {'t'}, dimensions={1}, use_global_device_ids=true | all-gather | bytes 819200 | tf_op jit(solution)/shard_map/all_gather | solution.py:316
  40.4 3.8 collective-permute-start.2
  48.4 3.3 collective-permute-done.1
  54.9 4.6 %collective-permute-start.5 = (bf16[4,72,512]{2,1,0:T(8,128)(2,1)S(1)}, bf16[4,72,512]{2,1,0:T(8,128)(2,1)S(1)}, u32[]{:S(2)}, u32[]{:S(2)}) collective-permute-start(bf16[4,72,512]{2,1,0:T(8,128)(2,1)S(1)} %get-tuple-element.69), channel_id=1, source_target_pairs={{0,96},{32,0},{64,32},{96,64},{1,97},{33,1},{65,33},{97,65},{2,98}... | collective-permute-start | bytes 884744 | tf_op jit(solution)/shard_map/ppermute | solution.py:64
  59.5 2.3 collective-permute-start.4
  61.8 2.6 collective-permute-start.3
  65.2 3.4 collective-permute-done.4
  68.6 3.4 collective-permute-done.3
  72.3 4.4 %collective-permute-start.8 = (bf16[16,40,512]{2,1,0:T(8,128)(2,1)S(1)}, bf16[16,40,512]{2,1,0:T(8,128)(2,1)S(1)}, u32[]{:S(2)}, u32[]{:S(2)}) collective-permute-start(bf16[16,40,512]{2,1,0:T(8,128)(2,1)S(1)} %get-tuple-element.49), channel_id=1, source_target_pairs={{0,24},{8,0},{16,8},{24,16},{1,25},{9,1},{17,9},{25,17},{2,26},{10... | collective-permute-start | bytes 1966088 | tf_op jit(solution)/shard_map/ppermute | solution.py:70
  78.6 5.6 %collective-permute-done.8 = bf16[16,40,512]{2,1,0:T(8,128)(2,1)S(1)} collective-permute-done((bf16[16,40,512]{2,1,0:T(8,128)(2,1)S(1)}, bf16[16,40,512]{2,1,0:T(8,128)(2,1)S(1)}, u32[]{:S(2)}, u32[]{:S(2)}) %collective-permute-start.8) | collective-permute-done | bytes 655392 | tf_op jit(solution)/shard_map/ppermute | solution.py:70
  84.2 5.0 %collective-permute-start.9 = (bf16[8,40,512]{2,1,0:T(8,128)(2,1)S(1)}, bf16[8,40,512]{2,1,0:T(8,128)(2,1)S(1)}, u32[]{:S(2)}, u32[]{:S(2)}) collective-permute-start(bf16[8,40,512]{2,1,0:T(8,128)(2,1)S(1)} %slice.181), channel_id=1, source_target_pairs={{0,24},{8,0},{16,8},{24,16},{1,25},{9,1},{17,9},{25,17},{2,26},{10... | collective-permute-start | bytes 983048 | tf_op jit(solution)/shard_map/ppermute | solution.py:71
  91.2 3.6 collective-permute-done.9
  94.8 5.3 %collective-permute-done.7 = bf16[8,40,512]{2,1,0:T(8,128)(2,1)S(1)} collective-permute-done((bf16[8,40,512]{2,1,0:T(8,128)(2,1)S(1)}, bf16[8,40,512]{2,1,0:T(8,128)(2,1)S(1)}, u32[]{:S(2)}, u32[]{:S(2)}) %collective-permute-start.7) | collective-permute-done | bytes 327712 | tf_op jit(solution)/shard_map/ppermute | solution.py:71
  100.6 11.0 %collective-permute-start.12 = (bf16[64,40,512]{2,1,0:T(8,128)(2,1)S(1)}, bf16[64,40,512]{2,1,0:T(8,128)(2,1)}, u32[]{:S(2)}, u32[]{:S(2)}) collective-permute-start(bf16[64,40,512]{2,1,0:T(8,128)(2,1)S(1)} %bitcast.118), channel_id=1, source_target_pairs={{0,4},{4,0},{1,5},{5,1},{2,6},{6,2},{3,7},{7,3},{8,12},{12,8},{9,1... | collective-permute-start | bytes 7864328 | tf_op jit(solution)/shard_map/ppermute | solution.py:76
  115.0 4.6 %collective-permute-start.11 = (bf16[16,32,512]{2,1,0:T(8,128)(2,1)S(1)}, bf16[16,32,512]{2,1,0:T(8,128)(2,1)S(1)}, u32[]{:S(2)}, u32[]{:S(2)}) collective-permute-start(bf16[16,32,512]{2,1,0:T(8,128)(2,1)S(1)} %slice.178), channel_id=1, source_target_pairs={{0,24},{8,0},{16,8},{24,16},{1,25},{9,1},{17,9},{25,17},{2,26},{10... | collective-permute-start | bytes 1572872 | tf_op jit(solution)/shard_map/ppermute | solution.py:327
  121.4 8.3 %collective-permute-done.10 = bf16[16,32,512]{2,1,0:T(8,128)(2,1)S(1)} collective-permute-done((bf16[16,32,512]{2,1,0:T(8,128)(2,1)S(1)}, bf16[16,32,512]{2,1,0:T(8,128)(2,1)S(1)}, u32[]{:S(2)}, u32[]{:S(2)}) %collective-permute-start.10) | collective-permute-done | bytes 524320 | tf_op jit(solution)/shard_map/ppermute | solution.py:326
  131.5 7.2 %attention.1 = (bf16[128,256]{1,0:T(8,128)(2,1)}, bf16[128,512]{1,0:T(8,128)(2,1)}, bf16[128,128]{1,0:T(8,128)(2,1)}, bf16[512,512]{1,0:T(8,128)(2,1)}) custom-call(s32[5]{0:T(128)} %stack.113.place_ref, bf16[160,2048]{1,0:T(8,128)(2,1)} %all_gather.6.in_ref, bf16[64,40,512]{2,1,0:T(8,128)(2,1)} %bitcast.119, ...), custom_call_target="tpu_custom_call" | custom-call | tf_op jit(solution)/shard_map/attention/pallas_call | solution.py:222
  138.7 5.3 %collective-permute-start.14 = (bf16[8,32,512]{2,1,0:T(8,128)(2,1)}, bf16[8,32,512]{2,1,0:T(8,128)(2,1)S(1)}, u32[]{:S(2)}, u32[]{:S(2)}) collective-permute-start(bf16[8,32,512]{2,1,0:T(8,128)(2,1)} %slice.183), channel_id=1, source_target_pairs={{0,24},{8,0},{16,8},{24,16},{1,25},{9,1},{17,9},{25,17},{2,26},{10... | collective-permute-start | bytes 786440 | tf_op jit(solution)/shard_map/ppermute | solution.py:353
  145.9 2.8 collective-permute-done.14
  148.7 4.9 %collective-permute-done.13 = bf16[8,32,512]{2,1,0:T(8,128)(2,1)S(1)} collective-permute-done((bf16[8,32,512]{2,1,0:T(8,128)(2,1)}, bf16[8,32,512]{2,1,0:T(8,128)(2,1)S(1)}, u32[]{:S(2)}, u32[]{:S(2)}) %collective-permute-start.13) | collective-permute-done | bytes 262176 | tf_op jit(solution)/shard_map/ppermute | solution.py:353
  155.4 4.4 %collective-permute-start.15 = (bf16[64,32,512]{2,1,0:T(8,128)(2,1)S(1)}, bf16[64,32,512]{2,1,0:T(8,128)(2,1)}, u32[]{:S(2)}, u32[]{:S(2)}) collective-permute-start(bf16[64,32,512]{2,1,0:T(8,128)(2,1)S(1)} %bitcast.120), channel_id=1, source_target_pairs={{0,4},{4,0},{1,5},{5,1},{2,6},{6,2},{3,7},{7,3},{8,12},{12,8},{9,1... | collective-permute-start | bytes 6291464 | tf_op jit(solution)/shard_map/ppermute | solution.py:76
  160.3 18.6 %all_gather.7.attended_ref = bf16[128,1024]{1,0:T(8,128)(2,1)} all-gather(bf16[128,256]{1,0:T(8,128)(2,1)S(1)} %copy-done.21), channel_id=1, replica_groups=mesh['zl'=4,'y'=4,'x'=4,'c'=2,'t'=4] {'t'}, dimensions={1}, use_global_device_ids=true | all-gather | bytes 327680 | tf_op jit(solution)/shard_map/all_gather | solution.py:355
  178.9 7.2 %mix.1 = (bf16[256,1024]{1,0:T(8,128)(2,1)}, bf16[128,512]{1,0:T(8,128)(2,1)}, bf16[2048,256]{1,0:T(8,128)(2,1)}) custom-call(s32[5]{0:T(128)} %stack.113.place_ref, bf16[160,2048]{1,0:T(8,128)(2,1)} %all_gather.6.in_ref, bf16[128,1024]{1,0:T(8,128)(2,1)} %all_gather.7.attended_ref, bf16[64,32,512]{2,1,0:T(8,128)(2,1)} %bitcast.121, ...), custom_call_target="tpu_custom_call" | custom-call | tf_op jit(solution)/shard_map/mix/pallas_call | solution.py:280
  186.2 6.7 %collective-permute-start.18 = (bf16[256,1024]{1,0:T(8,128)(2,1)}, bf16[256,1024]{1,0:T(8,128)(2,1)}, u32[]{:S(2)}, u32[]{:S(2)}) collective-permute-start(bf16[256,1024]{1,0:T(8,128)(2,1)} %get-tuple-element.21), channel_id=1, source_target_pairs={{0,387},{128,0},{256,128},{384,256},{1,384},{129,1},{257,129},{385... | collective-permute-start | bytes 1572872 | tf_op jit(solution)/shard_map/ppermute | solution.py:398
  194.8 2.4 add_convert_fusion.3
  197.8 6.0 %collective-permute-done.18 = bf16[256,1024]{1,0:T(8,128)(2,1)} collective-permute-done((bf16[256,1024]{1,0:T(8,128)(2,1)}, bf16[256,1024]{1,0:T(8,128)(2,1)}, u32[]{:S(2)}, u32[]{:S(2)}) %collective-permute-start.18) | collective-permute-done | bytes 524320 | tf_op jit(solution)/shard_map/ppermute | solution.py:398
  204.8 5.3 %collective-permute-start.19 = (bf16[128,1024]{1,0:T(8,128)(2,1)S(1)}, bf16[128,1024]{1,0:T(8,128)(2,1)S(1)}, u32[]{:S(2)}, u32[]{:S(2)}) collective-permute-start(bf16[128,1024]{1,0:T(8,128)(2,1)S(1)} %get-tuple-element.61), channel_id=1, source_target_pairs={{0,387},{128,0},{256,128},{384,256},{1,384},{129,1},{257,129},{385... | collective-permute-start | bytes 786440 | tf_op jit(solution)/shard_map/ppermute | solution.py:400
  214.3 6.1 %collective-permute-done.17 = bf16[128,1024]{1,0:T(8,128)(2,1)S(1)} collective-permute-done((bf16[128,1024]{1,0:T(8,128)(2,1)S(1)}, bf16[128,1024]{1,0:T(8,128)(2,1)S(1)}, u32[]{:S(2)}, u32[]{:S(2)}) %collective-permute-start.17) | collective-permute-done | bytes 262176 | tf_op jit(solution)/shard_map/ppermute | solution.py:399
  222.5 51.2 %all_to_all.21 = bf16[32,56,1024]{2,1,0:T(8,128)(2,1)} all-to-all(bf16[32,56,1024]{2,1,0:T(8,128)(2,1)S(1)} %bitcast.124), channel_id=1, replica_groups=mesh['zl'=4,'y'=4,'x'=4,'c'=2,'t'=4] {'c','y','x'}, dimensions={0} | all-to-all | bytes 7340032 | tf_op jit(solution)/shard_map/all_to_all | solution.py:410
  273.7 3.2 collective-permute-start.20
  276.9 3.4 fusion.23
  280.3 3.4 fusion.26
  283.7 3.4 convolution_add_fusion.1
  287.2 3.6 fusion.1
  292.7 7.3 %collective-permute-start.21 = (bf16[176,1792]{1,0:T(8,128)(2,1)S(1)}, bf16[176,1792]{1,0:T(8,128)(2,1)S(1)}, u32[]{:S(2)}, u32[]{:S(2)}) collective-permute-start(bf16[176,1792]{1,0:T(8,128)(2,1)S(1)} %fusion.1), channel_id=1, source_target_pairs={{0,1},{1,2},{2,3},{3,0},{4,5},{5,6},{6,7},{7,4},{8,9},{9,10},{10,1... | collective-permute-start | bytes 1892360 | tf_op jit(solution)/shard_map/ppermute | solution.py:418
  300.0 51.1 %collective-permute-done.22 = bf16[176,1792]{1,0:T(8,128)(2,1)S(1)} collective-permute-done((bf16[176,1792]{1,0:T(8,128)(2,1)S(1)}, bf16[176,1792]{1,0:T(8,128)(2,1)S(1)}, u32[]{:S(2)}, u32[]{:S(2)}) %collective-permute-start.22) | collective-permute-done | bytes 630816 | tf_op jit(solution)/shard_map/ppermute | solution.py:419
  351.9 3.8 collective-permute-start.24
  356.6 5.4 %collective-permute-start.23 = (bf16[88,1792]{1,0:T(8,128)(2,1)S(1)}, bf16[88,1792]{1,0:T(8,128)(2,1)}, u32[]{:S(2)}, u32[]{:S(2)}) collective-permute-start(bf16[88,1792]{1,0:T(8,128)(2,1)S(1)} %slice.200), channel_id=1, source_target_pairs={{0,1},{1,2},{2,3},{3,0},{4,5},{5,6},{6,7},{7,4},{8,9},{9,10},{10,1... | collective-permute-start | bytes 946184 | tf_op jit(solution)/shard_map/ppermute | solution.py:420
  362.2 12.5 %collective-permute-done.24 = bf16[88,1792]{1,0:T(8,128)(2,1)S(1)} collective-permute-done((bf16[88,1792]{1,0:T(8,128)(2,1)S(1)}, bf16[88,1792]{1,0:T(8,128)(2,1)S(1)}, u32[]{:S(2)}, u32[]{:S(2)}) %collective-permute-start.24) | collective-permute-done | bytes 315424 | tf_op jit(solution)/shard_map/ppermute | solution.py:421
  374.7 8.2 %collective-permute-done.23 = bf16[88,1792]{1,0:T(8,128)(2,1)} collective-permute-done((bf16[88,1792]{1,0:T(8,128)(2,1)S(1)}, bf16[88,1792]{1,0:T(8,128)(2,1)}, u32[]{:S(2)}, u32[]{:S(2)}) %collective-permute-start.23) | collective-permute-done | bytes 315424 | tf_op jit(solution)/shard_map/ppermute | solution.py:420
  387.2 2.4 collective-permute-start.25
  389.6 2.4 collective-permute-done.25
  392.0 2.4 add_convert_fusion.1
  394.4 4.0 all-to-all-start.1
  398.4 15.2 %all-to-all-done.1 = bf16[32,56,256]{2,1,0:T(8,128)(2,1)S(1)} async-done(((bf16[32,56,256]{2,1,0:T(8,128)(2,1)}), bf16[32,56,256]{2,1,0:T(8,128)(2,1)S(1)}, u32[]{:S(2)}, u32[]{:S(2)}) %all-to-all-start.1) | async-done | bytes 917536 | tf_op jit(solution)/shard_map/all_to_all | solution.py:434
  415.4 3.6 collective-permute-start.28
  421.0 4.0 collective-permute-start.26
  426.0 4.7 %collective-permute-done.27 = bf16[2,128,256]{2,1,0:T(8,128)(2,1)S(1)} collective-permute-done((bf16[2,128,256]{2,1,0:T(8,128)(2,1)S(1)}, bf16[2,128,256]{2,1,0:T(8,128)(2,1)S(1)}, u32[]{:S(2)}, u32[]{:S(2)}) %collective-permute-start.27) | collective-permute-done | bytes 131104 | tf_op jit(solution)/shard_map/ppermute | solution.py:444
  (128 shorter events, 51.7 us)
Async XLA Ops:
  0.6 279.7 %copy-start = (bf16[1,2048,176]{1,2,0:T(8,128)(2,1)S(1)}, bf16[1,2048,176]{1,2,0:T(8,128)(2,1)}, u32[]{:S(2)}) copy-start(bf16[1,2048,176]{1,2,0:T(8,128)(2,1)} %param.25) | copy-start | bytes 2162692
  40.4 8.0 %collective-permute-start.2 = (bf16[88,512]{1,0:T(8,128)(2,1)}, bf16[88,512]{1,0:T(8,128)(2,1)S(1)}, u32[]{:S(2)}, u32[]{:S(2)}) collective-permute-start(bf16[88,512]{1,0:T(8,128)(2,1)} %pick_rows.1), channel_id=1, source_target_pairs={{0,384},{128,0},{256,128},{384,256},{1,385},{129,1},{257,129},{385... | collective-permute-start | bytes 270344 | tf_op jit(solution)/shard_map/ppermute | solution.py:64
  44.3 7.5 %collective-permute-start.1 = (bf16[88,512]{1,0:T(8,128)(2,1)}, bf16[88,512]{1,0:T(8,128)(2,1)S(1)}, u32[]{:S(2)}, u32[]{:S(2)}) collective-permute-start(bf16[88,512]{1,0:T(8,128)(2,1)} %pick_rows.1), channel_id=1, source_target_pairs={{0,256},{128,384},{256,0},{384,128},{1,257},{129,385},{257,1},{385... | collective-permute-start | bytes 270344 | tf_op jit(solution)/shard_map/ppermute | solution.py:64
  46.2 7.7 %collective-permute-start = (bf16[88,512]{1,0:T(8,128)(2,1)}, bf16[88,512]{1,0:T(8,128)(2,1)S(1)}, u32[]{:S(2)}, u32[]{:S(2)}) collective-permute-start(bf16[88,512]{1,0:T(8,128)(2,1)} %pick_rows.1), channel_id=1, source_target_pairs={{0,128},{128,256},{256,384},{384,0},{1,129},{129,257},{257,385},{3... | collective-permute-start | bytes 270344 | tf_op jit(solution)/shard_map/ppermute | solution.py:64
  53.9 18.2 %copy-start.5 = (bf16[88,512]{1,0:T(8,128)(2,1)}, bf16[88,512]{1,0:T(8,128)(2,1)S(1)}, u32[]{:S(2)}) copy-start(bf16[88,512]{1,0:T(8,128)(2,1)S(1)} %collective-permute-done) | copy-start | bytes 270340
  54.9 10.3 %collective-permute-start.5 = (bf16[4,72,512]{2,1,0:T(8,128)(2,1)S(1)}, bf16[4,72,512]{2,1,0:T(8,128)(2,1)S(1)}, u32[]{:S(2)}, u32[]{:S(2)}) collective-permute-start(bf16[4,72,512]{2,1,0:T(8,128)(2,1)S(1)} %get-tuple-element.69), channel_id=1, source_target_pairs={{0,96},{32,0},{64,32},{96,64},{1,97},{33,1},{65,33},{97,65},{2,98}... | collective-permute-start | bytes 884744 | tf_op jit(solution)/shard_map/ppermute | solution.py:64
  59.5 9.1 %collective-permute-start.4 = (bf16[4,72,512]{2,1,0:T(8,128)(2,1)S(1)}, bf16[4,72,512]{2,1,0:T(8,128)(2,1)S(1)}, u32[]{:S(2)}, u32[]{:S(2)}) collective-permute-start(bf16[4,72,512]{2,1,0:T(8,128)(2,1)S(1)} %get-tuple-element.69), channel_id=1, source_target_pairs={{0,64},{32,96},{64,0},{96,32},{1,65},{33,97},{65,1},{97,33},{2,66}... | collective-permute-start | bytes 884744 | tf_op jit(solution)/shard_map/ppermute | solution.py:64
  61.8 10.2 %collective-permute-start.3 = (bf16[4,72,512]{2,1,0:T(8,128)(2,1)S(1)}, bf16[4,72,512]{2,1,0:T(8,128)(2,1)S(1)}, u32[]{:S(2)}, u32[]{:S(2)}) collective-permute-start(bf16[4,72,512]{2,1,0:T(8,128)(2,1)S(1)} %get-tuple-element.69), channel_id=1, source_target_pairs={{0,32},{32,64},{64,96},{96,0},{1,33},{33,65},{65,97},{97,1},{2,34}... | collective-permute-start | bytes 884744 | tf_op jit(solution)/shard_map/ppermute | solution.py:64
  72.2 28.0 %copy-start.3 = (bf16[4,4,72,512]{3,2,1,0:T(8,128)(2,1)}, bf16[4,4,72,512]{3,2,1,0:T(8,128)(2,1)S(1)}, u32[]{:S(2)}) copy-start(bf16[4,4,72,512]{3,2,1,0:T(8,128)(2,1)S(1)} %pad_maximum_fusion.2) | copy-start | bytes 3538948
  72.3 11.9 %collective-permute-start.8 = (bf16[16,40,512]{2,1,0:T(8,128)(2,1)S(1)}, bf16[16,40,512]{2,1,0:T(8,128)(2,1)S(1)}, u32[]{:S(2)}, u32[]{:S(2)}) collective-permute-start(bf16[16,40,512]{2,1,0:T(8,128)(2,1)S(1)} %get-tuple-element.49), channel_id=1, source_target_pairs={{0,24},{8,0},{16,8},{24,16},{1,25},{9,1},{17,9},{25,17},{2,26},{10... | collective-permute-start | bytes 1966088 | tf_op jit(solution)/shard_map/ppermute | solution.py:70
  76.7 12.6 %collective-permute-start.6 = (bf16[16,40,512]{2,1,0:T(8,128)(2,1)S(1)}, bf16[16,40,512]{2,1,0:T(8,128)(2,1)S(1)}, u32[]{:S(2)}, u32[]{:S(2)}) collective-permute-start(bf16[16,40,512]{2,1,0:T(8,128)(2,1)S(1)} %get-tuple-element.49), channel_id=1, source_target_pairs={{0,8},{8,16},{16,24},{24,0},{1,9},{9,17},{17,25},{25,1},{2,10},{10... | collective-permute-start | bytes 1966088 | tf_op jit(solution)/shard_map/ppermute | solution.py:70
  84.2 10.6 %collective-permute-start.9 = (bf16[8,40,512]{2,1,0:T(8,128)(2,1)S(1)}, bf16[8,40,512]{2,1,0:T(8,128)(2,1)S(1)}, u32[]{:S(2)}, u32[]{:S(2)}) collective-permute-start(bf16[8,40,512]{2,1,0:T(8,128)(2,1)S(1)} %slice.181), channel_id=1, source_target_pairs={{0,24},{8,0},{16,8},{24,16},{1,25},{9,1},{17,9},{25,17},{2,26},{10... | collective-permute-start | bytes 983048 | tf_op jit(solution)/shard_map/ppermute | solution.py:71
  89.3 10.8 %collective-permute-start.7 = (bf16[8,40,512]{2,1,0:T(8,128)(2,1)S(1)}, bf16[8,40,512]{2,1,0:T(8,128)(2,1)S(1)}, u32[]{:S(2)}, u32[]{:S(2)}) collective-permute-start(bf16[8,40,512]{2,1,0:T(8,128)(2,1)S(1)} %slice.180), channel_id=1, source_target_pairs={{0,8},{8,16},{16,24},{24,0},{1,9},{9,17},{17,25},{25,1},{2,10},{10... | collective-permute-start | bytes 983048 | tf_op jit(solution)/shard_map/ppermute | solution.py:71
  100.2 11.4 %copy-start.24 = (s32[1,4]{1,0:T(1,128)S(1)}, s32[1,4]{1,0:T(1,128)}, u32[]{:S(2)}) copy-start(s32[1,4]{1,0:T(1,128)} %param.15) | copy-start | bytes 52
  100.6 30.9 %copy-start.1 = (bf16[4,16,40,512]{3,2,1,0:T(8,128)(2,1)}, bf16[4,16,40,512]{3,2,1,0:T(8,128)(2,1)S(1)}, u32[]{:S(2)}) copy-start(bf16[4,16,40,512]{3,2,1,0:T(8,128)(2,1)S(1)} %pad_maximum_fusion) | copy-start | bytes 7864324
  100.6 30.8 %collective-permute-start.12 = (bf16[64,40,512]{2,1,0:T(8,128)(2,1)S(1)}, bf16[64,40,512]{2,1,0:T(8,128)(2,1)}, u32[]{:S(2)}, u32[]{:S(2)}) collective-permute-start(bf16[64,40,512]{2,1,0:T(8,128)(2,1)S(1)} %bitcast.118), channel_id=1, source_target_pairs={{0,4},{4,0},{1,5},{5,1},{2,6},{6,2},{3,7},{7,3},{8,12},{12,8},{9,1... | collective-permute-start | bytes 7864328 | tf_op jit(solution)/shard_map/ppermute | solution.py:76
  113.1 18.3 %copy-start.7 = (bf16[16,32,512]{2,1,0:T(8,128)(2,1)}, bf16[16,32,512]{2,1,0:T(8,128)(2,1)S(1)}, u32[]{:S(2)}) copy-start(bf16[16,32,512]{2,1,0:T(8,128)(2,1)S(1)} %slice.178) | copy-start | bytes 1572868
  113.1 16.6 %collective-permute-start.10 = (bf16[16,32,512]{2,1,0:T(8,128)(2,1)S(1)}, bf16[16,32,512]{2,1,0:T(8,128)(2,1)S(1)}, u32[]{:S(2)}, u32[]{:S(2)}) collective-permute-start(bf16[16,32,512]{2,1,0:T(8,128)(2,1)S(1)} %slice.178), channel_id=1, source_target_pairs={{0,8},{8,16},{16,24},{24,0},{1,9},{9,17},{17,25},{25,1},{2,10},{10... | collective-permute-start | bytes 1572872 | tf_op jit(solution)/shard_map/ppermute | solution.py:326
  115.0 15.6 %collective-permute-start.11 = (bf16[16,32,512]{2,1,0:T(8,128)(2,1)S(1)}, bf16[16,32,512]{2,1,0:T(8,128)(2,1)S(1)}, u32[]{:S(2)}, u32[]{:S(2)}) collective-permute-start(bf16[16,32,512]{2,1,0:T(8,128)(2,1)S(1)} %slice.178), channel_id=1, source_target_pairs={{0,24},{8,0},{16,8},{24,16},{1,25},{9,1},{17,9},{25,17},{2,26},{10... | collective-permute-start | bytes 1572872 | tf_op jit(solution)/shard_map/ppermute | solution.py:327
  138.7 10.1 %collective-permute-start.14 = (bf16[8,32,512]{2,1,0:T(8,128)(2,1)}, bf16[8,32,512]{2,1,0:T(8,128)(2,1)S(1)}, u32[]{:S(2)}, u32[]{:S(2)}) collective-permute-start(bf16[8,32,512]{2,1,0:T(8,128)(2,1)} %slice.183), channel_id=1, source_target_pairs={{0,24},{8,0},{16,8},{24,16},{1,25},{9,1},{17,9},{25,17},{2,26},{10... | collective-permute-start | bytes 786440 | tf_op jit(solution)/shard_map/ppermute | solution.py:353
  144.0 9.7 %collective-permute-start.13 = (bf16[8,32,512]{2,1,0:T(8,128)(2,1)}, bf16[8,32,512]{2,1,0:T(8,128)(2,1)S(1)}, u32[]{:S(2)}, u32[]{:S(2)}) collective-permute-start(bf16[8,32,512]{2,1,0:T(8,128)(2,1)} %slice.182), channel_id=1, source_target_pairs={{0,8},{8,16},{16,24},{24,0},{1,9},{9,17},{17,25},{25,1},{2,10},{10... | collective-permute-start | bytes 786440 | tf_op jit(solution)/shard_map/ppermute | solution.py:353
  153.7 6.1 %copy-start.4 = (bf16[88,512]{1,0:T(8,128)(2,1)S(1)}, bf16[88,512]{1,0:T(8,128)(2,1)}, u32[]{:S(2)}) copy-start(bf16[88,512]{1,0:T(8,128)(2,1)} %pick_rows.1) | copy-start | bytes 270340
  155.4 23.5 %copy-start.2 = (bf16[4,16,32,512]{3,2,1,0:T(8,128)(2,1)}, bf16[4,16,32,512]{3,2,1,0:T(8,128)(2,1)S(1)}, u32[]{:S(2)}) copy-start(bf16[4,16,32,512]{3,2,1,0:T(8,128)(2,1)S(1)} %pad_maximum_fusion.1) | copy-start | bytes 6291460
  155.4 23.5 %collective-permute-start.15 = (bf16[64,32,512]{2,1,0:T(8,128)(2,1)S(1)}, bf16[64,32,512]{2,1,0:T(8,128)(2,1)}, u32[]{:S(2)}, u32[]{:S(2)}) collective-permute-start(bf16[64,32,512]{2,1,0:T(8,128)(2,1)S(1)} %bitcast.120), channel_id=1, source_target_pairs={{0,4},{4,0},{1,5},{5,1},{2,6},{6,2},{3,7},{7,3},{8,12},{12,8},{9,1... | collective-permute-start | bytes 6291464 | tf_op jit(solution)/shard_map/ppermute | solution.py:76
  186.2 17.6 %collective-permute-start.18 = (bf16[256,1024]{1,0:T(8,128)(2,1)}, bf16[256,1024]{1,0:T(8,128)(2,1)}, u32[]{:S(2)}, u32[]{:S(2)}) collective-permute-start(bf16[256,1024]{1,0:T(8,128)(2,1)} %get-tuple-element.21), channel_id=1, source_target_pairs={{0,387},{128,0},{256,128},{384,256},{1,384},{129,1},{257,129},{385... | collective-permute-start | bytes 1572872 | tf_op jit(solution)/shard_map/ppermute | solution.py:398
  192.9 17.3 %collective-permute-start.16 = (bf16[256,1024]{1,0:T(8,128)(2,1)}, bf16[256,1024]{1,0:T(8,128)(2,1)}, u32[]{:S(2)}, u32[]{:S(2)}) collective-permute-start(bf16[256,1024]{1,0:T(8,128)(2,1)} %get-tuple-element.21), channel_id=1, source_target_pairs={{0,128},{128,256},{256,384},{384,1},{1,129},{129,257},{257,385},{3... | collective-permute-start | bytes 1572872 | tf_op jit(solution)/shard_map/ppermute | solution.py:397
  197.8 15.4 %copy-start.11 = (bf16[256,1024]{1,0:T(8,128)(2,1)S(1)}, bf16[256,1024]{1,0:T(8,128)(2,1)}, u32[]{:S(2)}) copy-start(bf16[256,1024]{1,0:T(8,128)(2,1)} %get-tuple-element.21) | copy-start | bytes 1572868
  204.8 9.4 %collective-permute-start.19 = (bf16[128,1024]{1,0:T(8,128)(2,1)S(1)}, bf16[128,1024]{1,0:T(8,128)(2,1)S(1)}, u32[]{:S(2)}, u32[]{:S(2)}) collective-permute-start(bf16[128,1024]{1,0:T(8,128)(2,1)S(1)} %get-tuple-element.61), channel_id=1, source_target_pairs={{0,387},{128,0},{256,128},{384,256},{1,384},{129,1},{257,129},{385... | collective-permute-start | bytes 786440 | tf_op jit(solution)/shard_map/ppermute | solution.py:400
  211.3 9.1 %collective-permute-start.17 = (bf16[128,1024]{1,0:T(8,128)(2,1)S(1)}, bf16[128,1024]{1,0:T(8,128)(2,1)S(1)}, u32[]{:S(2)}, u32[]{:S(2)}) collective-permute-start(bf16[128,1024]{1,0:T(8,128)(2,1)S(1)} %get-tuple-element.58), channel_id=1, source_target_pairs={{0,128},{128,256},{256,384},{384,1},{1,129},{129,257},{257,385},{3... | collective-permute-start | bytes 786440 | tf_op jit(solution)/shard_map/ppermute | solution.py:399
  222.5 54.4 %copy-start.13 = (bf16[1,2048,176]{1,2,0:T(8,128)(2,1)S(1)}, bf16[1,2048,176]{1,2,0:T(8,128)(2,1)}, u32[]{:S(2)}) copy-start(bf16[1,2048,176]{1,2,0:T(8,128)(2,1)} %param.26) | copy-start | bytes 2162692
  273.7 10.0 %collective-permute-start.20 = (bf16[1792,1024]{1,0:T(8,128)(2,1)}, bf16[1792,1024]{1,0:T(8,128)(2,1)}, u32[]{:S(2)}, u32[]{:S(2)}) collective-permute-start(bf16[1792,1024]{1,0:T(8,128)(2,1)} %bitcast.60), channel_id=1, source_target_pairs={{0,4},{4,0},{1,5},{5,1},{2,6},{6,2},{3,7},{7,3},{8,12},{12,8},{9,1... | collective-permute-start | bytes 11010056 | tf_op jit(solution)/shard_map/ppermute | solution.py:76
  287.2 74.9 %copy-start.10 = (bf16[1,704,512]{2,1,0:T(8,128)(2,1)S(1)}, bf16[1,704,512]{2,1,0:T(8,128)(2,1)}, u32[]{:S(2)}) copy-start(bf16[1,704,512]{2,1,0:T(8,128)(2,1)} %param.27) | copy-start | bytes 2162692
  290.7 65.9 %copy-start.22 = (bf16[176,1792]{1,0:T(8,128)(2,1)}, bf16[176,1792]{1,0:T(8,128)(2,1)S(1)}, u32[]{:S(2)}) copy-start(bf16[176,1792]{1,0:T(8,128)(2,1)S(1)} %fusion.1) | copy-start | bytes 1892356
  290.7 60.3 %collective-permute-start.22 = (bf16[176,1792]{1,0:T(8,128)(2,1)S(1)}, bf16[176,1792]{1,0:T(8,128)(2,1)S(1)}, u32[]{:S(2)}, u32[]{:S(2)}) collective-permute-start(bf16[176,1792]{1,0:T(8,128)(2,1)S(1)} %fusion.1), channel_id=1, source_target_pairs={{0,3},{1,0},{2,1},{3,2},{4,7},{5,4},{6,5},{7,6},{8,11},{9,8},{10,9... | collective-permute-start | bytes 1892360 | tf_op jit(solution)/shard_map/ppermute | solution.py:419
  292.7 63.1 %collective-permute-start.21 = (bf16[176,1792]{1,0:T(8,128)(2,1)S(1)}, bf16[176,1792]{1,0:T(8,128)(2,1)S(1)}, u32[]{:S(2)}, u32[]{:S(2)}) collective-permute-start(bf16[176,1792]{1,0:T(8,128)(2,1)S(1)} %fusion.1), channel_id=1, source_target_pairs={{0,1},{1,2},{2,3},{3,0},{4,5},{5,6},{6,7},{7,4},{8,9},{9,10},{10,1... | collective-permute-start | bytes 1892360 | tf_op jit(solution)/shard_map/ppermute | solution.py:418
  351.9 22.8 %collective-permute-start.24 = (bf16[88,1792]{1,0:T(8,128)(2,1)S(1)}, bf16[88,1792]{1,0:T(8,128)(2,1)S(1)}, u32[]{:S(2)}, u32[]{:S(2)}) collective-permute-start(bf16[88,1792]{1,0:T(8,128)(2,1)S(1)} %slice.201), channel_id=1, source_target_pairs={{0,3},{1,0},{2,1},{3,2},{4,7},{5,4},{6,5},{7,6},{8,11},{9,8},{10,9... | collective-permute-start | bytes 946184 | tf_op jit(solution)/shard_map/ppermute | solution.py:421
  356.6 26.3 %collective-permute-start.23 = (bf16[88,1792]{1,0:T(8,128)(2,1)S(1)}, bf16[88,1792]{1,0:T(8,128)(2,1)}, u32[]{:S(2)}, u32[]{:S(2)}) collective-permute-start(bf16[88,1792]{1,0:T(8,128)(2,1)S(1)} %slice.200), channel_id=1, source_target_pairs={{0,1},{1,2},{2,3},{3,0},{4,5},{5,6},{6,7},{7,4},{8,9},{9,10},{10,1... | collective-permute-start | bytes 946184 | tf_op jit(solution)/shard_map/ppermute | solution.py:420
  362.1 22.4 %copy-start.15 = (bf16[176,1792]{1,0:T(8,128)(2,1)S(1)}, bf16[176,1792]{1,0:T(8,128)(2,1)}, u32[]{:S(2)}) copy-start(bf16[176,1792]{1,0:T(8,128)(2,1)} %copy-done.14) | copy-start | bytes 1892356
  362.2 22.4 %copy-start.17 = (bf16[176,1792]{1,0:T(8,128)(2,1)S(1)}, bf16[176,1792]{1,0:T(8,128)(2,1)}, u32[]{:S(2)}) copy-start(bf16[176,1792]{1,0:T(8,128)(2,1)} %copy-done.16) | copy-start | bytes 1892356
  362.2 22.4 %copy-start.23 = (bf16[176,1792]{1,0:T(8,128)(2,1)S(1)}, bf16[176,1792]{1,0:T(8,128)(2,1)}, u32[]{:S(2)}) copy-start(bf16[176,1792]{1,0:T(8,128)(2,1)} %copy-done.22) | copy-start | bytes 1892356
  387.2 4.8 %collective-permute-start.25 = (bf16[1792,256]{1,0:T(8,128)(2,1)}, bf16[1792,256]{1,0:T(8,128)(2,1)}, u32[]{:S(2)}, u32[]{:S(2)}) collective-permute-start(bf16[1792,256]{1,0:T(8,128)(2,1)} %constant_dynamic-slice_fusion), channel_id=1, source_target_pairs={{0,4},{4,0},{1,5},{5,1},{2,6},{6,2},{3,7},{7,3},{8,12},{12,8},{9,1... | collective-permute-start | bytes 2752520 | tf_op jit(solution)/shard_map/ppermute | solution.py:76
  394.4 19.2 %all-to-all-start.1 = ((bf16[32,56,256]{2,1,0:T(8,128)(2,1)}), bf16[32,56,256]{2,1,0:T(8,128)(2,1)S(1)}, u32[]{:S(2)}, u32[]{:S(2)}) async-start(bf16[32,56,256]{2,1,0:T(8,128)(2,1)} %bitcast.68), calls=%async_computation.1 | async-start | bytes 1835008 | tf_op jit(solution)/shard_map/all_to_all | solution.py:434
  413.7 11.3 %copy-start.19 = (bf16[128,128]{1,0:T(8,128)(2,1)S(1)}, bf16[128,128]{1,0:T(8,128)(2,1)}, u32[]{:S(2)}) copy-start(bf16[128,128]{1,0:T(8,128)(2,1)} %get-tuple-element.25) | copy-start | bytes 98308
  413.7 11.4 %copy-start.18 = (bf16[128,512]{1,0:T(8,128)(2,1)S(1)}, bf16[128,512]{1,0:T(8,128)(2,1)}, u32[]{:S(2)}) copy-start(bf16[128,512]{1,0:T(8,128)(2,1)} %get-tuple-element.24) | copy-start | bytes 393220
  414.4 17.3 %copy-start.20 = (bf16[128,512]{1,0:T(8,128)(2,1)S(1)}, bf16[128,512]{1,0:T(8,128)(2,1)}, u32[]{:S(2)}) copy-start(bf16[128,512]{1,0:T(8,128)(2,1)} %get-tuple-element.20) | copy-start | bytes 393220
  415.4 10.5 %collective-permute-start.28 = (bf16[2,128,256]{2,1,0:T(8,128)(2,1)S(1)}, bf16[2,128,256]{2,1,0:T(8,128)(2,1)S(1)}, u32[]{:S(2)}, u32[]{:S(2)}) collective-permute-start(bf16[2,128,256]{2,1,0:T(8,128)(2,1)S(1)} %get-tuple-element.54), channel_id=1, source_target_pairs={{0,128},{128,256},{256,384},{384,0},{1,129},{129,257},{257,385},{3... | collective-permute-start | bytes 393224 | tf_op jit(solution)/shard_map/ppermute | solution.py:444
  419.1 11.6 %collective-permute-start.27 = (bf16[2,128,256]{2,1,0:T(8,128)(2,1)S(1)}, bf16[2,128,256]{2,1,0:T(8,128)(2,1)S(1)}, u32[]{:S(2)}, u32[]{:S(2)}) collective-permute-start(bf16[2,128,256]{2,1,0:T(8,128)(2,1)S(1)} %get-tuple-element.55), channel_id=1, source_target_pairs={{0,256},{128,384},{256,0},{384,128},{1,257},{129,385},{257,1},{385... | collective-permute-start | bytes 393224 | tf_op jit(solution)/shard_map/ppermute | solution.py:444
  421.0 9.6 %collective-permute-start.26 = (bf16[2,128,256]{2,1,0:T(8,128)(2,1)S(1)}, bf16[2,128,256]{2,1,0:T(8,128)(2,1)S(1)}, u32[]{:S(2)}, u32[]{:S(2)}) collective-permute-start(bf16[2,128,256]{2,1,0:T(8,128)(2,1)S(1)} %get-tuple-element.53), channel_id=1, source_target_pairs={{0,384},{128,0},{256,128},{384,256},{1,385},{129,1},{257,129},{385... | collective-permute-start | bytes 393224 | tf_op jit(solution)/shard_map/ppermute | solution.py:444
  (7 other events, 16.2 us)

commit v5 on v4

--- a/solution.py
+++ b/solution.py
@@ -244,7 +244,7 @@
 def mix(place, everything, attended, mine, theirs, moe_gain):
     def kernel(
         place_ref, in_ref, attended_ref, mine_ref, theirs_ref, gain_ref,
-        moe_ref, cols_ref, server_ref, w_first, w_second,
+        moe_ref, left_ref, right_ref, cols_ref, server_ref, w_first, w_second,
     ):
         c, t = place_ref[3], place_ref[4]
 
@@ -273,6 +273,8 @@
         moe = rms_norm(mixed, gain_ref[...]).astype(BF)
         moe_ref[0:128, :] = moe[:, 0:1024]
         moe_ref[128:256, :] = moe[:, 1024:2048]
+        left_ref[...] = moe[:, 0:1024]
+        right_ref[...] = moe[:, 1024:2048]
 
     def whole(*shape):
         return pl.BlockSpec(shape, lambda i: (0,) * len(shape))
@@ -282,11 +284,15 @@
         grid=(1,),
         out_shape=[
             jax.ShapeDtypeStruct((256, 1024), BF),
+            jax.ShapeDtypeStruct((128, 1024), BF),
+            jax.ShapeDtypeStruct((128, 1024), BF),
             jax.ShapeDtypeStruct((128, 512), BF),
             jax.ShapeDtypeStruct((2048, 256), BF),
         ],
         in_specs=[SMEM, whole(128, 2048), whole(128, 1024), VMEM, VMEM, whole(1, 2048)],
-        out_specs=[whole(256, 1024), whole(128, 512), whole(2048, 256)],
+        out_specs=[
+            whole(256, 1024), whole(128, 1024), whole(128, 1024), whole(128, 512), whole(2048, 256)
+        ],
         scratch_shapes=[pltpu.VMEM((2048, 512), BF), pltpu.VMEM((2048, 512), BF)],
         name="mix",
     )(place, everything, attended, mine, theirs, moe_gain.reshape(1, 2048))
@@ -318,11 +324,19 @@
     gathered = jnp.stack(shifted(rows, "zl"))
     column_routes = gathered[:, 72:78, 0:128].astype(jnp.int32)
     column_gates = gathered[:, 80:86, 0:128].astype(F32)
+    down_mine, _ = lax.optimization_barrier((expert_down[0], column_routes))
+    below_a = lax.ppermute(down_mine[:352], T, UP)
+    above_a = lax.ppermute(down_mine[352:], T, DOWN)
     gathered = jnp.stack(shifted(gathered[:, :72], "y")).reshape(16, 72, 512)
     first_set = gathered[:, :40]
     first_mine = jnp.stack(ring(first_set, "x")).reshape(64, 40, 512)
+    first_mine, below_a, above_a, down_mine = lax.optimization_barrier(
+        (first_mine, below_a, above_a, down_mine)
+    )
     first_theirs = other_core(first_mine)
-    second_set, _ = lax.optimization_barrier((gathered[:, 40:], first_mine))
+    below_b = lax.ppermute(down_mine[352:], T, UP)
+    above_b = lax.ppermute(down_mine[:352], T, DOWN)
+    second_set, _ = lax.optimization_barrier((gathered[:, 40:], first_theirs))
     second_below = lax.ppermute(second_set, "x", UP)
     second_above = lax.ppermute(second_set, "x", DOWN)
 
@@ -346,16 +360,21 @@
     )
     cache_full = jnp.concatenate([latent_normed, key_rope[:, 0:32], key_rope[:, 64:96]], axis=1)
     cache_cols = lax.dynamic_slice_in_dim(cache_full, rank * 144, 144, 1)
-    below_part, above_part, attended = lax.optimization_barrier(
-        (second_below[:8], second_above[8:], attended)
-    )
-    second_far = jnp.concatenate(
-        [lax.ppermute(below_part, "x", UP), lax.ppermute(above_part, "x", DOWN)]
-    )
+    second_below, second_above, attended = lax.optimization_barrier(
+        (second_below, second_above, attended)
+    )
+    far_first = lax.ppermute(second_below[:8], "x", UP)
+    far_second = lax.ppermute(second_above[8:], "x", DOWN)
+    attended, below_b, above_b = lax.optimization_barrier((attended, below_b, above_b))
     attended_full = lax.all_gather(attended, T, axis=1, tiled=True)
-    second_mine = jnp.stack([second_set, second_below, second_far, second_above]).reshape(64, 32, 512)
+    far_first, far_second, attended_full = lax.optimization_barrier(
+        (far_first, far_second, attended_full)
+    )
+    second_mine = jnp.stack(
+        [second_set, second_below, jnp.concatenate([far_first, far_second]), second_above]
+    ).reshape(64, 32, 512)
     second_theirs = other_core(second_mine)
-    moe_halves, mixed_cols, output_block = mix(
+    moe_both, moe_left, moe_right, mixed_cols, output_block = mix(
         place, everything, attended_full, second_mine, second_theirs, moe_gain
     )
 
@@ -367,26 +386,31 @@
     )
     row_ids = jnp.arange(LAYER_ROWS, dtype=jnp.int32)[:, None]
     dispatch = jnp.zeros((LAYER_ROWS, 4 * TOK), F32)
-    combine = jnp.zeros((LAYER_ROWS, 4 * TOK), F32)
     for k in range(6):
-        hit = row_ids == target[:, k].reshape(1, 4 * TOK)
-        dispatch = dispatch + hit.astype(F32)
-        combine = combine + jnp.where(hit, column_gates[:, k].reshape(1, 4 * TOK), 0.0)
+        dispatch = dispatch + (row_ids == target[:, k].reshape(1, 4 * TOK)).astype(F32)
     dispatch = jnp.broadcast_to(dispatch.astype(BF)[None], (2, LAYER_ROWS, 4 * TOK))
-    combine = jnp.broadcast_to(combine.astype(BF)[None], (2, LAYER_ROWS, 4 * TOK))
-
-    def halves(matrix):
-        return (
-            lax.dynamic_slice_in_dim(matrix, core * (D // 2), D // 2, 0),
-            lax.dynamic_slice_in_dim(matrix, (1 - core) * (D // 2), D // 2, 0),
-        )
-
-    gate_mine, gate_other = halves(expert_gate[0])
-    up_mine, up_other = halves(expert_up[0])
-    around = [(rank + 4 - back) % 4 for back in (0, 1, 3, 2)]
-    down_around = jnp.concatenate(
-        [lax.dynamic_slice_in_dim(expert_down[0], at * 176, 176, 0) for at in around], axis=0
-    )
+
+    at_zl = lax.axis_index("zl")
+    served = (at_zl - rank + 4) % 4
+    slots = jnp.arange(16 * 16, dtype=jnp.int32)[:, None]
+    back = target - group * CAP
+    back = jnp.where(target >= 0, back // (4 * CAP) * 16 + back % (4 * CAP), -1)
+    back = lax.dynamic_index_in_dim(back, served, 0, keepdims=False)
+    back_gates = lax.dynamic_index_in_dim(column_gates, served, 0, keepdims=False)
+    combine = jnp.zeros((16 * 16, TOK), F32)
+    for k in range(6):
+        combine = combine + jnp.where(slots == back[k][None], back_gates[k][None], 0.0)
+    combine = jnp.broadcast_to(combine.astype(BF)[None], (2, 16 * 16, TOK))
+
+    place_ids = jnp.arange(4 * 512, dtype=jnp.int32)
+    to_plane, source, slot = place_ids // 512, place_ids // 16 % 32, place_ids % 16
+    wanted = source * (4 * CAP) + (at_zl - to_plane + 4) % 4 * CAP + slot
+    wanted = jnp.where(slot < CAP, wanted, -1)
+    spread = (jnp.arange(2 * LAYER_ROWS, dtype=jnp.int32)[:, None] == wanted[None, :]).astype(BF)
+
+    both_up = jnp.concatenate([expert_gate[0], expert_up[0]], axis=1)
+    up_mine = lax.dynamic_slice_in_dim(both_up, core * (D // 2), D // 2, 0)
+    up_other = lax.dynamic_slice_in_dim(both_up, (1 - core) * (D // 2), D // 2, 0)
 
     def rows_by(weight, rows):
         return lax.dot_general(weight, rows, (((0,), (1,)), ((), ())), preferred_element_type=F32)
@@ -394,56 +418,68 @@
     at_z = [(z % 4) * 4 + z // 4 for z in range(16)]
     z_up = [(at_z[z], at_z[(z + 1) % 16]) for z in range(16)]
     z_down = [(at_z[z], at_z[(z + 15) % 16]) for z in range(16)]
-    back_one = lax.ppermute(moe_halves, ("zl", T), z_up)
-    on_one = lax.ppermute(moe_halves, ("zl", T), z_down)
-    far_left = lax.ppermute(back_one[:TOK], ("zl", T), z_up)
-    far_right = lax.ppermute(on_one[TOK:], ("zl", T), z_down)
+    back_one = lax.ppermute(moe_both, ("zl", T), z_up)
+    on_one = lax.ppermute(moe_both, ("zl", T), z_down)
+    far_left = lax.ppermute(moe_left, ("zl", T), [(at_z[z], at_z[(z + 2) % 16]) for z in range(16)])
+    far_right = lax.ppermute(
+        moe_right, ("zl", T), [(at_z[z], at_z[(z + 14) % 16]) for z in range(16)]
+    )
     tokens = jnp.stack(
         [
-            jnp.concatenate([moe_halves[:TOK], back_one[:TOK], far_left, on_one[:TOK]]),
-            jnp.concatenate([moe_halves[TOK:], back_one[TOK:], far_right, on_one[TOK:]]),
+            jnp.concatenate([moe_left, back_one[:TOK], far_left, on_one[:TOK]]),
+            jnp.concatenate([moe_right, back_one[TOK:], far_right, on_one[TOK:]]),
         ]
     )
     outgoing = lax.dot_general(
         dispatch, tokens, (((2,), (1,)), ((0,), (0,))), preferred_element_type=F32
     ).astype(BF)
+    below_a, above_a, outgoing = lax.optimization_barrier((below_a, above_a, outgoing))
+    down_first = lax.ppermute(below_a, T, UP)
+    down_second = lax.ppermute(above_a, T, DOWN)
     mine = lax.all_to_all(
         outgoing.reshape(2 * LAYER_ROWS, D // 2), LAYER, split_axis=0, concat_axis=0, tiled=True
     )
+    mine, down_first, down_second = lax.optimization_barrier((mine, down_first, down_second))
+    down_far = jnp.concatenate([down_first, down_second])
     theirs = other_core(mine)
-    gate_part = rows_by(gate_mine, mine) + rows_by(gate_other, theirs)
-    up_part = rows_by(up_mine, mine) + rows_by(up_other, theirs)
-    own = (jax.nn.silu(gate_part) * up_part).astype(BF)
-
-    below = lax.ppermute(own, T, UP)
-    above = lax.ppermute(own, T, DOWN)
-    far_first = lax.ppermute(below[:88], T, UP)
-    far_second = lax.ppermute(above[88:], T, DOWN)
-
-    def out_of(pieces, at):
-        rows = jnp.concatenate(pieces, axis=0)
+    pre = rows_by(up_mine, mine) + rows_by(up_other, theirs)
+    own = (jax.nn.silu(pre[:176]) * pre[176:]).astype(BF)
+    own = jnp.dot(own, spread, preferred_element_type=F32).astype(BF)
+    own = own.reshape(176, 4, 512).transpose(1, 0, 2)
+    hidden = lax.all_to_all(own, T, split_axis=0, concat_axis=0, tiled=True).reshape(704, 512)
+
+    down_below = jnp.concatenate([below_a, below_b])
+    down_above = jnp.concatenate([above_b, above_a])
+    down_all = jnp.stack([down_mine, down_below, down_far, down_above])
+
+    def half_out(half):
+        quarters = [
+            lax.dynamic_index_in_dim(down_all, (rank + 8 - 2 * half - q) % 4, 0, keepdims=False)
+            for q in range(2)
+        ]
         return lax.dot_general(
-            rows, down_around[at : at + rows.shape[0]], (((0,), (0,)), ((), ())),
+            hidden, jnp.concatenate(quarters, axis=1), (((0,), (0,)), ((), ())),
             preferred_element_type=F32,
-        )
-
-    half_out = (out_of([own, below, above], 0) + out_of([far_first, far_second], 528)).astype(BF)
-    keep = lax.dynamic_slice_in_dim(half_out, core * 256, 256, 1)
-    give = lax.dynamic_slice_in_dim(half_out, (1 - core) * 256, 256, 1)
-    both = (keep.astype(F32) + other_core(give).astype(F32)).astype(BF)
+        ).astype(BF)
+
+    given = other_core(half_out(1 - core))
+    both = (half_out(core).astype(F32) + given.astype(F32)).astype(BF)
     returned = lax.all_to_all(both, LAYER, split_axis=0, concat_axis=0, tiled=True)
     partial = lax.dot_general(
         combine,
-        returned.reshape(2, LAYER_ROWS, 256),
+        returned.reshape(2, 16 * 16, D // 2),
         (((1,), (1,)), ((0,), (0,))),
         preferred_element_type=F32,
-    ).reshape(2, 4, TOK, 256)
-    sums = partial[:, 0]
+    )
+    partial = partial.reshape(2, TOK, 2, 512).transpose(0, 2, 1, 3).reshape(4, TOK, 512)
+    total = lax.dynamic_index_in_dim(partial, at_zl, 0, keepdims=False)
     for s in range(1, 4):
-        sent = partial[:, s].astype(BF)
-        sums = sums + lax.ppermute(sent, "zl", [(j, (j - s) % 4) for j in range(4)]).astype(F32)
+        sent = lax.dynamic_index_in_dim(partial, (at_zl + s) % 4, 0, keepdims=False).astype(BF)
+        total = total + lax.ppermute(sent, "zl", [(j, (j + s) % 4) for j in range(4)]).astype(F32)
+    home = [(a * 4 + b, b * 4 + a) for a in range(4) for b in range(4)]
+    sums = lax.ppermute(total.astype(BF), ("zl", T), home)
     result = mixed_cols.astype(F32)
-    hidden_out = (result + jnp.concatenate([sums[0], sums[1]], axis=1)).astype(BF)
+    hidden_out = (result + sums.astype(F32)).astype(BF)
     return (hidden_out, expand_block, output_block, cache_cols)
 
 

time: 435 us -> 449 us (1.032)
  the two profiles are of different devices: /device:TPU:1 before, /device:TPU:64 now
where the time goes in v5:
time: 449 us; the launch traced here: 447 us
  waiting for transfers between devices  180 us (40%)
  starting transfers between devices  140 us (31%)
  blocking collectives  67.4 us (15%)
  matrix products  19.4 us (4%)
  Pallas kernels  17.9 us (4%)
  other arithmetic  10.9 us (2%)
  local copies, waits for them, and re-layouts  9.49 us (2%)
    all_gather x1, blocking collectives, body(): everything = lax.all_gather(packed, T, axis=1, tiled=True)  35.9 us
    all_to_all x1, waiting for transfers between devices, body(): lax.all_to_all(own, T, split_axis=0, concat_axis=0, tiled=True)  33.1 us
    all_gather x1, blocking collectives, body(): attended_full = lax.all_gather(attended, T, axis=1, tiled=True)  31.4 us
    all_to_all x1, waiting for transfers between devices, body(): lax.all_to_all(outgoing.reshape(2 * LAYER_ROWS, D // 2), LAYER, split_axi...  21.3 us
    ppermute x6, starting transfers between devices, shifted(): lax.ppermute(block, axis, [(j, (j + s) % 4) for j in range(4)])  19.6 us
    all_to_all x1, waiting for transfers between devices, body(): lax.all_to_all(both, LAYER, split_axis=0, concat_axis=0, tiled=True)  17.3 us
    ppermute x4, waiting for transfers between devices, other_core(): return lax.ppermute(block, 'c', [(0, 1), (1, 0)])  15.2 us
    ppermute x6, waiting for transfers between devices, shifted(): lax.ppermute(block, axis, [(j, (j + s) % 4) for j in range(4)])  14.8 us
  transfers between devices with their start and end apart: 35, of which 24 were waited for; matrix products, arithmetic and copies ran while one was open for 3% of the time, Pallas kernels for 2%

profile of v5, /device:TPU:64, one launch (start us, length us, event | category | flops | bytes accessed | tf_op | source)
XLA Modules:
  0.0 447.4 jit_solution(529756530264791625)
XLA Ops:
  2.3 35.9 %all_gather.6.in_ref = bf16[160,2048]{1,0:T(8,128)(2,1)} all-gather(bf16[160,512]{1,0:T(8,128)(2,1)} %pack_rows.1), channel_id=1, replica_groups=mesh['zl'=4,'y'=4,'x'=4,'c'=2,'t'=4] {'t'}, dimensions={1}, use_global_device_ids=true | all-gather | bytes 819200 | tf_op jit(solution)/shard_map/all_gather | solution.py:322
  40.5 3.6 collective-permute-start.2
  44.1 3.8 collective-permute-start.1
  51.7 2.8 collective-permute-done
  55.5 4.9 %collective-permute-start.5 = (bf16[4,72,512]{2,1,0:T(8,128)(2,1)S(1)}, bf16[4,72,512]{2,1,0:T(8,128)(2,1)S(1)}, u32[]{:S(2)}, u32[]{:S(2)}) collective-permute-start(bf16[4,72,512]{2,1,0:T(8,128)(2,1)S(1)} %get-tuple-element.109), channel_id=1, source_target_pairs={{0,96},{32,0},{64,32},{96,64},{1,97},{33,1},{65,33},{97,65},{2,98}... | collective-permute-start | bytes 884744 | tf_op jit(solution)/shard_map/ppermute | solution.py:64
  63.0 2.9 collective-permute-start.3
  65.9 4.6 %collective-permute-done.5 = bf16[4,72,512]{2,1,0:T(8,128)(2,1)S(1)} collective-permute-done((bf16[4,72,512]{2,1,0:T(8,128)(2,1)S(1)}, bf16[4,72,512]{2,1,0:T(8,128)(2,1)S(1)}, u32[]{:S(2)}, u32[]{:S(2)}) %collective-permute-start.5) | collective-permute-done | bytes 294944 | tf_op jit(solution)/shard_map/ppermute | solution.py:64
  72.9 3.1 collective-permute-done.3
  76.3 4.8 %collective-permute-start.8 = (bf16[16,40,512]{2,1,0:T(8,128)(2,1)S(1)}, bf16[16,40,512]{2,1,0:T(8,128)(2,1)S(1)}, u32[]{:S(2)}, u32[]{:S(2)}) collective-permute-start(bf16[16,40,512]{2,1,0:T(8,128)(2,1)S(1)} %get-tuple-element.94), channel_id=1, source_target_pairs={{0,24},{8,0},{16,8},{24,16},{1,25},{9,1},{17,9},{25,17},{2,26},{10... | collective-permute-start | bytes 1966088 | tf_op jit(solution)/shard_map/ppermute | solution.py:70
  83.0 10.2 %collective-permute-done.8 = bf16[16,40,512]{2,1,0:T(8,128)(2,1)S(1)} collective-permute-done((bf16[16,40,512]{2,1,0:T(8,128)(2,1)S(1)}, bf16[16,40,512]{2,1,0:T(8,128)(2,1)S(1)}, u32[]{:S(2)}, u32[]{:S(2)}) %collective-permute-start.8) | collective-permute-done | bytes 655392 | tf_op jit(solution)/shard_map/ppermute | solution.py:70
  93.3 5.6 %collective-permute-start.9 = (bf16[8,40,512]{2,1,0:T(8,128)(2,1)S(1)}, bf16[8,40,512]{2,1,0:T(8,128)(2,1)S(1)}, u32[]{:S(2)}, u32[]{:S(2)}) collective-permute-start(bf16[8,40,512]{2,1,0:T(8,128)(2,1)S(1)} %slice.204), channel_id=1, source_target_pairs={{0,24},{8,0},{16,8},{24,16},{1,25},{9,1},{17,9},{25,17},{2,26},{10... | collective-permute-start | bytes 983048 | tf_op jit(solution)/shard_map/ppermute | solution.py:71
  101.0 4.3 collective-permute-start.10
  105.4 5.4 %collective-permute-start.11 = (bf16[352,512]{1,0:T(8,128)(2,1)S(1)}, bf16[352,512]{1,0:T(8,128)(2,1)S(1)}, u32[]{:S(2)}, u32[]{:S(2)}) collective-permute-start(bf16[352,512]{1,0:T(8,128)(2,1)S(1)} %get-tuple-element.102), channel_id=1, source_target_pairs={{0,3},{1,0},{2,1},{3,2},{4,7},{5,4},{6,5},{7,6},{8,11},{9,8},{10,9... | collective-permute-start | bytes 1081352 | tf_op jit(solution)/shard_map/ppermute | solution.py:329
  111.2 14.7 %collective-permute-done.10 = bf16[352,512]{1,0:T(8,128)(2,1)S(1)} collective-permute-done((bf16[352,512]{1,0:T(8,128)(2,1)S(1)}, bf16[352,512]{1,0:T(8,128)(2,1)S(1)}, u32[]{:S(2)}, u32[]{:S(2)}) %collective-permute-start.10) | collective-permute-done | bytes 360480 | tf_op jit(solution)/shard_map/ppermute | solution.py:328
  136.7 5.1 %collective-permute-start.14 = (bf16[16,32,512]{2,1,0:T(8,128)(2,1)}, bf16[16,32,512]{2,1,0:T(8,128)(2,1)}, u32[]{:S(2)}, u32[]{:S(2)}) collective-permute-start(bf16[16,32,512]{2,1,0:T(8,128)(2,1)} %slice.201), channel_id=1, source_target_pairs={{0,24},{8,0},{16,8},{24,16},{1,25},{9,1},{17,9},{25,17},{2,26},{10... | collective-permute-start | bytes 1572872 | tf_op jit(solution)/shard_map/ppermute | solution.py:341
  143.6 6.9 %collective-permute-start.17 = (bf16[352,512]{1,0:T(8,128)(2,1)}, bf16[352,512]{1,0:T(8,128)(2,1)}, u32[]{:S(2)}, u32[]{:S(2)}) collective-permute-start(bf16[352,512]{1,0:T(8,128)(2,1)} %get-tuple-element.101), channel_id=1, source_target_pairs={{0,1},{1,2},{2,3},{3,0},{4,5},{5,6},{6,7},{7,4},{8,9},{9,10},{10,1... | collective-permute-start | bytes 1081352 | tf_op jit(solution)/shard_map/ppermute | solution.py:337
  150.5 2.8 collective-permute-start.18
  154.1 7.2 %attention.1 = (bf16[128,256]{1,0:T(8,128)(2,1)}, bf16[128,512]{1,0:T(8,128)(2,1)}, bf16[128,128]{1,0:T(8,128)(2,1)}, bf16[512,512]{1,0:T(8,128)(2,1)}) custom-call(s32[5]{0:T(128)} %stack.128.place_ref, bf16[160,2048]{1,0:T(8,128)(2,1)} %all_gather.6.in_ref, bf16[64,40,512]{2,1,0:T(8,128)(2,1)} %bitcast.138, ...), custom_call_target="tpu_custom_call" | custom-call | tf_op jit(solution)/shard_map/attention/pallas_call | solution.py:222
  165.1 5.1 %collective-permute-start.16 = (bf16[8,32,512]{2,1,0:T(8,128)(2,1)S(1)}, bf16[8,32,512]{2,1,0:T(8,128)(2,1)S(1)}, u32[]{:S(2)}, u32[]{:S(2)}) collective-permute-start(bf16[8,32,512]{2,1,0:T(8,128)(2,1)S(1)} %slice.162), channel_id=1, source_target_pairs={{0,24},{8,0},{16,8},{24,16},{1,25},{9,1},{17,9},{25,17},{2,26},{10... | collective-permute-start | bytes 786440 | tf_op jit(solution)/shard_map/ppermute | solution.py:367
  170.3 31.4 %all_gather.7.attended_ref = bf16[128,1024]{1,0:T(8,128)(2,1)} all-gather(bf16[128,256]{1,0:T(8,128)(2,1)} %get-tuple-element.42), channel_id=1, replica_groups=mesh['zl'=4,'y'=4,'x'=4,'c'=2,'t'=4] {'t'}, dimensions={1}, use_global_device_ids=true | all-gather | bytes 327680 | tf_op jit(solution)/shard_map/all_gather | solution.py:369
  205.7 3.9 collective-permute-done.19.theirs_ref
  209.6 7.4 %mix.1 = (bf16[256,1024]{1,0:T(8,128)(2,1)}, bf16[128,1024]{1,0:T(8,128)(2,1)}, bf16[128,1024]{1,0:T(8,128)(2,1)}, bf16[128,512]{1,0:T(8,128)(2,1)}, bf16[2048,256]{1,0:T(8,128)(2,1)}) custom-call(s32[5]{0:T(128)} %stack.128.place_ref, bf16[160,2048]{1,0:T(8,128)(2,1)} %all_gather.6.in_ref, bf16[128,1024]{1,0:T(8,128)(2,1)} %all_gather.7.attended_ref, ...), custom_call_target="tpu_custom_call" | custom-call | tf_op jit(solution)/shard_map/mix/pallas_call | solution.py:282
  217.1 8.8 %collective-permute-start.22 = (bf16[256,1024]{1,0:T(8,128)(2,1)}, bf16[256,1024]{1,0:T(8,128)(2,1)S(1)}, u32[]{:S(2)}, u32[]{:S(2)}) collective-permute-start(bf16[256,1024]{1,0:T(8,128)(2,1)} %get-tuple-element.50), channel_id=1, source_target_pairs={{0,387},{128,0},{256,128},{384,256},{1,384},{129,1},{257,129},{385... | collective-permute-start | bytes 1572872 | tf_op jit(solution)/shard_map/ppermute | solution.py:422
  226.0 4.6 %collective-permute-start.20 = (bf16[256,1024]{1,0:T(8,128)(2,1)}, bf16[256,1024]{1,0:T(8,128)(2,1)S(1)}, u32[]{:S(2)}, u32[]{:S(2)}) collective-permute-start(bf16[256,1024]{1,0:T(8,128)(2,1)} %get-tuple-element.50), channel_id=1, source_target_pairs={{0,128},{128,256},{256,384},{384,1},{1,129},{129,257},{257,385},{3... | collective-permute-start | bytes 1572872 | tf_op jit(solution)/shard_map/ppermute | solution.py:421
  232.0 5.0 %collective-permute-start.23 = (bf16[128,1024]{1,0:T(8,128)(2,1)}, bf16[128,1024]{1,0:T(8,128)(2,1)S(1)}, u32[]{:S(2)}, u32[]{:S(2)}) collective-permute-start(bf16[128,1024]{1,0:T(8,128)(2,1)} %get-tuple-element.51), channel_id=1, source_target_pairs={{0,259},{128,387},{256,0},{384,128},{1,256},{129,384},{257,1},{385... | collective-permute-start | bytes 786440 | tf_op jit(solution)/shard_map/ppermute | solution.py:424
  237.1 3.0 collective-permute-start.21
  241.5 4.8 %collective-permute-done.20 = bf16[256,1024]{1,0:T(8,128)(2,1)S(1)} collective-permute-done((bf16[256,1024]{1,0:T(8,128)(2,1)}, bf16[256,1024]{1,0:T(8,128)(2,1)S(1)}, u32[]{:S(2)}, u32[]{:S(2)}) %collective-permute-start.20) | collective-permute-done | bytes 524320 | tf_op jit(solution)/shard_map/ppermute | solution.py:421
  246.3 8.3 %collective-permute-done.23 = bf16[128,1024]{1,0:T(8,128)(2,1)S(1)} collective-permute-done((bf16[128,1024]{1,0:T(8,128)(2,1)}, bf16[128,1024]{1,0:T(8,128)(2,1)S(1)}, u32[]{:S(2)}, u32[]{:S(2)}) %collective-permute-start.23) | collective-permute-done | bytes 262176 | tf_op jit(solution)/shard_map/ppermute | solution.py:424
  255.7 3.9 convolution_convert_fusion
  259.6 5.4 %all-to-all-start = ((bf16[32,56,1024]{2,1,0:T(8,128)(2,1)}), bf16[32,56,1024]{2,1,0:T(8,128)(2,1)}, u32[]{:S(2)}, u32[]{:S(2)}) async-start(bf16[32,56,1024]{2,1,0:T(8,128)(2,1)} %bitcast.146), calls=%async_computation | async-start | bytes 7340032 | tf_op jit(solution)/shard_map/all_to_all | solution.py:439
  265.0 4.9 %collective-permute-start.24 = (bf16[352,512]{1,0:T(8,128)(2,1)S(1)}, bf16[352,512]{1,0:T(8,128)(2,1)S(1)}, u32[]{:S(2)}, u32[]{:S(2)}) collective-permute-start(bf16[352,512]{1,0:T(8,128)(2,1)S(1)} %copy-done.10), channel_id=1, source_target_pairs={{0,1},{1,2},{2,3},{3,0},{4,5},{5,6},{6,7},{7,4},{8,9},{9,10},{10,1... | collective-permute-start | bytes 1081352 | tf_op jit(solution)/shard_map/ppermute | solution.py:437
  269.9 4.8 %collective-permute-start.25 = (bf16[352,512]{1,0:T(8,128)(2,1)S(1)}, bf16[352,512]{1,0:T(8,128)(2,1)S(1)}, u32[]{:S(2)}, u32[]{:S(2)}) collective-permute-start(bf16[352,512]{1,0:T(8,128)(2,1)S(1)} %copy-done.12), channel_id=1, source_target_pairs={{0,3},{1,0},{2,1},{3,2},{4,7},{5,4},{6,5},{7,6},{8,11},{9,8},{10,9... | collective-permute-start | bytes 1081352 | tf_op jit(solution)/shard_map/ppermute | solution.py:438
  274.7 7.3 %collective-permute-done.24 = bf16[352,512]{1,0:T(8,128)(2,1)S(1)} collective-permute-done((bf16[352,512]{1,0:T(8,128)(2,1)S(1)}, bf16[352,512]{1,0:T(8,128)(2,1)S(1)}, u32[]{:S(2)}, u32[]{:S(2)}) %collective-permute-start.24) | collective-permute-done | bytes 360480 | tf_op jit(solution)/shard_map/ppermute | solution.py:437
  282.1 10.1 %collective-permute-done.25 = bf16[352,512]{1,0:T(8,128)(2,1)S(1)} collective-permute-done((bf16[352,512]{1,0:T(8,128)(2,1)S(1)}, bf16[352,512]{1,0:T(8,128)(2,1)S(1)}, u32[]{:S(2)}, u32[]{:S(2)}) %collective-permute-start.25) | collective-permute-done | bytes 360480 | tf_op jit(solution)/shard_map/ppermute | solution.py:438
  292.1 21.3 %all-to-all-done = bf16[32,56,1024]{2,1,0:T(8,128)(2,1)} async-done(((bf16[32,56,1024]{2,1,0:T(8,128)(2,1)}), bf16[32,56,1024]{2,1,0:T(8,128)(2,1)}, u32[]{:S(2)}, u32[]{:S(2)}) %all-to-all-start) | async-done | bytes 3670048 | tf_op jit(solution)/shard_map/all_to_all | solution.py:439
  315.8 6.3 %collective-permute-done.26 = bf16[1792,1024]{1,0:T(8,128)(2,1)} collective-permute-done((bf16[1792,1024]{1,0:T(8,128)(2,1)}, bf16[1792,1024]{1,0:T(8,128)(2,1)}, u32[]{:S(2)}, u32[]{:S(2)}) %collective-permute-start.26) | collective-permute-done | bytes 3670048 | tf_op jit(solution)/shard_map/ppermute | solution.py:76
  322.1 3.9 fusion.17
  326.0 3.6 convolution_add_fusion
  329.5 3.4 fusion.2
  333.9 6.9 %all-to-all-start.1 = ((bf16[4,176,512]{2,1,0:T(8,128)(2,1)}), bf16[4,176,512]{2,1,0:T(8,128)(2,1)S(1)}, u32[]{:S(2)}, u32[]{:S(2)}) async-start(bf16[4,176,512]{2,1,0:T(8,128)(2,1)} %bitcast.136), calls=%async_computation.1 | async-start | bytes 1441792 | tf_op jit(solution)/shard_map/all_to_all | solution.py:449
  344.4 33.1 %all-to-all-done.1 = bf16[4,176,512]{2,1,0:T(8,128)(2,1)S(1)} async-done(((bf16[4,176,512]{2,1,0:T(8,128)(2,1)}), bf16[4,176,512]{2,1,0:T(8,128)(2,1)S(1)}, u32[]{:S(2)}, u32[]{:S(2)}) %all-to-all-start.1) | async-done | bytes 720928 | tf_op jit(solution)/shard_map/all_to_all | solution.py:449
  381.5 2.6 collective-permute-done.27
  386.1 4.5 all-to-all-start.2
  391.1 17.3 %all-to-all-done.2 = bf16[32,16,1024]{2,1,0:T(8,128)(2,1)S(1)} async-done(((bf16[32,16,1024]{2,1,0:T(8,128)(2,1)}), bf16[32,16,1024]{2,1,0:T(8,128)(2,1)S(1)}, u32[]{:S(2)}, u32[]{:S(2)}) %all-to-all-start.2) | async-done | bytes 1048608 | tf_op jit(solution)/shard_map/all_to_all | solution.py:467
  410.9 10.5 %collective-permute-start.29 = (bf16[128,512]{1,0:T(8,128)(2,1)S(1)}, bf16[128,512]{1,0:T(8,128)(2,1)S(1)}, u32[]{:S(2)}, u32[]{:S(2)}) collective-permute-start(bf16[128,512]{1,0:T(8,128)(2,1)S(1)} %get-tuple-element.97), channel_id=1, source_target_pairs={{0,256},{128,384},{256,0},{384,128},{1,257},{129,385},{257,1},{385... | collective-permute-start | bytes 393224 | tf_op jit(solution)/shard_map/ppermute | solution.py:478
  423.3 4.1 collective-permute-done.29
  427.4 2.9 collective-permute-done.28
  433.8 12.9 %collective-permute-done.31 = bf16[128,512]{1,0:T(8,128)(2,1)S(1)} collective-permute-done((bf16[128,512]{1,0:T(8,128)(2,1)S(1)}, bf16[128,512]{1,0:T(8,128)(2,1)S(1)}, u32[]{:S(2)}, u32[]{:S(2)}) %collective-permute-start.31) | collective-permute-done | bytes 131104 | tf_op jit(solution)/shard_map/ppermute | solution.py:480
  (135 shorter events, 65.2 us)
Async XLA Ops:
  40.5 9.3 %collective-permute-start.2 = (bf16[88,512]{1,0:T(8,128)(2,1)}, bf16[88,512]{1,0:T(8,128)(2,1)S(1)}, u32[]{:S(2)}, u32[]{:S(2)}) collective-permute-start(bf16[88,512]{1,0:T(8,128)(2,1)} %pick_rows.1), channel_id=1, source_target_pairs={{0,384},{128,0},{256,128},{384,256},{1,385},{129,1},{257,129},{385... | collective-permute-start | bytes 270344 | tf_op jit(solution)/shard_map/ppermute | solution.py:64
  44.1 7.6 %collective-permute-start.1 = (bf16[88,512]{1,0:T(8,128)(2,1)}, bf16[88,512]{1,0:T(8,128)(2,1)S(1)}, u32[]{:S(2)}, u32[]{:S(2)}) collective-permute-start(bf16[88,512]{1,0:T(8,128)(2,1)} %pick_rows.1), channel_id=1, source_target_pairs={{0,256},{128,384},{256,0},{384,128},{1,257},{129,385},{257,1},{385... | collective-permute-start | bytes 270344 | tf_op jit(solution)/shard_map/ppermute | solution.py:64
  47.8 6.6 %collective-permute-start = (bf16[88,512]{1,0:T(8,128)(2,1)}, bf16[88,512]{1,0:T(8,128)(2,1)S(1)}, u32[]{:S(2)}, u32[]{:S(2)}) collective-permute-start(bf16[88,512]{1,0:T(8,128)(2,1)} %pick_rows.1), channel_id=1, source_target_pairs={{0,128},{128,256},{256,384},{384,0},{1,129},{129,257},{257,385},{3... | collective-permute-start | bytes 270344 | tf_op jit(solution)/shard_map/ppermute | solution.py:64
  51.7 49.2 %copy-start.5 = (bf16[88,512]{1,0:T(8,128)(2,1)}, bf16[88,512]{1,0:T(8,128)(2,1)S(1)}, u32[]{:S(2)}) copy-start(bf16[88,512]{1,0:T(8,128)(2,1)S(1)} %collective-permute-done.1) | copy-start | bytes 270340
  54.5 46.4 %copy-start.7 = (bf16[88,512]{1,0:T(8,128)(2,1)}, bf16[88,512]{1,0:T(8,128)(2,1)S(1)}, u32[]{:S(2)}) copy-start(bf16[88,512]{1,0:T(8,128)(2,1)S(1)} %collective-permute-done) | copy-start | bytes 270340
  55.5 14.9 %collective-permute-start.5 = (bf16[4,72,512]{2,1,0:T(8,128)(2,1)S(1)}, bf16[4,72,512]{2,1,0:T(8,128)(2,1)S(1)}, u32[]{:S(2)}, u32[]{:S(2)}) collective-permute-start(bf16[4,72,512]{2,1,0:T(8,128)(2,1)S(1)} %get-tuple-element.109), channel_id=1, source_target_pairs={{0,96},{32,0},{64,32},{96,64},{1,97},{33,1},{65,33},{97,65},{2,98}... | collective-permute-start | bytes 884744 | tf_op jit(solution)/shard_map/ppermute | solution.py:64
  60.4 12.5 %collective-permute-start.4 = (bf16[4,72,512]{2,1,0:T(8,128)(2,1)S(1)}, bf16[4,72,512]{2,1,0:T(8,128)(2,1)S(1)}, u32[]{:S(2)}, u32[]{:S(2)}) collective-permute-start(bf16[4,72,512]{2,1,0:T(8,128)(2,1)S(1)} %get-tuple-element.109), channel_id=1, source_target_pairs={{0,64},{32,96},{64,0},{96,32},{1,65},{33,97},{65,1},{97,33},{2,66}... | collective-permute-start | bytes 884744 | tf_op jit(solution)/shard_map/ppermute | solution.py:64
  63.0 13.0 %collective-permute-start.3 = (bf16[4,72,512]{2,1,0:T(8,128)(2,1)S(1)}, bf16[4,72,512]{2,1,0:T(8,128)(2,1)S(1)}, u32[]{:S(2)}, u32[]{:S(2)}) collective-permute-start(bf16[4,72,512]{2,1,0:T(8,128)(2,1)S(1)} %get-tuple-element.109), channel_id=1, source_target_pairs={{0,32},{32,64},{64,96},{96,0},{1,33},{33,65},{65,97},{97,1},{2,34}... | collective-permute-start | bytes 884744 | tf_op jit(solution)/shard_map/ppermute | solution.py:64
  76.2 24.8 %copy-start.3 = (bf16[4,4,72,512]{3,2,1,0:T(8,128)(2,1)}, bf16[4,4,72,512]{3,2,1,0:T(8,128)(2,1)S(1)}, u32[]{:S(2)}) copy-start(bf16[4,4,72,512]{3,2,1,0:T(8,128)(2,1)S(1)} %pad_maximum_fusion.3) | copy-start | bytes 3538948
  76.2 24.7 %copy-start.4 = (bf16[88,512]{1,0:T(8,128)(2,1)S(1)}, bf16[88,512]{1,0:T(8,128)(2,1)}, u32[]{:S(2)}) copy-start(bf16[88,512]{1,0:T(8,128)(2,1)} %pick_rows.1) | copy-start | bytes 270340
  76.2 24.7 %copy-start.2 = (bf16[1,704,512]{2,1,0:T(8,128)(2,1)S(1)}, bf16[1,704,512]{2,1,0:T(8,128)(2,1)}, u32[]{:S(2)}) copy-start(bf16[1,704,512]{2,1,0:T(8,128)(2,1)} %param.27) | copy-start | bytes 2162692
  76.3 17.0 %collective-permute-start.8 = (bf16[16,40,512]{2,1,0:T(8,128)(2,1)S(1)}, bf16[16,40,512]{2,1,0:T(8,128)(2,1)S(1)}, u32[]{:S(2)}, u32[]{:S(2)}) collective-permute-start(bf16[16,40,512]{2,1,0:T(8,128)(2,1)S(1)} %get-tuple-element.94), channel_id=1, source_target_pairs={{0,24},{8,0},{16,8},{24,16},{1,25},{9,1},{17,9},{25,17},{2,26},{10... | collective-permute-start | bytes 1966088 | tf_op jit(solution)/shard_map/ppermute | solution.py:70
  81.1 17.8 %collective-permute-start.6 = (bf16[16,40,512]{2,1,0:T(8,128)(2,1)S(1)}, bf16[16,40,512]{2,1,0:T(8,128)(2,1)S(1)}, u32[]{:S(2)}, u32[]{:S(2)}) collective-permute-start(bf16[16,40,512]{2,1,0:T(8,128)(2,1)S(1)} %get-tuple-element.94), channel_id=1, source_target_pairs={{0,8},{8,16},{16,24},{24,0},{1,9},{9,17},{17,25},{25,1},{2,10},{10... | collective-permute-start | bytes 1966088 | tf_op jit(solution)/shard_map/ppermute | solution.py:70
  93.3 17.5 %collective-permute-start.9 = (bf16[8,40,512]{2,1,0:T(8,128)(2,1)S(1)}, bf16[8,40,512]{2,1,0:T(8,128)(2,1)S(1)}, u32[]{:S(2)}, u32[]{:S(2)}) collective-permute-start(bf16[8,40,512]{2,1,0:T(8,128)(2,1)S(1)} %slice.204), channel_id=1, source_target_pairs={{0,24},{8,0},{16,8},{24,16},{1,25},{9,1},{17,9},{25,17},{2,26},{10... | collective-permute-start | bytes 983048 | tf_op jit(solution)/shard_map/ppermute | solution.py:71
  99.0 11.8 %collective-permute-start.7 = (bf16[8,40,512]{2,1,0:T(8,128)(2,1)S(1)}, bf16[8,40,512]{2,1,0:T(8,128)(2,1)S(1)}, u32[]{:S(2)}, u32[]{:S(2)}) collective-permute-start(bf16[8,40,512]{2,1,0:T(8,128)(2,1)S(1)} %slice.203), channel_id=1, source_target_pairs={{0,8},{8,16},{16,24},{24,0},{1,9},{9,17},{17,25},{25,1},{2,10},{10... | collective-permute-start | bytes 983048 | tf_op jit(solution)/shard_map/ppermute | solution.py:71
  101.0 25.0 %collective-permute-start.10 = (bf16[352,512]{1,0:T(8,128)(2,1)S(1)}, bf16[352,512]{1,0:T(8,128)(2,1)S(1)}, u32[]{:S(2)}, u32[]{:S(2)}) collective-permute-start(bf16[352,512]{1,0:T(8,128)(2,1)S(1)} %get-tuple-element.103), channel_id=1, source_target_pairs={{0,1},{1,2},{2,3},{3,0},{4,5},{5,6},{6,7},{7,4},{8,9},{9,10},{10,1... | collective-permute-start | bytes 1081352 | tf_op jit(solution)/shard_map/ppermute | solution.py:328
  105.4 21.7 %collective-permute-start.11 = (bf16[352,512]{1,0:T(8,128)(2,1)S(1)}, bf16[352,512]{1,0:T(8,128)(2,1)S(1)}, u32[]{:S(2)}, u32[]{:S(2)}) collective-permute-start(bf16[352,512]{1,0:T(8,128)(2,1)S(1)} %get-tuple-element.102), channel_id=1, source_target_pairs={{0,3},{1,0},{2,1},{3,2},{4,7},{5,4},{6,5},{7,6},{8,11},{9,8},{10,9... | collective-permute-start | bytes 1081352 | tf_op jit(solution)/shard_map/ppermute | solution.py:329
  110.9 18.9 %copy-start.20 = (s32[1,4]{1,0:T(1,128)S(1)}, s32[1,4]{1,0:T(1,128)}, u32[]{:S(2)}) copy-start(s32[1,4]{1,0:T(1,128)} %param.15) | copy-start | bytes 52
  111.2 42.9 %copy-start = (bf16[4,16,40,512]{3,2,1,0:T(8,128)(2,1)}, bf16[4,16,40,512]{3,2,1,0:T(8,128)(2,1)S(1)}, u32[]{:S(2)}) copy-start(bf16[4,16,40,512]{3,2,1,0:T(8,128)(2,1)S(1)} %pad_maximum_fusion.1) | copy-start | bytes 7864324
  127.9 6.9 %collective-permute-start.12 = (bf16[64,40,512]{2,1,0:T(8,128)(2,1)S(1)}, bf16[64,40,512]{2,1,0:T(8,128)(2,1)}, u32[]{:S(2)}, u32[]{:S(2)}) collective-permute-start(bf16[64,40,512]{2,1,0:T(8,128)(2,1)S(1)} %bitcast.137), channel_id=1, source_target_pairs={{0,4},{4,0},{1,5},{5,1},{2,6},{6,2},{3,7},{7,3},{8,12},{12,8},{9,1... | collective-permute-start | bytes 7864328 | tf_op jit(solution)/shard_map/ppermute | solution.py:76
  134.8 26.4 %collective-permute-start.13 = (bf16[16,32,512]{2,1,0:T(8,128)(2,1)}, bf16[16,32,512]{2,1,0:T(8,128)(2,1)}, u32[]{:S(2)}, u32[]{:S(2)}) collective-permute-start(bf16[16,32,512]{2,1,0:T(8,128)(2,1)} %slice.201), channel_id=1, source_target_pairs={{0,8},{8,16},{16,24},{24,0},{1,9},{9,17},{17,25},{25,1},{2,10},{10... | collective-permute-start | bytes 1572872 | tf_op jit(solution)/shard_map/ppermute | solution.py:340
  136.7 24.5 %collective-permute-start.14 = (bf16[16,32,512]{2,1,0:T(8,128)(2,1)}, bf16[16,32,512]{2,1,0:T(8,128)(2,1)}, u32[]{:S(2)}, u32[]{:S(2)}) collective-permute-start(bf16[16,32,512]{2,1,0:T(8,128)(2,1)} %slice.201), channel_id=1, source_target_pairs={{0,24},{8,0},{16,8},{24,16},{1,25},{9,1},{17,9},{25,17},{2,26},{10... | collective-permute-start | bytes 1572872 | tf_op jit(solution)/shard_map/ppermute | solution.py:341
  143.6 26.7 %collective-permute-start.17 = (bf16[352,512]{1,0:T(8,128)(2,1)}, bf16[352,512]{1,0:T(8,128)(2,1)}, u32[]{:S(2)}, u32[]{:S(2)}) collective-permute-start(bf16[352,512]{1,0:T(8,128)(2,1)} %get-tuple-element.101), channel_id=1, source_target_pairs={{0,1},{1,2},{2,3},{3,0},{4,5},{5,6},{6,7},{7,4},{8,9},{9,10},{10,1... | collective-permute-start | bytes 1081352 | tf_op jit(solution)/shard_map/ppermute | solution.py:337
  150.5 19.8 %collective-permute-start.18 = (bf16[352,512]{1,0:T(8,128)(2,1)}, bf16[352,512]{1,0:T(8,128)(2,1)}, u32[]{:S(2)}, u32[]{:S(2)}) collective-permute-start(bf16[352,512]{1,0:T(8,128)(2,1)} %get-tuple-element.100), channel_id=1, source_target_pairs={{0,3},{1,0},{2,1},{3,2},{4,7},{5,4},{6,5},{7,6},{8,11},{9,8},{10,9... | collective-permute-start | bytes 1081352 | tf_op jit(solution)/shard_map/ppermute | solution.py:338
  162.2 39.5 %collective-permute-start.15 = (bf16[8,32,512]{2,1,0:T(8,128)(2,1)S(1)}, bf16[8,32,512]{2,1,0:T(8,128)(2,1)S(1)}, u32[]{:S(2)}, u32[]{:S(2)}) collective-permute-start(bf16[8,32,512]{2,1,0:T(8,128)(2,1)S(1)} %slice.161), channel_id=1, source_target_pairs={{0,8},{8,16},{16,24},{24,0},{1,9},{9,17},{17,25},{25,1},{2,10},{10... | collective-permute-start | bytes 786440 | tf_op jit(solution)/shard_map/ppermute | solution.py:366
  165.1 36.6 %collective-permute-start.16 = (bf16[8,32,512]{2,1,0:T(8,128)(2,1)S(1)}, bf16[8,32,512]{2,1,0:T(8,128)(2,1)S(1)}, u32[]{:S(2)}, u32[]{:S(2)}) collective-permute-start(bf16[8,32,512]{2,1,0:T(8,128)(2,1)S(1)} %slice.162), channel_id=1, source_target_pairs={{0,24},{8,0},{16,8},{24,16},{1,25},{9,1},{17,9},{25,17},{2,26},{10... | collective-permute-start | bytes 786440 | tf_op jit(solution)/shard_map/ppermute | solution.py:367
  203.4 6.2 %collective-permute-start.19 = (bf16[64,32,512]{2,1,0:T(8,128)(2,1)S(1)}, bf16[64,32,512]{2,1,0:T(8,128)(2,1)}, u32[]{:S(2)}, u32[]{:S(2)}) collective-permute-start(bf16[64,32,512]{2,1,0:T(8,128)(2,1)S(1)} %bitcast.139), channel_id=1, source_target_pairs={{0,4},{4,0},{1,5},{5,1},{2,6},{6,2},{3,7},{7,3},{8,12},{12,8},{9,1... | collective-permute-start | bytes 6291464 | tf_op jit(solution)/shard_map/ppermute | solution.py:76
  209.6 16.2 %copy-start.8 = (bf16[88,512]{1,0:T(8,128)(2,1)S(1)}, bf16[88,512]{1,0:T(8,128)(2,1)}, u32[]{:S(2)}) copy-start(bf16[88,512]{1,0:T(8,128)(2,1)} %copy-done.7) | copy-start | bytes 270340
  217.1 37.6 %copy-start.14 = (bf16[128,1024]{1,0:T(8,128)(2,1)S(1)}, bf16[128,1024]{1,0:T(8,128)(2,1)}, u32[]{:S(2)}) copy-start(bf16[128,1024]{1,0:T(8,128)(2,1)} %get-tuple-element.51) | copy-start | bytes 786436
  217.1 24.4 %collective-permute-start.22 = (bf16[256,1024]{1,0:T(8,128)(2,1)}, bf16[256,1024]{1,0:T(8,128)(2,1)S(1)}, u32[]{:S(2)}, u32[]{:S(2)}) collective-permute-start(bf16[256,1024]{1,0:T(8,128)(2,1)} %get-tuple-element.50), channel_id=1, source_target_pairs={{0,387},{128,0},{256,128},{384,256},{1,384},{129,1},{257,129},{385... | collective-permute-start | bytes 1572872 | tf_op jit(solution)/shard_map/ppermute | solution.py:422
  226.0 20.3 %collective-permute-start.20 = (bf16[256,1024]{1,0:T(8,128)(2,1)}, bf16[256,1024]{1,0:T(8,128)(2,1)S(1)}, u32[]{:S(2)}, u32[]{:S(2)}) collective-permute-start(bf16[256,1024]{1,0:T(8,128)(2,1)} %get-tuple-element.50), channel_id=1, source_target_pairs={{0,128},{128,256},{256,384},{384,1},{1,129},{129,257},{257,385},{3... | collective-permute-start | bytes 1572872 | tf_op jit(solution)/shard_map/ppermute | solution.py:421
  232.0 22.6 %collective-permute-start.23 = (bf16[128,1024]{1,0:T(8,128)(2,1)}, bf16[128,1024]{1,0:T(8,128)(2,1)S(1)}, u32[]{:S(2)}, u32[]{:S(2)}) collective-permute-start(bf16[128,1024]{1,0:T(8,128)(2,1)} %get-tuple-element.51), channel_id=1, source_target_pairs={{0,259},{128,387},{256,0},{384,128},{1,256},{129,384},{257,1},{385... | collective-permute-start | bytes 786440 | tf_op jit(solution)/shard_map/ppermute | solution.py:424
  237.1 18.6 %copy-start.13 = (bf16[128,1024]{1,0:T(8,128)(2,1)S(1)}, bf16[128,1024]{1,0:T(8,128)(2,1)}, u32[]{:S(2)}) copy-start(bf16[128,1024]{1,0:T(8,128)(2,1)} %get-tuple-element.49) | copy-start | bytes 786436
  237.1 18.5 %collective-permute-start.21 = (bf16[128,1024]{1,0:T(8,128)(2,1)}, bf16[128,1024]{1,0:T(8,128)(2,1)S(1)}, u32[]{:S(2)}, u32[]{:S(2)}) collective-permute-start(bf16[128,1024]{1,0:T(8,128)(2,1)} %get-tuple-element.49), channel_id=1, source_target_pairs={{0,256},{128,384},{256,1},{384,129},{1,257},{129,385},{257,2},{385... | collective-permute-start | bytes 786440 | tf_op jit(solution)/shard_map/ppermute | solution.py:423
  259.6 53.9 %all-to-all-start = ((bf16[32,56,1024]{2,1,0:T(8,128)(2,1)}), bf16[32,56,1024]{2,1,0:T(8,128)(2,1)}, u32[]{:S(2)}, u32[]{:S(2)}) async-start(bf16[32,56,1024]{2,1,0:T(8,128)(2,1)} %bitcast.146), calls=%async_computation | async-start | bytes 7340032 | tf_op jit(solution)/shard_map/all_to_all | solution.py:439
  265.0 17.1 %collective-permute-start.24 = (bf16[352,512]{1,0:T(8,128)(2,1)S(1)}, bf16[352,512]{1,0:T(8,128)(2,1)S(1)}, u32[]{:S(2)}, u32[]{:S(2)}) collective-permute-start(bf16[352,512]{1,0:T(8,128)(2,1)S(1)} %copy-done.10), channel_id=1, source_target_pairs={{0,1},{1,2},{2,3},{3,0},{4,5},{5,6},{6,7},{7,4},{8,9},{9,10},{10,1... | collective-permute-start | bytes 1081352 | tf_op jit(solution)/shard_map/ppermute | solution.py:437
  269.9 22.2 %collective-permute-start.25 = (bf16[352,512]{1,0:T(8,128)(2,1)S(1)}, bf16[352,512]{1,0:T(8,128)(2,1)S(1)}, u32[]{:S(2)}, u32[]{:S(2)}) collective-permute-start(bf16[352,512]{1,0:T(8,128)(2,1)S(1)} %copy-done.12), channel_id=1, source_target_pairs={{0,3},{1,0},{2,1},{3,2},{4,7},{5,4},{6,5},{7,6},{8,11},{9,8},{10,9... | collective-permute-start | bytes 1081352 | tf_op jit(solution)/shard_map/ppermute | solution.py:438
  313.4 8.6 %collective-permute-start.26 = (bf16[1792,1024]{1,0:T(8,128)(2,1)}, bf16[1792,1024]{1,0:T(8,128)(2,1)}, u32[]{:S(2)}, u32[]{:S(2)}) collective-permute-start(bf16[1792,1024]{1,0:T(8,128)(2,1)} %bitcast.68), channel_id=1, source_target_pairs={{0,4},{4,0},{1,5},{5,1},{2,6},{6,2},{3,7},{7,3},{8,12},{12,8},{9,1... | collective-permute-start | bytes 11010056 | tf_op jit(solution)/shard_map/ppermute | solution.py:76
  333.9 43.5 %all-to-all-start.1 = ((bf16[4,176,512]{2,1,0:T(8,128)(2,1)}), bf16[4,176,512]{2,1,0:T(8,128)(2,1)S(1)}, u32[]{:S(2)}, u32[]{:S(2)}) async-start(bf16[4,176,512]{2,1,0:T(8,128)(2,1)} %bitcast.136), calls=%async_computation.1 | async-start | bytes 1441792 | tf_op jit(solution)/shard_map/all_to_all | solution.py:449
  379.6 4.6 %collective-permute-start.27 = (bf16[512,1024]{1,0:T(8,128)(2,1)S(1)}, bf16[512,1024]{1,0:T(8,128)(2,1)S(1)}, u32[]{:S(2)}, u32[]{:S(2)}) collective-permute-start(bf16[512,1024]{1,0:T(8,128)(2,1)S(1)} %convolution_convert_fusion.1), channel_id=1, source_target_pairs={{0,4},{4,0},{1,5},{5,1},{2,6},{6,2},{3,7},{7,3},{8,12},{12,8},{9,1... | collective-permute-start | bytes 3145736 | tf_op jit(solution)/shard_map/ppermute | solution.py:76
  386.1 22.2 %all-to-all-start.2 = ((bf16[32,16,1024]{2,1,0:T(8,128)(2,1)}), bf16[32,16,1024]{2,1,0:T(8,128)(2,1)S(1)}, u32[]{:S(2)}, u32[]{:S(2)}) async-start(bf16[32,16,1024]{2,1,0:T(8,128)(2,1)} %bitcast.79), calls=%async_computation.2 | async-start | bytes 2097152 | tf_op jit(solution)/shard_map/all_to_all | solution.py:467
  408.8 24.1 %copy-start.17 = (bf16[128,128]{1,0:T(8,128)(2,1)S(1)}, bf16[128,128]{1,0:T(8,128)(2,1)}, u32[]{:S(2)}) copy-start(bf16[128,128]{1,0:T(8,128)(2,1)} %get-tuple-element.63) | copy-start | bytes 98308
  408.8 24.2 %copy-start.16 = (bf16[128,512]{1,0:T(8,128)(2,1)S(1)}, bf16[128,512]{1,0:T(8,128)(2,1)}, u32[]{:S(2)}) copy-start(bf16[128,512]{1,0:T(8,128)(2,1)} %get-tuple-element.62) | copy-start | bytes 393220
  408.8 37.9 %copy-start.15 = (bf16[128,512]{1,0:T(8,128)(2,1)S(1)}, bf16[128,512]{1,0:T(8,128)(2,1)}, u32[]{:S(2)}) copy-start(bf16[128,512]{1,0:T(8,128)(2,1)} %get-tuple-element.46) | copy-start | bytes 393220
  409.0 14.4 %collective-permute-start.30 = (bf16[128,512]{1,0:T(8,128)(2,1)S(1)}, bf16[128,512]{1,0:T(8,128)(2,1)S(1)}, u32[]{:S(2)}, u32[]{:S(2)}) collective-permute-start(bf16[128,512]{1,0:T(8,128)(2,1)S(1)} %get-tuple-element.96), channel_id=1, source_target_pairs={{0,384},{128,0},{256,128},{384,256},{1,385},{129,1},{257,129},{385... | collective-permute-start | bytes 393224 | tf_op jit(solution)/shard_map/ppermute | solution.py:478
  410.9 16.6 %collective-permute-start.29 = (bf16[128,512]{1,0:T(8,128)(2,1)S(1)}, bf16[128,512]{1,0:T(8,128)(2,1)S(1)}, u32[]{:S(2)}, u32[]{:S(2)}) collective-permute-start(bf16[128,512]{1,0:T(8,128)(2,1)S(1)} %get-tuple-element.97), channel_id=1, source_target_pairs={{0,256},{128,384},{256,0},{384,128},{1,257},{129,385},{257,1},{385... | collective-permute-start | bytes 393224 | tf_op jit(solution)/shard_map/ppermute | solution.py:478
  421.4 8.9 %collective-permute-start.28 = (bf16[128,512]{1,0:T(8,128)(2,1)S(1)}, bf16[128,512]{1,0:T(8,128)(2,1)S(1)}, u32[]{:S(2)}, u32[]{:S(2)}) collective-permute-start(bf16[128,512]{1,0:T(8,128)(2,1)S(1)} %get-tuple-element.95), channel_id=1, source_target_pairs={{0,128},{128,256},{256,384},{384,0},{1,129},{129,257},{257,385},{3... | collective-permute-start | bytes 393224 | tf_op jit(solution)/shard_map/ppermute | solution.py:478
  430.4 16.4 %collective-permute-start.31 = (bf16[128,512]{1,0:T(8,128)(2,1)S(1)}, bf16[128,512]{1,0:T(8,128)(2,1)S(1)}, u32[]{:S(2)}, u32[]{:S(2)}) collective-permute-start(bf16[128,512]{1,0:T(8,128)(2,1)S(1)} %fusion.24), channel_id=1, source_target_pairs={{0,0},{1,128},{2,256},{3,384},{128,1},{129,129},{130,257},{131,385... | collective-permute-start | bytes 393224 | tf_op jit(solution)/shard_map/ppermute | solution.py:480
  (8 other events, 47.8 us)

commit v6 on v4

--- a/solution.py
+++ b/solution.py
@@ -81,9 +81,8 @@
 NT = (((1,), (1,)), ((), ()))
 
 
-def pack_rows(hidden_in, query, latent, expand, output):
-    def kernel(hidden_ref, q_ref, l_ref, e_ref, o_ref, out_ref, rows):
-        out_ref[0:128, :] = hidden_ref[...]
+def pack_rows(query, latent, expand, output, routes, gates):
+    def kernel(q_ref, l_ref, e_ref, o_ref, routes_ref, gates_ref, out_ref, rows):
         tail_a, tail_b = l_ref[:, 512:544], l_ref[:, 544:576]
         tail = [tail_a, tail_a, tail_b, tail_b]
         for t in range(4):
@@ -97,20 +96,23 @@
         rows[16:20, :] = l_ref[:, 0:512]
         rows[24:28, :] = o_ref[:, 0:512]
         rows[28:32, :] = o_ref[:, 512:1024]
-        out_ref[128:160, :] = rows[...].astype(BF)
+        rows[32:48, :] = jnp.zeros((16, 512), F32)
+        rows[32:38, 0:128] = routes_ref[...].astype(F32)
+        rows[40:46, 0:128] = gates_ref[...].astype(F32)
+        out_ref[...] = rows[...].astype(BF)
 
     return pl.pallas_call(
         kernel,
-        out_shape=jax.ShapeDtypeStruct((160, 512), BF),
-        in_specs=[VMEM] * 5,
+        out_shape=jax.ShapeDtypeStruct((48, 512), BF),
+        in_specs=[VMEM] * 6,
         out_specs=VMEM,
-        scratch_shapes=[pltpu.VMEM((32, 512), F32)],
+        scratch_shapes=[pltpu.VMEM((48, 512), F32)],
         name="pack_rows",
-    )(hidden_in, query, latent, expand, output)
-
-
-def pick_rows(place, everything, routes, gates):
-    def kernel(place_ref, in_ref, routes_ref, gates_ref, out_ref, wide, rows):
+    )(query, latent, expand, output, routes.T, gates.T)
+
+
+def pick_rows(place, everything):
+    def kernel(place_ref, in_ref, out_ref, wide, rows):
         t = place_ref[4]
         wide[...] = in_ref[...].astype(F32)
         for s in range(4):
@@ -126,31 +128,30 @@
             rows[36 + s : 37 + s, :] = e
             rows[40 + s * 4 : 44 + s * 4, :] = wide[24:28, lanes]
             rows[56 + s * 4 : 60 + s * 4, :] = wide[28:32, lanes]
-        rows[72:88, :] = jnp.zeros((16, 512), F32)
-        rows[72:78, 0:128] = routes_ref[...].astype(F32)
-        rows[80:86, 0:128] = gates_ref[...].astype(F32)
-        out_ref[...] = rows[...].astype(BF)
-
-    def small(rows):
-        return pl.BlockSpec((rows, 128), lambda i: (0, 0))
+        out_ref[0] = rows[...].astype(BF)
 
     return pl.pallas_call(
         kernel,
-        grid=(1,),
-        out_shape=jax.ShapeDtypeStruct((88, 512), BF),
-        in_specs=[SMEM, pl.BlockSpec((32, 2048), lambda i: (4, 0)), small(6), small(6)],
-        out_specs=pl.BlockSpec((88, 512), lambda i: (0, 0)),
-        scratch_shapes=[pltpu.VMEM((32, 2048), F32), pltpu.VMEM((88, 512), F32)],
+        grid=(4,),
+        out_shape=jax.ShapeDtypeStruct((4, 72, 512), BF),
+        in_specs=[SMEM, pl.BlockSpec((32, 2048), lambda i: (0, i))],
+        out_specs=pl.BlockSpec((1, 72, 512), lambda i: (i, 0, 0)),
+        scratch_shapes=[pltpu.VMEM((32, 2048), F32), pltpu.VMEM((72, 512), F32)],
         name="pick_rows",
-    )(place, everything, routes.T, gates.T)
+    )(place, everything)
+
+
+def residual(place_ref, parts_ref):
+    t = place_ref[4]
+    return jnp.concatenate([parts_ref[(t - q + 4) % 4] for q in range(4)], axis=1).astype(F32)
 
 
 def in_order(place_ref, visit):
-    zl, y, x = place_ref[0], place_ref[1], place_ref[2]
+    y, x = place_ref[1], place_ref[2]
 
     def source_of(i):
         row_zl, row_y, row_x = i // 16, (i // 4) % 4, i % 4
-        return ((x - row_x + 4) % 4 * 4 + (y - row_y + 4) % 4) * 4 + (zl - row_zl + 4) % 4
+        return ((x - row_x + 4) % 4 * 4 + (y - row_y + 4) % 4) * 4 + row_zl
 
     def step(j, carry):
         visit(j, (source_of(2 * j), source_of(2 * j + 1)))
@@ -183,7 +184,7 @@
             expand_ref[pl.ds(row, 16), :] = jnp.concatenate(pair, axis=0).astype(BF)
 
         in_order(place_ref, visit)
-        normed = rms_norm(in_ref[...].astype(F32), norm_ref[...]).astype(BF)
+        normed = rms_norm(residual(place_ref, in_ref), norm_ref[...]).astype(BF)
         query = jnp.dot(normed, q_rows[...], preferred_element_type=F32)
         latent = jnp.dot(normed, l_rows[...], preferred_element_type=F32).astype(BF)
         latent = rms_norm(latent.astype(F32), gain_ref[...]).astype(BF)
@@ -229,7 +230,7 @@
             jax.ShapeDtypeStruct((512, 512), BF),
         ],
         in_specs=[
-            SMEM, whole(128, 2048), VMEM, VMEM,
+            SMEM, whole(4, 128, 512), VMEM, VMEM,
             whole(1, 2048), whole(1, 512), whole(128, 128), whole(128, 128), whole(128, 128),
         ],
         out_specs=[whole(128, 256), whole(128, 512), whole(128, 128), whole(512, 512)],
@@ -265,7 +266,7 @@
         ) + lax.dot_general(
             attended_ref[:, 512:1024], w_second[...], NT, preferred_element_type=F32
         )
-        mixed = (in_ref[...].astype(F32) + total).astype(BF).astype(F32)
+        mixed = (residual(place_ref, in_ref) + total).astype(BF).astype(F32)
         cols = mixed[:, 0:512]
         for k in range(1, 4):
             cols = jnp.where(t == k, mixed[:, k * 512 : (k + 1) * 512], cols)
@@ -285,7 +286,7 @@
             jax.ShapeDtypeStruct((128, 512), BF),
             jax.ShapeDtypeStruct((2048, 256), BF),
         ],
-        in_specs=[SMEM, whole(128, 2048), whole(128, 1024), VMEM, VMEM, whole(1, 2048)],
+        in_specs=[SMEM, whole(4, 128, 512), whole(128, 1024), VMEM, VMEM, whole(1, 2048)],
         out_specs=[whole(256, 1024), whole(128, 512), whole(2048, 256)],
         scratch_shapes=[pltpu.VMEM((2048, 512), BF), pltpu.VMEM((2048, 512), BF)],
         name="mix",
@@ -312,17 +313,27 @@
     core = lax.axis_index("c")
     place = jnp.stack([lax.axis_index(a) for a in DP + (T,)]).astype(jnp.int32)
 
-    packed = pack_rows(hidden_in, query_train, latent_train, expand_train, output_train)
-    everything = lax.all_gather(packed, T, axis=1, tiled=True)
-    rows = pick_rows(place, everything, routes, gate_weights)
-    gathered = jnp.stack(shifted(rows, "zl"))
-    column_routes = gathered[:, 72:78, 0:128].astype(jnp.int32)
-    column_gates = gathered[:, 80:86, 0:128].astype(F32)
-    gathered = jnp.stack(shifted(gathered[:, :72], "y")).reshape(16, 72, 512)
+    packed = pack_rows(
+        query_train, latent_train, expand_train, output_train, routes, gate_weights
+    )
+    everything = lax.all_gather(packed, ("zl", T), axis=1, tiled=True)
+    picked = pick_rows(place, everything)
+    meta = everything[32:48].reshape(16, 4, 2048)[:, :, 0:128].transpose(1, 0, 2)
+    at_zl = lax.axis_index("zl")
+    meta = jnp.stack(
+        [lax.dynamic_index_in_dim(meta, (at_zl - s + 4) % 4, 0, keepdims=False) for s in range(4)]
+    )
+    column_routes = meta[:, 0:6].astype(jnp.int32)
+    column_gates = meta[:, 8:14].astype(F32)
+    gathered = jnp.stack(shifted(picked, "y")).reshape(16, 72, 512)
+    hidden_gated, _ = lax.optimization_barrier((hidden_in, picked))
+    hidden_parts = shifted(hidden_gated, T)
+    gathered, *hidden_parts = lax.optimization_barrier((gathered, *hidden_parts))
+    hidden_parts = jnp.stack(hidden_parts)
     first_set = gathered[:, :40]
     first_mine = jnp.stack(ring(first_set, "x")).reshape(64, 40, 512)
     first_theirs = other_core(first_mine)
-    second_set, _ = lax.optimization_barrier((gathered[:, 40:], first_mine))
+    second_set, _ = lax.optimization_barrier((gathered[:, 40:], first_theirs))
     second_below = lax.ppermute(second_set, "x", UP)
     second_above = lax.ppermute(second_set, "x", DOWN)
 
@@ -335,7 +346,7 @@
     allowed = (segment[:, None] == segment[None, :]) & (token_index[None, :] <= token_index[:, None])
     attended, latent_normed, key_rope, expand_block = attention(
         place,
-        everything,
+        hidden_parts,
         first_mine,
         first_theirs,
         norm_gain,
@@ -346,21 +357,25 @@
     )
     cache_full = jnp.concatenate([latent_normed, key_rope[:, 0:32], key_rope[:, 64:96]], axis=1)
     cache_cols = lax.dynamic_slice_in_dim(cache_full, rank * 144, 144, 1)
-    below_part, above_part, attended = lax.optimization_barrier(
-        (second_below[:8], second_above[8:], attended)
-    )
-    second_far = jnp.concatenate(
-        [lax.ppermute(below_part, "x", UP), lax.ppermute(above_part, "x", DOWN)]
-    )
+    second_below, second_above, attended = lax.optimization_barrier(
+        (second_below, second_above, attended)
+    )
+    far_first = lax.ppermute(second_below[:8], "x", UP)
+    far_second = lax.ppermute(second_above[8:], "x", DOWN)
     attended_full = lax.all_gather(attended, T, axis=1, tiled=True)
-    second_mine = jnp.stack([second_set, second_below, second_far, second_above]).reshape(64, 32, 512)
+    far_first, far_second, attended_full = lax.optimization_barrier(
+        (far_first, far_second, attended_full)
+    )
+    second_mine = jnp.stack(
+        [second_set, second_below, jnp.concatenate([far_first, far_second]), second_above]
+    ).reshape(64, 32, 512)
     second_theirs = other_core(second_mine)
     moe_halves, mixed_cols, output_block = mix(
-        place, everything, attended_full, second_mine, second_theirs, moe_gain
+        place, hidden_parts, attended_full, second_mine, second_theirs, moe_gain
     )
 
     slot_rank = expert_ranks(column_routes)
-    local = column_routes - lax.axis_index("zl") * 16
+    local = column_routes - at_zl * 16
     group = jnp.arange(4, dtype=jnp.int32)[:, None, None]
     target = jnp.where(
         (local >= 0) & (local < 16), local * (4 * CAP) + group * CAP + slot_rank, -1

time: 435 us -> 477 us (1.097)
  blocking collectives: 106 us -> 137 us
  waiting for transfers between devices: 151 us -> 161 us
  starting transfers between devices: 113 us -> 106 us
  local copies, waits for them, and re-layouts: 10.9 us -> 15.7 us
    all_gather x1, blocking collectives: 35.8 us -> 70.4 us  [body(): everything = lax.all_gather(packed, ('zl', T), axis=1, tiled=True)]
    ppermute x6, waiting for transfers between devices: 13.1 us -> 22.7 us  [shifted(): lax.ppermute(block, axis, [(j, (j + s) % 4) for j in range(4)])]
    ppermute x1, waiting for transfers between devices: 8.28 us -> 0.01 us  [body(): second_below = lax.ppermute(second_set, 'x', UP)]
    ppermute x2, waiting for transfers between devices: 7.78 us -> 0.01 us  [the longest x1 0.01 us: body(): far_first = lax.ppermute(second_below[:8], 'x', UP)]
    ppermute x1, waiting for transfers between devices: 5.58 us -> 11.7 us  [ring(): lax.ppermute(block, axis, DOWN)]
    ppermute x4, waiting for transfers between devices: 2.42 us -> 8.21 us  [other_core(): return lax.ppermute(block, 'c', [(0, 1), (1, 0)])]
    ppermute x1, waiting for transfers between devices: 12.5 us -> 17.6 us  [body(): far_second = lax.ppermute(above[88:], T, DOWN)]
    ppermute x1, starting transfers between devices: 6.71 us -> 1.91 us  [body(): on_one = lax.ppermute(moe_halves, ('zl', T), z_down)]
  transfers between devices with their start and end apart: 30 -> 30, of which waited for: 21 -> 19; matrix products, arithmetic and copies ran while one was open for 4% -> 5% of each run, Pallas kernels for 0% -> 1%
where the time goes in v6:
time: 477 us; the launch traced here: 474 us
  waiting for transfers between devices  161 us (34%)
  blocking collectives  137 us (29%)
  starting transfers between devices  106 us (22%)
  matrix products  20.2 us (4%)
  Pallas kernels  18.8 us (4%)
  local copies, waits for them, and re-layouts  15.7 us (3%)
  other arithmetic  14.2 us (3%)
    all_gather x1, blocking collectives, body(): everything = lax.all_gather(packed, ('zl', T), axis=1, tiled=True)  70.4 us
    ppermute x1, waiting for transfers between devices, body(): above = lax.ppermute(own, T, DOWN)  52 us
    all_to_all x1, blocking collectives, body(): lax.all_to_all(outgoing.reshape(2 * LAYER_ROWS, D // 2), LAYER, split_axi...  50.6 us
    ppermute x6, waiting for transfers between devices, shifted(): lax.ppermute(block, axis, [(j, (j + s) % 4) for j in range(4)])  22.7 us
    ppermute x6, starting transfers between devices, shifted(): lax.ppermute(block, axis, [(j, (j + s) % 4) for j in range(4)])  20.6 us
    ppermute x1, waiting for transfers between devices, body(): far_second = lax.ppermute(above[88:], T, DOWN)  17.6 us
    ppermute x4, starting transfers between devices, other_core(): return lax.ppermute(block, 'c', [(0, 1), (1, 0)])  17.1 us
    all_gather x1, blocking collectives, body(): attended_full = lax.all_gather(attended, T, axis=1, tiled=True)  16.1 us
  transfers between devices with their start and end apart: 30, of which 19 were waited for; matrix products, arithmetic and copies ran while one was open for 5% of the time, Pallas kernels for 1%

profile of v6, /device:TPU:1, one launch (start us, length us, event | category | flops | bytes accessed | tf_op | source)
XLA Modules:
  0.0 474.2 jit_solution(8250672132387247886)
XLA Ops:
  2.3 70.4 %all_gather.6.in_ref = bf16[48,8192]{1,0:T(8,128)(2,1)} all-gather(bf16[48,512]{1,0:T(8,128)(2,1)} %pack_rows.1), channel_id=1, replica_groups=mesh['zl'=4,'y'=4,'x'=4,'c'=2,'t'=4] {'zl','t'}, dimensions={1}, use_global_device_ids=true | all-gather | bytes 835584 | tf_op jit(solution)/shard_map/all_gather | solution.py:319
  73.4 3.2 pick_rows.1
  76.6 4.6 collective-permute-start.2
  83.5 2.6 collective-permute-start
  88.1 4.0 collective-permute-start.4
  92.1 5.1 %collective-permute-start.5 = (bf16[128,512]{1,0:T(8,128)(2,1)S(1)}, bf16[128,512]{1,0:T(8,128)(2,1)S(1)}, u32[]{:S(2)}, u32[]{:S(2)}) collective-permute-start(bf16[128,512]{1,0:T(8,128)(2,1)S(1)} %copy-done.15), channel_id=1, source_target_pairs={{0,3},{1,0},{2,1},{3,2},{4,7},{5,4},{6,5},{7,6},{8,11},{9,8},{10,9... | collective-permute-start | bytes 393224 | tf_op jit(solution)/shard_map/ppermute | solution.py:64
  97.3 2.8 collective-permute-done
  101.2 3.3 collective-permute-done.3
  104.5 6.6 %collective-permute-done.4 = bf16[128,512]{1,0:T(8,128)(2,1)S(1)} collective-permute-done((bf16[128,512]{1,0:T(8,128)(2,1)S(1)}, bf16[128,512]{1,0:T(8,128)(2,1)S(1)}, u32[]{:S(2)}, u32[]{:S(2)}) %collective-permute-start.4) | collective-permute-done | bytes 131104 | tf_op jit(solution)/shard_map/ppermute | solution.py:64
  111.1 10.0 %collective-permute-done.5 = bf16[128,512]{1,0:T(8,128)(2,1)S(1)} collective-permute-done((bf16[128,512]{1,0:T(8,128)(2,1)S(1)}, bf16[128,512]{1,0:T(8,128)(2,1)S(1)}, u32[]{:S(2)}, u32[]{:S(2)}) %collective-permute-start.5) | collective-permute-done | bytes 131104 | tf_op jit(solution)/shard_map/ppermute | solution.py:64
  121.2 4.4 collective-permute-start.8
  127.5 11.7 %collective-permute-done.8 = bf16[16,40,512]{2,1,0:T(8,128)(2,1)S(1)} collective-permute-done((bf16[16,40,512]{2,1,0:T(8,128)(2,1)S(1)}, bf16[16,40,512]{2,1,0:T(8,128)(2,1)S(1)}, u32[]{:S(2)}, u32[]{:S(2)}) %collective-permute-start.8) | collective-permute-done | bytes 655392 | tf_op jit(solution)/shard_map/ppermute | solution.py:70
  139.2 5.3 %collective-permute-start.9 = (bf16[8,40,512]{2,1,0:T(8,128)(2,1)S(1)}, bf16[8,40,512]{2,1,0:T(8,128)(2,1)S(1)}, u32[]{:S(2)}, u32[]{:S(2)}) collective-permute-start(bf16[8,40,512]{2,1,0:T(8,128)(2,1)S(1)} %slice.182), channel_id=1, source_target_pairs={{0,24},{8,0},{16,8},{24,16},{1,25},{9,1},{17,9},{25,17},{2,26},{10... | collective-permute-start | bytes 983048 | tf_op jit(solution)/shard_map/ppermute | solution.py:71
  146.5 3.7 collective-permute-done.9
  150.2 5.1 %collective-permute-done.7 = bf16[8,40,512]{2,1,0:T(8,128)(2,1)S(1)} collective-permute-done((bf16[8,40,512]{2,1,0:T(8,128)(2,1)S(1)}, bf16[8,40,512]{2,1,0:T(8,128)(2,1)S(1)}, u32[]{:S(2)}, u32[]{:S(2)}) %collective-permute-start.7) | collective-permute-done | bytes 327712 | tf_op jit(solution)/shard_map/ppermute | solution.py:71
  155.7 4.4 collective-permute-start.10
  162.5 2.4 collective-permute-done.10.theirs_ref
  166.8 4.6 collective-permute-start.12
  178.7 7.0 %attention.1 = (bf16[128,256]{1,0:T(8,128)(2,1)}, bf16[128,512]{1,0:T(8,128)(2,1)}, bf16[128,128]{1,0:T(8,128)(2,1)}, bf16[512,512]{1,0:T(8,128)(2,1)}) custom-call(s32[5]{0:T(128)} %stack.120.place_ref, bf16[4,128,512]{2,1,0:T(8,128)(2,1)} %pad_maximum_fusion.3.in_ref, bf16[64,40,512]{2,1,0:T(8,128)(2,1)} %bitcast.150, ...), custom_call_target="tpu_custom_call" | custom-call | tf_op jit(solution)/shard_map/attention/pallas_call | solution.py:223
  189.5 4.6 collective-permute-start.14
  194.2 16.1 %all_gather.7.attended_ref = bf16[128,1024]{1,0:T(8,128)(2,1)} all-gather(bf16[128,256]{1,0:T(8,128)(2,1)} %get-tuple-element.34), channel_id=1, replica_groups=mesh['zl'=4,'y'=4,'x'=4,'c'=2,'t'=4] {'t'}, dimensions={1}, use_global_device_ids=true | all-gather | bytes 327680 | tf_op jit(solution)/shard_map/all_gather | solution.py:365
  212.0 7.1 %collective-permute-start.15 = (bf16[64,32,512]{2,1,0:T(8,128)(2,1)S(1)}, bf16[64,32,512]{2,1,0:T(8,128)(2,1)}, u32[]{:S(2)}, u32[]{:S(2)}) collective-permute-start(bf16[64,32,512]{2,1,0:T(8,128)(2,1)S(1)} %bitcast.151), channel_id=1, source_target_pairs={{0,4},{4,0},{1,5},{5,1},{2,6},{6,2},{3,7},{7,3},{8,12},{12,8},{9,1... | collective-permute-start | bytes 6291464 | tf_op jit(solution)/shard_map/ppermute | solution.py:76
  219.5 3.4 collective-permute-done.15.theirs_ref
  222.9 7.0 %mix.1 = (bf16[256,1024]{1,0:T(8,128)(2,1)}, bf16[128,512]{1,0:T(8,128)(2,1)}, bf16[2048,256]{1,0:T(8,128)(2,1)}) custom-call(s32[5]{0:T(128)} %stack.120.place_ref, bf16[4,128,512]{2,1,0:T(8,128)(2,1)} %pad_maximum_fusion.3.in_ref, bf16[128,1024]{1,0:T(8,128)(2,1)} %all_gather.7.attended_ref, bf16[64,32,512]{2,1,0:T(8,128)(2,1)} %bitcast.152, ...), custom_call_target="tpu_custom_call" | custom-call | tf_op jit(solution)/shard_map/mix/pallas_call | solution.py:281
  231.9 3.4 collective-permute-start.16
  235.2 2.4 add_convert_fusion.3
  238.2 7.0 %collective-permute-done.18 = bf16[256,1024]{1,0:T(8,128)(2,1)} collective-permute-done((bf16[256,1024]{1,0:T(8,128)(2,1)}, bf16[256,1024]{1,0:T(8,128)(2,1)}, u32[]{:S(2)}, u32[]{:S(2)}) %collective-permute-start.18) | collective-permute-done | bytes 524320 | tf_op jit(solution)/shard_map/ppermute | solution.py:413
  246.3 3.4 collective-permute-start.19
  254.9 5.7 %collective-permute-done.17 = bf16[128,1024]{1,0:T(8,128)(2,1)S(1)} collective-permute-done((bf16[128,1024]{1,0:T(8,128)(2,1)S(1)}, bf16[128,1024]{1,0:T(8,128)(2,1)S(1)}, u32[]{:S(2)}, u32[]{:S(2)}) %collective-permute-start.17) | collective-permute-done | bytes 262176 | tf_op jit(solution)/shard_map/ppermute | solution.py:414
  262.8 50.6 %all_to_all.21 = bf16[32,56,1024]{2,1,0:T(8,128)(2,1)} all-to-all(bf16[32,56,1024]{2,1,0:T(8,128)(2,1)S(1)} %bitcast.155), channel_id=1, replica_groups=mesh['zl'=4,'y'=4,'x'=4,'c'=2,'t'=4] {'c','y','x'}, dimensions={0} | all-to-all | bytes 7340032 | tf_op jit(solution)/shard_map/all_to_all | solution.py:425
  313.4 3.2 collective-permute-start.20
  316.6 3.4 fusion.23
  320.0 3.4 fusion.26
  323.5 3.4 convolution_add_fusion.1
  326.9 3.6 fusion.1
  330.5 4.3 collective-permute-start.22
  334.8 4.9 %collective-permute-start.21 = (bf16[176,1792]{1,0:T(8,128)(2,1)S(1)}, bf16[176,1792]{1,0:T(8,128)(2,1)S(1)}, u32[]{:S(2)}, u32[]{:S(2)}) collective-permute-start(bf16[176,1792]{1,0:T(8,128)(2,1)S(1)} %fusion.1), channel_id=1, source_target_pairs={{0,1},{1,2},{2,3},{3,0},{4,5},{5,6},{6,7},{7,4},{8,9},{9,10},{10,1... | collective-permute-start | bytes 1892360 | tf_op jit(solution)/shard_map/ppermute | solution.py:433
  339.7 52.0 %collective-permute-done.22 = bf16[176,1792]{1,0:T(8,128)(2,1)S(1)} collective-permute-done((bf16[176,1792]{1,0:T(8,128)(2,1)S(1)}, bf16[176,1792]{1,0:T(8,128)(2,1)S(1)}, u32[]{:S(2)}, u32[]{:S(2)}) %collective-permute-start.22) | collective-permute-done | bytes 630816 | tf_op jit(solution)/shard_map/ppermute | solution.py:434
  392.6 4.3 collective-permute-start.24
  397.9 4.7 collective-permute-start.23
  402.8 17.6 %collective-permute-done.24 = bf16[88,1792]{1,0:T(8,128)(2,1)S(1)} collective-permute-done((bf16[88,1792]{1,0:T(8,128)(2,1)S(1)}, bf16[88,1792]{1,0:T(8,128)(2,1)S(1)}, u32[]{:S(2)}, u32[]{:S(2)}) %collective-permute-start.24) | collective-permute-done | bytes 315424 | tf_op jit(solution)/shard_map/ppermute | solution.py:436
  420.4 5.2 %collective-permute-done.23 = bf16[88,1792]{1,0:T(8,128)(2,1)} collective-permute-done((bf16[88,1792]{1,0:T(8,128)(2,1)S(1)}, bf16[88,1792]{1,0:T(8,128)(2,1)}, u32[]{:S(2)}, u32[]{:S(2)}) %collective-permute-start.23) | collective-permute-done | bytes 315424 | tf_op jit(solution)/shard_map/ppermute | solution.py:435
  429.9 2.4 collective-permute-start.25
  432.3 2.4 collective-permute-done.25
  437.1 4.0 all-to-all-start.1
  441.1 15.2 %all-to-all-done.1 = bf16[32,56,256]{2,1,0:T(8,128)(2,1)S(1)} async-done(((bf16[32,56,256]{2,1,0:T(8,128)(2,1)}), bf16[32,56,256]{2,1,0:T(8,128)(2,1)S(1)}, u32[]{:S(2)}, u32[]{:S(2)}) %all-to-all-start.1) | async-done | bytes 917536 | tf_op jit(solution)/shard_map/all_to_all | solution.py:449
  462.0 5.2 %collective-permute-start.26 = (bf16[2,128,256]{2,1,0:T(8,128)(2,1)S(1)}, bf16[2,128,256]{2,1,0:T(8,128)(2,1)S(1)}, u32[]{:S(2)}, u32[]{:S(2)}) collective-permute-start(bf16[2,128,256]{2,1,0:T(8,128)(2,1)S(1)} %get-tuple-element.71), channel_id=1, source_target_pairs={{0,384},{128,0},{256,128},{384,256},{1,385},{129,1},{257,129},{385... | collective-permute-start | bytes 393224 | tf_op jit(solution)/shard_map/ppermute | solution.py:459
  468.1 4.3 collective-permute-done.27
  (130 shorter events, 57.1 us)
Async XLA Ops:
  0.6 319.4 %copy-start = (bf16[1,2048,176]{1,2,0:T(8,128)(2,1)S(1)}, bf16[1,2048,176]{1,2,0:T(8,128)(2,1)}, u32[]{:S(2)}) copy-start(bf16[1,2048,176]{1,2,0:T(8,128)(2,1)} %param.25) | copy-start | bytes 2162692
  0.6 85.5 %copy-start.15 = (bf16[128,512]{1,0:T(8,128)(2,1)S(1)}, bf16[128,512]{1,0:T(8,128)(2,1)}, u32[]{:S(2)}) copy-start(bf16[128,512]{1,0:T(8,128)(2,1)} %param.14) | copy-start | bytes 393220
  76.6 15.5 %collective-permute-start.2 = (bf16[4,72,512]{2,1,0:T(8,128)(2,1)}, bf16[4,72,512]{2,1,0:T(8,128)(2,1)S(1)}, u32[]{:S(2)}, u32[]{:S(2)}) collective-permute-start(bf16[4,72,512]{2,1,0:T(8,128)(2,1)} %pick_rows.1), channel_id=1, source_target_pairs={{0,96},{32,0},{64,32},{96,64},{1,97},{33,1},{65,33},{97,65},{2,98}... | collective-permute-start | bytes 884744 | tf_op jit(solution)/shard_map/ppermute | solution.py:64
  81.2 16.0 %collective-permute-start.1 = (bf16[4,72,512]{2,1,0:T(8,128)(2,1)}, bf16[4,72,512]{2,1,0:T(8,128)(2,1)S(1)}, u32[]{:S(2)}, u32[]{:S(2)}) collective-permute-start(bf16[4,72,512]{2,1,0:T(8,128)(2,1)} %pick_rows.1), channel_id=1, source_target_pairs={{0,64},{32,96},{64,0},{96,32},{1,65},{33,97},{65,1},{97,33},{2,66}... | collective-permute-start | bytes 884744 | tf_op jit(solution)/shard_map/ppermute | solution.py:64
  83.5 16.6 %collective-permute-start = (bf16[4,72,512]{2,1,0:T(8,128)(2,1)}, bf16[4,72,512]{2,1,0:T(8,128)(2,1)S(1)}, u32[]{:S(2)}, u32[]{:S(2)}) collective-permute-start(bf16[4,72,512]{2,1,0:T(8,128)(2,1)} %pick_rows.1), channel_id=1, source_target_pairs={{0,32},{32,64},{64,96},{96,0},{1,33},{33,65},{65,97},{97,1},{2,34}... | collective-permute-start | bytes 884744 | tf_op jit(solution)/shard_map/ppermute | solution.py:64
  86.1 18.4 %collective-permute-start.3 = (bf16[128,512]{1,0:T(8,128)(2,1)S(1)}, bf16[128,512]{1,0:T(8,128)(2,1)S(1)}, u32[]{:S(2)}, u32[]{:S(2)}) collective-permute-start(bf16[128,512]{1,0:T(8,128)(2,1)S(1)} %copy-done.15), channel_id=1, source_target_pairs={{0,1},{1,2},{2,3},{3,0},{4,5},{5,6},{6,7},{7,4},{8,9},{9,10},{10,1... | collective-permute-start | bytes 393224 | tf_op jit(solution)/shard_map/ppermute | solution.py:64
  88.1 23.1 %collective-permute-start.4 = (bf16[128,512]{1,0:T(8,128)(2,1)S(1)}, bf16[128,512]{1,0:T(8,128)(2,1)S(1)}, u32[]{:S(2)}, u32[]{:S(2)}) collective-permute-start(bf16[128,512]{1,0:T(8,128)(2,1)S(1)} %copy-done.15), channel_id=1, source_target_pairs={{0,2},{1,3},{2,0},{3,1},{4,6},{5,7},{6,4},{7,5},{8,10},{9,11},{10,... | collective-permute-start | bytes 393224 | tf_op jit(solution)/shard_map/ppermute | solution.py:64
  92.1 29.0 %collective-permute-start.5 = (bf16[128,512]{1,0:T(8,128)(2,1)S(1)}, bf16[128,512]{1,0:T(8,128)(2,1)S(1)}, u32[]{:S(2)}, u32[]{:S(2)}) collective-permute-start(bf16[128,512]{1,0:T(8,128)(2,1)S(1)} %copy-done.15), channel_id=1, source_target_pairs={{0,3},{1,0},{2,1},{3,2},{4,7},{5,4},{6,5},{7,6},{8,11},{9,8},{10,9... | collective-permute-start | bytes 393224 | tf_op jit(solution)/shard_map/ppermute | solution.py:64
  101.2 54.1 %copy-start.3 = (bf16[4,4,72,512]{3,2,1,0:T(8,128)(2,1)}, bf16[4,4,72,512]{3,2,1,0:T(8,128)(2,1)S(1)}, u32[]{:S(2)}) copy-start(bf16[4,4,72,512]{3,2,1,0:T(8,128)(2,1)S(1)} %pad_maximum_fusion.2) | copy-start | bytes 3538948
  104.5 50.9 %copy-start.16 = (bf16[128,512]{1,0:T(8,128)(2,1)}, bf16[128,512]{1,0:T(8,128)(2,1)S(1)}, u32[]{:S(2)}) copy-start(bf16[128,512]{1,0:T(8,128)(2,1)S(1)} %collective-permute-done.3) | copy-start | bytes 393220
  111.1 44.2 %copy-start.17 = (bf16[128,512]{1,0:T(8,128)(2,1)}, bf16[128,512]{1,0:T(8,128)(2,1)S(1)}, u32[]{:S(2)}) copy-start(bf16[128,512]{1,0:T(8,128)(2,1)S(1)} %collective-permute-done.4) | copy-start | bytes 393220
  121.1 34.3 %copy-start.18 = (bf16[128,512]{1,0:T(8,128)(2,1)}, bf16[128,512]{1,0:T(8,128)(2,1)S(1)}, u32[]{:S(2)}) copy-start(bf16[128,512]{1,0:T(8,128)(2,1)S(1)} %collective-permute-done.5) | copy-start | bytes 393220
  121.2 18.0 %collective-permute-start.8 = (bf16[16,40,512]{2,1,0:T(8,128)(2,1)S(1)}, bf16[16,40,512]{2,1,0:T(8,128)(2,1)S(1)}, u32[]{:S(2)}, u32[]{:S(2)}) collective-permute-start(bf16[16,40,512]{2,1,0:T(8,128)(2,1)S(1)} %get-tuple-element.67), channel_id=1, source_target_pairs={{0,24},{8,0},{16,8},{24,16},{1,25},{9,1},{17,9},{25,17},{2,26},{10... | collective-permute-start | bytes 1966088 | tf_op jit(solution)/shard_map/ppermute | solution.py:70
  125.6 18.9 %collective-permute-start.6 = (bf16[16,40,512]{2,1,0:T(8,128)(2,1)S(1)}, bf16[16,40,512]{2,1,0:T(8,128)(2,1)S(1)}, u32[]{:S(2)}, u32[]{:S(2)}) collective-permute-start(bf16[16,40,512]{2,1,0:T(8,128)(2,1)S(1)} %get-tuple-element.67), channel_id=1, source_target_pairs={{0,8},{8,16},{16,24},{24,0},{1,9},{9,17},{17,25},{25,1},{2,10},{10... | collective-permute-start | bytes 1966088 | tf_op jit(solution)/shard_map/ppermute | solution.py:70
  139.2 11.0 %collective-permute-start.9 = (bf16[8,40,512]{2,1,0:T(8,128)(2,1)S(1)}, bf16[8,40,512]{2,1,0:T(8,128)(2,1)S(1)}, u32[]{:S(2)}, u32[]{:S(2)}) collective-permute-start(bf16[8,40,512]{2,1,0:T(8,128)(2,1)S(1)} %slice.182), channel_id=1, source_target_pairs={{0,24},{8,0},{16,8},{24,16},{1,25},{9,1},{17,9},{25,17},{2,26},{10... | collective-permute-start | bytes 983048 | tf_op jit(solution)/shard_map/ppermute | solution.py:71
  144.6 10.7 %collective-permute-start.7 = (bf16[8,40,512]{2,1,0:T(8,128)(2,1)S(1)}, bf16[8,40,512]{2,1,0:T(8,128)(2,1)S(1)}, u32[]{:S(2)}, u32[]{:S(2)}) collective-permute-start(bf16[8,40,512]{2,1,0:T(8,128)(2,1)S(1)} %slice.181), channel_id=1, source_target_pairs={{0,8},{8,16},{16,24},{24,0},{1,9},{9,17},{17,25},{25,1},{2,10},{10... | collective-permute-start | bytes 983048 | tf_op jit(solution)/shard_map/ppermute | solution.py:71
  155.7 22.9 %copy-start.1 = (bf16[4,16,40,512]{3,2,1,0:T(8,128)(2,1)}, bf16[4,16,40,512]{3,2,1,0:T(8,128)(2,1)S(1)}, u32[]{:S(2)}) copy-start(bf16[4,16,40,512]{3,2,1,0:T(8,128)(2,1)S(1)} %pad_maximum_fusion) | copy-start | bytes 7864324
  155.7 9.1 %collective-permute-start.10 = (bf16[64,40,512]{2,1,0:T(8,128)(2,1)S(1)}, bf16[64,40,512]{2,1,0:T(8,128)(2,1)}, u32[]{:S(2)}, u32[]{:S(2)}) collective-permute-start(bf16[64,40,512]{2,1,0:T(8,128)(2,1)S(1)} %bitcast.149), channel_id=1, source_target_pairs={{0,4},{4,0},{1,5},{5,1},{2,6},{6,2},{3,7},{7,3},{8,12},{12,8},{9,1... | collective-permute-start | bytes 7864328 | tf_op jit(solution)/shard_map/ppermute | solution.py:76
  164.8 20.8 %collective-permute-start.11 = (bf16[16,32,512]{2,1,0:T(8,128)(2,1)}, bf16[16,32,512]{2,1,0:T(8,128)(2,1)}, u32[]{:S(2)}, u32[]{:S(2)}) collective-permute-start(bf16[16,32,512]{2,1,0:T(8,128)(2,1)} %slice.137), channel_id=1, source_target_pairs={{0,8},{8,16},{16,24},{24,0},{1,9},{9,17},{17,25},{25,1},{2,10},{10... | collective-permute-start | bytes 1572872 | tf_op jit(solution)/shard_map/ppermute | solution.py:337
  166.8 18.9 %collective-permute-start.12 = (bf16[16,32,512]{2,1,0:T(8,128)(2,1)}, bf16[16,32,512]{2,1,0:T(8,128)(2,1)}, u32[]{:S(2)}, u32[]{:S(2)}) collective-permute-start(bf16[16,32,512]{2,1,0:T(8,128)(2,1)} %slice.137), channel_id=1, source_target_pairs={{0,24},{8,0},{16,8},{24,16},{1,25},{9,1},{17,9},{25,17},{2,26},{10... | collective-permute-start | bytes 1572872 | tf_op jit(solution)/shard_map/ppermute | solution.py:338
  178.7 15.4 %slice-start = ((bf16[16,4,2048]{2,1,0:T(4,128)(2,1)}), bf16[16,4,128]{2,1,0:T(4,128)(2,1)S(1)}, s32[]{:S(2)}) async-start(bf16[16,4,2048]{2,1,0:T(4,128)(2,1)} %reshape.599), calls=%async_computation.2 | async-start | bytes 32768 | tf_op jit(solution)/shard_map/slice | solution.py:321
  186.6 23.7 %collective-permute-start.13 = (bf16[8,32,512]{2,1,0:T(8,128)(2,1)S(1)}, bf16[8,32,512]{2,1,0:T(8,128)(2,1)S(1)}, u32[]{:S(2)}, u32[]{:S(2)}) collective-permute-start(bf16[8,32,512]{2,1,0:T(8,128)(2,1)S(1)} %slice.141), channel_id=1, source_target_pairs={{0,8},{8,16},{16,24},{24,0},{1,9},{9,17},{17,25},{25,1},{2,10},{10... | collective-permute-start | bytes 786440 | tf_op jit(solution)/shard_map/ppermute | solution.py:363
  189.5 20.8 %collective-permute-start.14 = (bf16[8,32,512]{2,1,0:T(8,128)(2,1)S(1)}, bf16[8,32,512]{2,1,0:T(8,128)(2,1)S(1)}, u32[]{:S(2)}, u32[]{:S(2)}) collective-permute-start(bf16[8,32,512]{2,1,0:T(8,128)(2,1)S(1)} %slice.142), channel_id=1, source_target_pairs={{0,24},{8,0},{16,8},{24,16},{1,25},{9,1},{17,9},{25,17},{2,26},{10... | collective-permute-start | bytes 786440 | tf_op jit(solution)/shard_map/ppermute | solution.py:364
  212.0 11.0 %copy-start.2 = (bf16[4,16,32,512]{3,2,1,0:T(8,128)(2,1)}, bf16[4,16,32,512]{3,2,1,0:T(8,128)(2,1)S(1)}, u32[]{:S(2)}) copy-start(bf16[4,16,32,512]{3,2,1,0:T(8,128)(2,1)S(1)} %pad_maximum_fusion.1) | copy-start | bytes 6291460
  212.0 11.0 %collective-permute-start.15 = (bf16[64,32,512]{2,1,0:T(8,128)(2,1)S(1)}, bf16[64,32,512]{2,1,0:T(8,128)(2,1)}, u32[]{:S(2)}, u32[]{:S(2)}) collective-permute-start(bf16[64,32,512]{2,1,0:T(8,128)(2,1)S(1)} %bitcast.151), channel_id=1, source_target_pairs={{0,4},{4,0},{1,5},{5,1},{2,6},{6,2},{3,7},{7,3},{8,12},{12,8},{9,1... | collective-permute-start | bytes 6291464 | tf_op jit(solution)/shard_map/ppermute | solution.py:76
  229.9 15.3 %collective-permute-start.18 = (bf16[256,1024]{1,0:T(8,128)(2,1)}, bf16[256,1024]{1,0:T(8,128)(2,1)}, u32[]{:S(2)}, u32[]{:S(2)}) collective-permute-start(bf16[256,1024]{1,0:T(8,128)(2,1)} %get-tuple-element.39), channel_id=1, source_target_pairs={{0,387},{128,0},{256,128},{384,256},{1,384},{129,1},{257,129},{385... | collective-permute-start | bytes 1572872 | tf_op jit(solution)/shard_map/ppermute | solution.py:413
  231.9 17.9 %collective-permute-start.16 = (bf16[256,1024]{1,0:T(8,128)(2,1)}, bf16[256,1024]{1,0:T(8,128)(2,1)}, u32[]{:S(2)}, u32[]{:S(2)}) collective-permute-start(bf16[256,1024]{1,0:T(8,128)(2,1)} %get-tuple-element.39), channel_id=1, source_target_pairs={{0,128},{128,256},{256,384},{384,1},{1,129},{129,257},{257,385},{3... | collective-permute-start | bytes 1572872 | tf_op jit(solution)/shard_map/ppermute | solution.py:412
  238.2 14.6 %copy-start.5 = (bf16[256,1024]{1,0:T(8,128)(2,1)S(1)}, bf16[256,1024]{1,0:T(8,128)(2,1)}, u32[]{:S(2)}) copy-start(bf16[256,1024]{1,0:T(8,128)(2,1)} %get-tuple-element.39) | copy-start | bytes 1572868
  246.3 8.5 %collective-permute-start.19 = (bf16[128,1024]{1,0:T(8,128)(2,1)S(1)}, bf16[128,1024]{1,0:T(8,128)(2,1)S(1)}, u32[]{:S(2)}, u32[]{:S(2)}) collective-permute-start(bf16[128,1024]{1,0:T(8,128)(2,1)S(1)} %get-tuple-element.79), channel_id=1, source_target_pairs={{0,387},{128,0},{256,128},{384,256},{1,384},{129,1},{257,129},{385... | collective-permute-start | bytes 786440 | tf_op jit(solution)/shard_map/ppermute | solution.py:415
  250.9 9.7 %collective-permute-start.17 = (bf16[128,1024]{1,0:T(8,128)(2,1)S(1)}, bf16[128,1024]{1,0:T(8,128)(2,1)S(1)}, u32[]{:S(2)}, u32[]{:S(2)}) collective-permute-start(bf16[128,1024]{1,0:T(8,128)(2,1)S(1)} %get-tuple-element.76), channel_id=1, source_target_pairs={{0,128},{128,256},{256,384},{384,1},{1,129},{129,257},{257,385},{3... | collective-permute-start | bytes 786440 | tf_op jit(solution)/shard_map/ppermute | solution.py:414
  262.8 53.8 %copy-start.7 = (bf16[1,2048,176]{1,2,0:T(8,128)(2,1)S(1)}, bf16[1,2048,176]{1,2,0:T(8,128)(2,1)}, u32[]{:S(2)}) copy-start(bf16[1,2048,176]{1,2,0:T(8,128)(2,1)} %param.26) | copy-start | bytes 2162692
  313.4 10.0 %collective-permute-start.20 = (bf16[1792,1024]{1,0:T(8,128)(2,1)}, bf16[1792,1024]{1,0:T(8,128)(2,1)}, u32[]{:S(2)}, u32[]{:S(2)}) collective-permute-start(bf16[1792,1024]{1,0:T(8,128)(2,1)} %bitcast.64), channel_id=1, source_target_pairs={{0,4},{4,0},{1,5},{5,1},{2,6},{6,2},{3,7},{7,3},{8,12},{12,8},{9,1... | collective-permute-start | bytes 11010056 | tf_op jit(solution)/shard_map/ppermute | solution.py:76
  326.9 75.8 %copy-start.4 = (bf16[1,704,512]{2,1,0:T(8,128)(2,1)S(1)}, bf16[1,704,512]{2,1,0:T(8,128)(2,1)}, u32[]{:S(2)}) copy-start(bf16[1,704,512]{2,1,0:T(8,128)(2,1)} %param.27) | copy-start | bytes 2162692
  330.5 67.4 %copy-start.19 = (bf16[176,1792]{1,0:T(8,128)(2,1)}, bf16[176,1792]{1,0:T(8,128)(2,1)S(1)}, u32[]{:S(2)}) copy-start(bf16[176,1792]{1,0:T(8,128)(2,1)S(1)} %fusion.1) | copy-start | bytes 1892356
  330.5 61.2 %collective-permute-start.22 = (bf16[176,1792]{1,0:T(8,128)(2,1)S(1)}, bf16[176,1792]{1,0:T(8,128)(2,1)S(1)}, u32[]{:S(2)}, u32[]{:S(2)}) collective-permute-start(bf16[176,1792]{1,0:T(8,128)(2,1)S(1)} %fusion.1), channel_id=1, source_target_pairs={{0,3},{1,0},{2,1},{3,2},{4,7},{5,4},{6,5},{7,6},{8,11},{9,8},{10,9... | collective-permute-start | bytes 1892360 | tf_op jit(solution)/shard_map/ppermute | solution.py:434
  334.8 62.2 %collective-permute-start.21 = (bf16[176,1792]{1,0:T(8,128)(2,1)S(1)}, bf16[176,1792]{1,0:T(8,128)(2,1)S(1)}, u32[]{:S(2)}, u32[]{:S(2)}) collective-permute-start(bf16[176,1792]{1,0:T(8,128)(2,1)S(1)} %fusion.1), channel_id=1, source_target_pairs={{0,1},{1,2},{2,3},{3,0},{4,5},{5,6},{6,7},{7,4},{8,9},{9,10},{10,1... | collective-permute-start | bytes 1892360 | tf_op jit(solution)/shard_map/ppermute | solution.py:433
  392.6 27.8 %collective-permute-start.24 = (bf16[88,1792]{1,0:T(8,128)(2,1)S(1)}, bf16[88,1792]{1,0:T(8,128)(2,1)S(1)}, u32[]{:S(2)}, u32[]{:S(2)}) collective-permute-start(bf16[88,1792]{1,0:T(8,128)(2,1)S(1)} %slice.208), channel_id=1, source_target_pairs={{0,3},{1,0},{2,1},{3,2},{4,7},{5,4},{6,5},{7,6},{8,11},{9,8},{10,9... | collective-permute-start | bytes 946184 | tf_op jit(solution)/shard_map/ppermute | solution.py:436
  397.9 27.7 %collective-permute-start.23 = (bf16[88,1792]{1,0:T(8,128)(2,1)S(1)}, bf16[88,1792]{1,0:T(8,128)(2,1)}, u32[]{:S(2)}, u32[]{:S(2)}) collective-permute-start(bf16[88,1792]{1,0:T(8,128)(2,1)S(1)} %slice.207), channel_id=1, source_target_pairs={{0,1},{1,2},{2,3},{3,0},{4,5},{5,6},{6,7},{7,4},{8,9},{9,10},{10,1... | collective-permute-start | bytes 946184 | tf_op jit(solution)/shard_map/ppermute | solution.py:435
  402.8 24.5 %copy-start.9 = (bf16[176,1792]{1,0:T(8,128)(2,1)S(1)}, bf16[176,1792]{1,0:T(8,128)(2,1)}, u32[]{:S(2)}) copy-start(bf16[176,1792]{1,0:T(8,128)(2,1)} %copy-done.8) | copy-start | bytes 1892356
  402.8 24.5 %copy-start.11 = (bf16[176,1792]{1,0:T(8,128)(2,1)S(1)}, bf16[176,1792]{1,0:T(8,128)(2,1)}, u32[]{:S(2)}) copy-start(bf16[176,1792]{1,0:T(8,128)(2,1)} %copy-done.10) | copy-start | bytes 1892356
  402.8 24.5 %copy-start.20 = (bf16[176,1792]{1,0:T(8,128)(2,1)S(1)}, bf16[176,1792]{1,0:T(8,128)(2,1)}, u32[]{:S(2)}) copy-start(bf16[176,1792]{1,0:T(8,128)(2,1)} %copy-done.19) | copy-start | bytes 1892356
  429.9 4.8 %collective-permute-start.25 = (bf16[1792,256]{1,0:T(8,128)(2,1)}, bf16[1792,256]{1,0:T(8,128)(2,1)}, u32[]{:S(2)}, u32[]{:S(2)}) collective-permute-start(bf16[1792,256]{1,0:T(8,128)(2,1)} %constant_dynamic-slice_fusion), channel_id=1, source_target_pairs={{0,4},{4,0},{1,5},{5,1},{2,6},{6,2},{3,7},{7,3},{8,12},{12,8},{9,1... | collective-permute-start | bytes 2752520 | tf_op jit(solution)/shard_map/ppermute | solution.py:76
  437.1 19.2 %all-to-all-start.1 = ((bf16[32,56,256]{2,1,0:T(8,128)(2,1)}), bf16[32,56,256]{2,1,0:T(8,128)(2,1)S(1)}, u32[]{:S(2)}, u32[]{:S(2)}) async-start(bf16[32,56,256]{2,1,0:T(8,128)(2,1)} %bitcast.72), calls=%async_computation.1 | async-start | bytes 1835008 | tf_op jit(solution)/shard_map/all_to_all | solution.py:449
  456.4 10.9 %copy-start.12 = (bf16[128,512]{1,0:T(8,128)(2,1)S(1)}, bf16[128,512]{1,0:T(8,128)(2,1)}, u32[]{:S(2)}) copy-start(bf16[128,512]{1,0:T(8,128)(2,1)} %get-tuple-element.42) | copy-start | bytes 393220
  457.1 16.4 %copy-start.14 = (bf16[128,512]{1,0:T(8,128)(2,1)S(1)}, bf16[128,512]{1,0:T(8,128)(2,1)}, u32[]{:S(2)}) copy-start(bf16[128,512]{1,0:T(8,128)(2,1)} %get-tuple-element.38) | copy-start | bytes 393220
  458.1 10.0 %collective-permute-start.28 = (bf16[2,128,256]{2,1,0:T(8,128)(2,1)S(1)}, bf16[2,128,256]{2,1,0:T(8,128)(2,1)S(1)}, u32[]{:S(2)}, u32[]{:S(2)}) collective-permute-start(bf16[2,128,256]{2,1,0:T(8,128)(2,1)S(1)} %get-tuple-element.72), channel_id=1, source_target_pairs={{0,128},{128,256},{256,384},{384,0},{1,129},{129,257},{257,385},{3... | collective-permute-start | bytes 393224 | tf_op jit(solution)/shard_map/ppermute | solution.py:459
  460.1 12.4 %collective-permute-start.27 = (bf16[2,128,256]{2,1,0:T(8,128)(2,1)S(1)}, bf16[2,128,256]{2,1,0:T(8,128)(2,1)S(1)}, u32[]{:S(2)}, u32[]{:S(2)}) collective-permute-start(bf16[2,128,256]{2,1,0:T(8,128)(2,1)S(1)} %get-tuple-element.73), channel_id=1, source_target_pairs={{0,256},{128,384},{256,0},{384,128},{1,257},{129,385},{257,1},{385... | collective-permute-start | bytes 393224 | tf_op jit(solution)/shard_map/ppermute | solution.py:459
  462.0 10.5 %collective-permute-start.26 = (bf16[2,128,256]{2,1,0:T(8,128)(2,1)S(1)}, bf16[2,128,256]{2,1,0:T(8,128)(2,1)S(1)}, u32[]{:S(2)}, u32[]{:S(2)}) collective-permute-start(bf16[2,128,256]{2,1,0:T(8,128)(2,1)S(1)} %get-tuple-element.71), channel_id=1, source_target_pairs={{0,384},{128,0},{256,128},{384,256},{1,385},{129,1},{257,129},{385... | collective-permute-start | bytes 393224 | tf_op jit(solution)/shard_map/ppermute | solution.py:459
  (5 other events, 18.3 us)

commit v7 on v4

--- a/solution.py
+++ b/solution.py
@@ -322,9 +322,8 @@
     first_set = gathered[:, :40]
     first_mine = jnp.stack(ring(first_set, "x")).reshape(64, 40, 512)
     first_theirs = other_core(first_mine)
-    second_set, _ = lax.optimization_barrier((gathered[:, 40:], first_mine))
-    second_below = lax.ppermute(second_set, "x", UP)
-    second_above = lax.ppermute(second_set, "x", DOWN)
+    second_set, _ = lax.optimization_barrier((gathered[:, 40:], first_theirs))
+    second_parts = shifted(second_set, "x")
 
     segment, position = positions_of(lengths, TOK)
     segment = segment[0]
@@ -346,14 +345,9 @@
     )
     cache_full = jnp.concatenate([latent_normed, key_rope[:, 0:32], key_rope[:, 64:96]], axis=1)
     cache_cols = lax.dynamic_slice_in_dim(cache_full, rank * 144, 144, 1)
-    below_part, above_part, attended = lax.optimization_barrier(
-        (second_below[:8], second_above[8:], attended)
-    )
-    second_far = jnp.concatenate(
-        [lax.ppermute(below_part, "x", UP), lax.ppermute(above_part, "x", DOWN)]
-    )
     attended_full = lax.all_gather(attended, T, axis=1, tiled=True)
-    second_mine = jnp.stack([second_set, second_below, second_far, second_above]).reshape(64, 32, 512)
+    attended_full, *second_parts = lax.optimization_barrier((attended_full, *second_parts))
+    second_mine = jnp.stack(second_parts).reshape(64, 32, 512)
     second_theirs = other_core(second_mine)
     moe_halves, mixed_cols, output_block = mix(
         place, everything, attended_full, second_mine, second_theirs, moe_gain

time: 435 us -> 421 us (0.968)
  waiting for transfers between devices: 151 us -> 143 us
  starting transfers between devices: 113 us -> 108 us
    ppermute x4 -> x0, waiting for transfers between devices: 16.2 us -> none  [the longest x1 8.28 us: body(): second_below = lax.ppermute(second_set, 'x', UP)]
    ppermute x4 -> x0, starting transfers between devices: 13.7 us -> none  [the longest x1 5.31 us: body(): lax.ppermute(above_part, 'x', DOWN)]
    ppermute x6 -> x9, starting transfers between devices: 17.4 us -> 25.8 us  [shifted(): lax.ppermute(block, axis, [(j, (j + s) % 4) for j in range(4)])]
    ppermute x4, waiting for transfers between devices: 2.42 us -> 8.18 us  [other_core(): return lax.ppermute(block, 'c', [(0, 1), (1, 0)])]
    ppermute x6 -> x9, waiting for transfers between devices: 13.1 us -> 13.1 us  [shifted(): lax.ppermute(block, axis, [(j, (j + s) % 4) for j in range(4)])]
  transfers between devices with their start and end apart: 30 -> 29, of which waited for: 21 -> 19; matrix products, arithmetic and copies ran while one was open for 4% -> 4% of each run, Pallas kernels for 0% -> 2%
where the time goes in v7:
time: 421 us; the launch traced here: 419 us
  waiting for transfers between devices  143 us (34%)
  starting transfers between devices  108 us (26%)
  blocking collectives  106 us (25%)
  matrix products  20.2 us (5%)
  Pallas kernels  17.8 us (4%)
  other arithmetic  12.4 us (3%)
  local copies, waits for them, and re-layouts  9.2 us (2%)
    all_to_all x1, blocking collectives, body(): lax.all_to_all(outgoing.reshape(2 * LAYER_ROWS, D // 2), LAYER, split_axi...  51.8 us
    ppermute x1, waiting for transfers between devices, body(): above = lax.ppermute(own, T, DOWN)  50.5 us
    all_gather x1, blocking collectives, body(): everything = lax.all_gather(packed, T, axis=1, tiled=True)  35.8 us
    ppermute x9, starting transfers between devices, shifted(): lax.ppermute(block, axis, [(j, (j + s) % 4) for j in range(4)])  25.8 us
    ppermute x4, starting transfers between devices, other_core(): return lax.ppermute(block, 'c', [(0, 1), (1, 0)])  22.5 us
    all_gather x1, blocking collectives, body(): attended_full = lax.all_gather(attended, T, axis=1, tiled=True)  18.3 us
    ppermute x1, waiting for transfers between devices, body(): far_second = lax.ppermute(above[88:], T, DOWN)  15.9 us
    all_to_all x1, waiting for transfers between devices, body(): lax.all_to_all(both, LAYER, split_axis=0, concat_axis=0, tiled=True)  15.2 us
  transfers between devices with their start and end apart: 29, of which 19 were waited for; matrix products, arithmetic and copies ran while one was open for 4% of the time, Pallas kernels for 2%

profile of v7, /device:TPU:1, one launch (start us, length us, event | category | flops | bytes accessed | tf_op | source)
XLA Modules:
  0.0 418.6 jit_solution(8078827895805746086)
XLA Ops:
  2.4 35.8 %all_gather.6.in_ref = bf16[160,2048]{1,0:T(8,128)(2,1)} all-gather(bf16[160,512]{1,0:T(8,128)(2,1)} %pack_rows.1), channel_id=1, replica_groups=mesh['zl'=4,'y'=4,'x'=4,'c'=2,'t'=4] {'t'}, dimensions={1}, use_global_device_ids=true | all-gather | bytes 819200 | tf_op jit(solution)/shard_map/all_gather | solution.py:316
  40.5 3.8 collective-permute-start.2
  46.2 2.2 collective-permute-start
  48.4 3.3 collective-permute-done.1
  54.9 4.6 %collective-permute-start.5 = (bf16[4,72,512]{2,1,0:T(8,128)(2,1)S(1)}, bf16[4,72,512]{2,1,0:T(8,128)(2,1)S(1)}, u32[]{:S(2)}, u32[]{:S(2)}) collective-permute-start(bf16[4,72,512]{2,1,0:T(8,128)(2,1)S(1)} %get-tuple-element.73), channel_id=1, source_target_pairs={{0,96},{32,0},{64,32},{96,64},{1,97},{33,1},{65,33},{97,65},{2,98}... | collective-permute-start | bytes 884744 | tf_op jit(solution)/shard_map/ppermute | solution.py:64
  59.6 2.3 collective-permute-start.4
  61.8 2.6 collective-permute-start.3
  65.2 3.4 collective-permute-done.4
  68.6 3.4 collective-permute-done.3
  72.3 4.4 %collective-permute-start.8 = (bf16[16,40,512]{2,1,0:T(8,128)(2,1)S(1)}, bf16[16,40,512]{2,1,0:T(8,128)(2,1)S(1)}, u32[]{:S(2)}, u32[]{:S(2)}) collective-permute-start(bf16[16,40,512]{2,1,0:T(8,128)(2,1)S(1)} %get-tuple-element.53), channel_id=1, source_target_pairs={{0,24},{8,0},{16,8},{24,16},{1,25},{9,1},{17,9},{25,17},{2,26},{10... | collective-permute-start | bytes 1966088 | tf_op jit(solution)/shard_map/ppermute | solution.py:70
  78.6 5.6 %collective-permute-done.8 = bf16[16,40,512]{2,1,0:T(8,128)(2,1)S(1)} collective-permute-done((bf16[16,40,512]{2,1,0:T(8,128)(2,1)S(1)}, bf16[16,40,512]{2,1,0:T(8,128)(2,1)S(1)}, u32[]{:S(2)}, u32[]{:S(2)}) %collective-permute-start.8) | collective-permute-done | bytes 655392 | tf_op jit(solution)/shard_map/ppermute | solution.py:70
  84.2 5.0 %collective-permute-start.9 = (bf16[8,40,512]{2,1,0:T(8,128)(2,1)S(1)}, bf16[8,40,512]{2,1,0:T(8,128)(2,1)S(1)}, u32[]{:S(2)}, u32[]{:S(2)}) collective-permute-start(bf16[8,40,512]{2,1,0:T(8,128)(2,1)S(1)} %slice.172), channel_id=1, source_target_pairs={{0,24},{8,0},{16,8},{24,16},{1,25},{9,1},{17,9},{25,17},{2,26},{10... | collective-permute-start | bytes 983048 | tf_op jit(solution)/shard_map/ppermute | solution.py:71
  91.2 3.6 collective-permute-done.9
  94.8 5.3 %collective-permute-done.7 = bf16[8,40,512]{2,1,0:T(8,128)(2,1)S(1)} collective-permute-done((bf16[8,40,512]{2,1,0:T(8,128)(2,1)S(1)}, bf16[8,40,512]{2,1,0:T(8,128)(2,1)S(1)}, u32[]{:S(2)}, u32[]{:S(2)}) %collective-permute-start.7) | collective-permute-done | bytes 327712 | tf_op jit(solution)/shard_map/ppermute | solution.py:71
  100.6 11.0 %collective-permute-start.10 = (bf16[64,40,512]{2,1,0:T(8,128)(2,1)S(1)}, bf16[64,40,512]{2,1,0:T(8,128)(2,1)}, u32[]{:S(2)}, u32[]{:S(2)}) collective-permute-start(bf16[64,40,512]{2,1,0:T(8,128)(2,1)S(1)} %bitcast.117), channel_id=1, source_target_pairs={{0,4},{4,0},{1,5},{5,1},{2,6},{6,2},{3,7},{7,3},{8,12},{12,8},{9,1... | collective-permute-start | bytes 7864328 | tf_op jit(solution)/shard_map/ppermute | solution.py:76
  113.9 2.4 collective-permute-done.10.theirs_ref
  118.2 2.3 collective-permute-start.12
  120.5 4.2 collective-permute-start.13
  126.5 7.2 %attention.1 = (bf16[128,256]{1,0:T(8,128)(2,1)}, bf16[128,512]{1,0:T(8,128)(2,1)}, bf16[128,128]{1,0:T(8,128)(2,1)}, bf16[512,512]{1,0:T(8,128)(2,1)}) custom-call(s32[5]{0:T(128)} %stack.113.place_ref, bf16[160,2048]{1,0:T(8,128)(2,1)} %all_gather.6.in_ref, bf16[64,40,512]{2,1,0:T(8,128)(2,1)} %bitcast.118, ...), custom_call_target="tpu_custom_call" | custom-call | tf_op jit(solution)/shard_map/attention/pallas_call | solution.py:222
  133.7 18.3 %all_gather.7.attended_ref = bf16[128,1024]{1,0:T(8,128)(2,1)} all-gather(bf16[128,256]{1,0:T(8,128)(2,1)} %get-tuple-element.17), channel_id=1, replica_groups=mesh['zl'=4,'y'=4,'x'=4,'c'=2,'t'=4] {'t'}, dimensions={1}, use_global_device_ids=true | all-gather | bytes 327680 | tf_op jit(solution)/shard_map/all_gather | solution.py:348
  153.9 5.9 %collective-permute-start.14 = (bf16[64,32,512]{2,1,0:T(8,128)(2,1)S(1)}, bf16[64,32,512]{2,1,0:T(8,128)(2,1)}, u32[]{:S(2)}, u32[]{:S(2)}) collective-permute-start(bf16[64,32,512]{2,1,0:T(8,128)(2,1)S(1)} %bitcast.119), channel_id=1, source_target_pairs={{0,4},{4,0},{1,5},{5,1},{2,6},{6,2},{3,7},{7,3},{8,12},{12,8},{9,1... | collective-permute-start | bytes 6291464 | tf_op jit(solution)/shard_map/ppermute | solution.py:76
  160.4 3.4 collective-permute-done.14.theirs_ref
  163.7 7.2 %mix.1 = (bf16[256,1024]{1,0:T(8,128)(2,1)}, bf16[128,512]{1,0:T(8,128)(2,1)}, bf16[2048,256]{1,0:T(8,128)(2,1)}) custom-call(s32[5]{0:T(128)} %stack.113.place_ref, bf16[160,2048]{1,0:T(8,128)(2,1)} %all_gather.6.in_ref, bf16[128,1024]{1,0:T(8,128)(2,1)} %all_gather.7.attended_ref, bf16[64,32,512]{2,1,0:T(8,128)(2,1)} %bitcast.120, ...), custom_call_target="tpu_custom_call" | custom-call | tf_op jit(solution)/shard_map/mix/pallas_call | solution.py:280
  171.0 4.8 %collective-permute-start.17 = (bf16[256,1024]{1,0:T(8,128)(2,1)}, bf16[256,1024]{1,0:T(8,128)(2,1)}, u32[]{:S(2)}, u32[]{:S(2)}) collective-permute-start(bf16[256,1024]{1,0:T(8,128)(2,1)} %get-tuple-element.25), channel_id=1, source_target_pairs={{0,387},{128,0},{256,128},{384,256},{1,384},{129,1},{257,129},{385... | collective-permute-start | bytes 1572872 | tf_op jit(solution)/shard_map/ppermute | solution.py:392
  177.7 2.4 add_convert_fusion.3
  180.7 6.3 %collective-permute-done.17 = bf16[256,1024]{1,0:T(8,128)(2,1)} collective-permute-done((bf16[256,1024]{1,0:T(8,128)(2,1)}, bf16[256,1024]{1,0:T(8,128)(2,1)}, u32[]{:S(2)}, u32[]{:S(2)}) %collective-permute-start.17) | collective-permute-done | bytes 524320 | tf_op jit(solution)/shard_map/ppermute | solution.py:392
  188.1 5.3 %collective-permute-start.18 = (bf16[128,1024]{1,0:T(8,128)(2,1)S(1)}, bf16[128,1024]{1,0:T(8,128)(2,1)S(1)}, u32[]{:S(2)}, u32[]{:S(2)}) collective-permute-start(bf16[128,1024]{1,0:T(8,128)(2,1)S(1)} %get-tuple-element.65), channel_id=1, source_target_pairs={{0,387},{128,0},{256,128},{384,256},{1,384},{129,1},{257,129},{385... | collective-permute-start | bytes 786440 | tf_op jit(solution)/shard_map/ppermute | solution.py:394
  197.9 6.1 %collective-permute-done.16 = bf16[128,1024]{1,0:T(8,128)(2,1)S(1)} collective-permute-done((bf16[128,1024]{1,0:T(8,128)(2,1)S(1)}, bf16[128,1024]{1,0:T(8,128)(2,1)S(1)}, u32[]{:S(2)}, u32[]{:S(2)}) %collective-permute-start.16) | collective-permute-done | bytes 262176 | tf_op jit(solution)/shard_map/ppermute | solution.py:393
  206.1 51.8 %all_to_all.21 = bf16[32,56,1024]{2,1,0:T(8,128)(2,1)} all-to-all(bf16[32,56,1024]{2,1,0:T(8,128)(2,1)S(1)} %bitcast.123), channel_id=1, replica_groups=mesh['zl'=4,'y'=4,'x'=4,'c'=2,'t'=4] {'c','y','x'}, dimensions={0} | all-to-all | bytes 7340032 | tf_op jit(solution)/shard_map/all_to_all | solution.py:404
  257.9 3.2 collective-permute-start.19
  261.1 3.4 fusion.23
  264.5 3.4 fusion.26
  267.9 3.4 convolution_add_fusion.1
  271.4 3.6 fusion.1
  274.9 2.2 collective-permute-start.21
  277.1 7.0 %collective-permute-start.20 = (bf16[176,1792]{1,0:T(8,128)(2,1)S(1)}, bf16[176,1792]{1,0:T(8,128)(2,1)S(1)}, u32[]{:S(2)}, u32[]{:S(2)}) collective-permute-start(bf16[176,1792]{1,0:T(8,128)(2,1)S(1)} %fusion.1), channel_id=1, source_target_pairs={{0,1},{1,2},{2,3},{3,0},{4,5},{5,6},{6,7},{7,4},{8,9},{9,10},{10,1... | collective-permute-start | bytes 1892360 | tf_op jit(solution)/shard_map/ppermute | solution.py:412
  284.2 50.5 %collective-permute-done.21 = bf16[176,1792]{1,0:T(8,128)(2,1)S(1)} collective-permute-done((bf16[176,1792]{1,0:T(8,128)(2,1)S(1)}, bf16[176,1792]{1,0:T(8,128)(2,1)S(1)}, u32[]{:S(2)}, u32[]{:S(2)}) %collective-permute-start.21) | collective-permute-done | bytes 630816 | tf_op jit(solution)/shard_map/ppermute | solution.py:413
  334.7 4.8 %collective-permute-start.23 = (bf16[88,1792]{1,0:T(8,128)(2,1)S(1)}, bf16[88,1792]{1,0:T(8,128)(2,1)S(1)}, u32[]{:S(2)}, u32[]{:S(2)}) collective-permute-start(bf16[88,1792]{1,0:T(8,128)(2,1)S(1)} %slice.191), channel_id=1, source_target_pairs={{0,3},{1,0},{2,1},{3,2},{4,7},{5,4},{6,5},{7,6},{8,11},{9,8},{10,9... | collective-permute-start | bytes 946184 | tf_op jit(solution)/shard_map/ppermute | solution.py:415
  340.4 5.9 %collective-permute-start.22 = (bf16[88,1792]{1,0:T(8,128)(2,1)S(1)}, bf16[88,1792]{1,0:T(8,128)(2,1)}, u32[]{:S(2)}, u32[]{:S(2)}) collective-permute-start(bf16[88,1792]{1,0:T(8,128)(2,1)S(1)} %slice.190), channel_id=1, source_target_pairs={{0,1},{1,2},{2,3},{3,0},{4,5},{5,6},{6,7},{7,4},{8,9},{9,10},{10,1... | collective-permute-start | bytes 946184 | tf_op jit(solution)/shard_map/ppermute | solution.py:414
  346.4 15.9 %collective-permute-done.23 = bf16[88,1792]{1,0:T(8,128)(2,1)S(1)} collective-permute-done((bf16[88,1792]{1,0:T(8,128)(2,1)S(1)}, bf16[88,1792]{1,0:T(8,128)(2,1)S(1)}, u32[]{:S(2)}, u32[]{:S(2)}) %collective-permute-start.23) | collective-permute-done | bytes 315424 | tf_op jit(solution)/shard_map/ppermute | solution.py:415
  362.3 7.8 %collective-permute-done.22 = bf16[88,1792]{1,0:T(8,128)(2,1)} collective-permute-done((bf16[88,1792]{1,0:T(8,128)(2,1)S(1)}, bf16[88,1792]{1,0:T(8,128)(2,1)}, u32[]{:S(2)}, u32[]{:S(2)}) %collective-permute-start.22) | collective-permute-done | bytes 315424 | tf_op jit(solution)/shard_map/ppermute | solution.py:414
  374.4 2.4 collective-permute-start.24
  376.8 2.4 collective-permute-done.24
  379.2 2.4 add_convert_fusion.1
  381.5 4.0 all-to-all-start.1
  385.6 15.2 %all-to-all-done.1 = bf16[32,56,256]{2,1,0:T(8,128)(2,1)S(1)} async-done(((bf16[32,56,256]{2,1,0:T(8,128)(2,1)}), bf16[32,56,256]{2,1,0:T(8,128)(2,1)S(1)}, u32[]{:S(2)}, u32[]{:S(2)}) %all-to-all-start.1) | async-done | bytes 917536 | tf_op jit(solution)/shard_map/all_to_all | solution.py:428
  406.4 5.2 %collective-permute-start.25 = (bf16[2,128,256]{2,1,0:T(8,128)(2,1)S(1)}, bf16[2,128,256]{2,1,0:T(8,128)(2,1)S(1)}, u32[]{:S(2)}, u32[]{:S(2)}) collective-permute-start(bf16[2,128,256]{2,1,0:T(8,128)(2,1)S(1)} %get-tuple-element.57), channel_id=1, source_target_pairs={{0,384},{128,0},{256,128},{384,256},{1,385},{129,1},{257,129},{385... | collective-permute-start | bytes 393224 | tf_op jit(solution)/shard_map/ppermute | solution.py:438
  412.5 4.3 %collective-permute-done.26 = bf16[2,128,256]{2,1,0:T(8,128)(2,1)S(1)} collective-permute-done((bf16[2,128,256]{2,1,0:T(8,128)(2,1)S(1)}, bf16[2,128,256]{2,1,0:T(8,128)(2,1)S(1)}, u32[]{:S(2)}, u32[]{:S(2)}) %collective-permute-start.26) | collective-permute-done | bytes 131104 | tf_op jit(solution)/shard_map/ppermute | solution.py:438
  (115 shorter events, 46.2 us)
Async XLA Ops:
  0.6 263.9 %copy-start = (bf16[1,2048,176]{1,2,0:T(8,128)(2,1)S(1)}, bf16[1,2048,176]{1,2,0:T(8,128)(2,1)}, u32[]{:S(2)}) copy-start(bf16[1,2048,176]{1,2,0:T(8,128)(2,1)} %param.25) | copy-start | bytes 2162692
  40.5 8.0 %collective-permute-start.2 = (bf16[88,512]{1,0:T(8,128)(2,1)}, bf16[88,512]{1,0:T(8,128)(2,1)S(1)}, u32[]{:S(2)}, u32[]{:S(2)}) collective-permute-start(bf16[88,512]{1,0:T(8,128)(2,1)} %pick_rows.1), channel_id=1, source_target_pairs={{0,384},{128,0},{256,128},{384,256},{1,385},{129,1},{257,129},{385... | collective-permute-start | bytes 270344 | tf_op jit(solution)/shard_map/ppermute | solution.py:64
  44.3 7.5 %collective-permute-start.1 = (bf16[88,512]{1,0:T(8,128)(2,1)}, bf16[88,512]{1,0:T(8,128)(2,1)S(1)}, u32[]{:S(2)}, u32[]{:S(2)}) collective-permute-start(bf16[88,512]{1,0:T(8,128)(2,1)} %pick_rows.1), channel_id=1, source_target_pairs={{0,256},{128,384},{256,0},{384,128},{1,257},{129,385},{257,1},{385... | collective-permute-start | bytes 270344 | tf_op jit(solution)/shard_map/ppermute | solution.py:64
  46.2 7.7 %collective-permute-start = (bf16[88,512]{1,0:T(8,128)(2,1)}, bf16[88,512]{1,0:T(8,128)(2,1)S(1)}, u32[]{:S(2)}, u32[]{:S(2)}) collective-permute-start(bf16[88,512]{1,0:T(8,128)(2,1)} %pick_rows.1), channel_id=1, source_target_pairs={{0,128},{128,256},{256,384},{384,0},{1,129},{129,257},{257,385},{3... | collective-permute-start | bytes 270344 | tf_op jit(solution)/shard_map/ppermute | solution.py:64
  53.9 18.2 %copy-start.5 = (bf16[88,512]{1,0:T(8,128)(2,1)}, bf16[88,512]{1,0:T(8,128)(2,1)S(1)}, u32[]{:S(2)}) copy-start(bf16[88,512]{1,0:T(8,128)(2,1)S(1)} %collective-permute-done) | copy-start | bytes 270340
  54.9 10.3 %collective-permute-start.5 = (bf16[4,72,512]{2,1,0:T(8,128)(2,1)S(1)}, bf16[4,72,512]{2,1,0:T(8,128)(2,1)S(1)}, u32[]{:S(2)}, u32[]{:S(2)}) collective-permute-start(bf16[4,72,512]{2,1,0:T(8,128)(2,1)S(1)} %get-tuple-element.73), channel_id=1, source_target_pairs={{0,96},{32,0},{64,32},{96,64},{1,97},{33,1},{65,33},{97,65},{2,98}... | collective-permute-start | bytes 884744 | tf_op jit(solution)/shard_map/ppermute | solution.py:64
  59.6 9.1 %collective-permute-start.4 = (bf16[4,72,512]{2,1,0:T(8,128)(2,1)S(1)}, bf16[4,72,512]{2,1,0:T(8,128)(2,1)S(1)}, u32[]{:S(2)}, u32[]{:S(2)}) collective-permute-start(bf16[4,72,512]{2,1,0:T(8,128)(2,1)S(1)} %get-tuple-element.73), channel_id=1, source_target_pairs={{0,64},{32,96},{64,0},{96,32},{1,65},{33,97},{65,1},{97,33},{2,66}... | collective-permute-start | bytes 884744 | tf_op jit(solution)/shard_map/ppermute | solution.py:64
  61.8 10.2 %collective-permute-start.3 = (bf16[4,72,512]{2,1,0:T(8,128)(2,1)S(1)}, bf16[4,72,512]{2,1,0:T(8,128)(2,1)S(1)}, u32[]{:S(2)}, u32[]{:S(2)}) collective-permute-start(bf16[4,72,512]{2,1,0:T(8,128)(2,1)S(1)} %get-tuple-element.73), channel_id=1, source_target_pairs={{0,32},{32,64},{64,96},{96,0},{1,33},{33,65},{65,97},{97,1},{2,34}... | collective-permute-start | bytes 884744 | tf_op jit(solution)/shard_map/ppermute | solution.py:64
  72.2 28.0 %copy-start.3 = (bf16[4,4,72,512]{3,2,1,0:T(8,128)(2,1)}, bf16[4,4,72,512]{3,2,1,0:T(8,128)(2,1)S(1)}, u32[]{:S(2)}) copy-start(bf16[4,4,72,512]{3,2,1,0:T(8,128)(2,1)S(1)} %pad_maximum_fusion.2) | copy-start | bytes 3538948
  72.3 11.9 %collective-permute-start.8 = (bf16[16,40,512]{2,1,0:T(8,128)(2,1)S(1)}, bf16[16,40,512]{2,1,0:T(8,128)(2,1)S(1)}, u32[]{:S(2)}, u32[]{:S(2)}) collective-permute-start(bf16[16,40,512]{2,1,0:T(8,128)(2,1)S(1)} %get-tuple-element.53), channel_id=1, source_target_pairs={{0,24},{8,0},{16,8},{24,16},{1,25},{9,1},{17,9},{25,17},{2,26},{10... | collective-permute-start | bytes 1966088 | tf_op jit(solution)/shard_map/ppermute | solution.py:70
  76.7 12.6 %collective-permute-start.6 = (bf16[16,40,512]{2,1,0:T(8,128)(2,1)S(1)}, bf16[16,40,512]{2,1,0:T(8,128)(2,1)S(1)}, u32[]{:S(2)}, u32[]{:S(2)}) collective-permute-start(bf16[16,40,512]{2,1,0:T(8,128)(2,1)S(1)} %get-tuple-element.53), channel_id=1, source_target_pairs={{0,8},{8,16},{16,24},{24,0},{1,9},{9,17},{17,25},{25,1},{2,10},{10... | collective-permute-start | bytes 1966088 | tf_op jit(solution)/shard_map/ppermute | solution.py:70
  84.2 10.6 %collective-permute-start.9 = (bf16[8,40,512]{2,1,0:T(8,128)(2,1)S(1)}, bf16[8,40,512]{2,1,0:T(8,128)(2,1)S(1)}, u32[]{:S(2)}, u32[]{:S(2)}) collective-permute-start(bf16[8,40,512]{2,1,0:T(8,128)(2,1)S(1)} %slice.172), channel_id=1, source_target_pairs={{0,24},{8,0},{16,8},{24,16},{1,25},{9,1},{17,9},{25,17},{2,26},{10... | collective-permute-start | bytes 983048 | tf_op jit(solution)/shard_map/ppermute | solution.py:71
  89.3 10.8 %collective-permute-start.7 = (bf16[8,40,512]{2,1,0:T(8,128)(2,1)S(1)}, bf16[8,40,512]{2,1,0:T(8,128)(2,1)S(1)}, u32[]{:S(2)}, u32[]{:S(2)}) collective-permute-start(bf16[8,40,512]{2,1,0:T(8,128)(2,1)S(1)} %slice.171), channel_id=1, source_target_pairs={{0,8},{8,16},{16,24},{24,0},{1,9},{9,17},{17,25},{25,1},{2,10},{10... | collective-permute-start | bytes 983048 | tf_op jit(solution)/shard_map/ppermute | solution.py:71
  100.2 11.4 %copy-start.20 = (s32[1,4]{1,0:T(1,128)S(1)}, s32[1,4]{1,0:T(1,128)}, u32[]{:S(2)}) copy-start(s32[1,4]{1,0:T(1,128)} %param.15) | copy-start | bytes 52
  100.6 25.9 %copy-start.1 = (bf16[4,16,40,512]{3,2,1,0:T(8,128)(2,1)}, bf16[4,16,40,512]{3,2,1,0:T(8,128)(2,1)S(1)}, u32[]{:S(2)}) copy-start(bf16[4,16,40,512]{3,2,1,0:T(8,128)(2,1)S(1)} %pad_maximum_fusion) | copy-start | bytes 7864324
  100.6 15.7 %collective-permute-start.10 = (bf16[64,40,512]{2,1,0:T(8,128)(2,1)S(1)}, bf16[64,40,512]{2,1,0:T(8,128)(2,1)}, u32[]{:S(2)}, u32[]{:S(2)}) collective-permute-start(bf16[64,40,512]{2,1,0:T(8,128)(2,1)S(1)} %bitcast.117), channel_id=1, source_target_pairs={{0,4},{4,0},{1,5},{5,1},{2,6},{6,2},{3,7},{7,3},{8,12},{12,8},{9,1... | collective-permute-start | bytes 7864328 | tf_op jit(solution)/shard_map/ppermute | solution.py:76
  116.3 35.8 %collective-permute-start.11 = (bf16[16,32,512]{2,1,0:T(8,128)(2,1)}, bf16[16,32,512]{2,1,0:T(8,128)(2,1)}, u32[]{:S(2)}, u32[]{:S(2)}) collective-permute-start(bf16[16,32,512]{2,1,0:T(8,128)(2,1)} %slice.173), channel_id=1, source_target_pairs={{0,8},{8,16},{16,24},{24,0},{1,9},{9,17},{17,25},{25,1},{2,10},{10... | collective-permute-start | bytes 1572872 | tf_op jit(solution)/shard_map/ppermute | solution.py:64
  118.2 33.9 %collective-permute-start.12 = (bf16[16,32,512]{2,1,0:T(8,128)(2,1)}, bf16[16,32,512]{2,1,0:T(8,128)(2,1)}, u32[]{:S(2)}, u32[]{:S(2)}) collective-permute-start(bf16[16,32,512]{2,1,0:T(8,128)(2,1)} %slice.173), channel_id=1, source_target_pairs={{0,16},{8,24},{16,0},{24,8},{1,17},{9,25},{17,1},{25,9},{2,18},{10... | collective-permute-start | bytes 1572872 | tf_op jit(solution)/shard_map/ppermute | solution.py:64
  120.5 31.5 %collective-permute-start.13 = (bf16[16,32,512]{2,1,0:T(8,128)(2,1)}, bf16[16,32,512]{2,1,0:T(8,128)(2,1)}, u32[]{:S(2)}, u32[]{:S(2)}) collective-permute-start(bf16[16,32,512]{2,1,0:T(8,128)(2,1)} %slice.173), channel_id=1, source_target_pairs={{0,24},{8,0},{16,8},{24,16},{1,25},{9,1},{17,9},{25,17},{2,26},{10... | collective-permute-start | bytes 1572872 | tf_op jit(solution)/shard_map/ppermute | solution.py:64
  152.0 7.8 %copy-start.4 = (bf16[88,512]{1,0:T(8,128)(2,1)S(1)}, bf16[88,512]{1,0:T(8,128)(2,1)}, u32[]{:S(2)}) copy-start(bf16[88,512]{1,0:T(8,128)(2,1)} %pick_rows.1) | copy-start | bytes 270340
  152.0 7.8 %copy-start.6 = (bf16[88,512]{1,0:T(8,128)(2,1)S(1)}, bf16[88,512]{1,0:T(8,128)(2,1)}, u32[]{:S(2)}) copy-start(bf16[88,512]{1,0:T(8,128)(2,1)} %copy-done.5) | copy-start | bytes 270340
  153.9 9.9 %copy-start.2 = (bf16[4,16,32,512]{3,2,1,0:T(8,128)(2,1)}, bf16[4,16,32,512]{3,2,1,0:T(8,128)(2,1)S(1)}, u32[]{:S(2)}) copy-start(bf16[4,16,32,512]{3,2,1,0:T(8,128)(2,1)S(1)} %pad_maximum_fusion.1) | copy-start | bytes 6291460
  153.9 9.9 %collective-permute-start.14 = (bf16[64,32,512]{2,1,0:T(8,128)(2,1)S(1)}, bf16[64,32,512]{2,1,0:T(8,128)(2,1)}, u32[]{:S(2)}, u32[]{:S(2)}) collective-permute-start(bf16[64,32,512]{2,1,0:T(8,128)(2,1)S(1)} %bitcast.119), channel_id=1, source_target_pairs={{0,4},{4,0},{1,5},{5,1},{2,6},{6,2},{3,7},{7,3},{8,12},{12,8},{9,1... | collective-permute-start | bytes 6291464 | tf_op jit(solution)/shard_map/ppermute | solution.py:76
  171.0 16.1 %collective-permute-start.17 = (bf16[256,1024]{1,0:T(8,128)(2,1)}, bf16[256,1024]{1,0:T(8,128)(2,1)}, u32[]{:S(2)}, u32[]{:S(2)}) collective-permute-start(bf16[256,1024]{1,0:T(8,128)(2,1)} %get-tuple-element.25), channel_id=1, source_target_pairs={{0,387},{128,0},{256,128},{384,256},{1,384},{129,1},{257,129},{385... | collective-permute-start | bytes 1572872 | tf_op jit(solution)/shard_map/ppermute | solution.py:392
  175.8 17.6 %collective-permute-start.15 = (bf16[256,1024]{1,0:T(8,128)(2,1)}, bf16[256,1024]{1,0:T(8,128)(2,1)}, u32[]{:S(2)}, u32[]{:S(2)}) collective-permute-start(bf16[256,1024]{1,0:T(8,128)(2,1)} %get-tuple-element.25), channel_id=1, source_target_pairs={{0,128},{128,256},{256,384},{384,1},{1,129},{129,257},{257,385},{3... | collective-permute-start | bytes 1572872 | tf_op jit(solution)/shard_map/ppermute | solution.py:391
  180.7 15.7 %copy-start.8 = (bf16[256,1024]{1,0:T(8,128)(2,1)S(1)}, bf16[256,1024]{1,0:T(8,128)(2,1)}, u32[]{:S(2)}) copy-start(bf16[256,1024]{1,0:T(8,128)(2,1)} %get-tuple-element.25) | copy-start | bytes 1572868
  188.1 9.7 %collective-permute-start.18 = (bf16[128,1024]{1,0:T(8,128)(2,1)S(1)}, bf16[128,1024]{1,0:T(8,128)(2,1)S(1)}, u32[]{:S(2)}, u32[]{:S(2)}) collective-permute-start(bf16[128,1024]{1,0:T(8,128)(2,1)S(1)} %get-tuple-element.65), channel_id=1, source_target_pairs={{0,387},{128,0},{256,128},{384,256},{1,384},{129,1},{257,129},{385... | collective-permute-start | bytes 786440 | tf_op jit(solution)/shard_map/ppermute | solution.py:394
  194.5 9.4 %collective-permute-start.16 = (bf16[128,1024]{1,0:T(8,128)(2,1)S(1)}, bf16[128,1024]{1,0:T(8,128)(2,1)S(1)}, u32[]{:S(2)}, u32[]{:S(2)}) collective-permute-start(bf16[128,1024]{1,0:T(8,128)(2,1)S(1)} %get-tuple-element.62), channel_id=1, source_target_pairs={{0,128},{128,256},{256,384},{384,1},{1,129},{129,257},{257,385},{3... | collective-permute-start | bytes 786440 | tf_op jit(solution)/shard_map/ppermute | solution.py:393
  206.1 55.0 %copy-start.10 = (bf16[1,2048,176]{1,2,0:T(8,128)(2,1)S(1)}, bf16[1,2048,176]{1,2,0:T(8,128)(2,1)}, u32[]{:S(2)}) copy-start(bf16[1,2048,176]{1,2,0:T(8,128)(2,1)} %param.26) | copy-start | bytes 2162692
  257.9 10.0 %collective-permute-start.19 = (bf16[1792,1024]{1,0:T(8,128)(2,1)}, bf16[1792,1024]{1,0:T(8,128)(2,1)}, u32[]{:S(2)}, u32[]{:S(2)}) collective-permute-start(bf16[1792,1024]{1,0:T(8,128)(2,1)} %bitcast.60), channel_id=1, source_target_pairs={{0,4},{4,0},{1,5},{5,1},{2,6},{6,2},{3,7},{7,3},{8,12},{12,8},{9,1... | collective-permute-start | bytes 11010056 | tf_op jit(solution)/shard_map/ppermute | solution.py:76
  271.4 75.0 %copy-start.7 = (bf16[1,704,512]{2,1,0:T(8,128)(2,1)S(1)}, bf16[1,704,512]{2,1,0:T(8,128)(2,1)}, u32[]{:S(2)}) copy-start(bf16[1,704,512]{2,1,0:T(8,128)(2,1)} %param.27) | copy-start | bytes 2162692
  274.9 64.7 %copy-start.18 = (bf16[176,1792]{1,0:T(8,128)(2,1)}, bf16[176,1792]{1,0:T(8,128)(2,1)S(1)}, u32[]{:S(2)}) copy-start(bf16[176,1792]{1,0:T(8,128)(2,1)S(1)} %fusion.1) | copy-start | bytes 1892356
  274.9 59.7 %collective-permute-start.21 = (bf16[176,1792]{1,0:T(8,128)(2,1)S(1)}, bf16[176,1792]{1,0:T(8,128)(2,1)S(1)}, u32[]{:S(2)}, u32[]{:S(2)}) collective-permute-start(bf16[176,1792]{1,0:T(8,128)(2,1)S(1)} %fusion.1), channel_id=1, source_target_pairs={{0,3},{1,0},{2,1},{3,2},{4,7},{5,4},{6,5},{7,6},{8,11},{9,8},{10,9... | collective-permute-start | bytes 1892360 | tf_op jit(solution)/shard_map/ppermute | solution.py:413
  277.1 62.4 %collective-permute-start.20 = (bf16[176,1792]{1,0:T(8,128)(2,1)S(1)}, bf16[176,1792]{1,0:T(8,128)(2,1)S(1)}, u32[]{:S(2)}, u32[]{:S(2)}) collective-permute-start(bf16[176,1792]{1,0:T(8,128)(2,1)S(1)} %fusion.1), channel_id=1, source_target_pairs={{0,1},{1,2},{2,3},{3,0},{4,5},{5,6},{6,7},{7,4},{8,9},{9,10},{10,1... | collective-permute-start | bytes 1892360 | tf_op jit(solution)/shard_map/ppermute | solution.py:412
  334.7 4.9 %copy-start.11 = (bf16[176,1792]{1,0:T(8,128)(2,1)}, bf16[176,1792]{1,0:T(8,128)(2,1)S(1)}, u32[]{:S(2)}) copy-start(bf16[176,1792]{1,0:T(8,128)(2,1)S(1)} %collective-permute-done.21) | copy-start | bytes 1892356
  334.7 27.6 %collective-permute-start.23 = (bf16[88,1792]{1,0:T(8,128)(2,1)S(1)}, bf16[88,1792]{1,0:T(8,128)(2,1)S(1)}, u32[]{:S(2)}, u32[]{:S(2)}) collective-permute-start(bf16[88,1792]{1,0:T(8,128)(2,1)S(1)} %slice.191), channel_id=1, source_target_pairs={{0,3},{1,0},{2,1},{3,2},{4,7},{5,4},{6,5},{7,6},{8,11},{9,8},{10,9... | collective-permute-start | bytes 946184 | tf_op jit(solution)/shard_map/ppermute | solution.py:415
  340.4 29.7 %collective-permute-start.22 = (bf16[88,1792]{1,0:T(8,128)(2,1)S(1)}, bf16[88,1792]{1,0:T(8,128)(2,1)}, u32[]{:S(2)}, u32[]{:S(2)}) collective-permute-start(bf16[88,1792]{1,0:T(8,128)(2,1)S(1)} %slice.190), channel_id=1, source_target_pairs={{0,1},{1,2},{2,3},{3,0},{4,5},{5,6},{6,7},{7,4},{8,9},{9,10},{10,1... | collective-permute-start | bytes 946184 | tf_op jit(solution)/shard_map/ppermute | solution.py:414
  346.4 25.3 %copy-start.12 = (bf16[176,1792]{1,0:T(8,128)(2,1)S(1)}, bf16[176,1792]{1,0:T(8,128)(2,1)}, u32[]{:S(2)}) copy-start(bf16[176,1792]{1,0:T(8,128)(2,1)} %copy-done.11) | copy-start | bytes 1892356
  346.4 25.3 %copy-start.14 = (bf16[176,1792]{1,0:T(8,128)(2,1)S(1)}, bf16[176,1792]{1,0:T(8,128)(2,1)}, u32[]{:S(2)}) copy-start(bf16[176,1792]{1,0:T(8,128)(2,1)} %copy-done.13) | copy-start | bytes 1892356
  346.4 25.3 %copy-start.19 = (bf16[176,1792]{1,0:T(8,128)(2,1)S(1)}, bf16[176,1792]{1,0:T(8,128)(2,1)}, u32[]{:S(2)}) copy-start(bf16[176,1792]{1,0:T(8,128)(2,1)} %copy-done.18) | copy-start | bytes 1892356
  374.4 4.8 %collective-permute-start.24 = (bf16[1792,256]{1,0:T(8,128)(2,1)}, bf16[1792,256]{1,0:T(8,128)(2,1)}, u32[]{:S(2)}, u32[]{:S(2)}) collective-permute-start(bf16[1792,256]{1,0:T(8,128)(2,1)} %constant_dynamic-slice_fusion), channel_id=1, source_target_pairs={{0,4},{4,0},{1,5},{5,1},{2,6},{6,2},{3,7},{7,3},{8,12},{12,8},{9,1... | collective-permute-start | bytes 2752520 | tf_op jit(solution)/shard_map/ppermute | solution.py:76
  381.5 19.2 %all-to-all-start.1 = ((bf16[32,56,256]{2,1,0:T(8,128)(2,1)}), bf16[32,56,256]{2,1,0:T(8,128)(2,1)S(1)}, u32[]{:S(2)}, u32[]{:S(2)}) async-start(bf16[32,56,256]{2,1,0:T(8,128)(2,1)} %bitcast.68), calls=%async_computation.1 | async-start | bytes 1835008 | tf_op jit(solution)/shard_map/all_to_all | solution.py:428
  400.8 10.8 %copy-start.16 = (bf16[128,128]{1,0:T(8,128)(2,1)S(1)}, bf16[128,128]{1,0:T(8,128)(2,1)}, u32[]{:S(2)}) copy-start(bf16[128,128]{1,0:T(8,128)(2,1)} %get-tuple-element.29) | copy-start | bytes 98308
  400.8 10.9 %copy-start.15 = (bf16[128,512]{1,0:T(8,128)(2,1)S(1)}, bf16[128,512]{1,0:T(8,128)(2,1)}, u32[]{:S(2)}) copy-start(bf16[128,512]{1,0:T(8,128)(2,1)} %get-tuple-element.28) | copy-start | bytes 393220
  401.5 16.4 %copy-start.17 = (bf16[128,512]{1,0:T(8,128)(2,1)S(1)}, bf16[128,512]{1,0:T(8,128)(2,1)}, u32[]{:S(2)}) copy-start(bf16[128,512]{1,0:T(8,128)(2,1)} %get-tuple-element.24) | copy-start | bytes 393220
  402.5 10.0 %collective-permute-start.27 = (bf16[2,128,256]{2,1,0:T(8,128)(2,1)S(1)}, bf16[2,128,256]{2,1,0:T(8,128)(2,1)S(1)}, u32[]{:S(2)}, u32[]{:S(2)}) collective-permute-start(bf16[2,128,256]{2,1,0:T(8,128)(2,1)S(1)} %get-tuple-element.58), channel_id=1, source_target_pairs={{0,128},{128,256},{256,384},{384,0},{1,129},{129,257},{257,385},{3... | collective-permute-start | bytes 393224 | tf_op jit(solution)/shard_map/ppermute | solution.py:438
  404.5 12.4 %collective-permute-start.26 = (bf16[2,128,256]{2,1,0:T(8,128)(2,1)S(1)}, bf16[2,128,256]{2,1,0:T(8,128)(2,1)S(1)}, u32[]{:S(2)}, u32[]{:S(2)}) collective-permute-start(bf16[2,128,256]{2,1,0:T(8,128)(2,1)S(1)} %get-tuple-element.59), channel_id=1, source_target_pairs={{0,256},{128,384},{256,0},{384,128},{1,257},{129,385},{257,1},{385... | collective-permute-start | bytes 393224 | tf_op jit(solution)/shard_map/ppermute | solution.py:438
  406.4 10.5 %collective-permute-start.25 = (bf16[2,128,256]{2,1,0:T(8,128)(2,1)S(1)}, bf16[2,128,256]{2,1,0:T(8,128)(2,1)S(1)}, u32[]{:S(2)}, u32[]{:S(2)}) collective-permute-start(bf16[2,128,256]{2,1,0:T(8,128)(2,1)S(1)} %get-tuple-element.57), channel_id=1, source_target_pairs={{0,384},{128,0},{256,128},{384,256},{1,385},{129,1},{257,129},{385... | collective-permute-start | bytes 393224 | tf_op jit(solution)/shard_map/ppermute | solution.py:438
  (2 other events, 1.8 us)

commit v8 on v7

--- a/solution.py
+++ b/solution.py
@@ -244,7 +244,7 @@
 def mix(place, everything, attended, mine, theirs, moe_gain):
     def kernel(
         place_ref, in_ref, attended_ref, mine_ref, theirs_ref, gain_ref,
-        moe_ref, cols_ref, server_ref, w_first, w_second,
+        left_ref, right_ref, cols_ref, server_ref, w_first, w_second,
     ):
         c, t = place_ref[3], place_ref[4]
 
@@ -271,8 +271,8 @@
             cols = jnp.where(t == k, mixed[:, k * 512 : (k + 1) * 512], cols)
         cols_ref[...] = cols.astype(BF)
         moe = rms_norm(mixed, gain_ref[...]).astype(BF)
-        moe_ref[0:128, :] = moe[:, 0:1024]
-        moe_ref[128:256, :] = moe[:, 1024:2048]
+        left_ref[...] = moe[:, 0:1024]
+        right_ref[...] = moe[:, 1024:2048]
 
     def whole(*shape):
         return pl.BlockSpec(shape, lambda i: (0,) * len(shape))
@@ -281,12 +281,13 @@
         kernel,
         grid=(1,),
         out_shape=[
-            jax.ShapeDtypeStruct((256, 1024), BF),
+            jax.ShapeDtypeStruct((128, 1024), BF),
+            jax.ShapeDtypeStruct((128, 1024), BF),
             jax.ShapeDtypeStruct((128, 512), BF),
             jax.ShapeDtypeStruct((2048, 256), BF),
         ],
         in_specs=[SMEM, whole(128, 2048), whole(128, 1024), VMEM, VMEM, whole(1, 2048)],
-        out_specs=[whole(256, 1024), whole(128, 512), whole(2048, 256)],
+        out_specs=[whole(128, 1024), whole(128, 1024), whole(128, 512), whole(2048, 256)],
         scratch_shapes=[pltpu.VMEM((2048, 512), BF), pltpu.VMEM((2048, 512), BF)],
         name="mix",
     )(place, everything, attended, mine, theirs, moe_gain.reshape(1, 2048))
@@ -349,7 +350,7 @@
     attended_full, *second_parts = lax.optimization_barrier((attended_full, *second_parts))
     second_mine = jnp.stack(second_parts).reshape(64, 32, 512)
     second_theirs = other_core(second_mine)
-    moe_halves, mixed_cols, output_block = mix(
+    left, right, mixed_cols, output_block = mix(
         place, everything, attended_full, second_mine, second_theirs, moe_gain
     )
 
@@ -388,14 +389,16 @@
     at_z = [(z % 4) * 4 + z // 4 for z in range(16)]
     z_up = [(at_z[z], at_z[(z + 1) % 16]) for z in range(16)]
     z_down = [(at_z[z], at_z[(z + 15) % 16]) for z in range(16)]
-    back_one = lax.ppermute(moe_halves, ("zl", T), z_up)
-    on_one = lax.ppermute(moe_halves, ("zl", T), z_down)
-    far_left = lax.ppermute(back_one[:TOK], ("zl", T), z_up)
-    far_right = lax.ppermute(on_one[TOK:], ("zl", T), z_down)
+    back_left = lax.ppermute(left, ("zl", T), z_up)
+    on_right = lax.ppermute(right, ("zl", T), z_down)
+    back_right = lax.ppermute(right, ("zl", T), z_up)
+    on_left = lax.ppermute(left, ("zl", T), z_down)
+    far_left = lax.ppermute(back_left, ("zl", T), z_up)
+    far_right = lax.ppermute(on_right, ("zl", T), z_down)
     tokens = jnp.stack(
         [
-            jnp.concatenate([moe_halves[:TOK], back_one[:TOK], far_left, on_one[:TOK]]),
-            jnp.concatenate([moe_halves[TOK:], back_one[TOK:], far_right, on_one[TOK:]]),
+            jnp.concatenate([left, back_left, far_left, on_left]),
+            jnp.concatenate([right, back_right, far_right, on_right]),
         ]
     )
     outgoing = lax.dot_general(
@@ -409,10 +412,13 @@
     up_part = rows_by(up_mine, mine) + rows_by(up_other, theirs)
     own = (jax.nn.silu(gate_part) * up_part).astype(BF)
 
-    below = lax.ppermute(own, T, UP)
-    above = lax.ppermute(own, T, DOWN)
-    far_first = lax.ppermute(below[:88], T, UP)
-    far_second = lax.ppermute(above[88:], T, DOWN)
+    first, second = own[:88], own[88:]
+    below_first = lax.ppermute(first, T, UP)
+    above_second = lax.ppermute(second, T, DOWN)
+    below_second = lax.ppermute(second, T, UP)
+    above_first = lax.ppermute(first, T, DOWN)
+    far_first = lax.ppermute(below_first, T, UP)
+    far_second = lax.ppermute(above_second, T, DOWN)
 
     def out_of(pieces, at):
         rows = jnp.concatenate(pieces, axis=0)
@@ -421,7 +427,7 @@
             preferred_element_type=F32,
         )
 
-    half_out = (out_of([own, below, above], 0) + out_of([far_first, far_second], 528)).astype(BF)
+    half_out = (out_of([own, below_first, below_second, above_first, above_second], 0) + out_of([far_first, far_second], 528)).astype(BF)
     keep = lax.dynamic_slice_in_dim(half_out, core * 256, 256, 1)
     give = lax.dynamic_slice_in_dim(half_out, (1 - core) * 256, 256, 1)
     both = (keep.astype(F32) + other_core(give).astype(F32)).astype(BF)

time: 421 us -> 416 us (0.988)
  waiting for transfers between devices: 143 us -> 123 us
  starting transfers between devices: 108 us -> 119 us
    ppermute x8 -> x12, waiting for transfers between devices: 87.8 us -> 68.6 us  [the longest x1 56.8 us: body(): below_first = lax.ppermute(first, T, UP)]
    ppermute x8 -> x12, starting transfers between devices: 33.9 us -> 45.2 us  [the longest x1 5.03 us: body(): above_first = lax.ppermute(first, T, DOWN)]
    ppermute x1, waiting for transfers between devices: 0.01 us -> 9.07 us  [ring(): lax.ppermute(block, axis, UP)]
    ppermute x1, waiting for transfers between devices: 5.58 us -> 0.01 us  [ring(): lax.ppermute(block, axis, DOWN)]
  transfers between devices with their start and end apart: 29 -> 33, of which waited for: 19 -> 18; matrix products, arithmetic and copies ran while one was open for 4% -> 6% of each run, Pallas kernels for 2% -> 2%
where the time goes in v8:
time: 416 us; the launch traced here: 414 us
  waiting for transfers between devices  123 us (30%)
  starting transfers between devices  119 us (29%)
  blocking collectives  106 us (25%)
  matrix products  22.5 us (5%)
  Pallas kernels  17.7 us (4%)
  other arithmetic  14.7 us (4%)
  local copies, waits for them, and re-layouts  9.17 us (2%)
    ppermute x1, waiting for transfers between devices, body(): below_first = lax.ppermute(first, T, UP)  56.8 us
    all_to_all x1, blocking collectives, body(): lax.all_to_all(outgoing.reshape(2 * LAYER_ROWS, D // 2), LAYER, split_axi...  52.8 us
    all_gather x1, blocking collectives, body(): everything = lax.all_gather(packed, T, axis=1, tiled=True)  35.8 us
    ppermute x9, starting transfers between devices, shifted(): lax.ppermute(block, axis, [(j, (j + s) % 4) for j in range(4)])  29 us
    ppermute x4, starting transfers between devices, other_core(): return lax.ppermute(block, 'c', [(0, 1), (1, 0)])  20.5 us
    all_gather x1, blocking collectives, body(): attended_full = lax.all_gather(attended, T, axis=1, tiled=True)  17.6 us
    all_to_all x1, waiting for transfers between devices, body(): lax.all_to_all(both, LAYER, split_axis=0, concat_axis=0, tiled=True)  15.2 us
    dot_general x4, matrix products, rows_by(): lax.dot_general(weight, rows, (((0,), (1,)), ((), ())), preferred_element...  14.7 us
  transfers between devices with their start and end apart: 33, of which 18 were waited for; matrix products, arithmetic and copies ran while one was open for 6% of the time, Pallas kernels for 2%

profile of v8, /device:TPU:1, one launch (start us, length us, event | category | flops | bytes accessed | tf_op | source)
XLA Modules:
  0.0 413.6 jit_solution(10748560673170733363)
XLA Ops:
  2.4 35.8 %all_gather.6.in_ref = bf16[160,2048]{1,0:T(8,128)(2,1)} all-gather(bf16[160,512]{1,0:T(8,128)(2,1)} %pack_rows.1), channel_id=1, replica_groups=mesh['zl'=4,'y'=4,'x'=4,'c'=2,'t'=4] {'t'}, dimensions={1}, use_global_device_ids=true | all-gather | bytes 819200 | tf_op jit(solution)/shard_map/all_gather | solution.py:317
  40.4 3.8 collective-permute-start.2
  48.4 3.4 collective-permute-done
  54.9 3.2 collective-permute-start.3
  58.1 4.5 %collective-permute-start.4 = (bf16[4,72,512]{2,1,0:T(8,128)(2,1)S(1)}, bf16[4,72,512]{2,1,0:T(8,128)(2,1)S(1)}, u32[]{:S(2)}, u32[]{:S(2)}) collective-permute-start(bf16[4,72,512]{2,1,0:T(8,128)(2,1)S(1)} %get-tuple-element.71), channel_id=1, source_target_pairs={{0,64},{32,96},{64,0},{96,32},{1,65},{33,97},{65,1},{97,33},{2,66}... | collective-permute-start | bytes 884744 | tf_op jit(solution)/shard_map/ppermute | solution.py:64
  62.6 3.0 collective-permute-start.5
  65.6 4.6 %collective-permute-done.4 = bf16[4,72,512]{2,1,0:T(8,128)(2,1)S(1)} collective-permute-done((bf16[4,72,512]{2,1,0:T(8,128)(2,1)S(1)}, bf16[4,72,512]{2,1,0:T(8,128)(2,1)S(1)}, u32[]{:S(2)}, u32[]{:S(2)}) %collective-permute-start.4) | collective-permute-done | bytes 294944 | tf_op jit(solution)/shard_map/ppermute | solution.py:64
  70.3 3.1 collective-permute-done.5
  73.6 3.1 collective-permute-start.6
  76.8 3.4 collective-permute-start.8
  80.1 9.1 %collective-permute-done.6 = bf16[16,40,512]{2,1,0:T(8,128)(2,1)S(1)} collective-permute-done((bf16[16,40,512]{2,1,0:T(8,128)(2,1)S(1)}, bf16[16,40,512]{2,1,0:T(8,128)(2,1)S(1)}, u32[]{:S(2)}, u32[]{:S(2)}) %collective-permute-start.6) | collective-permute-done | bytes 655392 | tf_op jit(solution)/shard_map/ppermute | solution.py:70
  91.2 4.6 %collective-permute-start.9 = (bf16[8,40,512]{2,1,0:T(8,128)(2,1)S(1)}, bf16[8,40,512]{2,1,0:T(8,128)(2,1)S(1)}, u32[]{:S(2)}, u32[]{:S(2)}) collective-permute-start(bf16[8,40,512]{2,1,0:T(8,128)(2,1)S(1)} %slice.146), channel_id=1, source_target_pairs={{0,24},{8,0},{16,8},{24,16},{1,25},{9,1},{17,9},{25,17},{2,26},{10... | collective-permute-start | bytes 983048 | tf_op jit(solution)/shard_map/ppermute | solution.py:71
  95.8 2.5 collective-permute-done.7
  100.2 7.7 %collective-permute-start.10 = (bf16[64,40,512]{2,1,0:T(8,128)(2,1)S(1)}, bf16[64,40,512]{2,1,0:T(8,128)(2,1)}, u32[]{:S(2)}, u32[]{:S(2)}) collective-permute-start(bf16[64,40,512]{2,1,0:T(8,128)(2,1)S(1)} %bitcast.120), channel_id=1, source_target_pairs={{0,4},{4,0},{1,5},{5,1},{2,6},{6,2},{3,7},{7,3},{8,12},{12,8},{9,1... | collective-permute-start | bytes 7864328 | tf_op jit(solution)/shard_map/ppermute | solution.py:76
  112.6 2.6 collective-permute-start.11
  115.2 5.8 %collective-permute-start.12 = (bf16[16,32,512]{2,1,0:T(8,128)(2,1)}, bf16[16,32,512]{2,1,0:T(8,128)(2,1)}, u32[]{:S(2)}, u32[]{:S(2)}) collective-permute-start(bf16[16,32,512]{2,1,0:T(8,128)(2,1)} %slice.147), channel_id=1, source_target_pairs={{0,16},{8,24},{16,0},{24,8},{1,17},{9,25},{17,1},{25,9},{2,18},{10... | collective-permute-start | bytes 1572872 | tf_op jit(solution)/shard_map/ppermute | solution.py:64
  124.8 7.2 %attention.1 = (bf16[128,256]{1,0:T(8,128)(2,1)}, bf16[128,512]{1,0:T(8,128)(2,1)}, bf16[128,128]{1,0:T(8,128)(2,1)}, bf16[512,512]{1,0:T(8,128)(2,1)}) custom-call(s32[5]{0:T(128)} %stack.113.place_ref, bf16[160,2048]{1,0:T(8,128)(2,1)} %all_gather.6.in_ref, bf16[64,40,512]{2,1,0:T(8,128)(2,1)} %bitcast.121, ...), custom_call_target="tpu_custom_call" | custom-call | tf_op jit(solution)/shard_map/attention/pallas_call | solution.py:222
  132.0 17.6 %all_gather.7.attended_ref = bf16[128,1024]{1,0:T(8,128)(2,1)} all-gather(bf16[128,256]{1,0:T(8,128)(2,1)} %get-tuple-element.18), channel_id=1, replica_groups=mesh['zl'=4,'y'=4,'x'=4,'c'=2,'t'=4] {'t'}, dimensions={1}, use_global_device_ids=true | all-gather | bytes 327680 | tf_op jit(solution)/shard_map/all_gather | solution.py:349
  151.4 6.2 %collective-permute-start.14 = (bf16[64,32,512]{2,1,0:T(8,128)(2,1)S(1)}, bf16[64,32,512]{2,1,0:T(8,128)(2,1)}, u32[]{:S(2)}, u32[]{:S(2)}) collective-permute-start(bf16[64,32,512]{2,1,0:T(8,128)(2,1)S(1)} %bitcast.122), channel_id=1, source_target_pairs={{0,4},{4,0},{1,5},{5,1},{2,6},{6,2},{3,7},{7,3},{8,12},{12,8},{9,1... | collective-permute-start | bytes 6291464 | tf_op jit(solution)/shard_map/ppermute | solution.py:76
  158.2 3.4 collective-permute-done.14.theirs_ref
  161.6 7.1 %mix.1 = (bf16[128,1024]{1,0:T(8,128)(2,1)}, bf16[128,1024]{1,0:T(8,128)(2,1)}, bf16[128,512]{1,0:T(8,128)(2,1)}, bf16[2048,256]{1,0:T(8,128)(2,1)}) custom-call(s32[5]{0:T(128)} %stack.113.place_ref, bf16[160,2048]{1,0:T(8,128)(2,1)} %all_gather.6.in_ref, bf16[128,1024]{1,0:T(8,128)(2,1)} %all_gather.7.attended_ref, bf16[64,32,512]{2,1,0:T(8,128)(2,1)} %bitcast.123, ...), custom_call_target="tpu_custom_call" | custom-call | tf_op jit(solution)/shard_map/mix/pallas_call | solution.py:280
  170.6 4.6 %collective-permute-start.19 = (bf16[128,1024]{1,0:T(8,128)(2,1)}, bf16[128,1024]{1,0:T(8,128)(2,1)}, u32[]{:S(2)}, u32[]{:S(2)}) collective-permute-start(bf16[128,1024]{1,0:T(8,128)(2,1)} %get-tuple-element.27), channel_id=1, source_target_pairs={{0,387},{128,0},{256,128},{384,256},{1,384},{129,1},{257,129},{385... | collective-permute-start | bytes 786440 | tf_op jit(solution)/shard_map/ppermute | solution.py:393
  177.2 3.4 collective-permute-start.18
  182.5 4.6 %collective-permute-start.20 = (bf16[128,1024]{1,0:T(8,128)(2,1)}, bf16[128,1024]{1,0:T(8,128)(2,1)}, u32[]{:S(2)}, u32[]{:S(2)}) collective-permute-start(bf16[128,1024]{1,0:T(8,128)(2,1)} %collective-permute-done.19), channel_id=1, source_target_pairs={{0,387},{128,0},{256,128},{384,256},{1,384},{129,1},{257,129},{385... | collective-permute-start | bytes 786440 | tf_op jit(solution)/shard_map/ppermute | solution.py:397
  187.1 2.4 add_convert_fusion.3
  190.1 3.0 collective-permute-done.16
  197.6 52.8 %all_to_all.21 = bf16[32,56,1024]{2,1,0:T(8,128)(2,1)} all-to-all(bf16[32,56,1024]{2,1,0:T(8,128)(2,1)S(1)} %bitcast.126), channel_id=1, replica_groups=mesh['zl'=4,'y'=4,'x'=4,'c'=2,'t'=4] {'c','y','x'}, dimensions={0} | all-to-all | bytes 7340032 | tf_op jit(solution)/shard_map/all_to_all | solution.py:407
  250.5 3.2 collective-permute-start.21
  253.7 3.4 fusion.21
  257.1 3.4 fusion.18
  260.5 3.4 convolution_add_fusion.1
  263.9 4.4 %constant_dynamic-update-slice_fusion.4 = (bf16[528,1792]{1,0:T(8,128)(2,1)}, bf16[176,1792]{1,0:T(8,128)(2,1)S(1)}) fusion(f32[176,1792]{1,0:T(8,128)S(1)} %fusion.18, bf16[1792,1024]{1,0:T(8,128)(2,1)} %collective-permute-done.21, bf16[1,2048,176]{1,2,0:T(8,128)(2,1)S(1)} %copy-done, s32[]{:T(128)S(6)} %select_n.141, ...), kind=kOutput, calls=%fused_computation.103 | convolution fusion | flops 648130560 | bytes 7815172 | tf_op jit(solution)/shard_map/dot_general | solution.py:387
  268.4 4.2 %collective-permute-start.22 = (bf16[88,1792]{1,0:T(8,128)(2,1)S(1)}, bf16[88,1792]{1,0:T(8,128)(2,1)S(1)}, u32[]{:S(2)}, u32[]{:S(2)}) collective-permute-start(bf16[88,1792]{1,0:T(8,128)(2,1)S(1)} %get-tuple-element.60), channel_id=1, source_target_pairs={{0,1},{1,2},{2,3},{3,0},{4,5},{5,6},{6,7},{7,4},{8,9},{9,10},{10,1... | collective-permute-start | bytes 946184 | tf_op jit(solution)/shard_map/ppermute | solution.py:416
  272.7 5.0 %collective-permute-start.23 = (bf16[88,1792]{1,0:T(8,128)(2,1)S(1)}, bf16[88,1792]{1,0:T(8,128)(2,1)S(1)}, u32[]{:S(2)}, u32[]{:S(2)}) collective-permute-start(bf16[88,1792]{1,0:T(8,128)(2,1)S(1)} %get-tuple-element.59), channel_id=1, source_target_pairs={{0,1},{1,2},{2,3},{3,0},{4,5},{5,6},{6,7},{7,4},{8,9},{9,10},{10,1... | collective-permute-start | bytes 946184 | tf_op jit(solution)/shard_map/ppermute | solution.py:418
  277.7 4.2 %collective-permute-start.25 = (bf16[88,1792]{1,0:T(8,128)(2,1)S(1)}, bf16[88,1792]{1,0:T(8,128)(2,1)S(1)}, u32[]{:S(2)}, u32[]{:S(2)}) collective-permute-start(bf16[88,1792]{1,0:T(8,128)(2,1)S(1)} %get-tuple-element.59), channel_id=1, source_target_pairs={{0,3},{1,0},{2,1},{3,2},{4,7},{5,4},{6,5},{7,6},{8,11},{9,8},{10,9... | collective-permute-start | bytes 946184 | tf_op jit(solution)/shard_map/ppermute | solution.py:417
  281.9 5.0 %collective-permute-start.24 = (bf16[88,1792]{1,0:T(8,128)(2,1)S(1)}, bf16[88,1792]{1,0:T(8,128)(2,1)S(1)}, u32[]{:S(2)}, u32[]{:S(2)}) collective-permute-start(bf16[88,1792]{1,0:T(8,128)(2,1)S(1)} %get-tuple-element.60), channel_id=1, source_target_pairs={{0,3},{1,0},{2,1},{3,2},{4,7},{5,4},{6,5},{7,6},{8,11},{9,8},{10,9... | collective-permute-start | bytes 946184 | tf_op jit(solution)/shard_map/ppermute | solution.py:419
  287.0 56.8 %collective-permute-done.22 = bf16[88,1792]{1,0:T(8,128)(2,1)S(1)} collective-permute-done((bf16[88,1792]{1,0:T(8,128)(2,1)S(1)}, bf16[88,1792]{1,0:T(8,128)(2,1)S(1)}, u32[]{:S(2)}, u32[]{:S(2)}) %collective-permute-start.22) | collective-permute-done | bytes 315424 | tf_op jit(solution)/shard_map/ppermute | solution.py:416
  343.8 4.6 %collective-permute-start.26 = (bf16[88,1792]{1,0:T(8,128)(2,1)S(1)}, bf16[88,1792]{1,0:T(8,128)(2,1)S(1)}, u32[]{:S(2)}, u32[]{:S(2)}) collective-permute-start(bf16[88,1792]{1,0:T(8,128)(2,1)S(1)} %collective-permute-done.22), channel_id=1, source_target_pairs={{0,1},{1,2},{2,3},{3,0},{4,5},{5,6},{6,7},{7,4},{8,9},{9,10},{10,1... | collective-permute-start | bytes 946184 | tf_op jit(solution)/shard_map/ppermute | solution.py:420
  349.2 3.9 collective-permute-done.25
  353.1 3.9 collective-permute-start.27
  361.3 3.1 fusion.11
  364.5 2.8 collective-permute-done.27
  369.9 3.3 collective-permute-start.28
  373.2 2.4 collective-permute-done.28
  378.0 4.0 all-to-all-start.1
  382.0 15.2 %all-to-all-done.1 = bf16[32,56,256]{2,1,0:T(8,128)(2,1)S(1)} async-done(((bf16[32,56,256]{2,1,0:T(8,128)(2,1)}), bf16[32,56,256]{2,1,0:T(8,128)(2,1)S(1)}, u32[]{:S(2)}, u32[]{:S(2)}) %all-to-all-start.1) | async-done | bytes 917536 | tf_op jit(solution)/shard_map/all_to_all | solution.py:434
  402.8 3.4 collective-permute-start.31
  409.4 2.5 collective-permute-done.31
  (111 shorter events, 57.5 us)
Async XLA Ops:
  0.6 256.4 %copy-start = (bf16[1,2048,176]{1,2,0:T(8,128)(2,1)S(1)}, bf16[1,2048,176]{1,2,0:T(8,128)(2,1)}, u32[]{:S(2)}) copy-start(bf16[1,2048,176]{1,2,0:T(8,128)(2,1)} %param.26) | copy-start | bytes 2162692
  40.4 8.0 %collective-permute-start.2 = (bf16[88,512]{1,0:T(8,128)(2,1)}, bf16[88,512]{1,0:T(8,128)(2,1)S(1)}, u32[]{:S(2)}, u32[]{:S(2)}) collective-permute-start(bf16[88,512]{1,0:T(8,128)(2,1)} %pick_rows.1), channel_id=1, source_target_pairs={{0,384},{128,0},{256,128},{384,256},{1,385},{129,1},{257,129},{385... | collective-permute-start | bytes 270344 | tf_op jit(solution)/shard_map/ppermute | solution.py:64
  44.3 7.5 %collective-permute-start = (bf16[88,512]{1,0:T(8,128)(2,1)}, bf16[88,512]{1,0:T(8,128)(2,1)S(1)}, u32[]{:S(2)}, u32[]{:S(2)}) collective-permute-start(bf16[88,512]{1,0:T(8,128)(2,1)} %pick_rows.1), channel_id=1, source_target_pairs={{0,128},{128,256},{256,384},{384,0},{1,129},{129,257},{257,385},{3... | collective-permute-start | bytes 270344 | tf_op jit(solution)/shard_map/ppermute | solution.py:64
  46.2 7.7 %collective-permute-start.1 = (bf16[88,512]{1,0:T(8,128)(2,1)}, bf16[88,512]{1,0:T(8,128)(2,1)S(1)}, u32[]{:S(2)}, u32[]{:S(2)}) collective-permute-start(bf16[88,512]{1,0:T(8,128)(2,1)} %pick_rows.1), channel_id=1, source_target_pairs={{0,256},{128,384},{256,0},{384,128},{1,257},{129,385},{257,1},{385... | collective-permute-start | bytes 270344 | tf_op jit(solution)/shard_map/ppermute | solution.py:64
  53.9 19.5 %copy-start.5 = (bf16[88,512]{1,0:T(8,128)(2,1)}, bf16[88,512]{1,0:T(8,128)(2,1)S(1)}, u32[]{:S(2)}) copy-start(bf16[88,512]{1,0:T(8,128)(2,1)S(1)} %collective-permute-done.1) | copy-start | bytes 270340
  54.9 10.7 %collective-permute-start.3 = (bf16[4,72,512]{2,1,0:T(8,128)(2,1)S(1)}, bf16[4,72,512]{2,1,0:T(8,128)(2,1)S(1)}, u32[]{:S(2)}, u32[]{:S(2)}) collective-permute-start(bf16[4,72,512]{2,1,0:T(8,128)(2,1)S(1)} %get-tuple-element.71), channel_id=1, source_target_pairs={{0,32},{32,64},{64,96},{96,0},{1,33},{33,65},{65,97},{97,1},{2,34}... | collective-permute-start | bytes 884744 | tf_op jit(solution)/shard_map/ppermute | solution.py:64
  58.1 12.2 %collective-permute-start.4 = (bf16[4,72,512]{2,1,0:T(8,128)(2,1)S(1)}, bf16[4,72,512]{2,1,0:T(8,128)(2,1)S(1)}, u32[]{:S(2)}, u32[]{:S(2)}) collective-permute-start(bf16[4,72,512]{2,1,0:T(8,128)(2,1)S(1)} %get-tuple-element.71), channel_id=1, source_target_pairs={{0,64},{32,96},{64,0},{96,32},{1,65},{33,97},{65,1},{97,33},{2,66}... | collective-permute-start | bytes 884744 | tf_op jit(solution)/shard_map/ppermute | solution.py:64
  62.6 10.7 %collective-permute-start.5 = (bf16[4,72,512]{2,1,0:T(8,128)(2,1)S(1)}, bf16[4,72,512]{2,1,0:T(8,128)(2,1)S(1)}, u32[]{:S(2)}, u32[]{:S(2)}) collective-permute-start(bf16[4,72,512]{2,1,0:T(8,128)(2,1)S(1)} %get-tuple-element.71), channel_id=1, source_target_pairs={{0,96},{32,0},{64,32},{96,64},{1,97},{33,1},{65,33},{97,65},{2,98}... | collective-permute-start | bytes 884744 | tf_op jit(solution)/shard_map/ppermute | solution.py:64
  73.5 26.3 %copy-start.3 = (bf16[4,4,72,512]{3,2,1,0:T(8,128)(2,1)}, bf16[4,4,72,512]{3,2,1,0:T(8,128)(2,1)S(1)}, u32[]{:S(2)}) copy-start(bf16[4,4,72,512]{3,2,1,0:T(8,128)(2,1)S(1)} %pad_maximum_fusion.2) | copy-start | bytes 3538948
  73.6 15.6 %collective-permute-start.6 = (bf16[16,40,512]{2,1,0:T(8,128)(2,1)S(1)}, bf16[16,40,512]{2,1,0:T(8,128)(2,1)S(1)}, u32[]{:S(2)}, u32[]{:S(2)}) collective-permute-start(bf16[16,40,512]{2,1,0:T(8,128)(2,1)S(1)} %get-tuple-element.55), channel_id=1, source_target_pairs={{0,8},{8,16},{16,24},{24,0},{1,9},{9,17},{17,25},{25,1},{2,10},{10... | collective-permute-start | bytes 1966088 | tf_op jit(solution)/shard_map/ppermute | solution.py:70
  76.8 14.4 %collective-permute-start.8 = (bf16[16,40,512]{2,1,0:T(8,128)(2,1)S(1)}, bf16[16,40,512]{2,1,0:T(8,128)(2,1)S(1)}, u32[]{:S(2)}, u32[]{:S(2)}) collective-permute-start(bf16[16,40,512]{2,1,0:T(8,128)(2,1)S(1)} %get-tuple-element.55), channel_id=1, source_target_pairs={{0,24},{8,0},{16,8},{24,16},{1,25},{9,1},{17,9},{25,17},{2,26},{10... | collective-permute-start | bytes 1966088 | tf_op jit(solution)/shard_map/ppermute | solution.py:70
  89.2 9.0 %collective-permute-start.7 = (bf16[8,40,512]{2,1,0:T(8,128)(2,1)S(1)}, bf16[8,40,512]{2,1,0:T(8,128)(2,1)S(1)}, u32[]{:S(2)}, u32[]{:S(2)}) collective-permute-start(bf16[8,40,512]{2,1,0:T(8,128)(2,1)S(1)} %slice.145), channel_id=1, source_target_pairs={{0,8},{8,16},{16,24},{24,0},{1,9},{9,17},{17,25},{25,1},{2,10},{10... | collective-permute-start | bytes 983048 | tf_op jit(solution)/shard_map/ppermute | solution.py:71
  91.2 8.6 %collective-permute-start.9 = (bf16[8,40,512]{2,1,0:T(8,128)(2,1)S(1)}, bf16[8,40,512]{2,1,0:T(8,128)(2,1)S(1)}, u32[]{:S(2)}, u32[]{:S(2)}) collective-permute-start(bf16[8,40,512]{2,1,0:T(8,128)(2,1)S(1)} %slice.146), channel_id=1, source_target_pairs={{0,24},{8,0},{16,8},{24,16},{1,25},{9,1},{17,9},{25,17},{2,26},{10... | collective-permute-start | bytes 983048 | tf_op jit(solution)/shard_map/ppermute | solution.py:71
  99.8 8.1 %copy-start.14 = (s32[1,4]{1,0:T(1,128)S(1)}, s32[1,4]{1,0:T(1,128)}, u32[]{:S(2)}) copy-start(s32[1,4]{1,0:T(1,128)} %param.15) | copy-start | bytes 52
  100.2 24.6 %copy-start.1 = (bf16[4,16,40,512]{3,2,1,0:T(8,128)(2,1)}, bf16[4,16,40,512]{3,2,1,0:T(8,128)(2,1)S(1)}, u32[]{:S(2)}) copy-start(bf16[4,16,40,512]{3,2,1,0:T(8,128)(2,1)S(1)} %pad_maximum_fusion) | copy-start | bytes 7864324
  100.2 12.4 %collective-permute-start.10 = (bf16[64,40,512]{2,1,0:T(8,128)(2,1)S(1)}, bf16[64,40,512]{2,1,0:T(8,128)(2,1)}, u32[]{:S(2)}, u32[]{:S(2)}) collective-permute-start(bf16[64,40,512]{2,1,0:T(8,128)(2,1)S(1)} %bitcast.120), channel_id=1, source_target_pairs={{0,4},{4,0},{1,5},{5,1},{2,6},{6,2},{3,7},{7,3},{8,12},{12,8},{9,1... | collective-permute-start | bytes 7864328 | tf_op jit(solution)/shard_map/ppermute | solution.py:76
  112.6 37.0 %collective-permute-start.11 = (bf16[16,32,512]{2,1,0:T(8,128)(2,1)}, bf16[16,32,512]{2,1,0:T(8,128)(2,1)}, u32[]{:S(2)}, u32[]{:S(2)}) collective-permute-start(bf16[16,32,512]{2,1,0:T(8,128)(2,1)} %slice.147), channel_id=1, source_target_pairs={{0,8},{8,16},{16,24},{24,0},{1,9},{9,17},{17,25},{25,1},{2,10},{10... | collective-permute-start | bytes 1572872 | tf_op jit(solution)/shard_map/ppermute | solution.py:64
  115.2 34.4 %collective-permute-start.12 = (bf16[16,32,512]{2,1,0:T(8,128)(2,1)}, bf16[16,32,512]{2,1,0:T(8,128)(2,1)}, u32[]{:S(2)}, u32[]{:S(2)}) collective-permute-start(bf16[16,32,512]{2,1,0:T(8,128)(2,1)} %slice.147), channel_id=1, source_target_pairs={{0,16},{8,24},{16,0},{24,8},{1,17},{9,25},{17,1},{25,9},{2,18},{10... | collective-permute-start | bytes 1572872 | tf_op jit(solution)/shard_map/ppermute | solution.py:64
  121.0 28.6 %collective-permute-start.13 = (bf16[16,32,512]{2,1,0:T(8,128)(2,1)}, bf16[16,32,512]{2,1,0:T(8,128)(2,1)}, u32[]{:S(2)}, u32[]{:S(2)}) collective-permute-start(bf16[16,32,512]{2,1,0:T(8,128)(2,1)} %slice.147), channel_id=1, source_target_pairs={{0,24},{8,0},{16,8},{24,16},{1,25},{9,1},{17,9},{25,17},{2,26},{10... | collective-permute-start | bytes 1572872 | tf_op jit(solution)/shard_map/ppermute | solution.py:64
  149.6 8.1 %copy-start.4 = (bf16[88,512]{1,0:T(8,128)(2,1)S(1)}, bf16[88,512]{1,0:T(8,128)(2,1)}, u32[]{:S(2)}) copy-start(bf16[88,512]{1,0:T(8,128)(2,1)} %pick_rows.1) | copy-start | bytes 270340
  149.6 8.1 %copy-start.6 = (bf16[88,512]{1,0:T(8,128)(2,1)S(1)}, bf16[88,512]{1,0:T(8,128)(2,1)}, u32[]{:S(2)}) copy-start(bf16[88,512]{1,0:T(8,128)(2,1)} %copy-done.5) | copy-start | bytes 270340
  151.4 10.2 %copy-start.2 = (bf16[4,16,32,512]{3,2,1,0:T(8,128)(2,1)}, bf16[4,16,32,512]{3,2,1,0:T(8,128)(2,1)S(1)}, u32[]{:S(2)}) copy-start(bf16[4,16,32,512]{3,2,1,0:T(8,128)(2,1)S(1)} %pad_maximum_fusion.1) | copy-start | bytes 6291460
  151.4 10.2 %collective-permute-start.14 = (bf16[64,32,512]{2,1,0:T(8,128)(2,1)S(1)}, bf16[64,32,512]{2,1,0:T(8,128)(2,1)}, u32[]{:S(2)}, u32[]{:S(2)}) collective-permute-start(bf16[64,32,512]{2,1,0:T(8,128)(2,1)S(1)} %bitcast.122), channel_id=1, source_target_pairs={{0,4},{4,0},{1,5},{5,1},{2,6},{6,2},{3,7},{7,3},{8,12},{12,8},{9,1... | collective-permute-start | bytes 6291464 | tf_op jit(solution)/shard_map/ppermute | solution.py:76
  168.7 11.8 %collective-permute-start.15 = (bf16[128,1024]{1,0:T(8,128)(2,1)}, bf16[128,1024]{1,0:T(8,128)(2,1)}, u32[]{:S(2)}, u32[]{:S(2)}) collective-permute-start(bf16[128,1024]{1,0:T(8,128)(2,1)} %get-tuple-element.26), channel_id=1, source_target_pairs={{0,128},{128,256},{256,384},{384,1},{1,129},{129,257},{257,385},{3... | collective-permute-start | bytes 786440 | tf_op jit(solution)/shard_map/ppermute | solution.py:392
  170.6 11.9 %collective-permute-start.19 = (bf16[128,1024]{1,0:T(8,128)(2,1)}, bf16[128,1024]{1,0:T(8,128)(2,1)}, u32[]{:S(2)}, u32[]{:S(2)}) collective-permute-start(bf16[128,1024]{1,0:T(8,128)(2,1)} %get-tuple-element.27), channel_id=1, source_target_pairs={{0,387},{128,0},{256,128},{384,256},{1,384},{129,1},{257,129},{385... | collective-permute-start | bytes 786440 | tf_op jit(solution)/shard_map/ppermute | solution.py:393
  175.2 14.8 %collective-permute-start.17 = (bf16[128,1024]{1,0:T(8,128)(2,1)}, bf16[128,1024]{1,0:T(8,128)(2,1)}, u32[]{:S(2)}, u32[]{:S(2)}) collective-permute-start(bf16[128,1024]{1,0:T(8,128)(2,1)} %get-tuple-element.26), channel_id=1, source_target_pairs={{0,387},{128,0},{256,128},{384,256},{1,384},{129,1},{257,129},{385... | collective-permute-start | bytes 786440 | tf_op jit(solution)/shard_map/ppermute | solution.py:395
  177.2 17.2 %collective-permute-start.18 = (bf16[128,1024]{1,0:T(8,128)(2,1)}, bf16[128,1024]{1,0:T(8,128)(2,1)}, u32[]{:S(2)}, u32[]{:S(2)}) collective-permute-start(bf16[128,1024]{1,0:T(8,128)(2,1)} %get-tuple-element.27), channel_id=1, source_target_pairs={{0,128},{128,256},{256,384},{384,1},{1,129},{129,257},{257,385},{3... | collective-permute-start | bytes 786440 | tf_op jit(solution)/shard_map/ppermute | solution.py:394
  180.5 12.5 %collective-permute-start.16 = (bf16[128,1024]{1,0:T(8,128)(2,1)}, bf16[128,1024]{1,0:T(8,128)(2,1)}, u32[]{:S(2)}, u32[]{:S(2)}) collective-permute-start(bf16[128,1024]{1,0:T(8,128)(2,1)} %collective-permute-done.15), channel_id=1, source_target_pairs={{0,128},{128,256},{256,384},{384,1},{1,129},{129,257},{257,385},{3... | collective-permute-start | bytes 786440 | tf_op jit(solution)/shard_map/ppermute | solution.py:396
  182.5 11.9 %collective-permute-start.20 = (bf16[128,1024]{1,0:T(8,128)(2,1)}, bf16[128,1024]{1,0:T(8,128)(2,1)}, u32[]{:S(2)}, u32[]{:S(2)}) collective-permute-start(bf16[128,1024]{1,0:T(8,128)(2,1)} %collective-permute-done.19), channel_id=1, source_target_pairs={{0,387},{128,0},{256,128},{384,256},{1,384},{129,1},{257,129},{385... | collective-permute-start | bytes 786440 | tf_op jit(solution)/shard_map/ppermute | solution.py:397
  190.0 4.3 %copy-start.10 = (bf16[128,1024]{1,0:T(8,128)(2,1)S(1)}, bf16[128,1024]{1,0:T(8,128)(2,1)}, u32[]{:S(2)}) copy-start(bf16[128,1024]{1,0:T(8,128)(2,1)} %get-tuple-element.27) | copy-start | bytes 786436
  197.6 56.0 %copy-start.8 = (bf16[1,2048,176]{1,2,0:T(8,128)(2,1)S(1)}, bf16[1,2048,176]{1,2,0:T(8,128)(2,1)}, u32[]{:S(2)}) copy-start(bf16[1,2048,176]{1,2,0:T(8,128)(2,1)} %param.25) | copy-start | bytes 2162692
  250.5 10.0 %collective-permute-start.21 = (bf16[1792,1024]{1,0:T(8,128)(2,1)}, bf16[1792,1024]{1,0:T(8,128)(2,1)}, u32[]{:S(2)}, u32[]{:S(2)}) collective-permute-start(bf16[1792,1024]{1,0:T(8,128)(2,1)} %bitcast.60), channel_id=1, source_target_pairs={{0,4},{4,0},{1,5},{5,1},{2,6},{6,2},{3,7},{7,3},{8,12},{12,8},{9,1... | collective-permute-start | bytes 11010056 | tf_op jit(solution)/shard_map/ppermute | solution.py:76
  263.9 17.9 %copy-start.7 = (bf16[1,704,512]{2,1,0:T(8,128)(2,1)S(1)}, bf16[1,704,512]{2,1,0:T(8,128)(2,1)}, u32[]{:S(2)}) copy-start(bf16[1,704,512]{2,1,0:T(8,128)(2,1)} %param.27) | copy-start | bytes 2162692
  268.4 75.4 %collective-permute-start.22 = (bf16[88,1792]{1,0:T(8,128)(2,1)S(1)}, bf16[88,1792]{1,0:T(8,128)(2,1)S(1)}, u32[]{:S(2)}, u32[]{:S(2)}) collective-permute-start(bf16[88,1792]{1,0:T(8,128)(2,1)S(1)} %get-tuple-element.60), channel_id=1, source_target_pairs={{0,1},{1,2},{2,3},{3,0},{4,5},{5,6},{6,7},{7,4},{8,9},{9,10},{10,1... | collective-permute-start | bytes 946184 | tf_op jit(solution)/shard_map/ppermute | solution.py:416
  272.7 84.3 %collective-permute-start.23 = (bf16[88,1792]{1,0:T(8,128)(2,1)S(1)}, bf16[88,1792]{1,0:T(8,128)(2,1)S(1)}, u32[]{:S(2)}, u32[]{:S(2)}) collective-permute-start(bf16[88,1792]{1,0:T(8,128)(2,1)S(1)} %get-tuple-element.59), channel_id=1, source_target_pairs={{0,1},{1,2},{2,3},{3,0},{4,5},{5,6},{6,7},{7,4},{8,9},{9,10},{10,1... | collective-permute-start | bytes 946184 | tf_op jit(solution)/shard_map/ppermute | solution.py:418
  277.7 75.4 %collective-permute-start.25 = (bf16[88,1792]{1,0:T(8,128)(2,1)S(1)}, bf16[88,1792]{1,0:T(8,128)(2,1)S(1)}, u32[]{:S(2)}, u32[]{:S(2)}) collective-permute-start(bf16[88,1792]{1,0:T(8,128)(2,1)S(1)} %get-tuple-element.59), channel_id=1, source_target_pairs={{0,3},{1,0},{2,1},{3,2},{4,7},{5,4},{6,5},{7,6},{8,11},{9,8},{10,9... | collective-permute-start | bytes 946184 | tf_op jit(solution)/shard_map/ppermute | solution.py:417
  281.9 77.9 %collective-permute-start.24 = (bf16[88,1792]{1,0:T(8,128)(2,1)S(1)}, bf16[88,1792]{1,0:T(8,128)(2,1)S(1)}, u32[]{:S(2)}, u32[]{:S(2)}) collective-permute-start(bf16[88,1792]{1,0:T(8,128)(2,1)S(1)} %get-tuple-element.60), channel_id=1, source_target_pairs={{0,3},{1,0},{2,1},{3,2},{4,7},{5,4},{6,5},{7,6},{8,11},{9,8},{10,9... | collective-permute-start | bytes 946184 | tf_op jit(solution)/shard_map/ppermute | solution.py:419
  343.8 20.7 %collective-permute-start.26 = (bf16[88,1792]{1,0:T(8,128)(2,1)S(1)}, bf16[88,1792]{1,0:T(8,128)(2,1)S(1)}, u32[]{:S(2)}, u32[]{:S(2)}) collective-permute-start(bf16[88,1792]{1,0:T(8,128)(2,1)S(1)} %collective-permute-done.22), channel_id=1, source_target_pairs={{0,1},{1,2},{2,3},{3,0},{4,5},{5,6},{6,7},{7,4},{8,9},{9,10},{10,1... | collective-permute-start | bytes 946184 | tf_op jit(solution)/shard_map/ppermute | solution.py:420
  353.1 14.2 %collective-permute-start.27 = (bf16[88,1792]{1,0:T(8,128)(2,1)S(1)}, bf16[88,1792]{1,0:T(8,128)(2,1)S(1)}, u32[]{:S(2)}, u32[]{:S(2)}) collective-permute-start(bf16[88,1792]{1,0:T(8,128)(2,1)S(1)} %collective-permute-done.25), channel_id=1, source_target_pairs={{0,3},{1,0},{2,1},{3,2},{4,7},{5,4},{6,5},{7,6},{8,11},{9,8},{10,9... | collective-permute-start | bytes 946184 | tf_op jit(solution)/shard_map/ppermute | solution.py:421
  369.9 5.8 %collective-permute-start.28 = (bf16[1792,256]{1,0:T(8,128)(2,1)}, bf16[1792,256]{1,0:T(8,128)(2,1)}, u32[]{:S(2)}, u32[]{:S(2)}) collective-permute-start(bf16[1792,256]{1,0:T(8,128)(2,1)} %constant_dynamic-slice_fusion), channel_id=1, source_target_pairs={{0,4},{4,0},{1,5},{5,1},{2,6},{6,2},{3,7},{7,3},{8,12},{12,8},{9,1... | collective-permute-start | bytes 2752520 | tf_op jit(solution)/shard_map/ppermute | solution.py:76
  378.0 19.2 %all-to-all-start.1 = ((bf16[32,56,256]{2,1,0:T(8,128)(2,1)}), bf16[32,56,256]{2,1,0:T(8,128)(2,1)S(1)}, u32[]{:S(2)}, u32[]{:S(2)}) async-start(bf16[32,56,256]{2,1,0:T(8,128)(2,1)} %bitcast.68), calls=%async_computation.1 | async-start | bytes 1835008 | tf_op jit(solution)/shard_map/all_to_all | solution.py:434
  397.3 9.0 %copy-start.12 = (bf16[128,128]{1,0:T(8,128)(2,1)S(1)}, bf16[128,128]{1,0:T(8,128)(2,1)}, u32[]{:S(2)}) copy-start(bf16[128,128]{1,0:T(8,128)(2,1)} %get-tuple-element.31) | copy-start | bytes 98308
  397.3 9.1 %copy-start.11 = (bf16[128,512]{1,0:T(8,128)(2,1)S(1)}, bf16[128,512]{1,0:T(8,128)(2,1)}, u32[]{:S(2)}) copy-start(bf16[128,512]{1,0:T(8,128)(2,1)} %get-tuple-element.30) | copy-start | bytes 393220
  398.0 1.0 copy-start.9
  398.0 14.9 %copy-start.13 = (bf16[128,512]{1,0:T(8,128)(2,1)S(1)}, bf16[128,512]{1,0:T(8,128)(2,1)}, u32[]{:S(2)}) copy-start(bf16[128,512]{1,0:T(8,128)(2,1)} %get-tuple-element.25) | copy-start | bytes 393220
  399.0 8.2 %collective-permute-start.29 = (bf16[2,128,256]{2,1,0:T(8,128)(2,1)S(1)}, bf16[2,128,256]{2,1,0:T(8,128)(2,1)S(1)}, u32[]{:S(2)}, u32[]{:S(2)}) collective-permute-start(bf16[2,128,256]{2,1,0:T(8,128)(2,1)S(1)} %get-tuple-element.61), channel_id=1, source_target_pairs={{0,384},{128,0},{256,128},{384,256},{1,385},{129,1},{257,129},{385... | collective-permute-start | bytes 393224 | tf_op jit(solution)/shard_map/ppermute | solution.py:444
  400.9 8.5 %collective-permute-start.30 = (bf16[2,128,256]{2,1,0:T(8,128)(2,1)S(1)}, bf16[2,128,256]{2,1,0:T(8,128)(2,1)S(1)}, u32[]{:S(2)}, u32[]{:S(2)}) collective-permute-start(bf16[2,128,256]{2,1,0:T(8,128)(2,1)S(1)} %get-tuple-element.63), channel_id=1, source_target_pairs={{0,256},{128,384},{256,0},{384,128},{1,257},{129,385},{257,1},{385... | collective-permute-start | bytes 393224 | tf_op jit(solution)/shard_map/ppermute | solution.py:444
  402.8 9.0 %collective-permute-start.31 = (bf16[2,128,256]{2,1,0:T(8,128)(2,1)S(1)}, bf16[2,128,256]{2,1,0:T(8,128)(2,1)S(1)}, u32[]{:S(2)}, u32[]{:S(2)}) collective-permute-start(bf16[2,128,256]{2,1,0:T(8,128)(2,1)S(1)} %get-tuple-element.62), channel_id=1, source_target_pairs={{0,128},{128,256},{256,384},{384,0},{1,129},{129,257},{257,385},{3... | collective-permute-start | bytes 393224 | tf_op jit(solution)/shard_map/ppermute | solution.py:444

commit v9 on v8

--- a/solution.py
+++ b/solution.py
@@ -412,13 +412,10 @@
     up_part = rows_by(up_mine, mine) + rows_by(up_other, theirs)
     own = (jax.nn.silu(gate_part) * up_part).astype(BF)
 
-    first, second = own[:88], own[88:]
-    below_first = lax.ppermute(first, T, UP)
-    above_second = lax.ppermute(second, T, DOWN)
-    below_second = lax.ppermute(second, T, UP)
-    above_first = lax.ppermute(first, T, DOWN)
-    far_first = lax.ppermute(below_first, T, UP)
-    far_second = lax.ppermute(above_second, T, DOWN)
+    below = lax.ppermute(own, T, UP)
+    above = lax.ppermute(own, T, DOWN)
+    far_first = lax.ppermute(below[:88], T, UP)
+    far_second = lax.ppermute(above[88:], T, DOWN)
 
     def out_of(pieces, at):
         rows = jnp.concatenate(pieces, axis=0)
@@ -427,7 +424,7 @@
             preferred_element_type=F32,
         )
 
-    half_out = (out_of([own, below_first, below_second, above_first, above_second], 0) + out_of([far_first, far_second], 528)).astype(BF)
+    half_out = (out_of([own, below, above], 0) + out_of([far_first, far_second], 528)).astype(BF)
     keep = lax.dynamic_slice_in_dim(half_out, core * 256, 256, 1)
     give = lax.dynamic_slice_in_dim(half_out, (1 - core) * 256, 256, 1)
     both = (keep.astype(F32) + other_core(give).astype(F32)).astype(BF)

time: 416 us -> 416 us (level)
    ppermute x3, starting transfers between devices: 7.2 us -> 18.9 us  [body(): lax.ppermute(sent, 'zl', [(j, (j - s) % 4) for j in range(4)]).astype(F32)]
    ppermute x1, waiting for transfers between devices: 9.07 us -> 0.01 us  [ring(): lax.ppermute(block, axis, UP)]
    ppermute x6 -> x4, starting transfers between devices: 26.9 us -> 18.4 us  [the longest x1 5.68 us: body(): below = lax.ppermute(own, T, UP)]
    ppermute x1, waiting for transfers between devices: 0.01 us -> 5.58 us  [ring(): lax.ppermute(block, axis, DOWN)]
    ppermute x6 -> x4, waiting for transfers between devices: 65.6 us -> 64.8 us  [the longest x1 38.8 us: body(): above = lax.ppermute(own, T, DOWN)]
  transfers between devices with their start and end apart: 33 -> 31, of which waited for: 18 -> 18; matrix products, arithmetic and copies ran while one was open for 6% -> 4% of each run, Pallas kernels for 2% -> 2%
where the time goes in v9:
time: 416 us; the launch traced here: 414 us
  waiting for transfers between devices  126 us (30%)
  starting transfers between devices  121 us (29%)
  blocking collectives  106 us (25%)
  matrix products  20.1 us (5%)
  Pallas kernels  17.7 us (4%)
  other arithmetic  14.7 us (4%)
  local copies, waits for them, and re-layouts  7.01 us (2%)
    all_to_all x1, blocking collectives, body(): lax.all_to_all(outgoing.reshape(2 * LAYER_ROWS, D // 2), LAYER, split_axi...  51.8 us
    ppermute x1, waiting for transfers between devices, body(): above = lax.ppermute(own, T, DOWN)  38.8 us
    all_gather x1, blocking collectives, body(): everything = lax.all_gather(packed, T, axis=1, tiled=True)  35.8 us
    ppermute x1, waiting for transfers between devices, body(): far_second = lax.ppermute(above[88:], T, DOWN)  26 us
    ppermute x9, starting transfers between devices, shifted(): lax.ppermute(block, axis, [(j, (j + s) % 4) for j in range(4)])  25.8 us
    ppermute x4, starting transfers between devices, other_core(): return lax.ppermute(block, 'c', [(0, 1), (1, 0)])  22.5 us
    ppermute x3, starting transfers between devices, body(): lax.ppermute(sent, 'zl', [(j, (j - s) % 4) for j in range(4)]).astype(F32)  18.9 us
    all_gather x1, blocking collectives, body(): attended_full = lax.all_gather(attended, T, axis=1, tiled=True)  18.3 us
  transfers between devices with their start and end apart: 31, of which 18 were waited for; matrix products, arithmetic and copies ran while one was open for 4% of the time, Pallas kernels for 2%

profile of v9, /device:TPU:1, one launch (start us, length us, event | category | flops | bytes accessed | tf_op | source)
XLA Modules:
  0.0 414.1 jit_solution(14145944410995717257)
XLA Ops:
  2.4 35.8 %all_gather.6.in_ref = bf16[160,2048]{1,0:T(8,128)(2,1)} all-gather(bf16[160,512]{1,0:T(8,128)(2,1)} %pack_rows.1), channel_id=1, replica_groups=mesh['zl'=4,'y'=4,'x'=4,'c'=2,'t'=4] {'t'}, dimensions={1}, use_global_device_ids=true | all-gather | bytes 819200 | tf_op jit(solution)/shard_map/all_gather | solution.py:317
  40.4 3.8 collective-permute-start.2
  46.2 2.2 collective-permute-start
  48.4 3.3 collective-permute-done.1
  51.7 2.2 collective-permute-done
  54.9 4.6 %collective-permute-start.5 = (bf16[4,72,512]{2,1,0:T(8,128)(2,1)S(1)}, bf16[4,72,512]{2,1,0:T(8,128)(2,1)S(1)}, u32[]{:S(2)}, u32[]{:S(2)}) collective-permute-start(bf16[4,72,512]{2,1,0:T(8,128)(2,1)S(1)} %get-tuple-element.69), channel_id=1, source_target_pairs={{0,96},{32,0},{64,32},{96,64},{1,97},{33,1},{65,33},{97,65},{2,98}... | collective-permute-start | bytes 884744 | tf_op jit(solution)/shard_map/ppermute | solution.py:64
  59.5 2.3 collective-permute-start.4
  61.8 2.6 collective-permute-start.3
  65.2 3.4 collective-permute-done.4
  68.6 3.4 collective-permute-done.3
  72.3 4.4 %collective-permute-start.8 = (bf16[16,40,512]{2,1,0:T(8,128)(2,1)S(1)}, bf16[16,40,512]{2,1,0:T(8,128)(2,1)S(1)}, u32[]{:S(2)}, u32[]{:S(2)}) collective-permute-start(bf16[16,40,512]{2,1,0:T(8,128)(2,1)S(1)} %get-tuple-element.55), channel_id=1, source_target_pairs={{0,24},{8,0},{16,8},{24,16},{1,25},{9,1},{17,9},{25,17},{2,26},{10... | collective-permute-start | bytes 1966088 | tf_op jit(solution)/shard_map/ppermute | solution.py:70
  78.6 5.6 %collective-permute-done.8 = bf16[16,40,512]{2,1,0:T(8,128)(2,1)S(1)} collective-permute-done((bf16[16,40,512]{2,1,0:T(8,128)(2,1)S(1)}, bf16[16,40,512]{2,1,0:T(8,128)(2,1)S(1)}, u32[]{:S(2)}, u32[]{:S(2)}) %collective-permute-start.8) | collective-permute-done | bytes 655392 | tf_op jit(solution)/shard_map/ppermute | solution.py:70
  84.2 5.0 %collective-permute-start.9 = (bf16[8,40,512]{2,1,0:T(8,128)(2,1)S(1)}, bf16[8,40,512]{2,1,0:T(8,128)(2,1)S(1)}, u32[]{:S(2)}, u32[]{:S(2)}) collective-permute-start(bf16[8,40,512]{2,1,0:T(8,128)(2,1)S(1)} %slice.146), channel_id=1, source_target_pairs={{0,24},{8,0},{16,8},{24,16},{1,25},{9,1},{17,9},{25,17},{2,26},{10... | collective-permute-start | bytes 983048 | tf_op jit(solution)/shard_map/ppermute | solution.py:71
  91.2 3.6 collective-permute-done.9
  94.8 5.3 %collective-permute-done.7 = bf16[8,40,512]{2,1,0:T(8,128)(2,1)S(1)} collective-permute-done((bf16[8,40,512]{2,1,0:T(8,128)(2,1)S(1)}, bf16[8,40,512]{2,1,0:T(8,128)(2,1)S(1)}, u32[]{:S(2)}, u32[]{:S(2)}) %collective-permute-start.7) | collective-permute-done | bytes 327712 | tf_op jit(solution)/shard_map/ppermute | solution.py:71
  100.5 11.0 %collective-permute-start.10 = (bf16[64,40,512]{2,1,0:T(8,128)(2,1)S(1)}, bf16[64,40,512]{2,1,0:T(8,128)(2,1)}, u32[]{:S(2)}, u32[]{:S(2)}) collective-permute-start(bf16[64,40,512]{2,1,0:T(8,128)(2,1)S(1)} %bitcast.117), channel_id=1, source_target_pairs={{0,4},{4,0},{1,5},{5,1},{2,6},{6,2},{3,7},{7,3},{8,12},{12,8},{9,1... | collective-permute-start | bytes 7864328 | tf_op jit(solution)/shard_map/ppermute | solution.py:76
  113.8 2.4 collective-permute-done.10.theirs_ref
  118.1 2.3 collective-permute-start.12
  120.5 4.2 %collective-permute-start.13 = (bf16[16,32,512]{2,1,0:T(8,128)(2,1)}, bf16[16,32,512]{2,1,0:T(8,128)(2,1)}, u32[]{:S(2)}, u32[]{:S(2)}) collective-permute-start(bf16[16,32,512]{2,1,0:T(8,128)(2,1)} %slice.147), channel_id=1, source_target_pairs={{0,24},{8,0},{16,8},{24,16},{1,25},{9,1},{17,9},{25,17},{2,26},{10... | collective-permute-start | bytes 1572872 | tf_op jit(solution)/shard_map/ppermute | solution.py:64
  126.5 7.2 %attention.1 = (bf16[128,256]{1,0:T(8,128)(2,1)}, bf16[128,512]{1,0:T(8,128)(2,1)}, bf16[128,128]{1,0:T(8,128)(2,1)}, bf16[512,512]{1,0:T(8,128)(2,1)}) custom-call(s32[5]{0:T(128)} %stack.113.place_ref, bf16[160,2048]{1,0:T(8,128)(2,1)} %all_gather.6.in_ref, bf16[64,40,512]{2,1,0:T(8,128)(2,1)} %bitcast.118, ...), custom_call_target="tpu_custom_call" | custom-call | tf_op jit(solution)/shard_map/attention/pallas_call | solution.py:222
  133.7 18.3 %all_gather.7.attended_ref = bf16[128,1024]{1,0:T(8,128)(2,1)} all-gather(bf16[128,256]{1,0:T(8,128)(2,1)} %get-tuple-element.18), channel_id=1, replica_groups=mesh['zl'=4,'y'=4,'x'=4,'c'=2,'t'=4] {'t'}, dimensions={1}, use_global_device_ids=true | all-gather | bytes 327680 | tf_op jit(solution)/shard_map/all_gather | solution.py:349
  153.9 5.9 %collective-permute-start.14 = (bf16[64,32,512]{2,1,0:T(8,128)(2,1)S(1)}, bf16[64,32,512]{2,1,0:T(8,128)(2,1)}, u32[]{:S(2)}, u32[]{:S(2)}) collective-permute-start(bf16[64,32,512]{2,1,0:T(8,128)(2,1)S(1)} %bitcast.119), channel_id=1, source_target_pairs={{0,4},{4,0},{1,5},{5,1},{2,6},{6,2},{3,7},{7,3},{8,12},{12,8},{9,1... | collective-permute-start | bytes 6291464 | tf_op jit(solution)/shard_map/ppermute | solution.py:76
  160.3 3.4 collective-permute-done.14.theirs_ref
  163.7 7.1 %mix.1 = (bf16[128,1024]{1,0:T(8,128)(2,1)}, bf16[128,1024]{1,0:T(8,128)(2,1)}, bf16[128,512]{1,0:T(8,128)(2,1)}, bf16[2048,256]{1,0:T(8,128)(2,1)}) custom-call(s32[5]{0:T(128)} %stack.113.place_ref, bf16[160,2048]{1,0:T(8,128)(2,1)} %all_gather.6.in_ref, bf16[128,1024]{1,0:T(8,128)(2,1)} %all_gather.7.attended_ref, bf16[64,32,512]{2,1,0:T(8,128)(2,1)} %bitcast.120, ...), custom_call_target="tpu_custom_call" | custom-call | tf_op jit(solution)/shard_map/mix/pallas_call | solution.py:280
  170.9 4.8 %collective-permute-start.19 = (bf16[128,1024]{1,0:T(8,128)(2,1)}, bf16[128,1024]{1,0:T(8,128)(2,1)}, u32[]{:S(2)}, u32[]{:S(2)}) collective-permute-start(bf16[128,1024]{1,0:T(8,128)(2,1)} %get-tuple-element.27), channel_id=1, source_target_pairs={{0,387},{128,0},{256,128},{384,256},{1,384},{129,1},{257,129},{385... | collective-permute-start | bytes 786440 | tf_op jit(solution)/shard_map/ppermute | solution.py:393
  179.6 4.6 %collective-permute-start.17 = (bf16[128,1024]{1,0:T(8,128)(2,1)}, bf16[128,1024]{1,0:T(8,128)(2,1)}, u32[]{:S(2)}, u32[]{:S(2)}) collective-permute-start(bf16[128,1024]{1,0:T(8,128)(2,1)} %get-tuple-element.26), channel_id=1, source_target_pairs={{0,387},{128,0},{256,128},{384,256},{1,384},{129,1},{257,129},{385... | collective-permute-start | bytes 786440 | tf_op jit(solution)/shard_map/ppermute | solution.py:395
  184.2 3.4 collective-permute-start.20
  189.5 2.4 add_convert_fusion.3
  192.5 2.3 collective-permute-done.20
  200.3 51.8 %all_to_all.21 = bf16[32,56,1024]{2,1,0:T(8,128)(2,1)} all-to-all(bf16[32,56,1024]{2,1,0:T(8,128)(2,1)S(1)} %bitcast.123), channel_id=1, replica_groups=mesh['zl'=4,'y'=4,'x'=4,'c'=2,'t'=4] {'c','y','x'}, dimensions={0} | all-to-all | bytes 7340032 | tf_op jit(solution)/shard_map/all_to_all | solution.py:407
  252.1 3.2 collective-permute-start.21
  255.3 3.4 fusion.23
  258.7 3.4 fusion.26
  262.1 3.4 convolution_add_fusion.1
  265.6 3.6 fusion.1
  269.1 3.5 collective-permute-start.23
  272.7 5.7 %collective-permute-start.22 = (bf16[176,1792]{1,0:T(8,128)(2,1)S(1)}, bf16[176,1792]{1,0:T(8,128)(2,1)S(1)}, u32[]{:S(2)}, u32[]{:S(2)}) collective-permute-start(bf16[176,1792]{1,0:T(8,128)(2,1)S(1)} %fusion.1), channel_id=1, source_target_pairs={{0,1},{1,2},{2,3},{3,0},{4,5},{5,6},{6,7},{7,4},{8,9},{9,10},{10,1... | collective-permute-start | bytes 1892360 | tf_op jit(solution)/shard_map/ppermute | solution.py:415
  278.3 38.8 %collective-permute-done.23 = bf16[176,1792]{1,0:T(8,128)(2,1)S(1)} collective-permute-done((bf16[176,1792]{1,0:T(8,128)(2,1)S(1)}, bf16[176,1792]{1,0:T(8,128)(2,1)S(1)}, u32[]{:S(2)}, u32[]{:S(2)}) %collective-permute-start.23) | collective-permute-done | bytes 630816 | tf_op jit(solution)/shard_map/ppermute | solution.py:416
  317.2 4.6 %collective-permute-start.25 = (bf16[88,1792]{1,0:T(8,128)(2,1)S(1)}, bf16[88,1792]{1,0:T(8,128)(2,1)S(1)}, u32[]{:S(2)}, u32[]{:S(2)}) collective-permute-start(bf16[88,1792]{1,0:T(8,128)(2,1)S(1)} %slice.161), channel_id=1, source_target_pairs={{0,3},{1,0},{2,1},{3,2},{4,7},{5,4},{6,5},{7,6},{8,11},{9,8},{10,9... | collective-permute-start | bytes 946184 | tf_op jit(solution)/shard_map/ppermute | solution.py:418
  322.6 4.6 %collective-permute-start.24 = (bf16[88,1792]{1,0:T(8,128)(2,1)S(1)}, bf16[88,1792]{1,0:T(8,128)(2,1)}, u32[]{:S(2)}, u32[]{:S(2)}) collective-permute-start(bf16[88,1792]{1,0:T(8,128)(2,1)S(1)} %slice.160), channel_id=1, source_target_pairs={{0,1},{1,2},{2,3},{3,0},{4,5},{5,6},{6,7},{7,4},{8,9},{9,10},{10,1... | collective-permute-start | bytes 946184 | tf_op jit(solution)/shard_map/ppermute | solution.py:417
  327.4 26.0 %collective-permute-done.25 = bf16[88,1792]{1,0:T(8,128)(2,1)S(1)} collective-permute-done((bf16[88,1792]{1,0:T(8,128)(2,1)S(1)}, bf16[88,1792]{1,0:T(8,128)(2,1)S(1)}, u32[]{:S(2)}, u32[]{:S(2)}) %collective-permute-start.25) | collective-permute-done | bytes 315424 | tf_op jit(solution)/shard_map/ppermute | solution.py:418
  357.6 2.4 collective-permute-start.26
  360.0 2.4 collective-permute-done.26
  362.5 2.4 add_convert_fusion.1
  364.8 4.0 all-to-all-start.1
  368.8 15.2 %all-to-all-done.1 = bf16[32,56,256]{2,1,0:T(8,128)(2,1)S(1)} async-done(((bf16[32,56,256]{2,1,0:T(8,128)(2,1)}), bf16[32,56,256]{2,1,0:T(8,128)(2,1)S(1)}, u32[]{:S(2)}, u32[]{:S(2)}) %all-to-all-start.1) | async-done | bytes 917536 | tf_op jit(solution)/shard_map/all_to_all | solution.py:431
  387.8 15.0 %collective-permute-start.28 = (bf16[2,128,256]{2,1,0:T(8,128)(2,1)S(1)}, bf16[2,128,256]{2,1,0:T(8,128)(2,1)S(1)}, u32[]{:S(2)}, u32[]{:S(2)}) collective-permute-start(bf16[2,128,256]{2,1,0:T(8,128)(2,1)S(1)} %get-tuple-element.61), channel_id=1, source_target_pairs={{0,256},{128,384},{256,0},{384,128},{1,257},{129,385},{257,1},{385... | collective-permute-start | bytes 393224 | tf_op jit(solution)/shard_map/ppermute | solution.py:441
  405.7 4.7 %collective-permute-done.28 = bf16[2,128,256]{2,1,0:T(8,128)(2,1)S(1)} collective-permute-done((bf16[2,128,256]{2,1,0:T(8,128)(2,1)S(1)}, bf16[2,128,256]{2,1,0:T(8,128)(2,1)S(1)}, u32[]{:S(2)}, u32[]{:S(2)}) %collective-permute-start.28) | collective-permute-done | bytes 131104 | tf_op jit(solution)/shard_map/ppermute | solution.py:441
  (116 shorter events, 47.7 us)
Async XLA Ops:
  0.6 258.1 %copy-start = (bf16[1,2048,176]{1,2,0:T(8,128)(2,1)S(1)}, bf16[1,2048,176]{1,2,0:T(8,128)(2,1)}, u32[]{:S(2)}) copy-start(bf16[1,2048,176]{1,2,0:T(8,128)(2,1)} %param.25) | copy-start | bytes 2162692
  40.4 8.0 %collective-permute-start.2 = (bf16[88,512]{1,0:T(8,128)(2,1)}, bf16[88,512]{1,0:T(8,128)(2,1)S(1)}, u32[]{:S(2)}, u32[]{:S(2)}) collective-permute-start(bf16[88,512]{1,0:T(8,128)(2,1)} %pick_rows.1), channel_id=1, source_target_pairs={{0,384},{128,0},{256,128},{384,256},{1,385},{129,1},{257,129},{385... | collective-permute-start | bytes 270344 | tf_op jit(solution)/shard_map/ppermute | solution.py:64
  44.2 7.5 %collective-permute-start.1 = (bf16[88,512]{1,0:T(8,128)(2,1)}, bf16[88,512]{1,0:T(8,128)(2,1)S(1)}, u32[]{:S(2)}, u32[]{:S(2)}) collective-permute-start(bf16[88,512]{1,0:T(8,128)(2,1)} %pick_rows.1), channel_id=1, source_target_pairs={{0,256},{128,384},{256,0},{384,128},{1,257},{129,385},{257,1},{385... | collective-permute-start | bytes 270344 | tf_op jit(solution)/shard_map/ppermute | solution.py:64
  46.2 7.7 %collective-permute-start = (bf16[88,512]{1,0:T(8,128)(2,1)}, bf16[88,512]{1,0:T(8,128)(2,1)S(1)}, u32[]{:S(2)}, u32[]{:S(2)}) collective-permute-start(bf16[88,512]{1,0:T(8,128)(2,1)} %pick_rows.1), channel_id=1, source_target_pairs={{0,128},{128,256},{256,384},{384,0},{1,129},{129,257},{257,385},{3... | collective-permute-start | bytes 270344 | tf_op jit(solution)/shard_map/ppermute | solution.py:64
  53.9 18.2 %copy-start.5 = (bf16[88,512]{1,0:T(8,128)(2,1)}, bf16[88,512]{1,0:T(8,128)(2,1)S(1)}, u32[]{:S(2)}) copy-start(bf16[88,512]{1,0:T(8,128)(2,1)S(1)} %collective-permute-done) | copy-start | bytes 270340
  54.9 10.3 %collective-permute-start.5 = (bf16[4,72,512]{2,1,0:T(8,128)(2,1)S(1)}, bf16[4,72,512]{2,1,0:T(8,128)(2,1)S(1)}, u32[]{:S(2)}, u32[]{:S(2)}) collective-permute-start(bf16[4,72,512]{2,1,0:T(8,128)(2,1)S(1)} %get-tuple-element.69), channel_id=1, source_target_pairs={{0,96},{32,0},{64,32},{96,64},{1,97},{33,1},{65,33},{97,65},{2,98}... | collective-permute-start | bytes 884744 | tf_op jit(solution)/shard_map/ppermute | solution.py:64
  59.5 9.1 %collective-permute-start.4 = (bf16[4,72,512]{2,1,0:T(8,128)(2,1)S(1)}, bf16[4,72,512]{2,1,0:T(8,128)(2,1)S(1)}, u32[]{:S(2)}, u32[]{:S(2)}) collective-permute-start(bf16[4,72,512]{2,1,0:T(8,128)(2,1)S(1)} %get-tuple-element.69), channel_id=1, source_target_pairs={{0,64},{32,96},{64,0},{96,32},{1,65},{33,97},{65,1},{97,33},{2,66}... | collective-permute-start | bytes 884744 | tf_op jit(solution)/shard_map/ppermute | solution.py:64
  61.8 10.2 %collective-permute-start.3 = (bf16[4,72,512]{2,1,0:T(8,128)(2,1)S(1)}, bf16[4,72,512]{2,1,0:T(8,128)(2,1)S(1)}, u32[]{:S(2)}, u32[]{:S(2)}) collective-permute-start(bf16[4,72,512]{2,1,0:T(8,128)(2,1)S(1)} %get-tuple-element.69), channel_id=1, source_target_pairs={{0,32},{32,64},{64,96},{96,0},{1,33},{33,65},{65,97},{97,1},{2,34}... | collective-permute-start | bytes 884744 | tf_op jit(solution)/shard_map/ppermute | solution.py:64
  72.2 28.0 %copy-start.3 = (bf16[4,4,72,512]{3,2,1,0:T(8,128)(2,1)}, bf16[4,4,72,512]{3,2,1,0:T(8,128)(2,1)S(1)}, u32[]{:S(2)}) copy-start(bf16[4,4,72,512]{3,2,1,0:T(8,128)(2,1)S(1)} %pad_maximum_fusion.2) | copy-start | bytes 3538948
  72.3 11.9 %collective-permute-start.8 = (bf16[16,40,512]{2,1,0:T(8,128)(2,1)S(1)}, bf16[16,40,512]{2,1,0:T(8,128)(2,1)S(1)}, u32[]{:S(2)}, u32[]{:S(2)}) collective-permute-start(bf16[16,40,512]{2,1,0:T(8,128)(2,1)S(1)} %get-tuple-element.55), channel_id=1, source_target_pairs={{0,24},{8,0},{16,8},{24,16},{1,25},{9,1},{17,9},{25,17},{2,26},{10... | collective-permute-start | bytes 1966088 | tf_op jit(solution)/shard_map/ppermute | solution.py:70
  76.7 12.6 %collective-permute-start.6 = (bf16[16,40,512]{2,1,0:T(8,128)(2,1)S(1)}, bf16[16,40,512]{2,1,0:T(8,128)(2,1)S(1)}, u32[]{:S(2)}, u32[]{:S(2)}) collective-permute-start(bf16[16,40,512]{2,1,0:T(8,128)(2,1)S(1)} %get-tuple-element.55), channel_id=1, source_target_pairs={{0,8},{8,16},{16,24},{24,0},{1,9},{9,17},{17,25},{25,1},{2,10},{10... | collective-permute-start | bytes 1966088 | tf_op jit(solution)/shard_map/ppermute | solution.py:70
  84.2 10.6 %collective-permute-start.9 = (bf16[8,40,512]{2,1,0:T(8,128)(2,1)S(1)}, bf16[8,40,512]{2,1,0:T(8,128)(2,1)S(1)}, u32[]{:S(2)}, u32[]{:S(2)}) collective-permute-start(bf16[8,40,512]{2,1,0:T(8,128)(2,1)S(1)} %slice.146), channel_id=1, source_target_pairs={{0,24},{8,0},{16,8},{24,16},{1,25},{9,1},{17,9},{25,17},{2,26},{10... | collective-permute-start | bytes 983048 | tf_op jit(solution)/shard_map/ppermute | solution.py:71
  89.3 10.8 %collective-permute-start.7 = (bf16[8,40,512]{2,1,0:T(8,128)(2,1)S(1)}, bf16[8,40,512]{2,1,0:T(8,128)(2,1)S(1)}, u32[]{:S(2)}, u32[]{:S(2)}) collective-permute-start(bf16[8,40,512]{2,1,0:T(8,128)(2,1)S(1)} %slice.145), channel_id=1, source_target_pairs={{0,8},{8,16},{16,24},{24,0},{1,9},{9,17},{17,25},{25,1},{2,10},{10... | collective-permute-start | bytes 983048 | tf_op jit(solution)/shard_map/ppermute | solution.py:71
  100.2 11.4 %copy-start.20 = (s32[1,4]{1,0:T(1,128)S(1)}, s32[1,4]{1,0:T(1,128)}, u32[]{:S(2)}) copy-start(s32[1,4]{1,0:T(1,128)} %param.15) | copy-start | bytes 52
  100.5 26.0 %copy-start.1 = (bf16[4,16,40,512]{3,2,1,0:T(8,128)(2,1)}, bf16[4,16,40,512]{3,2,1,0:T(8,128)(2,1)S(1)}, u32[]{:S(2)}) copy-start(bf16[4,16,40,512]{3,2,1,0:T(8,128)(2,1)S(1)} %pad_maximum_fusion) | copy-start | bytes 7864324
  100.5 15.7 %collective-permute-start.10 = (bf16[64,40,512]{2,1,0:T(8,128)(2,1)S(1)}, bf16[64,40,512]{2,1,0:T(8,128)(2,1)}, u32[]{:S(2)}, u32[]{:S(2)}) collective-permute-start(bf16[64,40,512]{2,1,0:T(8,128)(2,1)S(1)} %bitcast.117), channel_id=1, source_target_pairs={{0,4},{4,0},{1,5},{5,1},{2,6},{6,2},{3,7},{7,3},{8,12},{12,8},{9,1... | collective-permute-start | bytes 7864328 | tf_op jit(solution)/shard_map/ppermute | solution.py:76
  116.2 35.8 %collective-permute-start.11 = (bf16[16,32,512]{2,1,0:T(8,128)(2,1)}, bf16[16,32,512]{2,1,0:T(8,128)(2,1)}, u32[]{:S(2)}, u32[]{:S(2)}) collective-permute-start(bf16[16,32,512]{2,1,0:T(8,128)(2,1)} %slice.147), channel_id=1, source_target_pairs={{0,8},{8,16},{16,24},{24,0},{1,9},{9,17},{17,25},{25,1},{2,10},{10... | collective-permute-start | bytes 1572872 | tf_op jit(solution)/shard_map/ppermute | solution.py:64
  118.1 33.9 %collective-permute-start.12 = (bf16[16,32,512]{2,1,0:T(8,128)(2,1)}, bf16[16,32,512]{2,1,0:T(8,128)(2,1)}, u32[]{:S(2)}, u32[]{:S(2)}) collective-permute-start(bf16[16,32,512]{2,1,0:T(8,128)(2,1)} %slice.147), channel_id=1, source_target_pairs={{0,16},{8,24},{16,0},{24,8},{1,17},{9,25},{17,1},{25,9},{2,18},{10... | collective-permute-start | bytes 1572872 | tf_op jit(solution)/shard_map/ppermute | solution.py:64
  120.5 31.5 %collective-permute-start.13 = (bf16[16,32,512]{2,1,0:T(8,128)(2,1)}, bf16[16,32,512]{2,1,0:T(8,128)(2,1)}, u32[]{:S(2)}, u32[]{:S(2)}) collective-permute-start(bf16[16,32,512]{2,1,0:T(8,128)(2,1)} %slice.147), channel_id=1, source_target_pairs={{0,24},{8,0},{16,8},{24,16},{1,25},{9,1},{17,9},{25,17},{2,26},{10... | collective-permute-start | bytes 1572872 | tf_op jit(solution)/shard_map/ppermute | solution.py:64
  152.0 7.8 %copy-start.4 = (bf16[88,512]{1,0:T(8,128)(2,1)S(1)}, bf16[88,512]{1,0:T(8,128)(2,1)}, u32[]{:S(2)}) copy-start(bf16[88,512]{1,0:T(8,128)(2,1)} %pick_rows.1) | copy-start | bytes 270340
  152.0 7.8 %copy-start.6 = (bf16[88,512]{1,0:T(8,128)(2,1)S(1)}, bf16[88,512]{1,0:T(8,128)(2,1)}, u32[]{:S(2)}) copy-start(bf16[88,512]{1,0:T(8,128)(2,1)} %copy-done.5) | copy-start | bytes 270340
  153.9 9.9 %copy-start.2 = (bf16[4,16,32,512]{3,2,1,0:T(8,128)(2,1)}, bf16[4,16,32,512]{3,2,1,0:T(8,128)(2,1)S(1)}, u32[]{:S(2)}) copy-start(bf16[4,16,32,512]{3,2,1,0:T(8,128)(2,1)S(1)} %pad_maximum_fusion.1) | copy-start | bytes 6291460
  153.9 9.9 %collective-permute-start.14 = (bf16[64,32,512]{2,1,0:T(8,128)(2,1)S(1)}, bf16[64,32,512]{2,1,0:T(8,128)(2,1)}, u32[]{:S(2)}, u32[]{:S(2)}) collective-permute-start(bf16[64,32,512]{2,1,0:T(8,128)(2,1)S(1)} %bitcast.119), channel_id=1, source_target_pairs={{0,4},{4,0},{1,5},{5,1},{2,6},{6,2},{3,7},{7,3},{8,12},{12,8},{9,1... | collective-permute-start | bytes 6291464 | tf_op jit(solution)/shard_map/ppermute | solution.py:76
  170.9 13.3 %collective-permute-start.19 = (bf16[128,1024]{1,0:T(8,128)(2,1)}, bf16[128,1024]{1,0:T(8,128)(2,1)}, u32[]{:S(2)}, u32[]{:S(2)}) collective-permute-start(bf16[128,1024]{1,0:T(8,128)(2,1)} %get-tuple-element.27), channel_id=1, source_target_pairs={{0,387},{128,0},{256,128},{384,256},{1,384},{129,1},{257,129},{385... | collective-permute-start | bytes 786440 | tf_op jit(solution)/shard_map/ppermute | solution.py:393
  175.7 11.9 %collective-permute-start.15 = (bf16[128,1024]{1,0:T(8,128)(2,1)}, bf16[128,1024]{1,0:T(8,128)(2,1)}, u32[]{:S(2)}, u32[]{:S(2)}) collective-permute-start(bf16[128,1024]{1,0:T(8,128)(2,1)} %get-tuple-element.26), channel_id=1, source_target_pairs={{0,128},{128,256},{256,384},{384,1},{1,129},{129,257},{257,385},{3... | collective-permute-start | bytes 786440 | tf_op jit(solution)/shard_map/ppermute | solution.py:392
  177.7 14.8 %collective-permute-start.18 = (bf16[128,1024]{1,0:T(8,128)(2,1)}, bf16[128,1024]{1,0:T(8,128)(2,1)}, u32[]{:S(2)}, u32[]{:S(2)}) collective-permute-start(bf16[128,1024]{1,0:T(8,128)(2,1)} %get-tuple-element.27), channel_id=1, source_target_pairs={{0,128},{128,256},{256,384},{384,1},{1,129},{129,257},{257,385},{3... | collective-permute-start | bytes 786440 | tf_op jit(solution)/shard_map/ppermute | solution.py:394
  179.6 16.5 %collective-permute-start.17 = (bf16[128,1024]{1,0:T(8,128)(2,1)}, bf16[128,1024]{1,0:T(8,128)(2,1)}, u32[]{:S(2)}, u32[]{:S(2)}) collective-permute-start(bf16[128,1024]{1,0:T(8,128)(2,1)} %get-tuple-element.26), channel_id=1, source_target_pairs={{0,387},{128,0},{256,128},{384,256},{1,384},{129,1},{257,129},{385... | collective-permute-start | bytes 786440 | tf_op jit(solution)/shard_map/ppermute | solution.py:395
  184.2 10.6 %collective-permute-start.20 = (bf16[128,1024]{1,0:T(8,128)(2,1)}, bf16[128,1024]{1,0:T(8,128)(2,1)}, u32[]{:S(2)}, u32[]{:S(2)}) collective-permute-start(bf16[128,1024]{1,0:T(8,128)(2,1)} %collective-permute-done.19), channel_id=1, source_target_pairs={{0,387},{128,0},{256,128},{384,256},{1,384},{129,1},{257,129},{385... | collective-permute-start | bytes 786440 | tf_op jit(solution)/shard_map/ppermute | solution.py:397
  187.6 9.4 %collective-permute-start.16 = (bf16[128,1024]{1,0:T(8,128)(2,1)}, bf16[128,1024]{1,0:T(8,128)(2,1)}, u32[]{:S(2)}, u32[]{:S(2)}) collective-permute-start(bf16[128,1024]{1,0:T(8,128)(2,1)} %collective-permute-done.15), channel_id=1, source_target_pairs={{0,128},{128,256},{256,384},{384,1},{1,129},{129,257},{257,385},{3... | collective-permute-start | bytes 786440 | tf_op jit(solution)/shard_map/ppermute | solution.py:396
  200.3 55.0 %copy-start.10 = (bf16[1,2048,176]{1,2,0:T(8,128)(2,1)S(1)}, bf16[1,2048,176]{1,2,0:T(8,128)(2,1)}, u32[]{:S(2)}) copy-start(bf16[1,2048,176]{1,2,0:T(8,128)(2,1)} %param.26) | copy-start | bytes 2162692
  252.1 10.0 %collective-permute-start.21 = (bf16[1792,1024]{1,0:T(8,128)(2,1)}, bf16[1792,1024]{1,0:T(8,128)(2,1)}, u32[]{:S(2)}, u32[]{:S(2)}) collective-permute-start(bf16[1792,1024]{1,0:T(8,128)(2,1)} %bitcast.60), channel_id=1, source_target_pairs={{0,4},{4,0},{1,5},{5,1},{2,6},{6,2},{3,7},{7,3},{8,12},{12,8},{9,1... | collective-permute-start | bytes 11010056 | tf_op jit(solution)/shard_map/ppermute | solution.py:76
  265.6 61.7 %copy-start.7 = (bf16[1,704,512]{2,1,0:T(8,128)(2,1)S(1)}, bf16[1,704,512]{2,1,0:T(8,128)(2,1)}, u32[]{:S(2)}) copy-start(bf16[1,704,512]{2,1,0:T(8,128)(2,1)} %param.27) | copy-start | bytes 2162692
  269.1 52.7 %copy-start.18 = (bf16[176,1792]{1,0:T(8,128)(2,1)}, bf16[176,1792]{1,0:T(8,128)(2,1)S(1)}, u32[]{:S(2)}) copy-start(bf16[176,1792]{1,0:T(8,128)(2,1)S(1)} %fusion.1) | copy-start | bytes 1892356
  269.1 48.0 %collective-permute-start.23 = (bf16[176,1792]{1,0:T(8,128)(2,1)S(1)}, bf16[176,1792]{1,0:T(8,128)(2,1)S(1)}, u32[]{:S(2)}, u32[]{:S(2)}) collective-permute-start(bf16[176,1792]{1,0:T(8,128)(2,1)S(1)} %fusion.1), channel_id=1, source_target_pairs={{0,3},{1,0},{2,1},{3,2},{4,7},{5,4},{6,5},{7,6},{8,11},{9,8},{10,9... | collective-permute-start | bytes 1892360 | tf_op jit(solution)/shard_map/ppermute | solution.py:416
  272.7 49.1 %collective-permute-start.22 = (bf16[176,1792]{1,0:T(8,128)(2,1)S(1)}, bf16[176,1792]{1,0:T(8,128)(2,1)S(1)}, u32[]{:S(2)}, u32[]{:S(2)}) collective-permute-start(bf16[176,1792]{1,0:T(8,128)(2,1)S(1)} %fusion.1), channel_id=1, source_target_pairs={{0,1},{1,2},{2,3},{3,0},{4,5},{5,6},{6,7},{7,4},{8,9},{9,10},{10,1... | collective-permute-start | bytes 1892360 | tf_op jit(solution)/shard_map/ppermute | solution.py:415
  317.2 36.2 %collective-permute-start.25 = (bf16[88,1792]{1,0:T(8,128)(2,1)S(1)}, bf16[88,1792]{1,0:T(8,128)(2,1)S(1)}, u32[]{:S(2)}, u32[]{:S(2)}) collective-permute-start(bf16[88,1792]{1,0:T(8,128)(2,1)S(1)} %slice.161), channel_id=1, source_target_pairs={{0,3},{1,0},{2,1},{3,2},{4,7},{5,4},{6,5},{7,6},{8,11},{9,8},{10,9... | collective-permute-start | bytes 946184 | tf_op jit(solution)/shard_map/ppermute | solution.py:418
  322.6 30.7 %collective-permute-start.24 = (bf16[88,1792]{1,0:T(8,128)(2,1)S(1)}, bf16[88,1792]{1,0:T(8,128)(2,1)}, u32[]{:S(2)}, u32[]{:S(2)}) collective-permute-start(bf16[88,1792]{1,0:T(8,128)(2,1)S(1)} %slice.160), channel_id=1, source_target_pairs={{0,1},{1,2},{2,3},{3,0},{4,5},{5,6},{6,7},{7,4},{8,9},{9,10},{10,1... | collective-permute-start | bytes 946184 | tf_op jit(solution)/shard_map/ppermute | solution.py:417
  327.3 27.7 %copy-start.12 = (bf16[176,1792]{1,0:T(8,128)(2,1)S(1)}, bf16[176,1792]{1,0:T(8,128)(2,1)}, u32[]{:S(2)}) copy-start(bf16[176,1792]{1,0:T(8,128)(2,1)} %copy-done.11) | copy-start | bytes 1892356
  327.3 27.7 %copy-start.14 = (bf16[176,1792]{1,0:T(8,128)(2,1)S(1)}, bf16[176,1792]{1,0:T(8,128)(2,1)}, u32[]{:S(2)}) copy-start(bf16[176,1792]{1,0:T(8,128)(2,1)} %copy-done.13) | copy-start | bytes 1892356
  327.4 27.7 %copy-start.19 = (bf16[176,1792]{1,0:T(8,128)(2,1)S(1)}, bf16[176,1792]{1,0:T(8,128)(2,1)}, u32[]{:S(2)}) copy-start(bf16[176,1792]{1,0:T(8,128)(2,1)} %copy-done.18) | copy-start | bytes 1892356
  357.6 4.8 %collective-permute-start.26 = (bf16[1792,256]{1,0:T(8,128)(2,1)}, bf16[1792,256]{1,0:T(8,128)(2,1)}, u32[]{:S(2)}, u32[]{:S(2)}) collective-permute-start(bf16[1792,256]{1,0:T(8,128)(2,1)} %constant_dynamic-slice_fusion), channel_id=1, source_target_pairs={{0,4},{4,0},{1,5},{5,1},{2,6},{6,2},{3,7},{7,3},{8,12},{12,8},{9,1... | collective-permute-start | bytes 2752520 | tf_op jit(solution)/shard_map/ppermute | solution.py:76
  364.8 19.2 %all-to-all-start.1 = ((bf16[32,56,256]{2,1,0:T(8,128)(2,1)}), bf16[32,56,256]{2,1,0:T(8,128)(2,1)S(1)}, u32[]{:S(2)}, u32[]{:S(2)}) async-start(bf16[32,56,256]{2,1,0:T(8,128)(2,1)} %bitcast.68), calls=%async_computation.1 | async-start | bytes 1835008 | tf_op jit(solution)/shard_map/all_to_all | solution.py:431
  384.1 20.6 %copy-start.16 = (bf16[128,128]{1,0:T(8,128)(2,1)S(1)}, bf16[128,128]{1,0:T(8,128)(2,1)}, u32[]{:S(2)}) copy-start(bf16[128,128]{1,0:T(8,128)(2,1)} %get-tuple-element.31) | copy-start | bytes 98308
  384.1 20.7 %copy-start.15 = (bf16[128,512]{1,0:T(8,128)(2,1)S(1)}, bf16[128,512]{1,0:T(8,128)(2,1)}, u32[]{:S(2)}) copy-start(bf16[128,512]{1,0:T(8,128)(2,1)} %get-tuple-element.30) | copy-start | bytes 393220
  384.8 28.6 %copy-start.17 = (bf16[128,512]{1,0:T(8,128)(2,1)S(1)}, bf16[128,512]{1,0:T(8,128)(2,1)}, u32[]{:S(2)}) copy-start(bf16[128,512]{1,0:T(8,128)(2,1)} %get-tuple-element.25) | copy-start | bytes 393220
  385.8 19.9 %collective-permute-start.29 = (bf16[2,128,256]{2,1,0:T(8,128)(2,1)S(1)}, bf16[2,128,256]{2,1,0:T(8,128)(2,1)S(1)}, u32[]{:S(2)}, u32[]{:S(2)}) collective-permute-start(bf16[2,128,256]{2,1,0:T(8,128)(2,1)S(1)} %get-tuple-element.60), channel_id=1, source_target_pairs={{0,128},{128,256},{256,384},{384,0},{1,129},{129,257},{257,385},{3... | collective-permute-start | bytes 393224 | tf_op jit(solution)/shard_map/ppermute | solution.py:441
  387.8 22.6 %collective-permute-start.28 = (bf16[2,128,256]{2,1,0:T(8,128)(2,1)S(1)}, bf16[2,128,256]{2,1,0:T(8,128)(2,1)S(1)}, u32[]{:S(2)}, u32[]{:S(2)}) collective-permute-start(bf16[2,128,256]{2,1,0:T(8,128)(2,1)S(1)} %get-tuple-element.61), channel_id=1, source_target_pairs={{0,256},{128,384},{256,0},{384,128},{1,257},{129,385},{257,1},{385... | collective-permute-start | bytes 393224 | tf_op jit(solution)/shard_map/ppermute | solution.py:441
  402.8 9.6 %collective-permute-start.27 = (bf16[2,128,256]{2,1,0:T(8,128)(2,1)S(1)}, bf16[2,128,256]{2,1,0:T(8,128)(2,1)S(1)}, u32[]{:S(2)}, u32[]{:S(2)}) collective-permute-start(bf16[2,128,256]{2,1,0:T(8,128)(2,1)S(1)} %get-tuple-element.59), channel_id=1, source_target_pairs={{0,384},{128,0},{256,128},{384,256},{1,385},{129,1},{257,129},{385... | collective-permute-start | bytes 393224 | tf_op jit(solution)/shard_map/ppermute | solution.py:441
  (4 other events, 11.0 us)
